TPU v7x, 32 devices: a whole 2x2x4 slice. The times are simulated.
32 devices in a mesh: ctx: 16 (over z, y, core), fsdp: 2 (over x).
Axes of the slice: x: 2, y: 2, z: 4, core: 2. Of those that a mesh axis runs over, the one named last changes fastest.
Arguments:
- tokens: bfloat16 [2, 16, 2, 128, 2048], P('fsdp', 'ctx'), may hold values from -6 to 6
- grad_out: bfloat16 [2, 16, 2, 128, 2048], P('fsdp', 'ctx'), may hold values from -6 to 6
- segments: int32 [2, 4096], replicated, may hold values from 0 to 3, as said below
- w_query: bfloat16 [2048, 2048], P('ctx', 'fsdp'), may hold values from -0.125 to 0.125
- key_weight_matrix: bfloat16 [2048, 1024], P('ctx', 'fsdp'), may hold values from -0.125 to 0.125
- value_weight_matrix: bfloat16 [2048, 1024], P('ctx', 'fsdp'), may hold values from -0.125 to 0.125
- w_output: bfloat16 [2048, 2048], P('ctx', 'fsdp'), may hold values from -0.75 to 0.75
- w_gate: bfloat16 [2048, 6144], P('ctx', 'fsdp'), may hold values from -0.125 to 0.125
- w_up: bfloat16 [2048, 6144], P('ctx', 'fsdp'), may hold values from -0.125 to 0.125
- w_down: bfloat16 [2048, 6144], P('ctx', 'fsdp'), may hold values from -0.078125 to 0.078125
- norm_attn: float32 [2048], replicated, may hold values from 0.5 to 1.5
- norm_mlp: float32 [2048], replicated, may hold values from 0.5 to 1.5
- norm_query: float32 [128], replicated, may hold values from 0.25 to 1.75
- norm_key: float32 [128], replicated, may hold values from 0.25 to 1.75
Outputs:
- out_tokens: bfloat16 [2, 16, 2, 128, 2048], P('fsdp', 'ctx')
- grad_tokens: float32 [2, 16, 2, 128, 2048], P('fsdp', 'ctx')
- grad_query: float32 [2048, 2048], P('ctx', 'fsdp')
- grad_key: float32 [2048, 1024], P('ctx', 'fsdp')
- grad_value: float32 [2048, 1024], P('ctx', 'fsdp')
- grad_output: float32 [2048, 2048], P('ctx', 'fsdp')
- grad_gate: float32 [2048, 6144], P('ctx', 'fsdp')
- grad_up: float32 [2048, 6144], P('ctx', 'fsdp')
- grad_down: float32 [2048, 6144], P('ctx', 'fsdp')
- grad_norm_attn: float32 [2048], replicated
- grad_norm_mlp: float32 [2048], replicated
- grad_norm_query: float32 [128], replicated
- grad_norm_key: float32 [128], replicated
Inputs may be any that keep to these rules, and one draw needn't show every extreme that they name: `segments`: in every sequence segment numbers never fall and each of 0 to 3 occurs; every document has 205 to 1843 tokens, and in every sequence one document has exactly 1843.
All inputs are finite; a program needn't handle non-finite values.
Results may differ from a plain program's by a relative error of at most 0.023.
Values may be sent and summed in bfloat16 or wider, within the bound.
No kernel may reach another device: no remote copies, remote signals or barrier semaphores. Data moves between devices by JAX's collectives and lax.ppermute only.
A program may use at most 320 MiB of HBM per device.

v0:
```python
import math

import jax
import jax.numpy as jnp
from jax import lax
from jax.sharding import PartitionSpec as P

QUERY_HEADS = 16
KEY_VALUE_HEADS = 8
HEAD_FEATURES = 128


eps = 1e-06
rope_base = 1000000.0
masked_value = -1e30


def rms_scale(values, gain):
    return values * lax.rsqrt(jnp.mean(values * values, axis=-1, keepdims=True) + eps) * gain


def rotate(values, cosine, sine):
    half_width = values.shape[-1] // 2
    turned = jnp.concatenate([-values[..., half_width:], values[..., :half_width]], axis=-1)
    return values * cosine + turned * sine


def doc_positions(segments):
    index = jnp.arange(segments.shape[-1], dtype=jnp.int32)
    first = jnp.concatenate(
        [jnp.ones_like(segments[..., :1], dtype=bool), segments[..., 1:] != segments[..., :-1]],
        axis=-1,
    )
    starts = lax.cummax(jnp.where(first, index, 0), axis=segments.ndim - 1)
    return index - starts


def rope_tables(positions):
    freq = jnp.exp(
        jnp.arange(HEAD_FEATURES // 2, dtype=jnp.float32)
        * (-2.0 * math.log(rope_base) / HEAD_FEATURES)
    )
    angle = positions.astype(jnp.float32)[..., None] * freq
    angle = jnp.concatenate([angle, angle], axis=-1)
    return (jnp.cos(angle), jnp.sin(angle))


def head_prep(values, gain, cosine, sine):
    return rotate(rms_scale(values, gain), cosine, sine)


def swiglu(gate, up_part):
    return gate / (1.0 + jnp.exp(-gate)) * up_part


def to_sequence(blocks):
    ordered = jnp.concatenate([blocks[:, :, 0], blocks[:, ::-1, 1]], axis=1)
    return ordered.reshape(blocks.shape[0], -1, blocks.shape[-1])


def to_blocks(ordered, block_rows):
    pair_count = ordered.shape[1] // (2 * block_rows)
    split = ordered.reshape(ordered.shape[0], 2 * pair_count, block_rows, ordered.shape[-1])
    return jnp.stack([split[:, :pair_count], split[:, pair_count:][:, ::-1]], axis=2)


def contract_rows(left, right):
    return lax.dot_general(
        left, right, (((0,), (0,)), ((), ())), preferred_element_type=jnp.float32
    )


def contract_cols(left, right):
    return lax.dot_general(
        left, right, (((1,), (1,)), ((), ())), preferred_element_type=jnp.float32
    )


def masked_scores(queries, keys, query_index, query_segment, key_index, key_segment):
    products = contract_cols(queries, keys) * HEAD_FEATURES ** (-0.5)
    valid = (query_segment[:, None] == key_segment[None, :]) & (
        key_index[None, :] <= query_index[:, None]
    )
    return jnp.where(valid, products, masked_value)


def key_parts(sequence_length):
    return [(None, 0, sequence_length)]


def add_window(running, part, start):
    current = lax.dynamic_slice_in_dim(running, start, part.shape[0], 0)
    return lax.dynamic_update_slice_in_dim(running, current + part, start, 0)


def attend_sequence(queries, keys, values, segment, query_index, heads_per_group):
    sequence_length = keys.shape[0]
    key_index = jnp.arange(sequence_length, dtype=jnp.int32)
    query_segment = segment[query_index]
    head_outputs, head_sums = ([], [])
    for head in range(keys.shape[1] // HEAD_FEATURES):
        head_keys = keys[:, head * HEAD_FEATURES : (head + 1) * HEAD_FEATURES]
        head_values = values[:, head * HEAD_FEATURES : (head + 1) * HEAD_FEATURES]
        part_outputs, part_sums = ([], [])
        for half, start, span_length in key_parts(sequence_length):
            rows = queries[:, :, head * heads_per_group : (head + 1) * heads_per_group]
            shape_rows = rows.shape
            scores = masked_scores(
                rows.reshape(-1, HEAD_FEATURES),
                head_keys,
                jnp.repeat(query_index.reshape(-1), heads_per_group),
                jnp.repeat(query_segment.reshape(-1), heads_per_group),
                key_index,
                segment,
            )
            peak = jnp.max(scores, axis=1, keepdims=True)
            exponent = jnp.exp(scores - peak)
            denominator = jnp.sum(exponent, axis=1, keepdims=True)
            weights = (exponent / denominator).astype(jnp.bfloat16)
            output_rows = jnp.dot(weights, head_values, preferred_element_type=jnp.float32)
            part_outputs.append(output_rows.reshape(shape_rows))
            part_sums.append((peak + jnp.log(denominator)).reshape(shape_rows[:3]))
        head_outputs.append(jnp.concatenate(part_outputs, axis=0))
        head_sums.append(jnp.concatenate(part_sums, axis=0))
    return (jnp.concatenate(head_outputs, axis=2), jnp.concatenate(head_sums, axis=2))


def attend_back(queries, keys, values, segment, sums, grads, query_index, heads_per_group):
    sequence_length = keys.shape[0]
    key_index = jnp.arange(sequence_length, dtype=jnp.int32)
    query_segment = segment[query_index]
    query_grads, key_grads, value_grads, head_deltas = ([], [], [], [])
    for head in range(keys.shape[1] // HEAD_FEATURES):
        head_keys = keys[:, head * HEAD_FEATURES : (head + 1) * HEAD_FEATURES]
        head_values = values[:, head * HEAD_FEATURES : (head + 1) * HEAD_FEATURES]
        key_grad = jnp.zeros((sequence_length, HEAD_FEATURES), jnp.float32)
        value_grad = jnp.zeros((sequence_length, HEAD_FEATURES), jnp.float32)
        part_grads, part_deltas = ([], [])
        for half, start, span_length in key_parts(sequence_length):
            columns = slice(head * heads_per_group, (head + 1) * heads_per_group)
            rows = queries[:, :, columns]
            shape_rows = rows.shape
            query_rows = rows.reshape(-1, HEAD_FEATURES)
            grad_rows = grads[:, :, columns].reshape(-1, HEAD_FEATURES)
            row_sums = sums[:, :, columns].reshape(-1)
            scores = masked_scores(
                query_rows,
                head_keys,
                jnp.repeat(query_index.reshape(-1), heads_per_group),
                jnp.repeat(query_segment.reshape(-1), heads_per_group),
                key_index,
                segment,
            )
            probs = jnp.exp(scores - row_sums[:, None])
            grad_prob = contract_cols(grad_rows, head_values)
            delta = jnp.sum(probs * grad_prob, axis=1, keepdims=True)
            grad_score = (probs * (grad_prob - delta)).astype(jnp.bfloat16)
            query_part = jnp.dot(
                grad_score, head_keys, preferred_element_type=jnp.float32
            ) * HEAD_FEATURES ** (-0.5)
            key_part = contract_rows(grad_score, query_rows) * HEAD_FEATURES ** (-0.5)
            value_part = contract_rows(probs.astype(jnp.bfloat16), grad_rows)
            key_grad = add_window(key_grad, key_part, start)
            value_grad = add_window(value_grad, value_part, start)
            part_grads.append(query_part.reshape(shape_rows))
            part_deltas.append(delta.reshape(shape_rows[:3]))
        query_grads.append(jnp.concatenate(part_grads, axis=0))
        head_deltas.append(jnp.concatenate(part_deltas, axis=0))
        key_grads.append(key_grad)
        value_grads.append(value_grad)
    return (
        jnp.concatenate(query_grads, axis=2),
        jnp.concatenate(key_grads, axis=1),
        jnp.concatenate(value_grads, axis=1),
    )


def project_rows(source, weight, count):
    return contract_cols(lax.slice_in_dim(source, 0, count, axis=0), weight)


def local(
    tokens,
    grad_out,
    segments,
    w_query,
    key_weight_matrix,
    value_weight_matrix,
    w_output,
    w_gate,
    w_up,
    w_down,
    norm_attn,
    norm_mlp,
    norm_query,
    norm_key,
):
    ctx_count = lax.axis_size("ctx")
    ctx_rank = lax.axis_index("ctx")
    block_rows = tokens.shape[3]
    width = tokens.shape[4]
    own_rows = 2 * block_rows
    sequence_count = segments.shape[0]
    heads_per_group = QUERY_HEADS // KEY_VALUE_HEADS
    full_query, full_key, full_value, full_output, full_gate, full_up, full_down = (
        lax.all_gather(w_query, "ctx", axis=0, tiled=True),
        lax.all_gather(key_weight_matrix, "ctx", axis=0, tiled=True),
        lax.all_gather(value_weight_matrix, "ctx", axis=0, tiled=True),
        lax.all_gather(w_output, "ctx", axis=0, tiled=True),
        lax.all_gather(w_gate, "ctx", axis=0, tiled=True),
        lax.all_gather(w_up, "ctx", axis=0, tiled=True),
        lax.all_gather(w_down, "ctx", axis=0, tiled=True),
    )
    local_heads = full_query.shape[1] // HEAD_FEATURES
    local_groups = full_key.shape[1] // HEAD_FEATURES
    inputs = tokens.reshape(own_rows, width).astype(jnp.float32)
    normalized_input, norm_pull = jax.vjp(rms_scale, inputs, norm_attn)
    normed_all = lax.all_gather(
        normalized_input.astype(jnp.bfloat16).reshape(1, own_rows, width),
        "fsdp",
        axis=0,
        tiled=True,
    ).reshape(-1, width)
    offsets = jnp.arange(block_rows, dtype=jnp.int32)
    query_index = jnp.stack(
        [ctx_rank * block_rows + offsets, (2 * ctx_count - 1 - ctx_rank) * block_rows + offsets]
    )
    positions = doc_positions(segments)
    cosine, sine = rope_tables(positions[:, query_index])
    cosine = cosine[:, :, :, None]
    sine = sine[:, :, :, None]
    query_raw = jnp.dot(normed_all, full_query, preferred_element_type=jnp.float32).reshape(
        sequence_count, 2, block_rows, local_heads, HEAD_FEATURES
    )
    unrotated_key = jnp.dot(normed_all, full_key, preferred_element_type=jnp.float32).reshape(
        sequence_count, 2, block_rows, local_groups, HEAD_FEATURES
    )
    value_low = jnp.dot(normed_all, full_value, preferred_element_type=jnp.float32).astype(
        jnp.bfloat16
    )
    query_prep, query_pull = jax.vjp(
        lambda values, gain: head_prep(values, gain, cosine, sine), query_raw, norm_query
    )
    key_prep, key_pull = jax.vjp(
        lambda values, gain: head_prep(values, gain, cosine, sine), unrotated_key, norm_key
    )
    query_low = query_prep.astype(jnp.bfloat16)
    key_low = key_prep.astype(jnp.bfloat16)
    kv_shape = (sequence_count, 1, 2, block_rows, local_groups * HEAD_FEATURES)
    key_all, value_all = (
        lax.all_gather(key_low.reshape(kv_shape), "ctx", axis=1, tiled=True),
        lax.all_gather(value_low.reshape(kv_shape), "ctx", axis=1, tiled=True),
    )
    key_seq = to_sequence(key_all)
    value_seq = to_sequence(value_all)
    heads_out, heads_sum = lax.map(
        lambda bundle: attend_sequence(
            bundle[0], bundle[1], bundle[2], bundle[3], query_index, heads_per_group
        ),
        (query_low, key_seq, value_seq, segments),
    )
    mixed = heads_out.astype(jnp.bfloat16).reshape(-1, local_heads * HEAD_FEATURES)
    branch = lax.psum_scatter(
        project_rows(mixed, full_output, own_rows * lax.axis_size("fsdp")).astype(jnp.bfloat16),
        "fsdp",
        scatter_dimension=0,
        tiled=True,
    ).astype(jnp.float32)
    middle = inputs + branch
    normed_mid, mid_pull = jax.vjp(rms_scale, middle, norm_mlp)
    mid_all = lax.all_gather(
        normed_mid.astype(jnp.bfloat16).reshape(1, own_rows, width), "fsdp", axis=0, tiled=True
    ).reshape(-1, width)
    gate = jnp.dot(mid_all, full_gate, preferred_element_type=jnp.float32)
    up_part = jnp.dot(mid_all, full_up, preferred_element_type=jnp.float32)
    active, swiglu_pull = jax.vjp(swiglu, gate, up_part)
    active_low = active.astype(jnp.bfloat16)
    feed_out = lax.psum_scatter(
        project_rows(active_low, full_down, own_rows * lax.axis_size("fsdp")).astype(jnp.bfloat16),
        "fsdp",
        scatter_dimension=0,
        tiled=True,
    ).astype(jnp.float32)
    result = middle + feed_out
    out_tokens = result.astype(jnp.bfloat16).reshape(tokens.shape)
    cot_own = grad_out.reshape(own_rows, width)
    cot_all = lax.all_gather(
        cot_own.reshape(1, own_rows, width), "fsdp", axis=0, tiled=True
    ).reshape(-1, width)
    grad_down = contract_rows(cot_all, active_low)
    grad_active = jnp.dot(cot_all, full_down, preferred_element_type=jnp.float32)
    grad_gate_full, grad_up_full = swiglu_pull(grad_active)
    gate_low = grad_gate_full.astype(jnp.bfloat16)
    up_low = grad_up_full.astype(jnp.bfloat16)
    grad_gate = contract_rows(mid_all, gate_low)
    grad_up = contract_rows(mid_all, up_low)
    grad_mid_norm = lax.psum_scatter(
        (contract_cols(gate_low, full_gate) + contract_cols(up_low, full_up)).astype(jnp.bfloat16),
        "fsdp",
        scatter_dimension=0,
        tiled=True,
    ).astype(jnp.float32)
    grad_middle_part, grad_norm_mlp = mid_pull(grad_mid_norm)
    grad_middle = cot_own.astype(jnp.float32) + grad_middle_part
    branch_all = lax.all_gather(
        grad_middle.astype(jnp.bfloat16).reshape(1, own_rows, width), "fsdp", axis=0, tiled=True
    ).reshape(-1, width)
    grad_output = contract_rows(branch_all, mixed)
    grad_heads = jnp.dot(branch_all, full_output, preferred_element_type=jnp.float32).astype(
        jnp.bfloat16
    )
    grad_heads = grad_heads.reshape(sequence_count, 2, block_rows, local_heads, HEAD_FEATURES)
    grad_q, grad_k, grad_v = lax.map(
        lambda bundle: attend_back(
            bundle[0],
            bundle[1],
            bundle[2],
            bundle[3],
            bundle[4],
            bundle[5],
            query_index,
            heads_per_group,
        ),
        (query_low, key_seq, value_seq, segments, heads_sum, grad_heads),
    )
    key_back, value_back = (
        lax.psum_scatter(
            to_blocks(grad_k, block_rows).astype(jnp.bfloat16),
            "ctx",
            scatter_dimension=1,
            tiled=True,
        ).astype(jnp.float32),
        lax.psum_scatter(
            to_blocks(grad_v, block_rows).astype(jnp.bfloat16),
            "ctx",
            scatter_dimension=1,
            tiled=True,
        ).astype(jnp.float32),
    )
    grad_query_raw, grad_norm_query = query_pull(grad_q)
    grad_key_raw, grad_norm_key = key_pull(
        key_back.reshape(sequence_count, 2, block_rows, local_groups, HEAD_FEATURES)
    )
    query_back = grad_query_raw.astype(jnp.bfloat16).reshape(-1, local_heads * HEAD_FEATURES)
    key_back_low = grad_key_raw.astype(jnp.bfloat16).reshape(-1, local_groups * HEAD_FEATURES)
    value_back_low = value_back.astype(jnp.bfloat16).reshape(-1, local_groups * HEAD_FEATURES)
    grad_query = contract_rows(normed_all, query_back)
    grad_key = contract_rows(normed_all, key_back_low)
    grad_value = contract_rows(normed_all, value_back_low)
    value_rows = lax.slice_in_dim(value_back_low, 0, own_rows * lax.axis_size("fsdp"), axis=0)
    grad_normed = lax.psum_scatter(
        (
            contract_cols(query_back, full_query)
            + contract_cols(key_back_low, full_key)
            + contract_cols(value_rows, full_value)
        ).astype(jnp.bfloat16),
        "fsdp",
        scatter_dimension=0,
        tiled=True,
    ).astype(jnp.float32)
    grad_inputs_part, grad_norm_attn = norm_pull(grad_normed)
    grad_tokens = (grad_middle + grad_inputs_part).reshape(tokens.shape)
    gain_attn, gain_mlp, gain_query, gain_key = lax.psum(
        (grad_norm_attn, grad_norm_mlp, grad_norm_query, grad_norm_key), ("ctx", "fsdp")
    )
    shard_query, shard_key, shard_value, shard_output, shard_gate, shard_up, shard_down = (
        lax.psum_scatter(
            grad_query.astype(jnp.bfloat16), "ctx", scatter_dimension=0, tiled=True
        ).astype(jnp.float32),
        lax.psum_scatter(
            grad_key.astype(jnp.bfloat16), "ctx", scatter_dimension=0, tiled=True
        ).astype(jnp.float32),
        lax.psum_scatter(
            grad_value.astype(jnp.bfloat16), "ctx", scatter_dimension=0, tiled=True
        ).astype(jnp.float32),
        lax.psum_scatter(
            grad_output.astype(jnp.bfloat16), "ctx", scatter_dimension=0, tiled=True
        ).astype(jnp.float32),
        lax.psum_scatter(
            grad_gate.astype(jnp.bfloat16), "ctx", scatter_dimension=0, tiled=True
        ).astype(jnp.float32),
        lax.psum_scatter(
            grad_up.astype(jnp.bfloat16), "ctx", scatter_dimension=0, tiled=True
        ).astype(jnp.float32),
        lax.psum_scatter(
            grad_down.astype(jnp.bfloat16), "ctx", scatter_dimension=0, tiled=True
        ).astype(jnp.float32),
    )
    return (
        out_tokens,
        grad_tokens,
        shard_query,
        shard_key,
        shard_value,
        shard_output,
        shard_gate,
        shard_up,
        shard_down,
        gain_attn,
        gain_mlp,
        gain_query,
        gain_key,
    )


def solution(mesh):
    return jax.shard_map(
        local,
        mesh=mesh,
        in_specs=(
            P("fsdp", "ctx", None, None, None),
            P("fsdp", "ctx", None, None, None),
            P(),
            P("ctx", "fsdp"),
            P("ctx", "fsdp"),
            P("ctx", "fsdp"),
            P("ctx", "fsdp"),
            P("ctx", "fsdp"),
            P("ctx", "fsdp"),
            P("ctx", "fsdp"),
            P(),
            P(),
            P(),
            P(),
        ),
        out_specs=(
            P("fsdp", "ctx", None, None, None),
            P("fsdp", "ctx", None, None, None),
            P("ctx", "fsdp"),
            P("ctx", "fsdp"),
            P("ctx", "fsdp"),
            P("ctx", "fsdp"),
            P("ctx", "fsdp"),
            P("ctx", "fsdp"),
            P("ctx", "fsdp"),
            P(),
            P(),
            P(),
            P(),
        ),
        check_vma=False,
    )
```

profile of v0, /device:TPU:0, one launch (start us, length us, event | category | flops | bytes accessed | tf_op | source)
XLA Modules:
  0.0 2396.9 jit_solution(3653461444145290873)
XLA Ops:
  21.4 33.0 %all-gather.20.cloned.1.call-done = bf16[2048,512]{1,0:T(8,128)(2,1)} async-done(((bf16[128,512]{1,0:T(8,128)(2,1)}), bf16[2048,512]{1,0:T(8,128)(2,1)}) %all-gather.20.cloned.1.call-update) | async-done | bytes 2097168 | tf_op jit(solution)/shard_map/all_gather | solution.py:207
  57.3 31.0 %all-gather.16.cloned.1.call-done = bf16[2,256,2048]{2,1,0:T(8,128)(2,1)} async-done(((bf16[1,256,2048]{2,1,0:T(8,128)(2,1)}), bf16[2,256,2048]{2,1,0:T(8,128)(2,1)}) %all-gather.16.cloned.1.call-update) | async-done | bytes 2097168 | tf_op jit(solution)/shard_map/all_gather | solution.py:218
  93.6 38.4 %all-gather.24.cloned.1.call-done = bf16[2048,512]{1,0:T(8,128)(2,1)} async-done(((bf16[128,512]{1,0:T(8,128)(2,1)}), bf16[2048,512]{1,0:T(8,128)(2,1)}) %all-gather.24.cloned.1.call-update) | async-done | bytes 2097168 | tf_op jit(solution)/shard_map/all_gather | solution.py:208
  137.5 45.6 %all-gather.18.cloned.1.call-done = bf16[2048,1024]{1,0:T(8,128)(2,1)} async-done(((bf16[128,1024]{1,0:T(8,128)(2,1)}), bf16[2048,1024]{1,0:T(8,128)(2,1)}) %all-gather.18.cloned.1.call-update) | async-done | bytes 4194320 | tf_op jit(solution)/shard_map/all_gather | solution.py:206
  183.1 6.7 copy.106
  196.8 61.8 %all-gather.22.cloned.1.call-done = bf16[2,16,2,128,512]{4,3,2,0,1:T(8,128)(2,1)} async-done(((bf16[2,1,2,128,512]{4,3,2,0,1:T(8,128)(2,1)}), bf16[2,16,2,128,512]{4,3,2,0,1:T(8,128)(2,1)}) %all-gather.22.cloned.1.call-update) | async-done | bytes 8388624 | tf_op jit(solution)/shard_map/all_gather | solution.py:251
  267.8 66.3 %all-gather.26.cloned.1.call-done = bf16[2,16,2,128,512]{4,3,2,0,1:T(8,128)(2,1)} async-done(((bf16[2,1,2,128,512]{4,3,2,0,1:T(8,128)(2,1)}), bf16[2,16,2,128,512]{4,3,2,0,1:T(8,128)(2,1)}) %all-gather.26.cloned.1.call-update) | async-done | bytes 8388624 | tf_op jit(solution)/shard_map/all_gather | solution.py:252
  341.9 7.6 pad_maximum_fusion
  349.5 7.8 copy_bitcast_fusion
  357.3 7.6 pad_maximum_fusion.1
  364.9 90.6 %while.26 = (s32[]{:T(128)}, bf16[2,2,128,8,128]{4,3,2,1,0:T(8,128)(2,1)S(1)}, f32[2,2,128,8]{2,3,1,0:T(8,128)S(1)}, s32[2,4096]{1,0:T(2,128)S(1)}, s32[2,128]{1...) while((s32[]{:T(128)}, ...), condition=%wide.region_14.15_spmd, body=%wide.region_5.14_spmd.sunk | while | flops 4389345280 | bytes 163831984 | solution.py:256
  455.5 6.3 convolution_convert_fusion.5
  462.6 29.9 %reduce-scatter.18.cloned.1.call-done = bf16[256,2048]{1,0:T(8,128)(2,1)} async-done(((bf16[512,2048]{1,0:T(8,128)(2,1)}), bf16[256,2048]{1,0:T(8,128)(2,1)}) %reduce-scatter.18.cloned.1.call-update) | async-done | bytes 1048592 | tf_op jit(solution)/shard_map/reduce_scatter | solution.py:263
  498.9 96.4 %all-gather.32.cloned.1.call-done = bf16[2048,3072]{1,0:T(8,128)(2,1)} async-done(((bf16[128,3072]{1,0:T(8,128)(2,1)}), bf16[2048,3072]{1,0:T(8,128)(2,1)}) %all-gather.32.cloned.1.call-update) | async-done | bytes 12582928 | tf_op jit(solution)/shard_map/all_gather | solution.py:211
  595.3 33.3 %all-gather.38.cloned.1.call-done = bf16[512,2048]{1,0:T(8,128)(2,1)} async-done(((bf16[256,2048]{1,0:T(8,128)(2,1)}), bf16[512,2048]{1,0:T(8,128)(2,1)}) %all-gather.38.cloned.1.call-update) | async-done | bytes 2097168 | tf_op jit(solution)/shard_map/all_gather | solution.py:271
  628.6 12.1 fusion.110
  640.7 90.6 %all-gather.30.cloned.1.call-done = bf16[2048,3072]{1,0:T(8,128)(2,1)} async-done(((bf16[128,3072]{1,0:T(8,128)(2,1)}), bf16[2048,3072]{1,0:T(8,128)(2,1)}) %all-gather.30.cloned.1.call-update) | async-done | bytes 12582928 | tf_op jit(solution)/shard_map/all_gather | solution.py:210
  731.4 11.9 fusion.109
  743.3 20.8 all-gather.36.cloned.1.call-done
  764.2 102.7 %all-gather.34.cloned.1.call-done = bf16[2048,3072]{1,0:T(8,128)(2,1)} async-done(((bf16[128,3072]{1,0:T(8,128)(2,1)}), bf16[2048,3072]{1,0:T(8,128)(2,1)}) %all-gather.34.cloned.1.call-update) | async-done | bytes 12582928 | tf_op jit(solution)/shard_map/all_gather | solution.py:212
  866.9 16.9 multiply_convert_fusion.4
  883.9 13.3 fusion.111
  897.2 13.4 add_convert_fusion.2
  910.7 30.2 %reduce-scatter.22.cloned.1.call-done = bf16[256,2048]{1,0:T(8,128)(2,1)} async-done(((bf16[512,2048]{1,0:T(8,128)(2,1)}), bf16[256,2048]{1,0:T(8,128)(2,1)}) %reduce-scatter.22.cloned.1.call-update) | async-done | bytes 1048592 | tf_op jit(solution)/shard_map/reduce_scatter | solution.py:297
  947.3 33.2 %all-gather.40.cloned.1.call-done = bf16[512,2048]{1,0:T(8,128)(2,1)} async-done(((bf16[256,2048]{1,0:T(8,128)(2,1)}), bf16[512,2048]{1,0:T(8,128)(2,1)}) %all-gather.40.cloned.1.call-update) | async-done | bytes 2097168 | tf_op jit(solution)/shard_map/all_gather | solution.py:305
  986.0 337.8 %while.27 = (s32[]{:T(128)}, f32[2,2,128,8,128]{2,4,3,1,0:T(8,128)}, bf16[2,4096,512]{1,2,0:T(8,128)(2,1)}, bf16[2,4096,512]{2,1,0:T(8,128)(2,1)}, s32[2,4096]{1...) while((s32[]{:T(128)}, ...), condition=%wide.region_25.26_spmd, body=%wide.region_20.25_spmd.sunk | while | flops 10876878848 | bytes 545489664 | solution.py:313
  1032.8 6.0 multiply_reduce_fusion.15
  1038.8 9.9 multiply_convert_fusion.11
  1058.3 8.2 multiply_reduce_fusion.16
  1066.5 10.0 multiply_convert_fusion.12
  1086.1 8.1 multiply_reduce_fusion.17
  1094.2 9.9 multiply_convert_fusion.13
  1114.1 8.1 multiply_reduce_fusion.18
  1122.2 7.9 multiply_convert_fusion.14
  1147.0 6.7 copy.215
  1185.6 6.0 multiply_reduce_fusion.15
  1191.6 9.9 multiply_convert_fusion.11
  1211.1 8.2 multiply_reduce_fusion.16
  1219.3 10.0 multiply_convert_fusion.12
  1238.9 8.1 multiply_reduce_fusion.17
  1247.0 9.9 multiply_convert_fusion.13
  1266.9 8.1 multiply_reduce_fusion.18
  1275.0 7.9 multiply_convert_fusion.14
  1299.8 6.7 copy.215
  1329.5 6.2 pad_maximum_fusion.3
  1335.8 9.6 copy.167
  1354.1 6.3 pad_maximum_fusion.2
  1372.9 6.3 convolution_convert_fusion.3
  1380.5 125.5 %all-reduce.9.cloned.1.call-done = bf16[2,16,2,128,512]{4,3,1,0,2:T(8,128)(2,1)} async-done(((bf16[2,16,2,128,512]{4,3,1,0,2:T(8,128)(2,1)}), bf16[2,16,2,128,512]{4,3,1,0,2:T(8,128)(2,1)}) %all-reduce.9.cloned.1.call-update) | async-done | bytes 8388624
  1512.0 11.8 convert_bitcast_fusion
  1523.9 17.0 copy.133
  1541.0 12.0 convolution_convert_fusion
  1553.1 12.2 convolution_convert_fusion.1
  1565.4 47.8 %reduce-scatter.24.cloned.1.call-done = bf16[2,1,2,128,512]{3,4,2,0,1:T(8,128)(2,1)} async-done(((bf16[2,16,2,128,512]{3,4,2,0,1:T(8,128)(2,1)}), bf16[2,1,2,128,512]{3,4,2,0,1:T(8,128)(2,1)}) %reduce-scatter.24.cloned.1.call-update) | async-done | bytes 524304 | tf_op jit(solution)/shard_map/reduce_scatter | solution.py:327
  1629.9 12.3 convolution_convert_fusion.4
  1642.2 47.2 %reduce-scatter.34.cloned.1.call-done = bf16[128,1024]{1,0:T(8,128)(2,1)} async-done(((bf16[2048,1024]{1,0:T(8,128)(2,1)}), bf16[128,1024]{1,0:T(8,128)(2,1)}) %reduce-scatter.34.cloned.1.call-update) | async-done | bytes 262160 | tf_op jit(solution)/shard_map/reduce_scatter | solution.py:376
  1691.2 73.9 %reduce-scatter.28.cloned.1.call-done = bf16[128,1024]{1,0:T(8,128)(2,1)} async-done(((bf16[2048,1024]{1,0:T(8,128)(2,1)}), bf16[128,1024]{1,0:T(8,128)(2,1)}) %reduce-scatter.28.cloned.1.call-update) | async-done | bytes 262160 | tf_op jit(solution)/shard_map/reduce_scatter | solution.py:367
  1766.9 62.7 %reduce-scatter.32.cloned.1.call-done = bf16[128,512]{1,0:T(8,128)(2,1)} async-done(((bf16[2048,512]{1,0:T(8,128)(2,1)}), bf16[128,512]{1,0:T(8,128)(2,1)}) %reduce-scatter.32.cloned.1.call-update) | async-done | bytes 131088 | tf_op jit(solution)/shard_map/reduce_scatter | solution.py:373
  1831.2 136.3 %reduce-scatter.40.cloned.1.call-done = bf16[128,3072]{1,0:T(8,128)(2,1)} async-done(((bf16[2048,3072]{1,0:T(8,128)(2,1)}), bf16[128,3072]{1,0:T(8,128)(2,1)}) %reduce-scatter.40.cloned.1.call-update) | async-done | bytes 786448
  1970.5 135.3 %reduce-scatter.38.cloned.1.call-done = bf16[128,3072]{1,0:T(8,128)(2,1)} async-done(((bf16[2048,3072]{1,0:T(8,128)(2,1)}), bf16[128,3072]{1,0:T(8,128)(2,1)}) %reduce-scatter.38.cloned.1.call-update) | async-done | bytes 786448 | tf_op jit(solution)/shard_map/reduce_scatter | solution.py:382
  2108.2 135.8 %reduce-scatter.36.cloned.1.call-done = bf16[128,3072]{1,0:T(8,128)(2,1)} async-done(((bf16[2048,3072]{1,0:T(8,128)(2,1)}), bf16[128,3072]{1,0:T(8,128)(2,1)}) %reduce-scatter.36.cloned.1.call-update) | async-done | bytes 786448 | tf_op jit(solution)/shard_map/reduce_scatter | solution.py:379
  2246.4 62.3 %reduce-scatter.30.cloned.1.call-done = bf16[128,512]{1,0:T(8,128)(2,1)} async-done(((bf16[2048,512]{1,0:T(8,128)(2,1)}), bf16[128,512]{1,0:T(8,128)(2,1)}) %reduce-scatter.30.cloned.1.call-update) | async-done | bytes 131088 | tf_op jit(solution)/shard_map/reduce_scatter | solution.py:370
  2310.3 32.1 %reduce-scatter.26.cloned.1.call-done = bf16[256,2048]{1,0:T(8,128)(2,1)} async-done(((bf16[512,2048]{1,0:T(8,128)(2,1)}), bf16[256,2048]{1,0:T(8,128)(2,1)}) %reduce-scatter.26.cloned.1.call-update) | async-done | bytes 1048592 | tf_op jit(solution)/shard_map/reduce_scatter | solution.py:351
  2344.7 40.2 %all-reduce.6 = (f32[2048]{0:T(1024)}, f32[2048]{0:T(1024)}, f32[128]{0:T(128)}, f32[128]{0:T(128)}) all-reduce(f32[2048]{0:T(1024)S(1)} %get-tuple-element.286, f32[2048]{0:T(1024)S(1)} %copy-done.53, f32[128]{0:T(128)S(1)} %get-tuple-element.280, f32[128]{0:T(128)S(1)} %get-tuple-element.284), channel_id=1, replica_groups=mesh['ctx'=16,'fsdp'=2] {'ctx','fsdp'}, use_global_device_ids=true, to_apply=%region_40.41 | all-reduce | flops 4352 | bytes 34816 | tf_op jit(solution)/shard_map/psum | solution.py:363
  (504 shorter events, 373.0 us)
Async XLA Ops:
  7.2 7.3 copy-start.42
  7.2 47.2 %all-gather.20.cloned.1.call-start = ((), (), s32[]{:S(2)}) async-start(), calls=%async_computation.14 | async-start | bytes 2228224 | tf_op jit(solution)/shard_map/all_gather | solution.py:207
  7.9 80.4 %all-gather.16.cloned.1.call-start = ((), (), s32[]{:S(2)}) async-start(), calls=%async_computation.12 | async-start | bytes 3145728 | tf_op jit(solution)/shard_map/all_gather | solution.py:218
  13.1 118.9 %all-gather.24.cloned.1.call-start = ((), (), s32[]{:S(2)}) async-start(), calls=%async_computation.16 | async-start | bytes 2228224 | tf_op jit(solution)/shard_map/all_gather | solution.py:208
  13.8 169.3 %all-gather.18.cloned.1.call-start = ((), (), s32[]{:S(2)}) async-start(), calls=%async_computation.13 | async-start | bytes 4456448 | tf_op jit(solution)/shard_map/all_gather | solution.py:206
  14.4 244.2 %all-gather.22.cloned.1.call-start = ((), (), s32[]{:S(2)}) async-start(), calls=%async_computation.15 | async-start | bytes 8912896 | tf_op jit(solution)/shard_map/all_gather | solution.py:251
  21.4 173.4 %copy-start.28 = (f32[2,2,128,128]{2,3,1,0:T(8,128)}, f32[2,2,128,128]{2,3,1,0:T(8,128)S(1)}, u32[]{:S(2)}) copy-start(f32[2,2,128,128]{2,3,1,0:T(8,128)S(1)} %get-tuple-element.390) | copy-start | bytes 786436
  21.4 173.4 %copy-start.34 = (f32[2,2,128,128]{2,3,1,0:T(8,128)}, f32[2,2,128,128]{2,3,1,0:T(8,128)S(1)}, u32[]{:S(2)}) copy-start(f32[2,2,128,128]{2,3,1,0:T(8,128)S(1)} %get-tuple-element.391) | copy-start | bytes 786436
  93.6 240.5 %all-gather.26.cloned.1.call-start = ((), (), s32[]{:S(2)}) async-start(), calls=%async_computation.17 | async-start | bytes 8912896 | tf_op jit(solution)/shard_map/all_gather | solution.py:252
  136.3 319.2 %all-gather.28.cloned.1.call-start = ((), (), s32[]{:S(2)}) async-start(), calls=%async_computation.18 | async-start | bytes 4456448 | tf_op jit(solution)/shard_map/all_gather | solution.py:209
  137.0 355.5 %reduce-scatter.18.cloned.1.call-start = ((), (), s32[]{:S(2)}) async-start(), calls=%async_computation.19 | async-start | bytes 3145728 | tf_op jit(solution)/shard_map/reduce_scatter | solution.py:263
  183.1 6.7 copy-start.68
  357.3 7.6 copy-start.70
  455.5 6.3 copy-start.71
  455.5 37.0 %copy-start.15 = (bf16[1,1,2,128,2048]{4,3,2,1,0:T(8,128)(2,1)S(1)}, bf16[1,1,2,128,2048]{4,3,2,1,0:T(8,128)(2,1)}, u32[]{:S(2)}) copy-start(bf16[1,1,2,128,2048]{4,3,2,1,0:T(8,128)(2,1)} %param.18) | copy-start | bytes 3145732
  461.8 32.4 %copy-start.48 = (f32[2048]{0:T(1024)S(1)}, f32[2048]{0:T(1024)}, u32[]{:S(2)}) copy-start(f32[2048]{0:T(1024)} %param.29) | copy-start | bytes 24580
  461.8 133.5 %all-gather.32.cloned.1.call-start = ((), (), s32[]{:S(2)}) async-start(), calls=%async_computation.21 | async-start | bytes 13369344 | tf_op jit(solution)/shard_map/all_gather | solution.py:211
  462.6 166.1 %all-gather.38.cloned.1.call-start = ((), (), s32[]{:S(2)}) async-start(), calls=%async_computation.34 | async-start | bytes 3145728 | tf_op jit(solution)/shard_map/all_gather | solution.py:271
  494.2 449.5 %copy-start.56 = (f32[256]{0:T(256)}, f32[256]{0:T(256)S(1)}, u32[]{:S(2)}) copy-start(f32[256]{0:T(256)S(1)} %fusion.92) | copy-start | bytes 3076
  496.8 234.6 %all-gather.30.cloned.1.call-start = ((), (), s32[]{:S(2)}) async-start(), calls=%async_computation.20 | async-start | bytes 13369344 | tf_op jit(solution)/shard_map/all_gather | solution.py:210
  497.6 266.6 %all-gather.36.cloned.1.call-start = ((), (), s32[]{:S(2)}) async-start(), calls=%async_computation.24 | async-start | bytes 3145728 | tf_op jit(solution)/shard_map/all_gather | solution.py:287
  498.1 368.8 %all-gather.34.cloned.1.call-start = ((), (), s32[]{:S(2)}) async-start(), calls=%async_computation.22 | async-start | bytes 13369344 | tf_op jit(solution)/shard_map/all_gather | solution.py:212
  498.9 442.1 %reduce-scatter.22.cloned.1.call-start = ((), (), s32[]{:S(2)}) async-start(), calls=%async_computation.25 | async-start | bytes 3145728 | tf_op jit(solution)/shard_map/reduce_scatter | solution.py:297
  883.9 13.3 copy-start.74
  883.9 13.3 copy-start.75
  897.2 43.8 %copy-start.21 = (bf16[256,2048]{1,0:T(8,128)(2,1)S(1)}, bf16[256,2048]{1,0:T(8,128)(2,1)}, u32[]{:S(2)}) copy-start(bf16[256,2048]{1,0:T(8,128)(2,1)} %reduce-scatter.18.cloned.1.call-done) | copy-start | bytes 3145732
  910.6 69.9 %all-gather.40.cloned.1.call-start = ((), (), s32[]{:S(2)}) async-start(), calls=%async_computation.35 | async-start | bytes 3145728 | tf_op jit(solution)/shard_map/all_gather | solution.py:305
  943.7 42.0 %copy-start.60 = (f32[256]{0:T(256)}, f32[256]{0:T(256)S(1)}, u32[]{:S(2)}) copy-start(f32[256]{0:T(256)S(1)} %multiply_multiply_fusion.5) | copy-start | bytes 3076
  947.3 558.7 %all-reduce.9.cloned.1.call-start = ((), (), s32[]{:S(2)}) async-start(), calls=%async_computation.37 | async-start | bytes 16777216
  1009.6 8.1 copy-start.17
  1017.7 15.1 copy-start.8
  1104.1 6.2 copy-start.11
  1147.0 6.7 copy-start.14
  1147.0 6.7 copy-start.30
  1162.5 8.0 copy-start.17
  1170.5 15.1 copy-start.8
  1299.8 6.7 copy-start.14
  1299.8 6.7 copy-start.30
  1335.8 277.5 %reduce-scatter.24.cloned.1.call-start = ((), (), s32[]{:S(2)}) async-start(), calls=%async_computation.26 | async-start | bytes 8912896 | tf_op jit(solution)/shard_map/reduce_scatter | solution.py:327
  1360.4 329.0 %reduce-scatter.34.cloned.1.call-start = ((), (), s32[]{:S(2)}) async-start(), calls=%async_computation.31 | async-start | bytes 4456448 | tf_op jit(solution)/shard_map/reduce_scatter | solution.py:376
  1366.7 398.4 %reduce-scatter.28.cloned.1.call-start = ((), (), s32[]{:S(2)}) async-start(), calls=%async_computation.28 | async-start | bytes 4456448 | tf_op jit(solution)/shard_map/reduce_scatter | solution.py:367
  1372.9 6.4 copy-start.43
  1379.3 450.2 %reduce-scatter.32.cloned.1.call-start = ((), (), s32[]{:S(2)}) async-start(), calls=%async_computation.30 | async-start | bytes 2228224 | tf_op jit(solution)/shard_map/reduce_scatter | solution.py:373
  1512.0 455.5 %reduce-scatter.40.cloned.1.call-start = ((), (), s32[]{:S(2)}) async-start(), calls=%async_computation.36 | async-start | bytes 13369344
  1540.9 564.8 %reduce-scatter.38.cloned.1.call-start = ((), (), s32[]{:S(2)}) async-start(), calls=%async_computation.33 | async-start | bytes 13369344 | tf_op jit(solution)/shard_map/reduce_scatter | solution.py:382
  1553.0 690.9 %reduce-scatter.36.cloned.1.call-start = ((), (), s32[]{:S(2)}) async-start(), calls=%async_computation.32 | async-start | bytes 13369344 | tf_op jit(solution)/shard_map/reduce_scatter | solution.py:379
  1565.3 48.0 %copy-start.36 = (f32[2,2,128,128]{2,3,1,0:T(8,128)S(1)}, f32[2,2,128,128]{2,3,1,0:T(8,128)}, u32[]{:S(2)}) copy-start(f32[2,2,128,128]{2,3,1,0:T(8,128)} %copy-done.34) | copy-start | bytes 786436
  1565.3 49.3 %copy-start.47 = (f32[2,2,128,4]{2,3,1,0:T(4,128)S(1)}, f32[2,2,128,4]{2,3,1,0:T(4,128)}, u32[]{:S(2)}) copy-start(f32[2,2,128,4]{2,3,1,0:T(4,128)} %copy-done.46) | copy-start | bytes 24580
  1565.3 49.3 %copy-start.67 = (f32[128]{0:T(128)S(1)}, f32[128]{0:T(128)}, u32[]{:S(2)}) copy-start(f32[128]{0:T(128)} %param.31) | copy-start | bytes 1540
  1565.3 49.2 %copy-start.24 = (f32[2,2,128,4,128]{2,4,3,1,0:T(8,128)S(1)}, f32[2,2,128,4,128]{2,4,3,1,0:T(8,128)}, u32[]{:S(2)}) copy-start(f32[2,2,128,4,128]{2,4,3,1,0:T(8,128)} %copy-done.23) | copy-start | bytes 3145732
  1565.3 49.7 %copy-start.55 = (f32[2,2,128,4]{2,3,1,0:T(4,128)S(1)}, f32[2,2,128,4]{2,3,1,0:T(4,128)}, u32[]{:S(2)}) copy-start(f32[2,2,128,4]{2,3,1,0:T(4,128)} %copy-done.54) | copy-start | bytes 24580
  1565.3 743.4 %reduce-scatter.30.cloned.1.call-start = ((), (), s32[]{:S(2)}) async-start(), calls=%async_computation.29 | async-start | bytes 2228224 | tf_op jit(solution)/shard_map/reduce_scatter | solution.py:370
  1620.2 722.2 %reduce-scatter.26.cloned.1.call-start = ((), (), s32[]{:S(2)}) async-start(), calls=%async_computation.27 | async-start | bytes 3145728 | tf_op jit(solution)/shard_map/reduce_scatter | solution.py:351
  1629.8 755.1 %reduce-scatter.20.cloned.1.call-start = ((), (), s32[]{:S(2)}) async-start(), calls=%async_computation.23 | async-start | bytes 3145728 | tf_op jit(solution)/shard_map/reduce_scatter | solution.py:278
  1831.2 511.2 %copy-start.16 = (bf16[1,1,2,128,2048]{4,3,2,1,0:T(8,128)(2,1)S(1)}, bf16[1,1,2,128,2048]{4,3,2,1,0:T(8,128)(2,1)}, u32[]{:S(2)}) copy-start(bf16[1,1,2,128,2048]{4,3,2,1,0:T(8,128)(2,1)} %param.18) | copy-start | bytes 3145732
  1831.2 511.2 %copy-start.50 = (f32[2048]{0:T(1024)S(1)}, f32[2048]{0:T(1024)}, u32[]{:S(2)}) copy-start(f32[2048]{0:T(1024)} %param.28) | copy-start | bytes 24580
  1831.2 511.2 %copy-start.59 = (f32[256]{0:T(256)S(1)}, f32[256]{0:T(256)}, u32[]{:S(2)}) copy-start(f32[256]{0:T(256)} %copy-done.58) | copy-start | bytes 3076
  1970.4 374.3 %copy-start.53 = (f32[2048]{0:T(1024)S(1)}, f32[2048]{0:T(1024)}, u32[]{:S(2)}) copy-start(f32[2048]{0:T(1024)} %get-tuple-element.282) | copy-start | bytes 24580
  1970.4 414.5 %copy-start.63 = (f32[2,128]{1,0:T(2,128)S(1)}, f32[2,128]{1,0:T(2,128)}, u32[]{:S(2)}) copy-start(f32[2,128]{1,0:T(2,128)} %copy-done.62) | copy-start | bytes 3076
  1970.4 414.5 %copy-start.22 = (bf16[256,2048]{1,0:T(8,128)(2,1)S(1)}, bf16[256,2048]{1,0:T(8,128)(2,1)}, u32[]{:S(2)}) copy-start(bf16[256,2048]{1,0:T(8,128)(2,1)} %reduce-scatter.18.cloned.1.call-done) | copy-start | bytes 3145732
  1970.4 414.5 %copy-start.27 = (bf16[1,1,2,128,2048]{4,3,2,1,0:T(8,128)(2,1)S(1)}, bf16[1,1,2,128,2048]{4,3,2,1,0:T(8,128)(2,1)}, u32[]{:S(2)}) copy-start(bf16[1,1,2,128,2048]{4,3,2,1,0:T(8,128)(2,1)} %param.19) | copy-start | bytes 3145732
  1970.4 414.5 %copy-start.49 = (f32[2048]{0:T(1024)S(1)}, f32[2048]{0:T(1024)}, u32[]{:S(2)}) copy-start(f32[2048]{0:T(1024)} %param.29) | copy-start | bytes 24580
  1970.4 414.5 %copy-start.57 = (f32[256]{0:T(256)S(1)}, f32[256]{0:T(256)}, u32[]{:S(2)}) copy-start(f32[256]{0:T(256)} %copy-done.56) | copy-start | bytes 3076
  1970.5 414.5 %copy-start.61 = (f32[256]{0:T(256)S(1)}, f32[256]{0:T(256)}, u32[]{:S(2)}) copy-start(f32[256]{0:T(256)} %copy-done.60) | copy-start | bytes 3076
  (62 other events, 190.7 us)
Sparse Core Ops, SparseCore 0:
  10.2 44.1 all-gather.19
  56.5 31.7 all-gather.15
  90.5 41.4 all-gather.23
  134.0 49.0 all-gather.17
  185.7 72.8 all-gather.21
  261.2 72.8 all-gather.25
  336.2 48.9 all-gather.27
  461.9 30.5 reduce-scatter.17
  494.8 100.4 all-gather.31
  597.3 31.3 all-gather.37
  630.9 100.4 all-gather.29
  732.8 31.3 all-gather.35
  766.4 100.4 all-gather.33
  910.8 30.1 reduce-scatter.21
  947.4 33.0 all-gather.39
  1335.9 170.0 all-reduce.8
  1509.9 103.2 reduce-scatter.23
  1616.9 72.3 reduce-scatter.33
  1693.2 71.7 reduce-scatter.27
  1768.7 60.8 reduce-scatter.31
  1833.6 133.8 reduce-scatter.39
  1971.5 134.1 reduce-scatter.37
  2109.8 134.1 reduce-scatter.35
  2247.6 61.0 reduce-scatter.29
  2311.5 30.8 reduce-scatter.25
  2344.5 32.5 reduce-scatter.19
where the time goes:
time: 2400 us
  waiting for transfers between devices  1580 us (66%)
  matrix products  374 us (16%)
  other arithmetic  173 us (7%)
  local copies, waits for them, and re-layouts  166 us (7%)
  loops' own time  49.2 us (2%)
  blocking collectives  40.2 us (2%)
    unnamed x28, waiting for transfers between devices  267 us
    dot_general x31, matrix products, contract_cols(): lax.dot_general(left, right, (((1,), (1,)), ((), ())), preferred_element_...  173 us
    reduce_scatter x1, waiting for transfers between devices, local(): lax.psum_scatter(grad_gate.astype(jnp.bfloat16), 'ctx', scatter_dimension...  136 us
    reduce_scatter x1, waiting for transfers between devices, local(): lax.psum_scatter(grad_up.astype(jnp.bfloat16), 'ctx', scatter_dimension=0...  135 us
    dot_general x23, matrix products, contract_rows(): lax.dot_general(left, right, (((0,), (0,)), ((), ())), preferred_element_...  107 us
    all_gather x1, waiting for transfers between devices, local(): lax.all_gather(w_down, 'ctx', axis=0, tiled=True)  103 us
    all_gather x1, waiting for transfers between devices, local(): lax.all_gather(w_up, 'ctx', axis=0, tiled=True)  96.4 us
    all_gather x1, waiting for transfers between devices, local(): lax.all_gather(w_gate, 'ctx', axis=0, tiled=True)  90.6 us
  transfers between devices with their start and end apart: 26, of which 24 were waited for; matrix products, arithmetic and copies ran while one was open for 13% of the time, Pallas kernels for 0%

commit v1 on v0

v1 whole, which is shorter than its diff:
```python
import functools
import math

import jax
import jax.numpy as jnp
from jax import lax
from jax.experimental import pallas as pl
from jax.experimental.pallas import tpu as pltpu
from jax.sharding import PartitionSpec as P

QUERY_HEADS = 16
KEY_VALUE_HEADS = 8
HD = 128
DOCS = 4
CHUNK = 256
eps = 1e-06
rope_base = 1000000.0
SCALE = HD ** (-0.5)
EXP2_SCALE = SCALE * math.log2(math.e)
F32 = jnp.float32
BF16 = jnp.bfloat16


def xor_send(value, axis, step):
    count = lax.axis_size(axis)
    return lax.ppermute(value, axis, [(i, i ^ step) for i in range(count)])


def stage_offsets(count):
    quarter = count // 4
    base = [4 * i for i in range(quarter)]
    return [b ^ low for low in (0, 2, 1, 3) for b in base]


def stage_gather(piece, axis):
    count = lax.axis_size(axis)
    first = jnp.concatenate(
        [piece[None]] + [xor_send(piece[None], axis, 4 * i) for i in range(1, count // 4)], axis=0
    )
    second = xor_send(first, axis, 2)
    return first, second, xor_send(first, axis, 1), xor_send(second, axis, 1)


def stage_scatter_tail(half, axis):
    count = lax.axis_size(axis)
    quarter = half.shape[0] // 2
    kept = half[:quarter].astype(F32) + xor_send(half[quarter:], axis, 2).astype(F32)
    kept = kept.astype(BF16)
    block = quarter // (count // 4)
    total = kept[:block].astype(F32)
    for i in range(1, count // 4):
        total = total + xor_send(kept[i * block : (i + 1) * block], axis, 4 * i).astype(F32)
    return total


def exchange_rows(rows, axis):
    return [rows] + [xor_send(rows, axis, r) for r in range(1, lax.axis_size(axis))]


def scatter_rows(partial, axis):
    count = lax.axis_size(axis)
    rows = partial.shape[0] // count
    total = partial[:rows].astype(F32)
    for r in range(1, count):
        total = total + xor_send(partial[r * rows : (r + 1) * rows], axis, r).astype(F32)
    return total


def dot(left, right):
    return jnp.dot(left, right, preferred_element_type=F32)


def dot_rows(left, right):
    return lax.dot_general(left, right, (((0,), (0,)), ((), ())), preferred_element_type=F32)


def dot_cols(left, right):
    return lax.dot_general(left, right, (((1,), (1,)), ((), ())), preferred_element_type=F32)


def vmem_limit(mib):
    return pltpu.CompilerParams(vmem_limit_bytes=mib * 1024 * 1024)


def permute_kernel(offsets, me_ref, x_ref, o_ref):
    me = me_ref[0]
    width = x_ref.shape[1] // len(offsets)
    for place, offset in enumerate(offsets):
        start = pl.multiple_of(lax.bitwise_xor(me, offset) * width, width)
        o_ref[:, place * width : (place + 1) * width] = x_ref[:, pl.ds(start, width)]


def permute_columns(x, me, count):
    rows, width = x.shape
    tile = min(rows, 256)
    return pl.pallas_call(
        functools.partial(permute_kernel, stage_offsets(count)),
        out_shape=jax.ShapeDtypeStruct(x.shape, x.dtype),
        grid_spec=pltpu.PrefetchScalarGridSpec(
            num_scalar_prefetch=1,
            grid=(rows // tile,),
            in_specs=[pl.BlockSpec((tile, width), lambda i, m: (i, 0))],
            out_specs=pl.BlockSpec((tile, width), lambda i, m: (i, 0)),
        ),
        cost_estimate=pl.CostEstimate(flops=0, bytes_accessed=2 * x.size * 2, transcendentals=0),
        name="permute_columns",
    )(me, x)


def prep_kernel(query_heads, groups, raw_ref, cos_ref, sin_ref, gq_ref, gk_ref, q_ref, kv_ref):
    cos = cos_ref[...]
    sin = sin_ref[...]

    def rotate_norm(x, gain):
        scale = lax.rsqrt(jnp.mean(x * x, axis=-1, keepdims=True) + eps)
        u = x * scale * gain
        return u * cos + pltpu.roll(u, HD // 2, 1) * sin

    for h in range(query_heads):
        cols = slice(h * HD, (h + 1) * HD)
        q_ref[:, cols] = rotate_norm(raw_ref[:, cols], gq_ref[...]).astype(BF16)
    for h in range(groups):
        k = raw_ref[:, (query_heads + h) * HD : (query_heads + h + 1) * HD]
        v = raw_ref[:, (query_heads + groups + h) * HD : (query_heads + groups + h + 1) * HD]
        kv_ref[:, 2 * h * HD : (2 * h + 1) * HD] = rotate_norm(k, gk_ref[...]).astype(BF16)
        kv_ref[:, (2 * h + 1) * HD : (2 * h + 2) * HD] = v.astype(BF16)


def head_prep(raw, cos, sin, gq, gk, query_heads, groups):
    rows, width = raw.shape
    tile = 128
    vec = pl.BlockSpec((1, HD), lambda i: (0, 0))
    tab = pl.BlockSpec((tile, HD), lambda i: (i, 0))
    return pl.pallas_call(
        functools.partial(prep_kernel, query_heads, groups),
        out_shape=(
            jax.ShapeDtypeStruct((rows, query_heads * HD), BF16),
            jax.ShapeDtypeStruct((rows, 2 * groups * HD), BF16),
        ),
        grid=(rows // tile,),
        in_specs=[pl.BlockSpec((tile, width), lambda i: (i, 0)), tab, tab, vec, vec],
        out_specs=(
            pl.BlockSpec((tile, query_heads * HD), lambda i: (i, 0)),
            pl.BlockSpec((tile, 2 * groups * HD), lambda i: (i, 0)),
        ),
        cost_estimate=pl.CostEstimate(
            flops=20 * raw.size, bytes_accessed=6 * raw.size, transcendentals=0
        ),
        name="head_prep",
    )(raw, cos, sin, gq, gk)


def prep_back_kernel(heads, stride, d_ref, raw_ref, cos_ref, sin_ref, g_ref, out_ref, gain_ref):
    cos = cos_ref[...]
    sin = sin_ref[...]
    gain = g_ref[...]
    gain_sum = jnp.zeros((1, HD), F32)
    for h in range(heads):
        cols = slice(h * HD, (h + 1) * HD)
        x = raw_ref[:, cols]
        d = d_ref[:, stride * h * HD : (stride * h + 1) * HD].astype(F32)
        t = d * cos - pltpu.roll(d, HD // 2, 1) * sin
        scale = lax.rsqrt(jnp.mean(x * x, axis=-1, keepdims=True) + eps)
        n = x * scale
        gain_sum = gain_sum + jnp.sum(t * n, axis=0, keepdims=True)
        e = t * gain
        out_ref[:, cols] = (scale * (e - n * jnp.mean(e * n, axis=-1, keepdims=True))).astype(BF16)

    @pl.when(pl.program_id(0) == 0)
    def _():
        gain_ref[...] = jnp.zeros_like(gain_ref)

    gain_ref[...] += gain_sum


def head_prep_back(grad, raw, cos, sin, gain, heads, stride, raw_block):
    rows = raw.shape[0]
    tile = 128
    width = heads * HD
    tab = pl.BlockSpec((tile, HD), lambda i: (i, 0))
    return pl.pallas_call(
        functools.partial(prep_back_kernel, heads, stride),
        out_shape=(
            jax.ShapeDtypeStruct((rows, width), BF16),
            jax.ShapeDtypeStruct((1, HD), F32),
        ),
        grid=(rows // tile,),
        in_specs=[
            pl.BlockSpec((tile, grad.shape[1]), lambda i: (i, 0)),
            pl.BlockSpec((tile, width), lambda i: (i, raw_block)),
            tab,
            tab,
            pl.BlockSpec((1, HD), lambda i: (0, 0)),
        ],
        out_specs=(
            pl.BlockSpec((tile, width), lambda i: (i, 0)),
            pl.BlockSpec((1, HD), lambda i: (0, 0)),
        ),
        cost_estimate=pl.CostEstimate(
            flops=20 * rows * width, bytes_accessed=10 * rows * width, transcendentals=0
        ),
        name="head_prep_back",
    )(grad, raw, cos, sin, gain)


def load_sequence(me, offsets, quarters, keys, values):
    per = len(offsets) // 4
    block = quarters[0].shape[2]
    for place, offset in enumerate(offsets):
        ref = quarters[place // per]
        owner = lax.bitwise_xor(me, offset)
        for half, index in ((0, owner), (1, 2 * len(offsets) - 1 - owner)):
            rows = pl.ds(pl.multiple_of(index * block, block), block)
            keys[rows, :] = ref[place % per, half, :, :HD]
            values[rows, :] = ref[place % per, half, :, HD:]


def stack_heads(tile, count):
    return jnp.concatenate([tile[:, h * HD : (h + 1) * HD] for h in range(count)], axis=0)


def row_positions(info_ref, half, block, count):
    first = info_ref[1 + 3 * half]
    lane = lax.broadcasted_iota(jnp.int32, (1, count * block), 1)
    position = first + lax.rem(lane, block)
    start_first, start_last = info_ref[2 + 3 * half], info_ref[3 + 3 * half]
    start = jnp.where(position >= start_last, start_last, start_first)
    return position, start, start_first // CHUNK, (first + block - 1) // CHUNK + 1


def valid_tile(chunk, position, start, shape):
    key_index = chunk * CHUNK + lax.broadcasted_iota(jnp.int32, shape, 0)
    return (key_index <= position) & (key_index >= start)


def forward_kernel(offsets, count, info_ref, q_ref, s0, s1, s2, s3, o_ref, lse_ref, keys, values):
    load_sequence(info_ref[0], offsets, (s0, s1, s2, s3), keys, values)
    block = q_ref.shape[1]
    columns = count * block
    for half in range(2):
        queries = stack_heads(q_ref[half], count)
        position, start, low, high = row_positions(info_ref, half, block, count)

        def body(chunk, carry):
            total, norm = carry
            rows = pl.ds(pl.multiple_of(chunk * CHUNK, CHUNK), CHUNK)
            score = dot_cols(keys[rows, :], queries)
            weight = jnp.where(
                valid_tile(chunk, position, start, score.shape), jnp.exp2(score * EXP2_SCALE), 0.0
            )
            norm = norm + jnp.sum(weight, axis=0, keepdims=True)
            total = total + dot_rows(values[rows, :], weight.astype(BF16))
            return total, norm

        total, norm = lax.fori_loop(
            low, high, body, (jnp.zeros((HD, columns), F32), jnp.zeros((1, columns), F32))
        )
        out = (total / norm).T.astype(BF16)
        for h in range(count):
            o_ref[half, :, h * HD : (h + 1) * HD] = out[h * block : (h + 1) * block]
        lse_ref[0, half] = jnp.log2(norm)


def backward_kernel(
    offsets, count, info_ref, q_ref, do_ref, o_ref, lse_ref, s0, s1, s2, s3,
    dq_ref, keep_ref, send_ref, keys, values, grad_k, grad_v,
):
    me = info_ref[0]
    load_sequence(me, offsets, (s0, s1, s2, s3), keys, values)
    block = q_ref.shape[1]
    columns = count * block
    grad_k[...] = jnp.zeros_like(grad_k)
    grad_v[...] = jnp.zeros_like(grad_v)
    for half in range(2):
        queries = stack_heads(q_ref[half], count)
        grads = stack_heads(do_ref[half], count)
        outs = stack_heads(o_ref[half], count)
        delta = jnp.sum((grads.astype(F32) * outs.astype(F32)).T, axis=0, keepdims=True)
        lse = lse_ref[0, half]
        position, start, low, high = row_positions(info_ref, half, block, count)

        def body(chunk, total):
            rows = pl.ds(pl.multiple_of(chunk * CHUNK, CHUNK), CHUNK)
            key_rows = keys[rows, :]
            score = dot_cols(key_rows, queries)
            prob = jnp.where(
                valid_tile(chunk, position, start, score.shape),
                jnp.exp2(score * EXP2_SCALE - lse),
                0.0,
            )
            grad_prob = dot_cols(values[rows, :], grads)
            grad_score = (prob * (grad_prob - delta)).astype(BF16)
            grad_v[rows, :] += dot(prob.astype(BF16), grads)
            grad_k[rows, :] += dot(grad_score, queries)
            return total + dot_rows(key_rows, grad_score)

        total = lax.fori_loop(low, high, body, jnp.zeros((HD, columns), F32))
        out = total.T * SCALE
        for h in range(count):
            dq_ref[half, :, h * HD : (h + 1) * HD] = out[h * block : (h + 1) * block]
    half_count = len(offsets) // 2
    for place, offset in enumerate(offsets):
        ref = (keep_ref, send_ref)[place // half_count]
        owner = lax.bitwise_xor(me, offset)
        for half, index in ((0, owner), (1, 2 * len(offsets) - 1 - owner)):
            rows = pl.ds(pl.multiple_of(index * block, block), block)
            ref[place % half_count, half, :, :HD] = (grad_k[rows, :] * SCALE).astype(BF16)
            ref[place % half_count, half, :, HD:] = grad_v[rows, :].astype(BF16)


def attend(info, q, quarters, count):
    _, block, width = q.shape
    per = quarters[0].shape[0]
    groups = quarters[0].shape[3] // (2 * HD)
    length = per * 8 * block
    row = pl.BlockSpec((2, block, count * HD), lambda n, i: (0, 0, n))
    part = pl.BlockSpec((per, 2, block, 2 * HD), lambda n, i: (0, 0, 0, n))
    return pl.pallas_call(
        functools.partial(forward_kernel, stage_offsets(4 * per), count),
        out_shape=(
            jax.ShapeDtypeStruct(q.shape, BF16),
            jax.ShapeDtypeStruct((groups, 2, 1, count * block), F32),
        ),
        grid_spec=pltpu.PrefetchScalarGridSpec(
            num_scalar_prefetch=1,
            grid=(groups,),
            in_specs=[row, part, part, part, part],
            out_specs=(
                row,
                pl.BlockSpec((1, 2, 1, count * block), lambda n, i: (n, 0, 0, 0)),
            ),
            scratch_shapes=[pltpu.VMEM((length, HD), BF16)] * 2,
        ),
        compiler_params=vmem_limit(48),
        cost_estimate=pl.CostEstimate(
            flops=groups * 2 * 8 * CHUNK * columns_of(count, block) * HD,
            bytes_accessed=groups * length * HD * 4,
            transcendentals=0,
        ),
        name="attend",
    )(info, q, *quarters)


def columns_of(count, block):
    return 2 * count * block


def attend_back(info, q, grad, out, lse, quarters, count):
    _, block, width = q.shape
    per = quarters[0].shape[0]
    groups = quarters[0].shape[3] // (2 * HD)
    length = per * 8 * block
    row = pl.BlockSpec((2, block, count * HD), lambda n, i: (0, 0, n))
    part = pl.BlockSpec((per, 2, block, 2 * HD), lambda n, i: (0, 0, 0, n))
    double = pl.BlockSpec((2 * per, 2, block, 2 * HD), lambda n, i: (0, 0, 0, n))
    kv_half = jax.ShapeDtypeStruct((2 * per,) + quarters[0].shape[1:], BF16)
    return pl.pallas_call(
        functools.partial(backward_kernel, stage_offsets(4 * per), count),
        out_shape=(jax.ShapeDtypeStruct(q.shape, F32), kv_half, kv_half),
        grid_spec=pltpu.PrefetchScalarGridSpec(
            num_scalar_prefetch=1,
            grid=(groups,),
            in_specs=[
                row,
                row,
                row,
                pl.BlockSpec((1, 2, 1, count * block), lambda n, i: (n, 0, 0, 0)),
                part,
                part,
                part,
                part,
            ],
            out_specs=(row, double, double),
            scratch_shapes=[pltpu.VMEM((length, HD), BF16)] * 2
            + [pltpu.VMEM((length, HD), F32)] * 2,
        ),
        compiler_params=vmem_limit(56),
        cost_estimate=pl.CostEstimate(
            flops=groups * 5 * 8 * CHUNK * columns_of(count, block) * HD,
            bytes_accessed=groups * length * HD * 8,
            transcendentals=0,
        ),
        name="attend_back",
    )(info, q, grad, out, lse, *quarters)


def unit_rows(values):
    scale = lax.rsqrt(jnp.mean(values * values, axis=-1, keepdims=True) + eps)
    return scale, values * scale


def unit_back(grad, gain, scale, unit):
    scaled = grad * gain
    return scale * (scaled - unit * jnp.mean(scaled * unit, axis=-1, keepdims=True))


def local(
    tokens,
    grad_out,
    segments,
    w_query,
    key_weight_matrix,
    value_weight_matrix,
    w_output,
    w_gate,
    w_up,
    w_down,
    norm_attn,
    norm_mlp,
    norm_query,
    norm_key,
):
    ctx_count = lax.axis_size("ctx")
    seq_count = lax.axis_size("fsdp")
    me = lax.axis_index("ctx").astype(jnp.int32)
    my_seq = lax.axis_index("fsdp").astype(jnp.int32)
    block = tokens.shape[3]
    width = tokens.shape[4]
    own = 2 * block
    query_heads = w_query.shape[1] // HD
    groups = key_weight_matrix.shape[1] // HD
    count = query_heads // groups
    q_width, k_width = query_heads * HD, groups * HD
    me_array = me.reshape(1)

    full_qkv = lax.all_gather(
        jnp.concatenate([w_query, key_weight_matrix, value_weight_matrix], axis=1),
        "ctx",
        axis=0,
        tiled=True,
    )
    full_output = lax.all_gather(w_output, "ctx", axis=0, tiled=True)
    full_gate = lax.all_gather(w_gate, "ctx", axis=0, tiled=True)
    full_up = lax.all_gather(w_up, "ctx", axis=0, tiled=True)
    full_down = lax.all_gather(w_down, "ctx", axis=0, tiled=True)

    inputs = tokens.reshape(own, width).astype(F32)
    r1, n1 = unit_rows(inputs)
    h1 = exchange_rows((n1 * norm_attn).astype(BF16), "fsdp")
    cot_own = grad_out.reshape(own, width)
    cot_all = jnp.concatenate(exchange_rows(cot_own, "fsdp"), axis=0)

    offsets = jnp.arange(block, dtype=jnp.int32)
    firsts = (me * block, (2 * ctx_count - 1 - me) * block)
    rows_index = jnp.concatenate([firsts[0] + offsets, firsts[1] + offsets])
    freq = jnp.exp(jnp.arange(HD // 2, dtype=F32) * (-2.0 * math.log(rope_base) / HD))
    infos, tables = [], []
    for r in range(seq_count):
        line = lax.dynamic_index_in_dim(
            segments, lax.bitwise_xor(my_seq, jnp.int32(r)), 0, keepdims=False
        )
        doc_first = [jnp.sum((line < d).astype(jnp.int32)) for d in range(DOCS)]
        mine = jnp.concatenate([lax.dynamic_slice_in_dim(line, f, block) for f in firsts])
        start = sum(jnp.where(mine == d, doc_first[d], 0) for d in range(DOCS))
        scalars = [me]
        for half in range(2):
            scalars += [firsts[half], start[half * block], start[(half + 1) * block - 1]]
        infos.append(jnp.stack(scalars))
        angle = (rows_index - start).astype(F32)[:, None] * freq
        cos, sin = jnp.cos(angle), jnp.sin(angle)
        tables.append((jnp.concatenate([cos, cos], 1), jnp.concatenate([-sin, sin], 1)))
    gain_q, gain_k = norm_query.reshape(1, HD), norm_key.reshape(1, HD)

    raws, queries, quarters = [], [], []
    for r in range(seq_count):
        raw = dot(h1[r], full_qkv)
        q, kv = head_prep(raw, *tables[r], gain_q, gain_k, query_heads, groups)
        raws.append(raw)
        queries.append(q.reshape(2, block, q_width))
        quarters.append(stage_gather(kv.reshape(2, block, 2 * k_width), "ctx"))
    heads, sums = [], []
    for r in range(seq_count):
        o, lse = attend(infos[r], queries[r], quarters[r], count)
        heads.append(o)
        sums.append(lse)
    mixed = jnp.concatenate([o.reshape(own, q_width) for o in heads], axis=0)
    x2 = inputs + scatter_rows(dot_cols(mixed, full_output).astype(BF16), "fsdp")

    r2, n2 = unit_rows(x2)
    h2 = jnp.concatenate(exchange_rows((n2 * norm_mlp).astype(BF16), "fsdp"), axis=0)
    gate = dot(h2, full_gate)
    up = dot(h2, full_up)
    sg = 1.0 / (1.0 + jnp.exp(-gate))
    silu = gate * sg
    act = (silu * up).astype(BF16)
    y = x2 + scatter_rows(dot_cols(act, full_down).astype(BF16), "fsdp")
    out_tokens = y.astype(BF16).reshape(tokens.shape)

    def scatter_weight(grad):
        return lax.psum_scatter(
            grad.astype(BF16), "ctx", scatter_dimension=0, tiled=True
        ).astype(F32)

    shard_down = scatter_weight(dot_rows(cot_all, act))
    d_act = dot(cot_all, full_down)
    d_gate = (d_act * up * sg * (1.0 + gate * (1.0 - sg))).astype(BF16)
    d_up = (d_act * silu).astype(BF16)
    d_h2 = scatter_rows(
        (dot_cols(d_gate, full_gate) + dot_cols(d_up, full_up)).astype(BF16), "fsdp"
    )
    shard_gate = scatter_weight(dot_rows(h2, d_gate))
    shard_up = scatter_weight(dot_rows(h2, d_up))
    gain_mlp = jnp.sum(d_h2 * n2, axis=0)
    d_x2 = cot_own.astype(F32) + unit_back(d_h2, norm_mlp, r2, n2)
    branch = jnp.concatenate(exchange_rows(d_x2.astype(BF16), "fsdp"), axis=0)
    d_att = dot(branch, full_output).astype(BF16)

    half_width = width // 2

    def scatter_staged(left, right):
        sent = dot_rows(left[:, half_width:], right).astype(BF16)
        kept = dot_rows(left[:, :half_width], right)
        return stage_scatter_tail(
            (kept + xor_send(sent, "ctx", 1).astype(F32)).astype(BF16), "ctx"
        )

    shard_output = scatter_staged(permute_columns(branch, me_array, ctx_count), mixed)
    h1_all = jnp.concatenate(h1, axis=0)
    h1_staged = permute_columns(h1_all, me_array, ctx_count)

    d_queries, d_kvs = [], []
    for r in range(seq_count):
        d_q, kept, sent = attend_back(
            infos[r],
            queries[r],
            d_att[r * own : (r + 1) * own].reshape(2, block, q_width),
            heads[r],
            sums[r],
            quarters[r],
            count,
        )
        d_queries.append(d_q.reshape(own, q_width))
        half = kept.astype(F32) + xor_send(sent, "ctx", 1).astype(F32)
        d_kvs.append(
            stage_scatter_tail(half.astype(BF16), "ctx").reshape(own, 2 * k_width)
        )
    d_qps, d_kps, d_vs = [], [], []
    gain_q_sum = jnp.zeros((1, HD), F32)
    gain_k_sum = jnp.zeros((1, HD), F32)
    for r in range(seq_count):
        d_qp, part = head_prep_back(
            d_queries[r], raws[r], *tables[r], gain_q, query_heads, 1, 0
        )
        gain_q_sum = gain_q_sum + part
        d_qps.append(d_qp)
        d_kp, part = head_prep_back(
            d_kvs[r], raws[r], *tables[r], gain_k, groups, 2, query_heads // groups
        )
        gain_k_sum = gain_k_sum + part
        d_kps.append(d_kp)
        d_vs.append(
            d_kvs[r].reshape(own, groups, 2, HD)[:, :, 1].reshape(own, k_width).astype(BF16)
        )
    d_qp_all = jnp.concatenate(d_qps, axis=0)
    d_kv_all = jnp.concatenate(
        [jnp.concatenate([k, v], axis=1) for k, v in zip(d_kps, d_vs)], axis=0
    )
    shard_query = scatter_staged(h1_staged, d_qp_all)
    shard_kv = scatter_staged(h1_staged, d_kv_all)
    d_h1 = scatter_rows(
        (
            dot_cols(d_qp_all, full_qkv[:, :q_width]) + dot_cols(d_kv_all, full_qkv[:, q_width:])
        ).astype(BF16),
        "fsdp",
    )
    gain_attn = jnp.sum(d_h1 * n1, axis=0)
    grad_tokens = (d_x2 + unit_back(d_h1, norm_attn, r1, n1)).reshape(tokens.shape)
    gains = lax.psum(
        jnp.concatenate([gain_attn, gain_mlp, gain_q_sum[0], gain_k_sum[0]]), ("ctx", "fsdp")
    )
    return (
        out_tokens,
        grad_tokens,
        shard_query,
        shard_kv[:, :k_width],
        shard_kv[:, k_width:],
        shard_output,
        shard_gate,
        shard_up,
        shard_down,
        gains[:width],
        gains[width : 2 * width],
        gains[2 * width : 2 * width + HD],
        gains[2 * width + HD :],
    )


def solution(mesh):
    block = P("fsdp", "ctx", None, None, None)
    weight = P("ctx", "fsdp")
    return jax.shard_map(
        local,
        mesh=mesh,
        in_specs=(block, block, P()) + (weight,) * 7 + (P(),) * 4,
        out_specs=(block, block) + (weight,) * 7 + (P(),) * 4,
        check_vma=False,
    )
```

time: 2400 us -> 1210 us (0.50)
  waiting for transfers between devices: 1580 us -> 646 us
  matrix products: 374 us -> 158 us
  local copies, waits for them, and re-layouts: 166 us -> 34.5 us
  starting transfers between devices: 1.43 us -> 118 us
  other arithmetic: 173 us -> 58.7 us
  Pallas kernels: 0 us -> 114 us
  loops' own time: 49.2 us -> 0 us
    reduce_scatter x11 -> x3, waiting for transfers between devices: 657 us -> 0.01 us  [scatter_weight(): lax.psum_scatter(grad.astype(BF16), 'ctx', scatter_dimension=0, tiled=True)]
    all_gather x13 -> x5, waiting for transfers between devices: 653 us -> 133 us  [the longest x1 84.7 us: local(): full_down = lax.all_gather(w_down, 'ctx', axis=0, tiled=True)]
    ppermute x0 -> x45, waiting for transfers between devices: none -> 510 us  [xor_send(): return lax.ppermute(value, axis, [(i, i ^ step) for i in range(count)])]
    unnamed x28 -> x8, waiting for transfers between devices: 267 us -> 2.5 us
    dot_general x77 -> x21, matrix products: 374 us -> 158 us  [the longest x6 59 us: dot(): return jnp.dot(left, right, preferred_element_type=F32)]
    ppermute x0 -> x45, starting transfers between devices: none -> 118 us  [xor_send(): return lax.ppermute(value, axis, [(i, i ^ step) for i in range(count)])]
    pallas_call x0 -> x12, Pallas kernels: none -> 114 us  [the longest x2 47.8 us: attend_back(): pl.pallas_call(functools.partial(backward_kernel, stage_offsets(4 * per),...]
    convert_element_type x22 -> x14, other arithmetic: 97.8 us -> 29.4 us  [the longest x2 8.64 us: local(): half.astype(BF16)]
  transfers between devices with their start and end apart: 26 -> 53, of which waited for: 24 -> 22; matrix products, arithmetic and copies ran while one was open for 13% -> 18% of each run, Pallas kernels for 0% -> 9%
where the time goes in v1:
time: 1210 us; the launch traced here: 1200 us
  waiting for transfers between devices  646 us (53%)
  matrix products  158 us (13%)
  starting transfers between devices  118 us (10%)
  Pallas kernels  114 us (9%)
  other arithmetic  58.7 us (5%)
  blocking collectives  56.3 us (5%)
  local copies, waits for them, and re-layouts  34.5 us (3%)
  between operations  15.6 us (1%)
    ppermute x45, waiting for transfers between devices, xor_send(): return lax.ppermute(value, axis, [(i, i ^ step) for i in range(count)])  510 us
    ppermute x45, starting transfers between devices, xor_send(): return lax.ppermute(value, axis, [(i, i ^ step) for i in range(count)])  118 us
    all_gather x1, waiting for transfers between devices, local(): full_down = lax.all_gather(w_down, 'ctx', axis=0, tiled=True)  84.7 us
    dot_general x6, matrix products, dot(): return jnp.dot(left, right, preferred_element_type=F32)  59 us
    psum x1, blocking collectives, local(): lax.psum(jnp.concatenate([gain_attn, gain_mlp, gain_q_sum[0], gain_k_sum[...  56.3 us
    dot_general x9, matrix products, dot_rows(): lax.dot_general(left, right, (((0,), (0,)), ((), ())), preferred_element_...  50 us
    dot_general x6, matrix products, dot_cols(): lax.dot_general(left, right, (((1,), (1,)), ((), ())), preferred_element_...  48.8 us
    all_gather x1, waiting for transfers between devices, local(): lax.all_gather(jnp.concatenate([w_query, key_weight_matrix, value_weight_...  48.8 us
  transfers between devices with their start and end apart: 53, of which 22 were waited for; matrix products, arithmetic and copies ran while one was open for 18% of the time, Pallas kernels for 9%

profile of v1, /device:TPU:0, one launch (start us, length us, event | category | flops | bytes accessed | tf_op | source)
XLA Modules:
  0.0 1201.1 jit_solution(8070915857531944015)
XLA Ops:
  12.8 3.0 collective-permute-start.6
  16.7 5.2 subtract_convert_fusion.1
  24.6 14.3 %collective-permute-done.6 = bf16[256,2048]{1,0:T(8,128)(2,1)S(1)} collective-permute-done((bf16[256,2048]{1,0:T(8,128)(2,1)S(1)}, bf16[256,2048]{1,0:T(8,128)(2,1)S(1)}, u32[]{:S(2)}, u32[]{:S(2)}) %collective-permute-start.6) | collective-permute-done | bytes 1048608 | tf_op jit(solution)/shard_map/ppermute | solution.py:26
  39.0 48.8 %all-gather.6.cloned.1.call-done = bf16[2048,2048]{1,0:T(8,128)(2,1)} async-done(((bf16[128,2048]{1,0:T(8,128)(2,1)}), bf16[2048,2048]{1,0:T(8,128)(2,1)}) %all-gather.6.cloned.1.call-update) | async-done | bytes 8388624 | tf_op jit(solution)/shard_map/all_gather | solution.py:426
  87.8 7.0 fusion.67.raw_ref
  94.8 5.1 head_prep.3
  104.3 7.1 fusion.66.raw_ref
  111.4 4.7 head_prep.2
  117.9 3.5 collective-permute-done.9
  121.4 22.7 %collective-permute-start = (bf16[1,2,128,1024]{3,2,1,0:T(8,128)(2,1)}, bf16[1,2,128,1024]{3,2,1,0:T(8,128)(2,1)S(1)}, u32[]{:S(2)}, u32[]{:S(2)}) collective-permute-start(bf16[1,2,128,1024]{3,2,1,0:T(8,128)(2,1)} %bitcast.121), channel_id=1, source_target_pairs={{0,8},{2,10},{4,12},{6,14},{8,0},{10,2},{12,4},{14,6},{16,24},{18,... | collective-permute-start | bytes 1572872 | tf_op jit(solution)/shard_map/ppermute | solution.py:26
  144.1 49.8 %collective-permute-done.8 = bf16[1,2,128,1024]{3,2,1,0:T(8,128)(2,1)S(1)} collective-permute-done((bf16[1,2,128,1024]{3,2,1,0:T(8,128)(2,1)}, bf16[1,2,128,1024]{3,2,1,0:T(8,128)(2,1)S(1)}, u32[]{:S(2)}, u32[]{:S(2)}) %collective-permute-start.8) | collective-permute-done | bytes 524320 | tf_op jit(solution)/shard_map/ppermute | solution.py:26
  197.4 40.7 %collective-permute-done.1 = bf16[1,2,128,1024]{3,2,1,0:T(8,128)(2,1)S(1)} collective-permute-done((bf16[1,2,128,1024]{3,2,1,0:T(8,128)(2,1)}, bf16[1,2,128,1024]{3,2,1,0:T(8,128)(2,1)S(1)}, u32[]{:S(2)}, u32[]{:S(2)}) %collective-permute-start.1) | collective-permute-done | bytes 524320 | tf_op jit(solution)/shard_map/ppermute | solution.py:26
  240.4 18.1 %collective-permute-done.10.s1 = bf16[4,2,128,1024]{3,2,1,0:T(8,128)(2,1)} collective-permute-done((bf16[4,2,128,1024]{3,2,1,0:T(8,128)(2,1)S(1)}, bf16[4,2,128,1024]{3,2,1,0:T(8,128)(2,1)}, u32[]{:S(2)}, u32[]{:S(2)}) %collective-permute-start.10) | collective-permute-done | bytes 2097184 | tf_op jit(solution)/shard_map/ppermute | solution.py:26
  259.1 71.4 %collective-permute-done.3.s1 = bf16[4,2,128,1024]{3,2,1,0:T(8,128)(2,1)} collective-permute-done((bf16[4,2,128,1024]{3,2,1,0:T(8,128)(2,1)}, bf16[4,2,128,1024]{3,2,1,0:T(8,128)(2,1)}, u32[]{:S(2)}, u32[]{:S(2)}) %collective-permute-start.3) | collective-permute-done | bytes 2097184 | tf_op jit(solution)/shard_map/ppermute | solution.py:26
  331.2 2.7 stack.21.info_ref
  333.9 2.7 stack.22.info_ref
  336.6 16.9 %attend.3 = (bf16[2,128,1024]{2,1,0:T(8,128)(2,1)S(1)}, f32[4,2,1,256]{3,2,1,0:T(1,128)S(1)}) custom-call(s32[7]{0:T(128)S(1)} %stack.22.info_ref, bf16[2,128,1024]{2,1,0:T(8,128)(2,1)S(1)} %bitcast.99, bf16[4,2,128,1024]{3,2,1,0:T(8,128)(2,1)S(1)} %pad_maximum_fusion.1.s0, bf16[4,2,128,1024]{3,2,1,0:T(8,128)(2,1)} %collective-permute-done.10.s1, ...), custom_call_target="tpu_custom_call" | custom-call | flops 1073741824 | bytes 8388608 | tf_op jit(solution)/shard_map/attend/pallas_call | solution.py:318
  354.2 18.4 %attend.2 = (bf16[2,128,1024]{2,1,0:T(8,128)(2,1)S(1)}, f32[4,2,1,256]{3,2,1,0:T(1,128)S(1)}) custom-call(s32[7]{0:T(128)S(1)} %stack.21.info_ref, bf16[2,128,1024]{2,1,0:T(8,128)(2,1)S(1)} %bitcast.97, bf16[4,2,128,1024]{3,2,1,0:T(8,128)(2,1)} %pad_maximum_fusion.s0, bf16[4,2,128,1024]{3,2,1,0:T(8,128)(2,1)} %collective-permute-done.3.s1, ...), custom_call_target="tpu_custom_call" | custom-call | flops 1073741824 | bytes 8388608 | tf_op jit(solution)/shard_map/attend/pallas_call | solution.py:318
  373.2 4.7 convolution_convert_fusion.4
  379.6 24.1 %collective-permute-done.13 = bf16[256,2048]{1,0:T(8,128)(2,1)S(1)} collective-permute-done((bf16[256,2048]{1,0:T(8,128)(2,1)S(1)}, bf16[256,2048]{1,0:T(8,128)(2,1)S(1)}, u32[]{:S(2)}, u32[]{:S(2)}) %collective-permute-start.13) | collective-permute-done | bytes 1048608 | tf_op jit(solution)/shard_map/ppermute | solution.py:26
  407.1 23.7 %collective-permute-done.14 = bf16[256,2048]{1,0:T(8,128)(2,1)} collective-permute-done((bf16[256,2048]{1,0:T(8,128)(2,1)S(1)}, bf16[256,2048]{1,0:T(8,128)(2,1)}, u32[]{:S(2)}, u32[]{:S(2)}) %collective-permute-start.14) | collective-permute-done | bytes 1048608 | tf_op jit(solution)/shard_map/ppermute | solution.py:26
  430.8 12.1 %fusion.48 = f32[512,3072]{1,0:T(8,128)} fusion(bf16[2048,3072]{1,0:T(8,128)(2,1)} %all-gather.12.cloned.1.call-done, bf16[256,2048]{1,0:T(8,128)(2,1)} %collective-permute-done.14, bf16[256,2048]{1,0:T(8,128)(2,1)} %copy-done.34), kind=kOutput, calls=%fused_computation.145 | convolution fusion | flops 6446645248 | bytes 20971520 | tf_op jit(solution)/shard_map/dot_general | solution.py:70
  442.9 12.0 fusion.49
  454.9 84.7 %all-gather.14.cloned.1.call-done = bf16[2048,3072]{1,0:T(8,128)(2,1)} async-done(((bf16[128,3072]{1,0:T(8,128)(2,1)}), bf16[2048,3072]{1,0:T(8,128)(2,1)}) %all-gather.14.cloned.1.call-update) | async-done | bytes 12582928 | tf_op jit(solution)/shard_map/all_gather | solution.py:435
  539.6 15.7 %multiply_convert_fusion = (bf16[512,3072]{1,0:T(8,128)(2,1)S(1)}, bf16[512,3072]{1,0:T(8,128)(2,1)}, bf16[512,3072]{1,0:T(8,128)(2,1)}) fusion(f32[512,3072]{1,0:T(8,128)} %fusion.49, f32[512,3072]{1,0:T(8,128)} %fusion.48, bf16[2048,3072]{1,0:T(8,128)(2,1)} %all-gather.14.cloned.1.call-done, bf16[256,2048]{1,0:T(8,128)(2,1)} %collective-permute-done.16, ...), kind=kOutput, calls=%fused_computation.5 | convolution fusion | flops 6470238208 | bytes 36700160 | tf_op jit(solution)/shard_map/dot_general | solution.py:70
  556.9 11.1 convolution_convert_fusion.1
  568.0 12.3 %convolution_convert_fusion.2 = bf16[2048,3072]{1,0:T(8,128)(2,1)} fusion(bf16[512,3072]{1,0:T(8,128)(2,1)} %get-tuple-element.80, bf16[256,2048]{1,0:T(8,128)(2,1)} %collective-permute-done.14, bf16[256,2048]{1,0:T(8,128)(2,1)} %copy-done.34), kind=kOutput, calls=%fused_computation.2 | convolution fusion | flops 6452936704 | bytes 17825792 | tf_op jit(solution)/shard_map/dot_general | solution.py:74
  580.4 13.4 %fusion.68 = f32[512,2048]{1,0:T(8,128)} fusion(bf16[512,3072]{1,0:T(8,128)(2,1)} %get-tuple-element.80, bf16[2048,3072]{1,0:T(8,128)(2,1)} %all-gather.10.cloned.1.call-done), kind=kOutput, calls=%fused_computation.163 | convolution fusion | flops 6442450944 | bytes 19922944 | tf_op jit(solution)/shard_map/dot_general | solution.py:78
  593.8 12.6 %add_convert_fusion.8 = bf16[512,2048]{1,0:T(8,128)(2,1)S(1)} fusion(f32[512,2048]{1,0:T(8,128)} %fusion.68, bf16[512,3072]{1,0:T(8,128)(2,1)} %copy-done.60, bf16[2048,3072]{1,0:T(8,128)(2,1)} %all-gather.12.cloned.1.call-done), kind=kOutput, calls=%fused_computation.20 | convolution fusion | flops 6444548096 | bytes 22020096 | tf_op jit(solution)/shard_map/dot_general | solution.py:78
  608.1 23.8 %collective-permute-done.17 = bf16[256,2048]{1,0:T(8,128)(2,1)S(1)} collective-permute-done((bf16[256,2048]{1,0:T(8,128)(2,1)S(1)}, bf16[256,2048]{1,0:T(8,128)(2,1)S(1)}, u32[]{:S(2)}, u32[]{:S(2)}) %collective-permute-start.17) | collective-permute-done | bytes 1048608 | tf_op jit(solution)/shard_map/ppermute | solution.py:26
  636.4 11.3 convolution_convert_fusion
  647.7 12.1 %collective-permute-done.18 = bf16[256,2048]{1,0:T(8,128)(2,1)} collective-permute-done((bf16[256,2048]{1,0:T(8,128)(2,1)}, bf16[256,2048]{1,0:T(8,128)(2,1)}, u32[]{:S(2)}, u32[]{:S(2)}) %collective-permute-start.18) | collective-permute-done | bytes 1048608 | tf_op jit(solution)/shard_map/ppermute | solution.py:26
  659.8 5.2 convolution_convert_fusion.8
  666.0 23.0 %attend_back.3 = (f32[2,128,1024]{2,1,0:T(8,128)}, bf16[8,2,128,1024]{3,2,1,0:T(8,128)(2,1)}, bf16[8,2,128,1024]{3,2,1,0:T(8,128)(2,1)}) custom-call(s32[7]{0:T(128)} %copy-done.10, bf16[2,128,1024]{2,1,0:T(8,128)(2,1)} %bitcast.98, bf16[2,128,1024]{2,1,0:T(8,128)(2,1)} %bitcast.113, bf16[2,128,1024]{2,1,0:T(8,128)(2,1)} %copy-done.3, ...), custom_call_target="tpu_custom_call" | custom-call | flops 2684354560 | bytes 16777216 | tf_op jit(solution)/shard_map/attend_back/pallas_call | solution.py:357
  689.1 24.8 %attend_back.2 = (f32[2,128,1024]{2,1,0:T(8,128)}, bf16[8,2,128,1024]{3,2,1,0:T(8,128)(2,1)}, bf16[8,2,128,1024]{3,2,1,0:T(8,128)(2,1)}) custom-call(s32[7]{0:T(128)} %copy-done.9, bf16[2,128,1024]{2,1,0:T(8,128)(2,1)} %bitcast.96, bf16[2,128,1024]{2,1,0:T(8,128)(2,1)} %bitcast.112, bf16[2,128,1024]{2,1,0:T(8,128)(2,1)} %copy-done.5, ...), custom_call_target="tpu_custom_call" | custom-call | flops 2684354560 | bytes 16777216 | tf_op jit(solution)/shard_map/attend_back/pallas_call | solution.py:357
  714.4 3.4 pad_maximum_fusion.4.x_ref
  717.7 3.2 permute_columns.3
  721.0 4.1 convolution_convert_fusion.5
  726.8 3.1 permute_columns.2
  729.9 4.1 head_prep_back.4
  734.0 4.2 head_prep_back.5
  743.0 3.0 add_convert_fusion.2
  747.2 4.3 add_convert_fusion
  755.1 4.3 add_convert_fusion.1
  762.4 10.9 convolution_convert_fusion.3
  776.1 2.9 add_convert_fusion.4
  783.5 67.4 %collective-permute-done.25 = bf16[4,2,128,1024]{3,2,1,0:T(8,128)(2,1)S(1)} collective-permute-done((bf16[4,2,128,1024]{3,2,1,0:T(8,128)(2,1)}, bf16[4,2,128,1024]{3,2,1,0:T(8,128)(2,1)S(1)}, u32[]{:S(2)}, u32[]{:S(2)}) %collective-permute-start.25) | collective-permute-done | bytes 2097184 | tf_op jit(solution)/shard_map/ppermute | solution.py:26
  856.0 39.7 %collective-permute-done.20 = bf16[4,2,128,1024]{3,2,1,0:T(8,128)(2,1)S(1)} collective-permute-done((bf16[4,2,128,1024]{3,2,1,0:T(8,128)(2,1)}, bf16[4,2,128,1024]{3,2,1,0:T(8,128)(2,1)S(1)}, u32[]{:S(2)}, u32[]{:S(2)}) %collective-permute-start.20) | collective-permute-done | bytes 2097184 | tf_op jit(solution)/shard_map/ppermute | solution.py:26
  902.4 55.3 %collective-permute-done.27 = bf16[1,2,128,1024]{3,2,1,0:T(8,128)(2,1)S(1)} collective-permute-done((bf16[1,2,128,1024]{3,2,1,0:T(8,128)(2,1)S(1)}, bf16[1,2,128,1024]{3,2,1,0:T(8,128)(2,1)S(1)}, u32[]{:S(2)}, u32[]{:S(2)}) %collective-permute-start.27) | collective-permute-done | bytes 524320 | tf_op jit(solution)/shard_map/ppermute | solution.py:26
  963.2 48.1 %collective-permute-start.43 = (bf16[128,1024]{1,0:T(8,128)(2,1)}, bf16[128,1024]{1,0:T(8,128)(2,1)}, u32[]{:S(2)}, u32[]{:S(2)}) collective-permute-start(bf16[128,1024]{1,0:T(8,128)(2,1)} %get-tuple-element.92), channel_id=1, source_target_pairs={{0,16},{2,18},{4,20},{6,22},{8,24},{10,26},{12,28},{14,30},{16,0},... | collective-permute-start | bytes 786440 | tf_op jit(solution)/shard_map/ppermute | solution.py:26
  1011.2 18.3 %collective-permute-done.22 = bf16[1,2,128,1024]{3,2,1,0:T(8,128)(2,1)} collective-permute-done((bf16[1,2,128,1024]{3,2,1,0:T(8,128)(2,1)}, bf16[1,2,128,1024]{3,2,1,0:T(8,128)(2,1)}, u32[]{:S(2)}, u32[]{:S(2)}) %collective-permute-start.22) | collective-permute-done | bytes 524320 | tf_op jit(solution)/shard_map/ppermute | solution.py:26
  1029.5 3.0 fusion.51
  1034.6 2.9 head_prep_back.7
  1037.5 3.2 head_prep_back.6
  1040.7 2.7 convolution_convert_fusion.6
  1043.5 4.7 fusion.1
  1060.6 12.6 %collective-permute-done.32 = bf16[128,1024]{1,0:T(8,128)(2,1)S(1)} collective-permute-done((bf16[128,1024]{1,0:T(8,128)(2,1)S(1)}, bf16[128,1024]{1,0:T(8,128)(2,1)S(1)}, u32[]{:S(2)}, u32[]{:S(2)}) %collective-permute-start.32) | collective-permute-done | bytes 262176 | tf_op jit(solution)/shard_map/ppermute | solution.py:26
  1074.7 4.4 collective-permute-done.34
  1079.1 10.3 collective-permute-done.33
  1096.6 56.3 %psum.7 = f32[4352]{0:T(1024)S(1)} all-reduce(f32[4352]{0:T(1024)S(1)} %pad_maximum_fusion.17), channel_id=1, replica_groups=mesh['ctx'=16,'fsdp'=2] {'ctx','fsdp'}, use_global_device_ids=true, to_apply=%region_17.18 | all-reduce | flops 4352 | bytes 34816 | tf_op jit(solution)/shard_map/psum | solution.py:568
  1152.9 5.5 fusion.15
  1164.8 7.7 collective-permute-done.37
  1172.4 2.8 collective-permute-done.39
  1175.3 10.2 collective-permute-done.38
  (284 shorter events, 114.4 us)
Async XLA Ops:
  7.2 80.6 %all-gather.6.cloned.1.call-start = ((), (), s32[]{:S(2)}) async-start(), calls=%async_computation.3 | async-start | bytes 8912896 | tf_op jit(solution)/shard_map/all_gather | solution.py:426
  9.3 363.9 %all-gather.8.cloned.1.call-start = ((), (), s32[]{:S(2)}) async-start(), calls=%async_computation.4 | async-start | bytes 4456448 | tf_op jit(solution)/shard_map/all_gather | solution.py:432
  10.0 420.8 %all-gather.12.cloned.1.call-start = ((), (), s32[]{:S(2)}) async-start(), calls=%async_computation.6 | async-start | bytes 13369344 | tf_op jit(solution)/shard_map/all_gather | solution.py:434
  10.7 432.2 %all-gather.10.cloned.1.call-start = ((), (), s32[]{:S(2)}) async-start(), calls=%async_computation.5 | async-start | bytes 13369344 | tf_op jit(solution)/shard_map/all_gather | solution.py:433
  11.3 528.2 %all-gather.14.cloned.1.call-start = ((), (), s32[]{:S(2)}) async-start(), calls=%async_computation.7 | async-start | bytes 13369344 | tf_op jit(solution)/shard_map/all_gather | solution.py:435
  11.9 1174.6 %reduce-scatter.6.cloned.1.call-start = ((), (), s32[]{:S(2)}) async-start(), calls=%async_computation.9 | async-start | bytes 13369344 | tf_op jit(solution)/shard_map/reduce_scatter | solution.py:490
  12.8 91.5 %copy-start.23 = (bf16[256,2048]{1,0:T(8,128)(2,1)}, bf16[256,2048]{1,0:T(8,128)(2,1)S(1)}, u32[]{:S(2)}) copy-start(bf16[256,2048]{1,0:T(8,128)(2,1)S(1)} %fusion.11) | copy-start | bytes 3145732
  12.8 26.1 %collective-permute-start.6 = (bf16[256,2048]{1,0:T(8,128)(2,1)S(1)}, bf16[256,2048]{1,0:T(8,128)(2,1)S(1)}, u32[]{:S(2)}, u32[]{:S(2)}) collective-permute-start(bf16[256,2048]{1,0:T(8,128)(2,1)S(1)} %fusion.11), channel_id=1, source_target_pairs={{0,1},{1,0},{2,3},{3,2},{4,5},{5,4},{6,7},{7,6},{8,9},{9,8},{10,11... | collective-permute-start | bytes 3145736 | tf_op jit(solution)/shard_map/ppermute | solution.py:26
  39.0 55.9 %copy-start.36 = (bf16[256,2048]{1,0:T(8,128)(2,1)}, bf16[256,2048]{1,0:T(8,128)(2,1)S(1)}, u32[]{:S(2)}) copy-start(bf16[256,2048]{1,0:T(8,128)(2,1)S(1)} %collective-permute-done.6) | copy-start | bytes 3145732
  99.9 21.5 %collective-permute-start.9 = (bf16[1,2,128,1024]{3,2,1,0:T(8,128)(2,1)}, bf16[1,2,128,1024]{3,2,1,0:T(8,128)(2,1)S(1)}, u32[]{:S(2)}, u32[]{:S(2)}) collective-permute-start(bf16[1,2,128,1024]{3,2,1,0:T(8,128)(2,1)} %bitcast.123), channel_id=1, source_target_pairs={{0,24},{2,26},{4,28},{6,30},{8,16},{10,18},{12,20},{14,22},{16,8},... | collective-permute-start | bytes 1572872 | tf_op jit(solution)/shard_map/ppermute | solution.py:26
  101.8 92.0 %collective-permute-start.8 = (bf16[1,2,128,1024]{3,2,1,0:T(8,128)(2,1)}, bf16[1,2,128,1024]{3,2,1,0:T(8,128)(2,1)S(1)}, u32[]{:S(2)}, u32[]{:S(2)}) collective-permute-start(bf16[1,2,128,1024]{3,2,1,0:T(8,128)(2,1)} %bitcast.124), channel_id=1, source_target_pairs={{0,16},{2,18},{4,20},{6,22},{8,24},{10,26},{12,28},{14,30},{16,0},... | collective-permute-start | bytes 1572872 | tf_op jit(solution)/shard_map/ppermute | solution.py:26
  102.6 92.0 %collective-permute-start.7 = (bf16[1,2,128,1024]{3,2,1,0:T(8,128)(2,1)}, bf16[1,2,128,1024]{3,2,1,0:T(8,128)(2,1)}, u32[]{:S(2)}, u32[]{:S(2)}) collective-permute-start(bf16[1,2,128,1024]{3,2,1,0:T(8,128)(2,1)} %bitcast.125), channel_id=1, source_target_pairs={{0,8},{2,10},{4,12},{6,14},{8,0},{10,2},{12,4},{14,6},{16,24},{18,... | collective-permute-start | bytes 1572872 | tf_op jit(solution)/shard_map/ppermute | solution.py:26
  111.4 83.2 %copy-start.39 = (bf16[256,1024]{1,0:T(8,128)(2,1)S(1)}, bf16[256,1024]{1,0:T(8,128)(2,1)}, u32[]{:S(2)}) copy-start(bf16[256,1024]{1,0:T(8,128)(2,1)} %get-tuple-element.39) | copy-start | bytes 1572868
  116.1 122.0 %copy-start.38 = (bf16[256,1024]{1,0:T(8,128)(2,1)S(1)}, bf16[256,1024]{1,0:T(8,128)(2,1)}, u32[]{:S(2)}) copy-start(bf16[256,1024]{1,0:T(8,128)(2,1)} %get-tuple-element.36) | copy-start | bytes 1572868
  116.1 81.3 %collective-permute-start.2 = (bf16[1,2,128,1024]{3,2,1,0:T(8,128)(2,1)}, bf16[1,2,128,1024]{3,2,1,0:T(8,128)(2,1)S(1)}, u32[]{:S(2)}, u32[]{:S(2)}) collective-permute-start(bf16[1,2,128,1024]{3,2,1,0:T(8,128)(2,1)} %bitcast.119), channel_id=1, source_target_pairs={{0,24},{2,26},{4,28},{6,30},{8,16},{10,18},{12,20},{14,22},{16,8},... | collective-permute-start | bytes 1572872 | tf_op jit(solution)/shard_map/ppermute | solution.py:26
  117.9 120.1 %collective-permute-start.1 = (bf16[1,2,128,1024]{3,2,1,0:T(8,128)(2,1)}, bf16[1,2,128,1024]{3,2,1,0:T(8,128)(2,1)S(1)}, u32[]{:S(2)}, u32[]{:S(2)}) collective-permute-start(bf16[1,2,128,1024]{3,2,1,0:T(8,128)(2,1)} %bitcast.120), channel_id=1, source_target_pairs={{0,16},{2,18},{4,20},{6,22},{8,24},{10,26},{12,28},{14,30},{16,0},... | collective-permute-start | bytes 1572872 | tf_op jit(solution)/shard_map/ppermute | solution.py:26
  121.4 116.6 %collective-permute-start = (bf16[1,2,128,1024]{3,2,1,0:T(8,128)(2,1)}, bf16[1,2,128,1024]{3,2,1,0:T(8,128)(2,1)S(1)}, u32[]{:S(2)}, u32[]{:S(2)}) collective-permute-start(bf16[1,2,128,1024]{3,2,1,0:T(8,128)(2,1)} %bitcast.121), channel_id=1, source_target_pairs={{0,8},{2,10},{4,12},{6,14},{8,0},{10,2},{12,4},{14,6},{16,24},{18,... | collective-permute-start | bytes 1572872 | tf_op jit(solution)/shard_map/ppermute | solution.py:26
  196.1 140.5 %copy-start = (bf16[4,2,128,1024]{3,2,1,0:T(8,128)(2,1)}, bf16[4,2,128,1024]{3,2,1,0:T(8,128)(2,1)S(1)}, u32[]{:S(2)}) copy-start(bf16[4,2,128,1024]{3,2,1,0:T(8,128)(2,1)S(1)} %pad_maximum_fusion.1.s0) | copy-start | bytes 6291460
  196.1 140.5 %copy-start.2 = (bf16[256,1024]{1,0:T(8,128)(2,1)S(1)}, bf16[256,1024]{1,0:T(8,128)(2,1)}, u32[]{:S(2)}) copy-start(bf16[256,1024]{1,0:T(8,128)(2,1)} %get-tuple-element.38) | copy-start | bytes 1572868
  196.1 62.4 %collective-permute-start.10 = (bf16[4,2,128,1024]{3,2,1,0:T(8,128)(2,1)S(1)}, bf16[4,2,128,1024]{3,2,1,0:T(8,128)(2,1)}, u32[]{:S(2)}, u32[]{:S(2)}) collective-permute-start(bf16[4,2,128,1024]{3,2,1,0:T(8,128)(2,1)S(1)} %pad_maximum_fusion.1.s0), channel_id=1, source_target_pairs={{0,4},{2,6},{4,0},{6,2},{8,12},{10,14},{12,8},{14,10},{16,20},{18,... | collective-permute-start | bytes 6291464 | tf_op jit(solution)/shard_map/ppermute | solution.py:26
  239.6 90.9 %collective-permute-start.3 = (bf16[4,2,128,1024]{3,2,1,0:T(8,128)(2,1)}, bf16[4,2,128,1024]{3,2,1,0:T(8,128)(2,1)}, u32[]{:S(2)}, u32[]{:S(2)}) collective-permute-start(bf16[4,2,128,1024]{3,2,1,0:T(8,128)(2,1)} %pad_maximum_fusion.s0), channel_id=1, source_target_pairs={{0,4},{2,6},{4,0},{6,2},{8,12},{10,14},{12,8},{14,10},{16,20},{18,... | collective-permute-start | bytes 6291464 | tf_op jit(solution)/shard_map/ppermute | solution.py:26
  240.4 96.2 %collective-permute-start.11 = (bf16[4,2,128,1024]{3,2,1,0:T(8,128)(2,1)S(1)}, bf16[4,2,128,1024]{3,2,1,0:T(8,128)(2,1)}, u32[]{:S(2)}, u32[]{:S(2)}) collective-permute-start(bf16[4,2,128,1024]{3,2,1,0:T(8,128)(2,1)S(1)} %pad_maximum_fusion.1.s0), channel_id=1, source_target_pairs={{0,2},{2,0},{4,6},{6,4},{8,10},{10,8},{12,14},{14,12},{16,18},{18,... | collective-permute-start | bytes 6291464 | tf_op jit(solution)/shard_map/ppermute | solution.py:26
  258.5 78.0 %collective-permute-start.12 = (bf16[4,2,128,1024]{3,2,1,0:T(8,128)(2,1)}, bf16[4,2,128,1024]{3,2,1,0:T(8,128)(2,1)}, u32[]{:S(2)}, u32[]{:S(2)}) collective-permute-start(bf16[4,2,128,1024]{3,2,1,0:T(8,128)(2,1)} %collective-permute-done.10.s1), channel_id=1, source_target_pairs={{0,2},{2,0},{4,6},{6,4},{8,10},{10,8},{12,14},{14,12},{16,18},{18,... | collective-permute-start | bytes 6291464 | tf_op jit(solution)/shard_map/ppermute | solution.py:26
  258.5 95.6 %collective-permute-start.4 = (bf16[4,2,128,1024]{3,2,1,0:T(8,128)(2,1)}, bf16[4,2,128,1024]{3,2,1,0:T(8,128)(2,1)}, u32[]{:S(2)}, u32[]{:S(2)}) collective-permute-start(bf16[4,2,128,1024]{3,2,1,0:T(8,128)(2,1)} %pad_maximum_fusion.s0), channel_id=1, source_target_pairs={{0,2},{2,0},{4,6},{6,4},{8,10},{10,8},{12,14},{14,12},{16,18},{18,... | collective-permute-start | bytes 6291464 | tf_op jit(solution)/shard_map/ppermute | solution.py:26
  330.5 23.7 %collective-permute-start.5 = (bf16[4,2,128,1024]{3,2,1,0:T(8,128)(2,1)}, bf16[4,2,128,1024]{3,2,1,0:T(8,128)(2,1)}, u32[]{:S(2)}, u32[]{:S(2)}) collective-permute-start(bf16[4,2,128,1024]{3,2,1,0:T(8,128)(2,1)} %collective-permute-done.3.s1), channel_id=1, source_target_pairs={{0,2},{2,0},{4,6},{6,4},{8,10},{10,8},{12,14},{14,12},{16,18},{18,... | collective-permute-start | bytes 6291464 | tf_op jit(solution)/shard_map/ppermute | solution.py:26
  378.0 25.6 %collective-permute-start.13 = (bf16[256,2048]{1,0:T(8,128)(2,1)S(1)}, bf16[256,2048]{1,0:T(8,128)(2,1)S(1)}, u32[]{:S(2)}, u32[]{:S(2)}) collective-permute-start(bf16[256,2048]{1,0:T(8,128)(2,1)S(1)} %slice.253), channel_id=1, source_target_pairs={{0,1},{1,0},{2,3},{3,2},{4,5},{5,4},{6,7},{7,6},{8,9},{9,8},{10,11... | collective-permute-start | bytes 3145736 | tf_op jit(solution)/shard_map/ppermute | solution.py:26
  404.6 26.2 %collective-permute-start.14 = (bf16[256,2048]{1,0:T(8,128)(2,1)S(1)}, bf16[256,2048]{1,0:T(8,128)(2,1)}, u32[]{:S(2)}, u32[]{:S(2)}) collective-permute-start(bf16[256,2048]{1,0:T(8,128)(2,1)S(1)} %multiply_convert_fusion.3), channel_id=1, source_target_pairs={{0,1},{1,0},{2,3},{3,2},{4,5},{5,4},{6,7},{7,6},{8,9},{9,8},{10,11... | collective-permute-start | bytes 3145736 | tf_op jit(solution)/shard_map/ppermute | solution.py:26
  406.1 48.7 %collective-permute-start.16 = (bf16[256,2048]{1,0:T(8,128)(2,1)S(1)}, bf16[256,2048]{1,0:T(8,128)(2,1)}, u32[]{:S(2)}, u32[]{:S(2)}) collective-permute-start(bf16[256,2048]{1,0:T(8,128)(2,1)S(1)} %bitcast.108), channel_id=1, source_target_pairs={{0,1},{1,0},{2,3},{3,2},{4,5},{5,4},{6,7},{7,6},{8,9},{9,8},{10,11... | collective-permute-start | bytes 3145736 | tf_op jit(solution)/shard_map/ppermute | solution.py:26
  568.0 620.9 %reduce-scatter.4.cloned.1.call-start = ((), (), s32[]{:S(2)}) async-start(), calls=%async_computation.8 | async-start | bytes 13369344 | tf_op jit(solution)/shard_map/reduce_scatter | solution.py:490
  580.3 611.0 %reduce-scatter.8.cloned.1.call-start = ((), (), s32[]{:S(2)}) async-start(), calls=%async_computation.10 | async-start | bytes 13369344 | tf_op jit(solution)/shard_map/reduce_scatter | solution.py:490
  606.5 25.4 %collective-permute-start.17 = (bf16[256,2048]{1,0:T(8,128)(2,1)S(1)}, bf16[256,2048]{1,0:T(8,128)(2,1)S(1)}, u32[]{:S(2)}, u32[]{:S(2)}) collective-permute-start(bf16[256,2048]{1,0:T(8,128)(2,1)S(1)} %slice.257), channel_id=1, source_target_pairs={{0,1},{1,0},{2,3},{3,2},{4,5},{5,4},{6,7},{7,6},{8,9},{9,8},{10,11... | collective-permute-start | bytes 3145736 | tf_op jit(solution)/shard_map/ppermute | solution.py:26
  634.9 24.9 %collective-permute-start.18 = (bf16[256,2048]{1,0:T(8,128)(2,1)}, bf16[256,2048]{1,0:T(8,128)(2,1)}, u32[]{:S(2)}, u32[]{:S(2)}) collective-permute-start(bf16[256,2048]{1,0:T(8,128)(2,1)} %fusion.50), channel_id=1, source_target_pairs={{0,1},{1,0},{2,3},{3,2},{4,5},{5,4},{6,7},{7,6},{8,9},{9,8},{10,11... | collective-permute-start | bytes 3145736 | tf_op jit(solution)/shard_map/ppermute | solution.py:26
  689.1 58.1 %collective-permute-start.24 = (bf16[8,2,128,1024]{3,2,1,0:T(8,128)(2,1)}, bf16[8,2,128,1024]{3,2,1,0:T(8,128)(2,1)}, u32[]{:S(2)}, u32[]{:S(2)}) collective-permute-start(bf16[8,2,128,1024]{3,2,1,0:T(8,128)(2,1)} %get-tuple-element.51), channel_id=1, source_target_pairs={{0,2},{2,0},{4,6},{6,4},{8,10},{10,8},{12,14},{14,12},{16,18},{18,... | collective-permute-start | bytes 12582920 | tf_op jit(solution)/shard_map/ppermute | solution.py:26
  713.9 41.2 %collective-permute-start.19 = (bf16[8,2,128,1024]{3,2,1,0:T(8,128)(2,1)}, bf16[8,2,128,1024]{3,2,1,0:T(8,128)(2,1)}, u32[]{:S(2)}, u32[]{:S(2)}) collective-permute-start(bf16[8,2,128,1024]{3,2,1,0:T(8,128)(2,1)} %get-tuple-element.48), channel_id=1, source_target_pairs={{0,2},{2,0},{4,6},{6,4},{8,10},{10,8},{12,14},{14,12},{16,18},{18,... | collective-permute-start | bytes 12582920 | tf_op jit(solution)/shard_map/ppermute | solution.py:26
  725.1 17.8 %collective-permute-start.40 = (bf16[1024,1024]{1,0:T(8,128)(2,1)}, bf16[1024,1024]{1,0:T(8,128)(2,1)}, u32[]{:S(2)}, u32[]{:S(2)}) collective-permute-start(bf16[1024,1024]{1,0:T(8,128)(2,1)} %convolution_convert_fusion.5), channel_id=1, source_target_pairs={{0,2},{2,0},{4,6},{6,4},{8,10},{10,8},{12,14},{14,12},{16,18},{18,... | collective-permute-start | bytes 6291464 | tf_op jit(solution)/shard_map/ppermute | solution.py:26
  742.3 32.1 %collective-permute-start.30 = (bf16[1024,1024]{1,0:T(8,128)(2,1)S(1)}, bf16[1024,1024]{1,0:T(8,128)(2,1)}, u32[]{:S(2)}, u32[]{:S(2)}) collective-permute-start(bf16[1024,1024]{1,0:T(8,128)(2,1)S(1)} %convolution_convert_fusion.7), channel_id=1, source_target_pairs={{0,2},{2,0},{4,6},{6,4},{8,10},{10,8},{12,14},{14,12},{16,18},{18,... | collective-permute-start | bytes 6291464 | tf_op jit(solution)/shard_map/ppermute | solution.py:26
  747.1 33.8 %collective-permute-start.41 = (bf16[512,1024]{1,0:T(8,128)(2,1)}, bf16[512,1024]{1,0:T(8,128)(2,1)S(1)}, u32[]{:S(2)}, u32[]{:S(2)}) collective-permute-start(bf16[512,1024]{1,0:T(8,128)(2,1)} %slice.297), channel_id=1, source_target_pairs={{0,4},{2,6},{4,0},{6,2},{8,12},{10,14},{12,8},{14,10},{16,20},{18,... | collective-permute-start | bytes 3145736 | tf_op jit(solution)/shard_map/ppermute | solution.py:26
  753.1 97.7 %collective-permute-start.25 = (bf16[4,2,128,1024]{3,2,1,0:T(8,128)(2,1)}, bf16[4,2,128,1024]{3,2,1,0:T(8,128)(2,1)S(1)}, u32[]{:S(2)}, u32[]{:S(2)}) collective-permute-start(bf16[4,2,128,1024]{3,2,1,0:T(8,128)(2,1)} %slice.269), channel_id=1, source_target_pairs={{0,4},{2,6},{4,0},{6,2},{8,12},{10,14},{12,8},{14,10},{16,20},{18,... | collective-permute-start | bytes 6291464 | tf_op jit(solution)/shard_map/ppermute | solution.py:26
  761.0 134.8 %collective-permute-start.20 = (bf16[4,2,128,1024]{3,2,1,0:T(8,128)(2,1)}, bf16[4,2,128,1024]{3,2,1,0:T(8,128)(2,1)S(1)}, u32[]{:S(2)}, u32[]{:S(2)}) collective-permute-start(bf16[4,2,128,1024]{3,2,1,0:T(8,128)(2,1)} %slice.262), channel_id=1, source_target_pairs={{0,4},{2,6},{4,0},{6,2},{8,12},{10,14},{12,8},{14,10},{16,20},{18,... | collective-permute-start | bytes 6291464 | tf_op jit(solution)/shard_map/ppermute | solution.py:26
  780.2 270.6 %collective-permute-start.31 = (bf16[512,1024]{1,0:T(8,128)(2,1)}, bf16[512,1024]{1,0:T(8,128)(2,1)}, u32[]{:S(2)}, u32[]{:S(2)}) collective-permute-start(bf16[512,1024]{1,0:T(8,128)(2,1)} %slice.281), channel_id=1, source_target_pairs={{0,4},{2,6},{4,0},{6,2},{8,12},{10,14},{12,8},{14,10},{16,20},{18,... | collective-permute-start | bytes 3145736 | tf_op jit(solution)/shard_map/ppermute | solution.py:26
  782.2 272.7 %collective-permute-start.42 = (bf16[128,1024]{1,0:T(8,128)(2,1)}, bf16[128,1024]{1,0:T(8,128)(2,1)}, u32[]{:S(2)}, u32[]{:S(2)}) collective-permute-start(bf16[128,1024]{1,0:T(8,128)(2,1)} %get-tuple-element.90), channel_id=1, source_target_pairs={{0,8},{2,10},{4,12},{6,14},{8,0},{10,2},{12,4},{14,6},{16,24},{18,... | collective-permute-start | bytes 786440 | tf_op jit(solution)/shard_map/ppermute | solution.py:26
  852.1 48.4 %collective-permute-start.26 = (bf16[1,2,128,1024]{3,2,1,0:T(8,128)(2,1)S(1)}, bf16[1,2,128,1024]{3,2,1,0:T(8,128)(2,1)S(1)}, u32[]{:S(2)}, u32[]{:S(2)}) collective-permute-start(bf16[1,2,128,1024]{3,2,1,0:T(8,128)(2,1)S(1)} %get-tuple-element.87), channel_id=1, source_target_pairs={{0,8},{2,10},{4,12},{6,14},{8,0},{10,2},{12,4},{14,6},{16,24},{18,... | collective-permute-start | bytes 1572872 | tf_op jit(solution)/shard_map/ppermute | solution.py:26
  853.6 48.2 %collective-permute-start.28 = (bf16[1,2,128,1024]{3,2,1,0:T(8,128)(2,1)S(1)}, bf16[1,2,128,1024]{3,2,1,0:T(8,128)(2,1)S(1)}, u32[]{:S(2)}, u32[]{:S(2)}) collective-permute-start(bf16[1,2,128,1024]{3,2,1,0:T(8,128)(2,1)S(1)} %get-tuple-element.88), channel_id=1, source_target_pairs={{0,24},{2,26},{4,28},{6,30},{8,16},{10,18},{12,20},{14,22},{16,8},... | collective-permute-start | bytes 1572872 | tf_op jit(solution)/shard_map/ppermute | solution.py:26
  895.8 61.9 %collective-permute-start.27 = (bf16[1,2,128,1024]{3,2,1,0:T(8,128)(2,1)S(1)}, bf16[1,2,128,1024]{3,2,1,0:T(8,128)(2,1)S(1)}, u32[]{:S(2)}, u32[]{:S(2)}) collective-permute-start(bf16[1,2,128,1024]{3,2,1,0:T(8,128)(2,1)S(1)} %get-tuple-element.89), channel_id=1, source_target_pairs={{0,16},{2,18},{4,20},{6,22},{8,24},{10,26},{12,28},{14,30},{16,0},... | collective-permute-start | bytes 1572872 | tf_op jit(solution)/shard_map/ppermute | solution.py:26
  899.3 59.8 %copy-start.15 = (bf16[4,2,128,1024]{3,2,1,0:T(8,128)(2,1)}, bf16[4,2,128,1024]{3,2,1,0:T(8,128)(2,1)S(1)}, u32[]{:S(2)}) copy-start(bf16[4,2,128,1024]{3,2,1,0:T(8,128)(2,1)S(1)} %add_convert_fusion.7) | copy-start | bytes 6291460
  900.5 60.7 %collective-permute-start.21 = (bf16[1,2,128,1024]{3,2,1,0:T(8,128)(2,1)}, bf16[1,2,128,1024]{3,2,1,0:T(8,128)(2,1)}, u32[]{:S(2)}, u32[]{:S(2)}) collective-permute-start(bf16[1,2,128,1024]{3,2,1,0:T(8,128)(2,1)} %get-tuple-element.84), channel_id=1, source_target_pairs={{0,8},{2,10},{4,12},{6,14},{8,0},{10,2},{12,4},{14,6},{16,24},{18,... | collective-permute-start | bytes 1572872 | tf_op jit(solution)/shard_map/ppermute | solution.py:26
  901.8 61.3 %collective-permute-start.23 = (bf16[1,2,128,1024]{3,2,1,0:T(8,128)(2,1)}, bf16[1,2,128,1024]{3,2,1,0:T(8,128)(2,1)}, u32[]{:S(2)}, u32[]{:S(2)}) collective-permute-start(bf16[1,2,128,1024]{3,2,1,0:T(8,128)(2,1)} %get-tuple-element.85), channel_id=1, source_target_pairs={{0,24},{2,26},{4,28},{6,30},{8,16},{10,18},{12,20},{14,22},{16,8},... | collective-permute-start | bytes 1572872 | tf_op jit(solution)/shard_map/ppermute | solution.py:26
  957.7 71.8 %collective-permute-start.22 = (bf16[1,2,128,1024]{3,2,1,0:T(8,128)(2,1)}, bf16[1,2,128,1024]{3,2,1,0:T(8,128)(2,1)}, u32[]{:S(2)}, u32[]{:S(2)}) collective-permute-start(bf16[1,2,128,1024]{3,2,1,0:T(8,128)(2,1)} %get-tuple-element.86), channel_id=1, source_target_pairs={{0,16},{2,18},{4,20},{6,22},{8,24},{10,26},{12,28},{14,30},{16,0},... | collective-permute-start | bytes 1572872 | tf_op jit(solution)/shard_map/ppermute | solution.py:26
  961.2 93.8 %collective-permute-start.44 = (bf16[128,1024]{1,0:T(8,128)(2,1)}, bf16[128,1024]{1,0:T(8,128)(2,1)}, u32[]{:S(2)}, u32[]{:S(2)}) collective-permute-start(bf16[128,1024]{1,0:T(8,128)(2,1)} %get-tuple-element.91), channel_id=1, source_target_pairs={{0,24},{2,26},{4,28},{6,30},{8,16},{10,18},{12,20},{14,22},{16,8},... | collective-permute-start | bytes 786440 | tf_op jit(solution)/shard_map/ppermute | solution.py:26
  963.2 94.1 %collective-permute-start.43 = (bf16[128,1024]{1,0:T(8,128)(2,1)}, bf16[128,1024]{1,0:T(8,128)(2,1)}, u32[]{:S(2)}, u32[]{:S(2)}) collective-permute-start(bf16[128,1024]{1,0:T(8,128)(2,1)} %get-tuple-element.92), channel_id=1, source_target_pairs={{0,16},{2,18},{4,20},{6,22},{8,24},{10,26},{12,28},{14,30},{16,0},... | collective-permute-start | bytes 786440 | tf_op jit(solution)/shard_map/ppermute | solution.py:26
  1043.5 47.9 %collective-permute-start.35 = (bf16[1024,1024]{1,0:T(8,128)(2,1)S(1)}, bf16[1024,1024]{1,0:T(8,128)(2,1)S(1)}, u32[]{:S(2)}, u32[]{:S(2)}) collective-permute-start(bf16[1024,1024]{1,0:T(8,128)(2,1)S(1)} %convolution_convert_fusion.6), channel_id=1, source_target_pairs={{0,2},{2,0},{4,6},{6,4},{8,10},{10,8},{12,14},{14,12},{16,18},{18,... | collective-permute-start | bytes 6291464 | tf_op jit(solution)/shard_map/ppermute | solution.py:26
  1050.7 39.7 %copy-start.17 = (bf16[512,2048]{1,0:T(8,128)(2,1)}, bf16[512,2048]{1,0:T(8,128)(2,1)S(1)}, u32[]{:S(2)}) copy-start(bf16[512,2048]{1,0:T(8,128)(2,1)S(1)} %add_convert_fusion.5) | copy-start | bytes 6291460
  1050.8 39.5 %collective-permute-start.29 = (bf16[256,2048]{1,0:T(8,128)(2,1)S(1)}, bf16[256,2048]{1,0:T(8,128)(2,1)S(1)}, u32[]{:S(2)}, u32[]{:S(2)}) collective-permute-start(bf16[256,2048]{1,0:T(8,128)(2,1)S(1)} %slice.277), channel_id=1, source_target_pairs={{0,1},{1,0},{2,3},{3,2},{4,5},{5,4},{6,7},{7,6},{8,9},{9,8},{10,11... | collective-permute-start | bytes 3145736 | tf_op jit(solution)/shard_map/ppermute | solution.py:26
  1054.8 35.6 %copy-start.13 = (bf16[1,1,2,128,2048]{4,3,2,1,0:T(8,128)(2,1)S(1)}, bf16[1,1,2,128,2048]{4,3,2,1,0:T(8,128)(2,1)}, u32[]{:S(2)}) copy-start(bf16[1,1,2,128,2048]{4,3,2,1,0:T(8,128)(2,1)} %param.14) | copy-start | bytes 3145732
  1054.8 35.6 %copy-start.48 = (f32[2048]{0:T(1024)S(1)}, f32[2048]{0:T(1024)}, u32[]{:S(2)}) copy-start(f32[2048]{0:T(1024)} %param.24) | copy-start | bytes 24580
  1054.8 35.6 %copy-start.51 = (f32[256]{0:T(256)S(1)}, f32[256]{0:T(256)}, u32[]{:S(2)}) copy-start(f32[256]{0:T(256)} %copy-done.50) | copy-start | bytes 3076
  1054.9 18.3 %collective-permute-start.32 = (bf16[128,1024]{1,0:T(8,128)(2,1)S(1)}, bf16[128,1024]{1,0:T(8,128)(2,1)S(1)}, u32[]{:S(2)}, u32[]{:S(2)}) collective-permute-start(bf16[128,1024]{1,0:T(8,128)(2,1)S(1)} %get-tuple-element.96), channel_id=1, source_target_pairs={{0,8},{2,10},{4,12},{6,14},{8,0},{10,2},{12,4},{14,6},{16,24},{18,... | collective-permute-start | bytes 786440 | tf_op jit(solution)/shard_map/ppermute | solution.py:26
  1055.0 24.1 %collective-permute-start.34 = (bf16[128,1024]{1,0:T(8,128)(2,1)S(1)}, bf16[128,1024]{1,0:T(8,128)(2,1)S(1)}, u32[]{:S(2)}, u32[]{:S(2)}) collective-permute-start(bf16[128,1024]{1,0:T(8,128)(2,1)S(1)} %get-tuple-element.97), channel_id=1, source_target_pairs={{0,24},{2,26},{4,28},{6,30},{8,16},{10,18},{12,20},{14,22},{16,8},... | collective-permute-start | bytes 786440 | tf_op jit(solution)/shard_map/ppermute | solution.py:26
  1057.3 32.1 %collective-permute-start.33 = (bf16[128,1024]{1,0:T(8,128)(2,1)S(1)}, bf16[128,1024]{1,0:T(8,128)(2,1)S(1)}, u32[]{:S(2)}, u32[]{:S(2)}) collective-permute-start(bf16[128,1024]{1,0:T(8,128)(2,1)S(1)} %get-tuple-element.98), channel_id=1, source_target_pairs={{0,16},{2,18},{4,20},{6,22},{8,24},{10,26},{12,28},{14,30},{16,0},... | collective-permute-start | bytes 786440 | tf_op jit(solution)/shard_map/ppermute | solution.py:26
  1073.1 79.7 %collective-permute-start.15 = (bf16[256,2048]{1,0:T(8,128)(2,1)}, bf16[256,2048]{1,0:T(8,128)(2,1)}, u32[]{:S(2)}, u32[]{:S(2)}) collective-permute-start(bf16[256,2048]{1,0:T(8,128)(2,1)} %slice.255), channel_id=1, source_target_pairs={{0,1},{1,0},{2,3},{3,2},{4,5},{5,4},{6,7},{7,6},{8,9},{9,8},{10,11... | collective-permute-start | bytes 3145736 | tf_op jit(solution)/shard_map/ppermute | solution.py:26
  1095.1 63.3 %collective-permute-start.36 = (bf16[512,1024]{1,0:T(8,128)(2,1)}, bf16[512,1024]{1,0:T(8,128)(2,1)}, u32[]{:S(2)}, u32[]{:S(2)}) collective-permute-start(bf16[512,1024]{1,0:T(8,128)(2,1)} %slice.287), channel_id=1, source_target_pairs={{0,4},{2,6},{4,0},{6,2},{8,12},{10,14},{12,8},{14,10},{16,20},{18,... | collective-permute-start | bytes 3145736 | tf_op jit(solution)/shard_map/ppermute | solution.py:26
  1160.1 12.4 %collective-permute-start.37 = (bf16[128,1024]{1,0:T(8,128)(2,1)S(1)}, bf16[128,1024]{1,0:T(8,128)(2,1)S(1)}, u32[]{:S(2)}, u32[]{:S(2)}) collective-permute-start(bf16[128,1024]{1,0:T(8,128)(2,1)S(1)} %get-tuple-element.93), channel_id=1, source_target_pairs={{0,8},{2,10},{4,12},{6,14},{8,0},{10,2},{12,4},{14,6},{16,24},{18,... | collective-permute-start | bytes 786440 | tf_op jit(solution)/shard_map/ppermute | solution.py:26
  1160.2 15.1 %collective-permute-start.39 = (bf16[128,1024]{1,0:T(8,128)(2,1)S(1)}, bf16[128,1024]{1,0:T(8,128)(2,1)S(1)}, u32[]{:S(2)}, u32[]{:S(2)}) collective-permute-start(bf16[128,1024]{1,0:T(8,128)(2,1)S(1)} %get-tuple-element.94), channel_id=1, source_target_pairs={{0,24},{2,26},{4,28},{6,30},{8,16},{10,18},{12,20},{14,22},{16,8},... | collective-permute-start | bytes 786440 | tf_op jit(solution)/shard_map/ppermute | solution.py:26
  1162.5 23.0 %collective-permute-start.38 = (bf16[128,1024]{1,0:T(8,128)(2,1)S(1)}, bf16[128,1024]{1,0:T(8,128)(2,1)S(1)}, u32[]{:S(2)}, u32[]{:S(2)}) collective-permute-start(bf16[128,1024]{1,0:T(8,128)(2,1)S(1)} %get-tuple-element.95), channel_id=1, source_target_pairs={{0,16},{2,18},{4,20},{6,22},{8,24},{10,26},{12,28},{14,30},{16,0},... | collective-permute-start | bytes 786440 | tf_op jit(solution)/shard_map/ppermute | solution.py:26
  (52 other events, 460.4 us)
Sparse Core Ops, SparseCore 0:
  10.7 77.0 all-gather.5
  89.9 102.5 all-gather.7
  194.8 142.9 all-gather.11
  340.0 98.7 all-gather.9
  440.8 98.6 all-gather.13
  568.1 133.1 reduce-scatter.5
  705.4 161.7 reduce-scatter.3
  871.2 201.9 reduce-scatter.7

commit v2 on v1

v2 whole, which is shorter than its diff:
```python
import functools
import math

import jax
import jax.numpy as jnp
from jax import lax
from jax.experimental import pallas as pl
from jax.experimental.pallas import tpu as pltpu
from jax.sharding import PartitionSpec as P

QUERY_HEADS = 16
KEY_VALUE_HEADS = 8
HD = 128
DOCS = 4
CHUNK = 256
eps = 1e-06
rope_base = 1000000.0
SCALE = HD ** (-0.5)
EXP2_SCALE = SCALE * math.log2(math.e)
F32 = jnp.float32
BF16 = jnp.bfloat16


def xor_send(value, axis, step):
    count = lax.axis_size(axis)
    return lax.ppermute(value, axis, [(i, i ^ step) for i in range(count)])


def exchange_rows(rows, axis):
    return [rows] + [xor_send(rows, axis, r) for r in range(1, lax.axis_size(axis))]


def scatter_rows(partial, axis):
    count = lax.axis_size(axis)
    rows = partial.shape[0] // count
    total = partial[:rows].astype(F32)
    for r in range(1, count):
        total = total + xor_send(partial[r * rows : (r + 1) * rows], axis, r).astype(F32)
    return total


def pair_groups(count):
    return [[i for i in range(count) if (i >> 1) & 1 == bit] for bit in (0, 1)]


def swap_blocks(x, count, axis):
    shape = x.shape
    split = x.reshape(shape[:axis] + (count // 4, 2, 2, shape[axis] // count) + shape[axis + 1 :])
    return split.swapaxes(axis + 1, axis + 2).reshape(shape)


def assemble_kernel(plan, *refs):
    out_ref = refs[-1]
    place = 0
    for index, start, number in plan:
        out_ref[place : place + number, :] = refs[index][start : start + number, :]
        place += number


def assemble(arrays, plan):
    width = arrays[0].shape[1]
    rows = sum(number for _, _, number in plan)
    return pl.pallas_call(
        functools.partial(assemble_kernel, plan),
        out_shape=jax.ShapeDtypeStruct((rows, width), arrays[0].dtype),
        compiler_params=vmem_limit(32),
        cost_estimate=pl.CostEstimate(
            flops=0, bytes_accessed=4 * rows * width, transcendentals=0
        ),
        name="assemble",
    )(*arrays)


def gather_rows(rows, ways):
    count = lax.axis_size("fsdp")
    total = rows.shape[0]
    if ways == 1:
        return assemble(exchange_rows(rows, "fsdp"), [(r, 0, total) for r in range(count)])
    block = total // 2
    low = rows[:block]
    lows = exchange_rows(low, "fsdp")
    high = jnp.concatenate([rows[block:], xor_send(rows[block:], "ctx", 2)], axis=0)
    highs = exchange_rows(high, "fsdp")
    others = xor_send(jnp.concatenate(lows, axis=0), "ctx", 2)
    plan = []
    for r in range(count):
        plan += [(1 + r, 0, block), (0, r * block, block), (1 + count + r, 0, 2 * block)]
    return assemble([others] + lows + highs, plan)


def return_rows(partial, ways):
    count = lax.axis_size("fsdp")
    if ways == 1:
        rows = partial.shape[0] // count
        terms = [partial[:rows]] + [
            xor_send(partial[r * rows : (r + 1) * rows], "fsdp", r) for r in range(1, count)
        ]
        return [t[: rows // 2] for t in terms], [t[rows // 2 :] for t in terms]
    block = partial.shape[0] // (4 * count)

    def rows(start, number):
        return partial[start * block : (start + number) * block]

    sent = jnp.concatenate([rows(4 * r + 1, 1) for r in range(count)], axis=0)
    pairs = [xor_send(rows(4 * r + 2, 2), "fsdp", r) for r in range(1, count)]
    other = xor_send(sent, "ctx", 2)
    first = [
        (rows(4 * r, 1).astype(F32) + other[r * block : (r + 1) * block].astype(F32)).astype(BF16)
        for r in range(count)
    ]
    second = rows(2, 2).astype(F32)
    for term in pairs:
        second = second + term.astype(F32)
    second = second.astype(BF16)
    lows = [first[0]] + [xor_send(first[r], "fsdp", r) for r in range(1, count)]
    return lows, [second[:block], xor_send(second[block:], "ctx", 2)]


def natural_columns(x, count):
    width = x.shape[1] // count
    order = [(i & ~3) | ((i & 1) << 1) | ((i >> 1) & 1) for i in range(count)]
    return jnp.concatenate([x[:, i * width : (i + 1) * width] for i in order], axis=1)


ROWS = 16


def over_rows(number, body, carry=None):
    def step(i, carry):
        return body(pl.multiple_of(i * ROWS, ROWS), carry)

    return lax.fori_loop(0, number // ROWS, step, carry)


def row_scale(x):
    return lax.rsqrt(jnp.mean(x * x, axis=-1, keepdims=True) + eps)


def entry_kernel(count, tok_ref, cot_ref, gain_ref, h_ref, x_ref, c_ref):
    def body(at, carry):
        rows = pl.ds(at, ROWS)
        x = natural_columns(tok_ref[rows, :], count)
        x_ref[rows, :] = x
        wide = x.astype(F32)
        h_ref[rows, :] = (wide * row_scale(wide) * gain_ref[...]).astype(BF16)
        c_ref[rows, :] = natural_columns(cot_ref[rows, :], count)
        return carry

    over_rows(tok_ref.shape[0], body, 0)


def sum_terms(refs, rows):
    total = refs[0][rows, :].astype(F32)
    for ref in refs[1:]:
        total = total + ref[rows, :].astype(F32)
    return total


def middle_kernel(lows, highs, *refs):
    x_ref, gain_ref, x2_ref, h_ref = refs[0], refs[1], refs[-2], refs[-1]
    block = x_ref.shape[0] // 2
    for half, terms in ((0, refs[2 : 2 + lows]), (1, refs[2 + lows : 2 + lows + highs])):

        def body(at, carry):
            rows = pl.ds(half * block + at, ROWS)
            x2 = x_ref[rows, :].astype(F32) + sum_terms(terms, pl.ds(at, ROWS))
            x2_ref[rows, :] = x2
            h_ref[rows, :] = (x2 * row_scale(x2) * gain_ref[...]).astype(BF16)
            return carry

        over_rows(block, body, 0)


def result_kernel(lows, highs, count, *refs):
    x_ref, out_ref = refs[0], refs[-1]
    block = x_ref.shape[0] // 2
    for half, terms in ((0, refs[1 : 1 + lows]), (1, refs[1 + lows : 1 + lows + highs])):

        def body(at, carry):
            rows = pl.ds(half * block + at, ROWS)
            total = x_ref[rows, :] + sum_terms(terms, pl.ds(at, ROWS))
            out_ref[rows, :] = natural_columns(total, count).astype(BF16)
            return carry

        over_rows(block, body, 0)


def back_kernel(lows, highs, count, *refs):
    base_ref, x_ref, gain_ref = refs[:3]
    wide_ref, gain_out = refs[3 + lows + highs], refs[-1]
    low_ref = refs[4 + lows + highs] if count is None else None
    block = x_ref.shape[0] // 2
    total = jnp.zeros((ROWS, x_ref.shape[1]), F32)
    for half, terms in ((0, refs[3 : 3 + lows]), (1, refs[3 + lows : 3 + lows + highs])):

        def body(at, carry):
            rows = pl.ds(half * block + at, ROWS)
            grad = sum_terms(terms, pl.ds(at, ROWS))
            x = x_ref[rows, :].astype(F32)
            scale = row_scale(x)
            unit = x * scale
            scaled = grad * gain_ref[...]
            out = base_ref[rows, :].astype(F32) + scale * (
                scaled - unit * jnp.mean(scaled * unit, axis=-1, keepdims=True)
            )
            if count is None:
                wide_ref[rows, :] = out
                low_ref[rows, :] = out.astype(BF16)
            else:
                wide_ref[rows, :] = natural_columns(out, count)
            return carry + grad * unit

        total = over_rows(block, body, total)
    gain_out[...] = jnp.sum(total, axis=0, keepdims=True)


def row_pass(kernel, args, outs, name):
    return pl.pallas_call(
        kernel,
        out_shape=outs,
        compiler_params=vmem_limit(40),
        cost_estimate=pl.CostEstimate(
            flops=10 * args[0].size, bytes_accessed=10 * args[0].size, transcendentals=0
        ),
        name=name,
    )(*args)


def pair_columns(weights, pair, ways):
    shares = []
    for place in (pair, 1 - pair):
        parts = []
        for weight in weights:
            columns = weight.shape[1] // ways
            parts.append(lax.dynamic_slice_in_dim(weight, place * columns, columns, 1))
        shares.append(jnp.concatenate(parts, axis=1))
    return shares


def swap_shards(mine, theirs, pair):
    theirs = xor_send(theirs, "ctx", 2)
    return jnp.concatenate(
        [jnp.where(pair == 0, mine, theirs), jnp.where(pair == 0, theirs, mine)], axis=0
    )


def ctx_gather(rows, ways):
    groups = pair_groups(lax.axis_size("ctx")) if ways == 2 else None
    return lax.all_gather(rows, "ctx", axis=0, tiled=True, axis_index_groups=groups)


def ctx_scatter(rows, ways):
    groups = pair_groups(lax.axis_size("ctx")) if ways == 2 else None
    return lax.psum_scatter(
        rows, "ctx", scatter_dimension=0, tiled=True, axis_index_groups=groups
    )


def gather_weight(shard, ways):
    full = ctx_gather(shard, ways)
    return swap_blocks(full, lax.axis_size("ctx"), 0) if ways == 1 else full


def scatter_weight(grad, ways):
    if ways == 1:
        grad = swap_blocks(grad, lax.axis_size("ctx"), 0)
    return ctx_scatter(grad, ways)


def own_rows(both, pair, ways):
    if ways == 1:
        return both.astype(F32)
    rows = both.shape[0] // 2
    kept = lax.dynamic_slice_in_dim(both, pair * rows, rows, 0)
    other = xor_send(lax.dynamic_slice_in_dim(both, (1 - pair) * rows, rows, 0), "ctx", 2)
    low, high = jnp.where(pair == 0, kept, other), jnp.where(pair == 0, other, kept)
    return jnp.concatenate([low, high], axis=1).astype(F32)


def butterfly_sum(value):
    for axis in ("ctx", "fsdp"):
        step = 1
        while step < lax.axis_size(axis):
            value = value + xor_send(value, axis, step)
            step *= 2
    return value


def dot(left, right):
    return jnp.dot(left, right, preferred_element_type=F32)


def dot_rows(left, right):
    return lax.dot_general(left, right, (((0,), (0,)), ((), ())), preferred_element_type=F32)


def dot_cols(left, right):
    return lax.dot_general(left, right, (((1,), (1,)), ((), ())), preferred_element_type=F32)


def vmem_limit(mib):
    return pltpu.CompilerParams(vmem_limit_bytes=mib * 1024 * 1024)


def prep_kernel(query_heads, groups, raw_ref, cos_ref, sin_ref, gq_ref, gk_ref, q_ref, kv_ref):
    cos = cos_ref[...]
    sin = sin_ref[...]

    def rotate_norm(x, gain):
        scale = lax.rsqrt(jnp.mean(x * x, axis=-1, keepdims=True) + eps)
        u = x * scale * gain
        return u * cos + pltpu.roll(u, HD // 2, 1) * sin

    for h in range(query_heads):
        cols = slice(h * HD, (h + 1) * HD)
        q_ref[:, cols] = rotate_norm(raw_ref[:, cols], gq_ref[...]).astype(BF16)
    for h in range(2 * groups):
        x = raw_ref[:, (query_heads + h) * HD : (query_heads + h + 1) * HD]
        if h % 2 == 0:
            x = rotate_norm(x, gk_ref[...])
        kv_ref[:, h * HD : (h + 1) * HD] = x.astype(BF16)


def head_prep(raw, cos, sin, gq, gk, query_heads, groups):
    rows, width = raw.shape
    tile = 256
    vec = pl.BlockSpec((1, HD), lambda i: (0, 0))
    tab = pl.BlockSpec((tile, HD), lambda i: (i, 0))
    return pl.pallas_call(
        functools.partial(prep_kernel, query_heads, groups),
        out_shape=(
            jax.ShapeDtypeStruct((rows, query_heads * HD), BF16),
            jax.ShapeDtypeStruct((rows, 2 * groups * HD), BF16),
        ),
        grid=(rows // tile,),
        in_specs=[pl.BlockSpec((tile, width), lambda i: (i, 0)), tab, tab, vec, vec],
        out_specs=(
            pl.BlockSpec((tile, query_heads * HD), lambda i: (i, 0)),
            pl.BlockSpec((tile, 2 * groups * HD), lambda i: (i, 0)),
        ),
        cost_estimate=pl.CostEstimate(
            flops=20 * raw.size, bytes_accessed=6 * raw.size, transcendentals=0
        ),
        name="head_prep",
    )(raw, cos, sin, gq, gk)


def prep_back_kernel(heads, plain, d_ref, raw_ref, cos_ref, sin_ref, g_ref, out_ref, gain_ref):
    cos = cos_ref[...]
    sin = sin_ref[...]
    gain = g_ref[...]
    gain_sum = jnp.zeros((1, HD), F32)
    for h in range(heads):
        cols = slice(h * HD, (h + 1) * HD)
        d = d_ref[:, cols]
        if plain and h % 2 == 1:
            out_ref[:, cols] = d.astype(BF16)
            continue
        x = raw_ref[:, cols]
        t = d * cos - pltpu.roll(d, HD // 2, 1) * sin
        scale = lax.rsqrt(jnp.mean(x * x, axis=-1, keepdims=True) + eps)
        n = x * scale
        gain_sum = gain_sum + jnp.sum(t * n, axis=0, keepdims=True)
        e = t * gain
        out_ref[:, cols] = (scale * (e - n * jnp.mean(e * n, axis=-1, keepdims=True))).astype(BF16)

    @pl.when(pl.program_id(0) == 0)
    def _():
        gain_ref[...] = jnp.zeros_like(gain_ref)

    gain_ref[...] += gain_sum


def head_prep_back(grad, raw, cos, sin, gain, raw_block, plain):
    rows, width = grad.shape
    tile = 256
    tab = pl.BlockSpec((tile, HD), lambda i: (i, 0))
    return pl.pallas_call(
        functools.partial(prep_back_kernel, width // HD, plain),
        out_shape=(
            jax.ShapeDtypeStruct((rows, width), BF16),
            jax.ShapeDtypeStruct((1, HD), F32),
        ),
        grid=(rows // tile,),
        in_specs=[
            pl.BlockSpec((tile, width), lambda i: (i, 0)),
            pl.BlockSpec((tile, width), lambda i: (i, raw_block)),
            tab,
            tab,
            pl.BlockSpec((1, HD), lambda i: (0, 0)),
        ],
        out_specs=(
            pl.BlockSpec((tile, width), lambda i: (i, 0)),
            pl.BlockSpec((1, HD), lambda i: (0, 0)),
        ),
        cost_estimate=pl.CostEstimate(
            flops=20 * rows * width, bytes_accessed=10 * rows * width, transcendentals=0
        ),
        name="head_prep_back",
    )(grad, raw, cos, sin, gain)


def block_place(pair, shard, place, ways, count):
    owner = shard
    if ways == 2:
        other = (pair + place % 2) % 2 if isinstance(pair, int) else lax.rem(pair + place % 2, 2)
        owner = (shard // 2) * 4 + 2 * other + shard % 2
    return owner if place < ways else 2 * count - 1 - owner


def load_sequence(pair, ways, kv_ref, keys, values):
    shards, _, _, block, _ = kv_ref.shape
    for shard in range(shards):
        for place in range(2 * ways):
            index = block_place(pair, shard, place, ways, shards * ways)
            rows = pl.ds(pl.multiple_of(index * block, block), block)
            keys[rows, :] = kv_ref[shard, 0, place, :, :HD]
            values[rows, :] = kv_ref[shard, 0, place, :, HD:]


def stack_heads(tile, count):
    return jnp.concatenate([tile[:, h * HD : (h + 1) * HD] for h in range(count)], axis=0)


def row_positions(info_ref, place, block, count):
    base = pl.program_id(0) * (info_ref.shape[0] // pl.num_programs(0)) + 1 + 3 * place
    first = info_ref[base]
    lane = lax.broadcasted_iota(jnp.int32, (1, count * block), 1)
    position = first + lax.rem(lane, block)
    start_first, start_last = info_ref[base + 1], info_ref[base + 2]
    start = jnp.where(position >= start_last, start_last, start_first)
    return position, start, start_first // CHUNK, (first + block - 1) // CHUNK + 1


def valid_tile(chunk, position, start, shape):
    key_index = chunk * CHUNK + lax.broadcasted_iota(jnp.int32, shape, 0)
    return (key_index <= position) & (key_index >= start)


def forward_kernel(ways, count, info_ref, q_ref, kv_ref, o_ref, lse_ref, keys, values):
    load_sequence(info_ref[0], ways, kv_ref, keys, values)
    block = q_ref.shape[2]
    columns = count * block
    for place in range(2 * ways):
        queries = stack_heads(q_ref[0, place], count)
        position, start, low, high = row_positions(info_ref, place, block, count)

        def body(chunk, carry):
            total, norm = carry
            rows = pl.ds(pl.multiple_of(chunk * CHUNK, CHUNK), CHUNK)
            score = dot_cols(keys[rows, :], queries)
            weight = jnp.where(
                valid_tile(chunk, position, start, score.shape), jnp.exp2(score * EXP2_SCALE), 0.0
            )
            norm = norm + jnp.sum(weight, axis=0, keepdims=True)
            total = total + dot_rows(values[rows, :], weight.astype(BF16))
            return total, norm

        total, norm = lax.fori_loop(
            low, high, body, (jnp.zeros((HD, columns), F32), jnp.zeros((1, columns), F32))
        )
        out = (total / norm).T.astype(BF16)
        for h in range(count):
            o_ref[0, place, :, h * HD : (h + 1) * HD] = out[h * block : (h + 1) * block]
        lse_ref[0, 0, place] = jnp.log2(norm)


def backward_kernel(
    ways, count, info_ref, q_ref, do_ref, o_ref, lse_ref, kv_ref,
    dq_ref, dkv_ref, keys, values, grad_k, grad_v,
):
    pair = info_ref[0]
    load_sequence(pair, ways, kv_ref, keys, values)
    block = q_ref.shape[2]
    columns = count * block
    grad_k[...] = jnp.zeros_like(grad_k)
    grad_v[...] = jnp.zeros_like(grad_v)
    for place in range(2 * ways):
        queries = stack_heads(q_ref[0, place], count)
        grads = stack_heads(do_ref[0, place], count)
        outs = stack_heads(o_ref[0, place], count)
        delta = jnp.sum((grads.astype(F32) * outs.astype(F32)).T, axis=0, keepdims=True)
        lse = lse_ref[0, 0, place]
        position, start, low, high = row_positions(info_ref, place, block, count)

        def body(chunk, total):
            rows = pl.ds(pl.multiple_of(chunk * CHUNK, CHUNK), CHUNK)
            key_rows = keys[rows, :]
            score = dot_cols(key_rows, queries)
            prob = jnp.where(
                valid_tile(chunk, position, start, score.shape),
                jnp.exp2(score * EXP2_SCALE - lse),
                0.0,
            )
            grad_prob = dot_cols(values[rows, :], grads)
            grad_score = (prob * (grad_prob - delta)).astype(BF16)
            grad_v[rows, :] += dot(prob.astype(BF16), grads)
            grad_k[rows, :] += dot(grad_score, queries)
            return total + dot_rows(key_rows, grad_score)

        total = lax.fori_loop(low, high, body, jnp.zeros((HD, columns), F32))
        out = total.T * SCALE
        for h in range(count):
            dq_ref[0, place, :, h * HD : (h + 1) * HD] = out[h * block : (h + 1) * block]
    shards = dkv_ref.shape[0]
    for shard in range(shards):
        for place in range(2 * ways):
            index = block_place(pair, shard, place, ways, shards * ways)
            rows = pl.ds(pl.multiple_of(index * block, block), block)
            dkv_ref[shard, 0, place, :, :HD] = (grad_k[rows, :] * SCALE).astype(BF16)
            dkv_ref[shard, 0, place, :, HD:] = grad_v[rows, :].astype(BF16)


def attention_specs(q, kv, count):
    shards, sequences, places, block, width = kv.shape
    row = pl.BlockSpec((1, places, block, count * HD), lambda s, n, i: (s, 0, 0, n))
    part = pl.BlockSpec((shards, 1, places, block, 2 * HD), lambda s, n, i: (0, s, 0, 0, n))
    sums = pl.BlockSpec((1, 1, places, 1, count * block), lambda s, n, i: (s, n, 0, 0, 0))
    sums_shape = (sequences, width // (2 * HD), places, 1, count * block)
    return row, part, sums, sums_shape, shards * places * block


def attend(info, q, kv, count, ways):
    row, part, sums, sums_shape, length = attention_specs(q, kv, count)
    return pl.pallas_call(
        functools.partial(forward_kernel, ways, count),
        out_shape=(
            jax.ShapeDtypeStruct(q.shape, BF16),
            jax.ShapeDtypeStruct(sums_shape, F32),
        ),
        grid_spec=pltpu.PrefetchScalarGridSpec(
            num_scalar_prefetch=1,
            grid=sums_shape[:2],
            in_specs=[row, part],
            out_specs=(row, sums),
            scratch_shapes=[pltpu.VMEM((length, HD), BF16)] * 2,
        ),
        compiler_params=vmem_limit(48),
        cost_estimate=pl.CostEstimate(
            flops=4 * 8 * CHUNK * q.size, bytes_accessed=2 * kv.size, transcendentals=0
        ),
        name="attend",
    )(info, q, kv)


def attend_back(info, q, grad, out, lse, kv, count, ways):
    row, part, sums, sums_shape, length = attention_specs(q, kv, count)
    return pl.pallas_call(
        functools.partial(backward_kernel, ways, count),
        out_shape=(
            jax.ShapeDtypeStruct(q.shape, F32),
            jax.ShapeDtypeStruct(kv.shape, BF16),
        ),
        grid_spec=pltpu.PrefetchScalarGridSpec(
            num_scalar_prefetch=1,
            grid=sums_shape[:2],
            in_specs=[row, row, row, sums, part],
            out_specs=(row, part),
            scratch_shapes=[pltpu.VMEM((length, HD), BF16)] * 2
            + [pltpu.VMEM((length, HD), F32)] * 2,
        ),
        compiler_params=vmem_limit(56),
        cost_estimate=pl.CostEstimate(
            flops=10 * 8 * CHUNK * q.size, bytes_accessed=4 * kv.size, transcendentals=0
        ),
        name="attend_back",
    )(info, q, grad, out, lse, kv)


def interleave_heads(first, second):
    rows, width = first.shape
    heads = width // HD
    both = jnp.stack([first.reshape(rows, heads, HD), second.reshape(rows, heads, HD)], axis=2)
    return both.reshape(rows, 2 * width)


def after(value, earlier):
    return lax.optimization_barrier((value, earlier))[0]


def local(
    tokens,
    grad_out,
    segments,
    w_query,
    key_weight_matrix,
    value_weight_matrix,
    w_output,
    w_gate,
    w_up,
    w_down,
    norm_attn,
    norm_mlp,
    norm_query,
    norm_key,
):
    ctx_count = lax.axis_size("ctx")
    seq_count = lax.axis_size("fsdp")
    me = lax.axis_index("ctx").astype(jnp.int32)
    my_seq = lax.axis_index("fsdp").astype(jnp.int32)
    pair = lax.rem(me // 2, 2)
    block = tokens.shape[3]
    width = tokens.shape[4]
    own = 2 * block
    ways = 2 if (key_weight_matrix.shape[1] // HD) % 2 == 0 else 1
    query_heads = w_query.shape[1] // HD // ways
    groups = key_weight_matrix.shape[1] // HD // ways
    count = query_heads // groups
    q_width, kv_width = query_heads * HD, 2 * groups * HD
    hidden = w_gate.shape[1] // 2

    w_kv = interleave_heads(key_weight_matrix, value_weight_matrix)
    gain_attn_row = swap_blocks(norm_attn[None], ctx_count, 1)
    gain_mlp_row = swap_blocks(norm_mlp[None], ctx_count, 1)

    qkv_width = q_width + kv_width
    if ways == 2:
        early = swap_shards(*pair_columns([w_query, w_kv, w_output], pair, 2), pair)
        qkv_shard, output_shard = early[:, :qkv_width], early[:, qkv_width:]
    else:
        qkv_shard, output_shard = jnp.concatenate([w_query, w_kv], axis=1), w_output
    full_qkv = gather_weight(qkv_shard, ways)
    full_output = gather_weight(output_shard, ways)

    row_bf16 = jax.ShapeDtypeStruct((own, width), BF16)
    row_f32 = jax.ShapeDtypeStruct((own, width), F32)
    gain_shape = jax.ShapeDtypeStruct((1, width), F32)
    h1_own, inputs, cot_own = row_pass(
        functools.partial(entry_kernel, ctx_count),
        (tokens.reshape(own, width), grad_out.reshape(own, width), gain_attn_row),
        (row_bf16, row_bf16, row_bf16),
        "entry",
    )
    h1 = gather_rows(h1_own, ways)

    offsets = jnp.arange(block, dtype=jnp.int32)
    owners = [me, me + 2 - 4 * pair][:ways]
    firsts = [o * block for o in owners + [2 * ctx_count - 1 - o for o in owners]]
    freq = jnp.exp(jnp.arange(HD // 2, dtype=F32) * (-2.0 * math.log(rope_base) / HD))
    infos, positions = [], []
    for r in range(seq_count):
        line = lax.dynamic_index_in_dim(
            segments, lax.bitwise_xor(my_seq, jnp.int32(r)), 0, keepdims=False
        )
        doc_first = [jnp.sum((line < d).astype(jnp.int32)) for d in range(DOCS)]
        scalars = [pair]
        for first in firsts:
            mine = lax.dynamic_slice_in_dim(line, first, block)
            start = sum(jnp.where(mine == d, doc_first[d], 0) for d in range(DOCS))
            scalars += [first, start[0], start[block - 1]]
            positions.append(first + offsets - start)
        infos += scalars
    info = jnp.stack(infos)
    angle = jnp.concatenate(positions).astype(F32)[:, None] * freq
    cos, sin = jnp.cos(angle), jnp.sin(angle)
    cos, sin = jnp.concatenate([cos, cos], 1), jnp.concatenate([-sin, sin], 1)
    gain_q, gain_k = norm_query.reshape(1, HD), norm_key.reshape(1, HD)

    raw = dot(h1, full_qkv)
    q, kv = head_prep(raw, cos, sin, gain_q, gain_k, query_heads, groups)
    q = q.reshape(seq_count, 2 * ways, block, q_width)

    mine, theirs = pair_columns([w_gate, w_up, w_down], pair, 2)
    shards = swap_shards(mine, after(theirs, h1), pair)
    full_kv = ctx_gather(after(kv, full_output), ways).reshape(-1, seq_count, 2 * ways, block, kv_width)
    shards = after(shards, kv)
    full_gate, full_up, full_down = (
        gather_weight(shards[:, i * hidden : (i + 1) * hidden], 2) for i in range(3)
    )
    cot_all = gather_rows(after(cot_own, shards), 2)

    q = after(q, cot_all)
    heads, lse = attend(info, q, full_kv, count, ways)
    mixed = heads.reshape(-1, q_width)
    lows, highs = return_rows(dot_cols(mixed, full_output).astype(BF16), ways)
    x2, h2_own = row_pass(
        functools.partial(middle_kernel, len(lows), len(highs)),
        (inputs, gain_mlp_row, *lows, *highs),
        (row_f32, row_bf16),
        "middle",
    )
    h2 = gather_rows(h2_own, 2)

    gate = dot(h2, full_gate)
    up = dot(h2, full_up)
    act = lax.optimization_barrier((gate / (1.0 + jnp.exp(-gate)) * up).astype(BF16))
    grad_down = dot_rows(cot_all, act).astype(BF16)
    d_act = dot(after(cot_all, grad_down), full_down)
    sg = 1.0 / (1.0 + jnp.exp(-gate))
    d_gate = (d_act * up * sg * (1.0 + gate * (1.0 - sg))).astype(BF16)
    d_up = (d_act * gate * sg).astype(BF16)
    d_h2_part = (dot_cols(d_gate, full_gate) + dot_cols(d_up, full_up)).astype(BF16)
    lows, highs = return_rows(d_h2_part, 2)
    h2_late, act_late = after((h2, act), d_h2_part)
    grad_gate = dot_rows(h2_late, d_gate).astype(BF16)
    grad_up = dot_rows(h2_late, d_up).astype(BF16)
    y_part = dot_cols(act_late, full_down).astype(BF16)
    lows[0] = after(lows[0], (grad_gate, grad_up, y_part))
    d_x2, d_x2_low, gain_mlp = row_pass(
        functools.partial(back_kernel, len(lows), len(highs), None),
        (cot_own, x2, gain_mlp_row, *lows, *highs),
        (row_f32, row_bf16, gain_shape),
        "middle_back",
    )
    branch = gather_rows(d_x2_low, ways)
    rows_down = scatter_weight(grad_down, 2)
    rows_gate = scatter_weight(after(grad_gate, rows_down), 2)
    grad_output = after(dot_rows(branch, mixed).astype(BF16), rows_gate)
    rows_output = scatter_weight(grad_output, ways)
    d_att = dot(branch, full_output).astype(BF16).reshape(q.shape)

    lows, highs = return_rows(after(y_part, branch), 2)
    out_tokens = row_pass(
        functools.partial(result_kernel, len(lows), len(highs), ctx_count),
        (x2, *lows, *highs),
        row_bf16,
        "result",
    ).reshape(tokens.shape)

    d_q, d_kv = attend_back(info, q, d_att, heads, lse, full_kv, count, ways)
    d_kv = after(d_kv.reshape(-1, kv_width), rows_output)
    d_kv = ctx_scatter(d_kv, ways).astype(F32)
    shard_down = own_rows(rows_down, pair, 2)
    shard_gate = own_rows(rows_gate, pair, 2)
    shard_output = own_rows(rows_output, pair, ways)
    d_kv = after(d_kv, (out_tokens, shard_down, shard_gate, shard_output))
    d_qp, gain_q_sum = head_prep_back(
        d_q.reshape(-1, q_width), raw, cos, sin, gain_q, 0, False
    )
    d_kvp, gain_k_sum = head_prep_back(d_kv, raw, cos, sin, gain_k, q_width // kv_width, True)
    d_h1 = (
        dot_cols(d_qp, full_qkv[:, :q_width]) + dot_cols(d_kvp, full_qkv[:, q_width:])
    ).astype(BF16)
    lows, highs = return_rows(d_h1, ways)
    d_raw = jnp.concatenate([d_qp, d_kvp], axis=1)
    grad_qkv = dot_rows(after(h1, d_h1), d_raw).astype(BF16)

    rows_up = scatter_weight(grad_up, 2)
    rows_qkv = scatter_weight(grad_qkv, ways)
    grad_tokens, gain_attn = row_pass(
        functools.partial(back_kernel, len(lows), len(highs), ctx_count),
        (d_x2, inputs, gain_attn_row, *lows, *highs),
        (row_f32, gain_shape),
        "entry_back",
    )
    rows_up, rows_qkv = after((rows_up, rows_qkv), gain_attn)
    shard_up = own_rows(rows_up, pair, 2)
    shard_query = own_rows(rows_qkv[:, :q_width], pair, ways)
    shard_kv = own_rows(rows_qkv[:, q_width:], pair, ways)
    shard_kv = shard_kv.reshape(shard_kv.shape[0], -1, 2, HD)
    grad_tokens = grad_tokens.reshape(tokens.shape)
    gains = butterfly_sum(
        jnp.concatenate([gain_attn[0], gain_mlp[0], gain_q_sum[0], gain_k_sum[0]])
    )
    return (
        out_tokens,
        grad_tokens,
        shard_query,
        shard_kv[:, :, 0].reshape(key_weight_matrix.shape),
        shard_kv[:, :, 1].reshape(value_weight_matrix.shape),
        shard_output,
        shard_gate,
        shard_up,
        shard_down,
        swap_blocks(gains[None, :width], ctx_count, 1)[0],
        swap_blocks(gains[None, width : 2 * width], ctx_count, 1)[0],
        gains[2 * width : 2 * width + HD],
        gains[2 * width + HD :],
    )


def solution(mesh):
    block = P("fsdp", "ctx", None, None, None)
    weight = P("ctx", "fsdp")
    return jax.shard_map(
        local,
        mesh=mesh,
        in_specs=(block, block, P()) + (weight,) * 7 + (P(),) * 4,
        out_specs=(block, block) + (weight,) * 7 + (P(),) * 4,
        check_vma=False,
    )
```

time: 1210 us -> 840 us (0.69)
  waiting for transfers between devices: 646 us -> 406 us
  blocking collectives: 56.3 us -> 0 us
  starting transfers between devices: 118 us -> 64.9 us
  Pallas kernels: 114 us -> 81 us
  local copies, waits for them, and re-layouts: 34.5 us -> 58.4 us
  matrix products: 158 us -> 143 us
    ppermute x45, waiting for transfers between devices: 510 us -> 236 us  [xor_send(): return lax.ppermute(value, axis, [(i, i ^ step) for i in range(count)])]
    reduce_scatter x3 -> x6, waiting for transfers between devices: 0.01 us -> 101 us  [ctx_scatter(): lax.psum_scatter(rows, 'ctx', scatter_dimension=0, tiled=True, axis_index...]
    all_gather x5 -> x6, waiting for transfers between devices: 133 us -> 67.9 us  [ctx_gather(): lax.all_gather(rows, 'ctx', axis=0, tiled=True, axis_index_groups=groups)]
    psum x1 -> x0, blocking collectives: 56.3 us -> none  [local(): lax.psum(jnp.concatenate([gain_attn, gain_mlp, gain_q_sum[0], gain_k_sum[...]
    ppermute x45, starting transfers between devices: 118 us -> 63.4 us  [xor_send(): return lax.ppermute(value, axis, [(i, i ^ step) for i in range(count)])]
    pallas_call x10 -> x13, Pallas kernels: 104 us -> 74.8 us  [the longest x1 27.3 us: attend_back(): pl.pallas_call(functools.partial(backward_kernel, ways, count), out_shape...]
    unnamed x1 -> x8, other arithmetic: 0.01 us -> 22.9 us
    dot_general x9 -> x5, matrix products: 50 us -> 38.3 us  [dot_rows(): lax.dot_general(left, right, (((0,), (0,)), ((), ())), preferred_element_...]
  transfers between devices with their start and end apart: 53 -> 57, of which waited for: 22 -> 41; matrix products, arithmetic and copies ran while one was open for 18% -> 29% of each run, Pallas kernels for 9% -> 10%
where the time goes in v2:
time: 840 us; the launch traced here: 832 us
  waiting for transfers between devices  406 us (48%)
  matrix products  143 us (17%)
  Pallas kernels  81 us (10%)
  starting transfers between devices  64.9 us (8%)
  other arithmetic  62.7 us (7%)
  local copies, waits for them, and re-layouts  58.4 us (7%)
  between operations  15.4 us (2%)
    ppermute x45, waiting for transfers between devices, xor_send(): return lax.ppermute(value, axis, [(i, i ^ step) for i in range(count)])  236 us
    reduce_scatter x6, waiting for transfers between devices, ctx_scatter(): lax.psum_scatter(rows, 'ctx', scatter_dimension=0, tiled=True, axis_index...  101 us
    all_gather x6, waiting for transfers between devices, ctx_gather(): lax.all_gather(rows, 'ctx', axis=0, tiled=True, axis_index_groups=groups)  67.9 us
    ppermute x45, starting transfers between devices, xor_send(): return lax.ppermute(value, axis, [(i, i ^ step) for i in range(count)])  63.4 us
    dot_general x5, matrix products, dot(): return jnp.dot(left, right, preferred_element_type=F32)  55.1 us
    dot_general x6, matrix products, dot_cols(): lax.dot_general(left, right, (((1,), (1,)), ((), ())), preferred_element_...  49.4 us
    dot_general x5, matrix products, dot_rows(): lax.dot_general(left, right, (((0,), (0,)), ((), ())), preferred_element_...  38.3 us
    pallas_call x1, Pallas kernels, attend_back(): pl.pallas_call(functools.partial(backward_kernel, ways, count), out_shape...  27.3 us
  transfers between devices with their start and end apart: 57, of which 41 were waited for; matrix products, arithmetic and copies ran while one was open for 29% of the time, Pallas kernels for 10%

profile of v2, /device:TPU:0, one launch (start us, length us, event | category | flops | bytes accessed | tf_op | source)
XLA Modules:
  0.0 831.5 jit_solution(4001430669447284958)
XLA Ops:
  12.8 3.1 collective-permute-start.4
  15.9 9.1 %collective-permute-done.4 = bf16[128,1536]{1,0:T(8,128)(2,1)S(1)} collective-permute-done((bf16[128,1536]{1,0:T(8,128)(2,1)S(1)}, bf16[128,1536]{1,0:T(8,128)(2,1)S(1)}, u32[]{:S(2)}, u32[]{:S(2)}) %collective-permute-start.4) | collective-permute-done | bytes 393248 | tf_op jit(solution)/shard_map/ppermute | solution.py:26
  39.8 3.2 constant_dynamic-update-slice_fusion.7
  43.0 3.2 constant_dynamic-update-slice_fusion.6
  46.2 3.2 constant_dynamic-update-slice_fusion.5
  52.4 3.2 constant_dynamic-update-slice_fusion.4
  55.6 3.4 constant_dynamic-update-slice_fusion.3
  59.0 3.4 constant_dynamic-update-slice_fusion.2
  62.3 3.4 constant_dynamic-update-slice_fusion.1
  65.7 3.4 constant_dynamic-update-slice_fusion
  77.0 9.9 %fusion.75.raw_ref = f32[1024,1024]{1,0:T(8,128)} fusion(bf16[1024,2048]{1,0:T(8,128)(2,1)} %copy-done.2, bf16[2048,1024]{1,0:T(8,128)(2,1)} %all-gather.7.cloned.1.call-done), kind=kOutput, calls=%fused_computation.226 | convolution fusion | flops 4294967296 | bytes 12582912 | tf_op jit(solution)/shard_map/dot_general | solution.py:290
  86.9 6.2 head_prep.1
  93.1 12.3 %all-gather.9.cloned.1.call-done = bf16[2048,512]{1,0:T(8,128)(2,1)} async-done(((bf16[256,512]{1,0:T(8,128)(2,1)}), bf16[2048,512]{1,0:T(8,128)(2,1)}) %all-gather.9.cloned.1.call-update) | async-done | bytes 2097168 | tf_op jit(solution)/shard_map/all_gather | solution.py:249
  108.7 26.6 %collective-permute-done.5 = bf16[128,4608]{1,0:T(8,128)(2,1)S(1)} collective-permute-done((bf16[128,4608]{1,0:T(8,128)(2,1)S(1)}, bf16[128,4608]{1,0:T(8,128)(2,1)S(1)}, u32[]{:S(2)}, u32[]{:S(2)}) %collective-permute-start.5) | collective-permute-done | bytes 1179680 | tf_op jit(solution)/shard_map/ppermute | solution.py:26
  141.4 10.4 %collective-permute-done.6.refs_2_ = bf16[128,2048]{1,0:T(8,128)(2,1)S(1)} collective-permute-done((bf16[128,2048]{1,0:T(8,128)(2,1)S(1)}, bf16[128,2048]{1,0:T(8,128)(2,1)S(1)}, u32[]{:S(2)}, u32[]{:S(2)}) %collective-permute-start.6) | collective-permute-done | bytes 524320 | tf_op jit(solution)/shard_map/ppermute | solution.py:26
  161.7 10.1 %stack.31.info_ref = s32[26]{0:T(128)S(1)} concatenate(s32[1]{0:T(128)} %bitcast.8, s32[1]{0:T(128)} %bitcast.9, s32[1]{0:T(128)} %bitcast.10, s32[1]{0:T(128)} %bitcast.11, s32[1]{0:T(128)} %bitcast.12, s32[1]{0:T(128)} %bitcast.13, s32[1]{0:T(128)} %bitcast.14, s32[1]{0:T(128)} %bitcast.15, s32[1]{0:T(128)} %bitcast.16, s32[1]{0:T(128)} %bitcast.17, s32[1]{0:T(128)} %bitcast.18, ...), dimensions={0} | concatenate | bytes 208 | tf_op jit(solution)/shard_map/stack | solution.py:653
  171.8 5.1 collective-permute-done.7.refs_0_
  183.2 5.9 all-gather.11.cloned.1.call-done
  190.3 20.0 %attend.1 = (bf16[2,4,128,512]{3,2,1,0:T(8,128)(2,1)S(1)}, f32[2,2,4,1,256]{4,3,2,1,0:T(1,128)S(1)}) custom-call(s32[26]{0:T(128)S(1)} %stack.31.info_ref, bf16[2,4,128,512]{3,2,1,0:T(8,128)(2,1)S(1)} %bitcast.133, bf16[8,2,4,128,512]{4,3,2,1,0:T(8,128)(2,1)} %bitcast.157), custom_call_target="tpu_custom_call" | custom-call | flops 4294967296 | bytes 8388608 | tf_op jit(solution)/shard_map/attend/pallas_call | solution.py:525
  218.2 21.4 %collective-permute-done.10 = bf16[256,2048]{1,0:T(8,128)(2,1)S(1)} collective-permute-done((bf16[256,2048]{1,0:T(8,128)(2,1)}, bf16[256,2048]{1,0:T(8,128)(2,1)S(1)}, u32[]{:S(2)}, u32[]{:S(2)}) %collective-permute-start.10) | collective-permute-done | bytes 1048608 | tf_op jit(solution)/shard_map/ppermute | solution.py:26
  246.0 8.6 %collective-permute-done.11.refs_3_ = bf16[128,2048]{1,0:T(8,128)(2,1)S(1)} collective-permute-done((bf16[128,2048]{1,0:T(8,128)(2,1)S(1)}, bf16[128,2048]{1,0:T(8,128)(2,1)S(1)}, u32[]{:S(2)}, u32[]{:S(2)}) %collective-permute-start.11) | collective-permute-done | bytes 524320 | tf_op jit(solution)/shard_map/ppermute | solution.py:26
  254.6 3.0 collective-permute-done.13.refs_5_
  261.8 10.1 %collective-permute-done.14.refs_2_ = bf16[128,2048]{1,0:T(8,128)(2,1)S(1)} collective-permute-done((bf16[128,2048]{1,0:T(8,128)(2,1)S(1)}, bf16[128,2048]{1,0:T(8,128)(2,1)S(1)}, u32[]{:S(2)}, u32[]{:S(2)}) %collective-permute-start.14) | collective-permute-done | bytes 524320 | tf_op jit(solution)/shard_map/ppermute | solution.py:26
  274.7 20.1 %collective-permute-done.15.refs_0_ = bf16[256,2048]{1,0:T(8,128)(2,1)S(1)} collective-permute-done((bf16[256,2048]{1,0:T(8,128)(2,1)S(1)}, bf16[256,2048]{1,0:T(8,128)(2,1)S(1)}, u32[]{:S(2)}, u32[]{:S(2)}) %collective-permute-start.15) | collective-permute-done | bytes 1048608 | tf_op jit(solution)/shard_map/ppermute | solution.py:26
  298.4 11.8 %fusion.76 = f32[1024,1536]{1,0:T(8,128)} fusion(bf16[1024,2048]{1,0:T(8,128)(2,1)} %copy-done.6, bf16[2048,1536]{1,0:T(8,128)(2,1)} %all-gather.13.cloned.1.call-done), kind=kOutput, calls=%fused_computation.227 | convolution fusion | flops 6442450944 | bytes 16777216 | tf_op jit(solution)/shard_map/dot_general | solution.py:290
  310.2 8.7 %all-gather.15.cloned.1.call-done = bf16[2048,1536]{1,0:T(8,128)(2,1)} async-done(((bf16[256,1536]{1,0:T(8,128)(2,1)}), bf16[2048,1536]{1,0:T(8,128)(2,1)}) %all-gather.15.cloned.1.call-update) | async-done | bytes 6291472 | tf_op jit(solution)/shard_map/all_gather | solution.py:249
  318.8 13.1 %multiply_convert_fusion.2 = (bf16[1024,1536]{1,0:T(8,128)(2,1)S(1)}, f32[1024,1536]{1,0:T(8,128)}) fusion(f32[1024,1536]{1,0:T(8,128)} %fusion.76, bf16[1024,2048]{1,0:T(8,128)(2,1)} %copy-done.6, bf16[2048,1536]{1,0:T(8,128)(2,1)} %all-gather.15.cloned.1.call-done), kind=kOutput, calls=%fused_computation.7 | convolution fusion | flops 6450315264 | bytes 26214400 | tf_op jit(solution)/shard_map/dot_general | solution.py:290
  333.6 8.9 %convolution_convert_fusion.2 = bf16[2048,1536]{1,0:T(8,128)(2,1)} fusion(bf16[1024,2048]{1,0:T(8,128)(2,1)S(1)} %copy-done.5, bf16[1024,1536]{1,0:T(8,128)(2,1)S(1)} %get-tuple-element.64), kind=kOutput, calls=%fused_computation.4 | convolution fusion | flops 6445596672 | bytes 13631488 | tf_op jit(solution)/shard_map/dot_general | solution.py:294
  342.7 41.0 %all-gather.17.cloned.1.call-done = bf16[2048,1536]{1,0:T(8,128)(2,1)} async-done(((bf16[256,1536]{1,0:T(8,128)(2,1)}), bf16[2048,1536]{1,0:T(8,128)(2,1)}) %all-gather.17.cloned.1.call-update) | async-done | bytes 6291472 | tf_op jit(solution)/shard_map/all_gather | solution.py:249
  383.7 14.2 %multiply_convert_fusion = (bf16[1024,1536]{1,0:T(8,128)(2,1)S(1)}, bf16[1024,1536]{1,0:T(8,128)(2,1)S(1)}) fusion(f32[1024,1536]{1,0:T(8,128)} %fusion.76, f32[1024,1536]{1,0:T(8,128)} %get-tuple-element.204, bf16[1024,2048]{1,0:T(8,128)(2,1)} %copy-done.4, bf16[2048,1536]{1,0:T(8,128)(2,1)} %all-gather.17.cloned.1.call-done), kind=kOutput, calls=%fused_computation.5 | convolution fusion | flops 6462898176 | bytes 29360128 | tf_op jit(solution)/shard_map/dot_general | solution.py:290
  397.9 10.0 %fusion.77 = f32[1024,2048]{1,0:T(8,128)S(1)} fusion(bf16[1024,1536]{1,0:T(8,128)(2,1)S(1)} %get-tuple-element.114, bf16[2048,1536]{1,0:T(8,128)(2,1)} %all-gather.13.cloned.1.call-done), kind=kOutput, calls=%fused_computation.228 | convolution fusion | flops 6442450944 | bytes 17825792 | tf_op jit(solution)/shard_map/dot_general | solution.py:298
  407.9 11.4 %add_convert_fusion.1 = bf16[1024,2048]{1,0:T(8,128)(2,1)} fusion(f32[1024,2048]{1,0:T(8,128)S(1)} %fusion.77, bf16[1024,1536]{1,0:T(8,128)(2,1)S(1)} %get-tuple-element.113, bf16[2048,1536]{1,0:T(8,128)(2,1)} %all-gather.15.cloned.1.call-done), kind=kOutput, calls=%fused_computation.1 | convolution fusion | flops 6446645248 | bytes 22020096 | tf_op jit(solution)/shard_map/dot_general | solution.py:298
  419.3 8.7 %convolution_convert_fusion.1 = bf16[2048,1536]{1,0:T(8,128)(2,1)} fusion(bf16[1024,2048]{1,0:T(8,128)(2,1)S(1)} %copy-done.7, bf16[1024,1536]{1,0:T(8,128)(2,1)S(1)} %get-tuple-element.114), kind=kOutput, calls=%fused_computation.3 | convolution fusion | flops 6445596672 | bytes 13631488 | tf_op jit(solution)/shard_map/dot_general | solution.py:294
  428.0 26.4 %reduce-scatter.7.cloned.1.call-done = bf16[256,1536]{1,0:T(8,128)(2,1)} async-done(((bf16[2048,1536]{1,0:T(8,128)(2,1)}), bf16[256,1536]{1,0:T(8,128)(2,1)}) %reduce-scatter.7.cloned.1.call-update) | async-done | bytes 786448 | tf_op jit(solution)/shard_map/reduce_scatter | solution.py:254
  462.7 10.6 %convolution_convert_fusion = bf16[2048,1536]{1,0:T(8,128)(2,1)} fusion(bf16[1024,2048]{1,0:T(8,128)(2,1)S(1)} %copy-done.8, bf16[1024,1536]{1,0:T(8,128)(2,1)} %copy-done.43), kind=kOutput, calls=%fused_computation.2 | convolution fusion | flops 6445596672 | bytes 13631488 | tf_op jit(solution)/shard_map/dot_general | solution.py:294
  473.3 9.8 %collective-permute-done.18 = bf16[256,2048]{1,0:T(8,128)(2,1)} collective-permute-done((bf16[256,2048]{1,0:T(8,128)(2,1)}, bf16[256,2048]{1,0:T(8,128)(2,1)}, u32[]{:S(2)}, u32[]{:S(2)}) %collective-permute-start.18) | collective-permute-done | bytes 1048608 | tf_op jit(solution)/shard_map/ppermute | solution.py:26
  490.1 11.1 %convolution_convert_fusion.3 = bf16[1024,2048]{1,0:T(8,128)(2,1)} fusion(bf16[1024,1536]{1,0:T(8,128)(2,1)S(1)} %copy-done.42, bf16[2048,1536]{1,0:T(8,128)(2,1)} %all-gather.17.cloned.1.call-done), kind=kOutput, calls=%fused_computation.10 | convolution fusion | flops 6444548096 | bytes 13631488 | tf_op jit(solution)/shard_map/dot_general | solution.py:298
  501.2 3.7 middle_back.1
  506.2 10.3 %collective-permute-done.22.refs_2_ = bf16[128,2048]{1,0:T(8,128)(2,1)S(1)} collective-permute-done((bf16[128,2048]{1,0:T(8,128)(2,1)S(1)}, bf16[128,2048]{1,0:T(8,128)(2,1)S(1)}, u32[]{:S(2)}, u32[]{:S(2)}) %collective-permute-start.22) | collective-permute-done | bytes 524320 | tf_op jit(solution)/shard_map/ppermute | solution.py:26
  519.9 18.4 %collective-permute-done.23.refs_0_ = bf16[256,2048]{1,0:T(8,128)(2,1)S(1)} collective-permute-done((bf16[256,2048]{1,0:T(8,128)(2,1)S(1)}, bf16[256,2048]{1,0:T(8,128)(2,1)S(1)}, u32[]{:S(2)}, u32[]{:S(2)}) %collective-permute-start.23) | collective-permute-done | bytes 1048608 | tf_op jit(solution)/shard_map/ppermute | solution.py:26
  540.6 3.7 convolution_convert_fusion.6
  544.4 6.2 convolution_convert_fusion.7
  550.5 27.3 %attend_back.1 = (f32[2,4,128,512]{3,2,1,0:T(8,128)}, bf16[8,2,4,128,512]{4,3,2,1,0:T(8,128)(2,1)}) custom-call(s32[26]{0:T(128)} %copy-done.19, bf16[2,4,128,512]{3,2,1,0:T(8,128)(2,1)} %bitcast.132, bf16[2,4,128,512]{3,2,1,0:T(8,128)(2,1)} %bitcast.160, bf16[2,4,128,512]{3,2,1,0:T(8,128)(2,1)} %copy-done.21, f32[2,2,4,1,256]{4,3,2,1,0:T(1,128)} %copy-done.23, ...), custom_call_target="tpu_custom_call" | custom-call | flops 10737418240 | bytes 16777216 | tf_op jit(solution)/shard_map/attend_back/pallas_call | solution.py:548
  577.8 7.3 reduce-scatter.11.cloned.1.call-done
  593.6 5.8 head_prep_back.2
  599.5 11.4 %collective-permute-done.26 = bf16[256,2048]{1,0:T(8,128)(2,1)} collective-permute-done((bf16[256,2048]{1,0:T(8,128)(2,1)}, bf16[256,2048]{1,0:T(8,128)(2,1)}, u32[]{:S(2)}, u32[]{:S(2)}) %collective-permute-start.26) | collective-permute-done | bytes 1048608 | tf_op jit(solution)/shard_map/ppermute | solution.py:26
  614.2 2.6 collective-permute-done.28
  621.0 5.7 fusion.2
  626.7 6.9 collective-permute-done.29.refs_4_
  635.1 3.8 collective-permute-done.30
  640.4 4.2 collective-permute-done.31
  650.6 35.2 %reduce-scatter.13.cloned.1.call-done = bf16[1024,512]{1,0:T(8,128)(2,1)} async-done(((bf16[8192,512]{1,0:T(8,128)(2,1)}), bf16[1024,512]{1,0:T(8,128)(2,1)}) %reduce-scatter.13.cloned.1.call-update) | async-done | bytes 1048592 | tf_op jit(solution)/shard_map/reduce_scatter | solution.py:254
  685.9 2.8 convert_element_type.255.d_ref
  688.7 4.9 head_prep_back.3
  693.7 8.9 %add_convert_fusion = bf16[1024,2048]{1,0:T(8,128)(2,1)} fusion(f32[1024,2048]{1,0:T(8,128)} %fusion.2, bf16[1024,512]{1,0:T(8,128)(2,1)} %get-tuple-element.78, bf16[2048,1024]{1,0:T(8,128)(2,1)} %all-gather.7.cloned.1.call-done), kind=kOutput, calls=%fused_computation | convolution fusion | flops 2151677952 | bytes 15728640 | tf_op jit(solution)/shard_map/dot_general | solution.py:298
  702.6 6.4 convolution_convert_fusion.5
  713.7 20.5 %collective-permute-done.33 = bf16[256,2048]{1,0:T(8,128)(2,1)S(1)} collective-permute-done((bf16[256,2048]{1,0:T(8,128)(2,1)S(1)}, bf16[256,2048]{1,0:T(8,128)(2,1)S(1)}, u32[]{:S(2)}, u32[]{:S(2)}) %collective-permute-start.33) | collective-permute-done | bytes 1048608 | tf_op jit(solution)/shard_map/ppermute | solution.py:26
  738.1 8.7 %collective-permute-done.34.refs_4_ = bf16[128,2048]{1,0:T(8,128)(2,1)S(1)} collective-permute-done((bf16[128,2048]{1,0:T(8,128)(2,1)S(1)}, bf16[128,2048]{1,0:T(8,128)(2,1)S(1)}, u32[]{:S(2)}, u32[]{:S(2)}) %collective-permute-start.34) | collective-permute-done | bytes 524320 | tf_op jit(solution)/shard_map/ppermute | solution.py:26
  748.0 5.2 entry_back.1
  758.3 4.1 collective-permute-start.42
  764.3 2.8 collective-permute-start.43
  767.1 2.7 collective-permute-done.43
  775.3 32.4 %reduce-scatter.17.cloned.1.call-done = bf16[256,1024]{1,0:T(8,128)(2,1)} async-done(((bf16[2048,1024]{1,0:T(8,128)(2,1)}), bf16[256,1024]{1,0:T(8,128)(2,1)}) %reduce-scatter.17.cloned.1.call-update) | async-done | bytes 524304 | tf_op jit(solution)/shard_map/reduce_scatter | solution.py:254
  813.4 4.6 collective-permute-done.38
  (292 shorter events, 165.9 us)
Async XLA Ops:
  7.2 69.8 %all-gather.7.cloned.1.call-start = ((), (), s32[]{:S(2)}) async-start(), calls=%async_computation.6 | async-start | bytes 4718592 | tf_op jit(solution)/shard_map/all_gather | solution.py:249
  12.8 12.2 %collective-permute-start.4 = (bf16[128,1536]{1,0:T(8,128)(2,1)S(1)}, bf16[128,1536]{1,0:T(8,128)(2,1)S(1)}, u32[]{:S(2)}, u32[]{:S(2)}) collective-permute-start(bf16[128,1536]{1,0:T(8,128)(2,1)S(1)} %pad_maximum_fusion.18), channel_id=1, source_target_pairs={{0,4},{2,6},{4,0},{6,2},{8,12},{10,14},{12,8},{14,10},{16,20},{18,... | collective-permute-start | bytes 1179656 | tf_op jit(solution)/shard_map/ppermute | solution.py:26
  26.8 78.7 %all-gather.9.cloned.1.call-start = ((), (), s32[]{:S(2)}) async-start(), calls=%async_computation.7 | async-start | bytes 2359296 | tf_op jit(solution)/shard_map/all_gather | solution.py:249
  30.9 107.4 %copy-start = (bf16[256,2048]{1,0:T(8,128)(2,1)}, bf16[256,2048]{1,0:T(8,128)(2,1)S(1)}, u32[]{:S(2)}) copy-start(bf16[256,2048]{1,0:T(8,128)(2,1)S(1)} %get-tuple-element.57.refs_0_) | copy-start | bytes 3145732
  32.7 156.4 %all-gather.11.cloned.1.call-start = ((), (), s32[]{:S(2)}) async-start(), calls=%async_computation.8 | async-start | bytes 9437184 | tf_op jit(solution)/shard_map/all_gather | solution.py:249
  34.8 14.6 %collective-permute-start = (bf16[128,2048]{1,0:T(8,128)(2,1)S(1)}, bf16[128,2048]{1,0:T(8,128)(2,1)S(1)}, u32[]{:S(2)}, u32[]{:S(2)}) collective-permute-start(bf16[128,2048]{1,0:T(8,128)(2,1)S(1)} %get-tuple-element.157.refs_1_), channel_id=1, source_target_pairs={{0,1},{1,0},{2,3},{3,2},{4,5},{5,4},{6,7},{7,6},{8,9},{9,8},{10,11... | collective-permute-start | bytes 1572872 | tf_op jit(solution)/shard_map/ppermute | solution.py:26
  36.5 13.6 %collective-permute-start.2 = (bf16[128,2048]{1,0:T(8,128)(2,1)}, bf16[128,2048]{1,0:T(8,128)(2,1)}, u32[]{:S(2)}, u32[]{:S(2)}) collective-permute-start(bf16[128,2048]{1,0:T(8,128)(2,1)} %get-tuple-element.156), channel_id=1, source_target_pairs={{0,4},{2,6},{4,0},{6,2},{8,12},{10,14},{12,8},{14,10},{16,20},{18,... | collective-permute-start | bytes 1572872 | tf_op jit(solution)/shard_map/ppermute | solution.py:26
  49.5 23.6 %collective-permute-start.1 = (bf16[256,2048]{1,0:T(8,128)(2,1)S(1)}, bf16[256,2048]{1,0:T(8,128)(2,1)S(1)}, u32[]{:S(2)}, u32[]{:S(2)}) collective-permute-start(bf16[256,2048]{1,0:T(8,128)(2,1)S(1)} %pad_maximum_fusion.3), channel_id=1, source_target_pairs={{0,4},{2,6},{4,0},{6,2},{8,12},{10,14},{12,8},{14,10},{16,20},{18,... | collective-permute-start | bytes 3145736 | tf_op jit(solution)/shard_map/ppermute | solution.py:26
  51.5 23.3 %collective-permute-start.3 = (bf16[256,2048]{1,0:T(8,128)(2,1)S(1)}, bf16[256,2048]{1,0:T(8,128)(2,1)S(1)}, u32[]{:S(2)}, u32[]{:S(2)}) collective-permute-start(bf16[256,2048]{1,0:T(8,128)(2,1)S(1)} %pad_maximum_fusion.4.refs_3_), channel_id=1, source_target_pairs={{0,1},{1,0},{2,3},{3,2},{4,5},{5,4},{6,7},{7,6},{8,9},{9,8},{10,11... | collective-permute-start | bytes 3145736 | tf_op jit(solution)/shard_map/ppermute | solution.py:26
  105.5 192.9 %all-gather.13.cloned.1.call-start = ((), (), s32[]{:S(2)}) async-start(), calls=%async_computation.9 | async-start | bytes 7077888 | tf_op jit(solution)/shard_map/all_gather | solution.py:249
  107.1 28.2 %collective-permute-start.5 = (bf16[128,4608]{1,0:T(8,128)(2,1)S(1)}, bf16[128,4608]{1,0:T(8,128)(2,1)S(1)}, u32[]{:S(2)}, u32[]{:S(2)}) collective-permute-start(bf16[128,4608]{1,0:T(8,128)(2,1)S(1)} %pad_maximum_fusion.2), channel_id=1, source_target_pairs={{0,4},{2,6},{4,0},{6,2},{8,12},{10,14},{12,8},{14,10},{16,20},{18,... | collective-permute-start | bytes 3538952 | tf_op jit(solution)/shard_map/ppermute | solution.py:26
  137.3 181.5 %all-gather.15.cloned.1.call-start = ((), (), s32[]{:S(2)}) async-start(), calls=%async_computation.10 | async-start | bytes 7077888 | tf_op jit(solution)/shard_map/all_gather | solution.py:249
  137.9 245.7 %all-gather.17.cloned.1.call-start = ((), (), s32[]{:S(2)}) async-start(), calls=%async_computation.11 | async-start | bytes 7077888 | tf_op jit(solution)/shard_map/all_gather | solution.py:249
  138.4 13.4 %collective-permute-start.6 = (bf16[128,2048]{1,0:T(8,128)(2,1)S(1)}, bf16[128,2048]{1,0:T(8,128)(2,1)S(1)}, u32[]{:S(2)}, u32[]{:S(2)}) collective-permute-start(bf16[128,2048]{1,0:T(8,128)(2,1)S(1)} %get-tuple-element.155.refs_1_), channel_id=1, source_target_pairs={{0,1},{1,0},{2,3},{3,2},{4,5},{5,4},{6,7},{7,6},{8,9},{9,8},{10,11... | collective-permute-start | bytes 1572872 | tf_op jit(solution)/shard_map/ppermute | solution.py:26
  140.0 14.3 %collective-permute-start.8 = (bf16[128,2048]{1,0:T(8,128)(2,1)S(1)}, bf16[128,2048]{1,0:T(8,128)(2,1)S(1)}, u32[]{:S(2)}, u32[]{:S(2)}) collective-permute-start(bf16[128,2048]{1,0:T(8,128)(2,1)S(1)} %get-tuple-element.154), channel_id=1, source_target_pairs={{0,4},{2,6},{4,0},{6,2},{8,12},{10,14},{12,8},{14,10},{16,20},{18,... | collective-permute-start | bytes 1572872 | tf_op jit(solution)/shard_map/ppermute | solution.py:26
  152.8 24.1 %collective-permute-start.7 = (bf16[256,2048]{1,0:T(8,128)(2,1)}, bf16[256,2048]{1,0:T(8,128)(2,1)}, u32[]{:S(2)}, u32[]{:S(2)}) collective-permute-start(bf16[256,2048]{1,0:T(8,128)(2,1)} %pad_maximum_fusion.5), channel_id=1, source_target_pairs={{0,4},{2,6},{4,0},{6,2},{8,12},{10,14},{12,8},{14,10},{16,20},{18,... | collective-permute-start | bytes 3145736 | tf_op jit(solution)/shard_map/ppermute | solution.py:26
  154.4 23.7 %collective-permute-start.9 = (bf16[256,2048]{1,0:T(8,128)(2,1)S(1)}, bf16[256,2048]{1,0:T(8,128)(2,1)}, u32[]{:S(2)}, u32[]{:S(2)}) collective-permute-start(bf16[256,2048]{1,0:T(8,128)(2,1)S(1)} %pad_maximum_fusion.6.refs_3_), channel_id=1, source_target_pairs={{0,1},{1,0},{2,3},{3,2},{4,5},{5,4},{6,7},{7,6},{8,9},{9,8},{10,11... | collective-permute-start | bytes 3145736 | tf_op jit(solution)/shard_map/ppermute | solution.py:26
  214.1 25.5 %collective-permute-start.10 = (bf16[256,2048]{1,0:T(8,128)(2,1)}, bf16[256,2048]{1,0:T(8,128)(2,1)S(1)}, u32[]{:S(2)}, u32[]{:S(2)}) collective-permute-start(bf16[256,2048]{1,0:T(8,128)(2,1)} %pad_maximum_fusion.7), channel_id=1, source_target_pairs={{0,4},{2,6},{4,0},{6,2},{8,12},{10,14},{12,8},{14,10},{16,20},{18,... | collective-permute-start | bytes 3145736 | tf_op jit(solution)/shard_map/ppermute | solution.py:26
  216.7 26.1 %collective-permute-start.12 = (bf16[256,2048]{1,0:T(8,128)(2,1)}, bf16[256,2048]{1,0:T(8,128)(2,1)S(1)}, u32[]{:S(2)}, u32[]{:S(2)}) collective-permute-start(bf16[256,2048]{1,0:T(8,128)(2,1)} %slice.345), channel_id=1, source_target_pairs={{0,1},{1,0},{2,3},{3,2},{4,5},{5,4},{6,7},{7,6},{8,9},{9,8},{10,11... | collective-permute-start | bytes 3145736 | tf_op jit(solution)/shard_map/ppermute | solution.py:26
  218.2 27.8 %copy-start.33 = (f32[2048]{0:T(1024)S(1)}, f32[2048]{0:T(1024)}, u32[]{:S(2)}) copy-start(f32[2048]{0:T(1024)} %param.25) | copy-start | bytes 24580
  218.2 236.2 %reduce-scatter.7.cloned.1.call-start = ((), (), s32[]{:S(2)}) async-start(), calls=%async_computation.12 | async-start | bytes 7077888 | tf_op jit(solution)/shard_map/reduce_scatter | solution.py:254
  241.2 13.4 %collective-permute-start.11 = (bf16[128,2048]{1,0:T(8,128)(2,1)S(1)}, bf16[128,2048]{1,0:T(8,128)(2,1)S(1)}, u32[]{:S(2)}, u32[]{:S(2)}) collective-permute-start(bf16[128,2048]{1,0:T(8,128)(2,1)S(1)} %get-tuple-element.121), channel_id=1, source_target_pairs={{0,1},{1,0},{2,3},{3,2},{4,5},{5,4},{6,7},{7,6},{8,9},{9,8},{10,11... | collective-permute-start | bytes 1572872 | tf_op jit(solution)/shard_map/ppermute | solution.py:26
  244.5 13.1 %collective-permute-start.13 = (bf16[128,2048]{1,0:T(8,128)(2,1)S(1)}, bf16[128,2048]{1,0:T(8,128)(2,1)S(1)}, u32[]{:S(2)}, u32[]{:S(2)}) collective-permute-start(bf16[128,2048]{1,0:T(8,128)(2,1)S(1)} %get-tuple-element.152), channel_id=1, source_target_pairs={{0,4},{2,6},{4,0},{6,2},{8,12},{10,14},{12,8},{14,10},{16,20},{18,... | collective-permute-start | bytes 1572872 | tf_op jit(solution)/shard_map/ppermute | solution.py:26
  259.7 12.2 %collective-permute-start.14 = (bf16[128,2048]{1,0:T(8,128)(2,1)S(1)}, bf16[128,2048]{1,0:T(8,128)(2,1)S(1)}, u32[]{:S(2)}, u32[]{:S(2)}) collective-permute-start(bf16[128,2048]{1,0:T(8,128)(2,1)S(1)} %get-tuple-element.151.refs_1_), channel_id=1, source_target_pairs={{0,1},{1,0},{2,3},{3,2},{4,5},{5,4},{6,7},{7,6},{8,9},{9,8},{10,11... | collective-permute-start | bytes 1572872 | tf_op jit(solution)/shard_map/ppermute | solution.py:26
  260.4 13.2 %collective-permute-start.16 = (bf16[128,2048]{1,0:T(8,128)(2,1)S(1)}, bf16[128,2048]{1,0:T(8,128)(2,1)S(1)}, u32[]{:S(2)}, u32[]{:S(2)}) collective-permute-start(bf16[128,2048]{1,0:T(8,128)(2,1)S(1)} %get-tuple-element.150), channel_id=1, source_target_pairs={{0,4},{2,6},{4,0},{6,2},{8,12},{10,14},{12,8},{14,10},{16,20},{18,... | collective-permute-start | bytes 1572872 | tf_op jit(solution)/shard_map/ppermute | solution.py:26
  272.1 22.7 %collective-permute-start.15 = (bf16[256,2048]{1,0:T(8,128)(2,1)S(1)}, bf16[256,2048]{1,0:T(8,128)(2,1)S(1)}, u32[]{:S(2)}, u32[]{:S(2)}) collective-permute-start(bf16[256,2048]{1,0:T(8,128)(2,1)S(1)} %pad_maximum_fusion.8), channel_id=1, source_target_pairs={{0,4},{2,6},{4,0},{6,2},{8,12},{10,14},{12,8},{14,10},{16,20},{18,... | collective-permute-start | bytes 3145736 | tf_op jit(solution)/shard_map/ppermute | solution.py:26
  273.7 22.5 %collective-permute-start.17 = (bf16[256,2048]{1,0:T(8,128)(2,1)S(1)}, bf16[256,2048]{1,0:T(8,128)(2,1)S(1)}, u32[]{:S(2)}, u32[]{:S(2)}) collective-permute-start(bf16[256,2048]{1,0:T(8,128)(2,1)S(1)} %pad_maximum_fusion.9.refs_3_), channel_id=1, source_target_pairs={{0,1},{1,0},{2,3},{3,2},{4,5},{5,4},{6,7},{7,6},{8,9},{9,8},{10,11... | collective-permute-start | bytes 3145736 | tf_op jit(solution)/shard_map/ppermute | solution.py:26
  342.5 201.8 %reduce-scatter.9.cloned.1.call-start = ((), (), s32[]{:S(2)}) async-start(), calls=%async_computation.13 | async-start | bytes 7077888 | tf_op jit(solution)/shard_map/reduce_scatter | solution.py:254
  454.4 130.6 %reduce-scatter.11.cloned.1.call-start = ((), (), s32[]{:S(2)}) async-start(), calls=%async_computation.14 | async-start | bytes 2359296 | tf_op jit(solution)/shard_map/reduce_scatter | solution.py:254
  459.7 23.3 %collective-permute-start.18 = (bf16[256,2048]{1,0:T(8,128)(2,1)}, bf16[256,2048]{1,0:T(8,128)(2,1)}, u32[]{:S(2)}, u32[]{:S(2)}) collective-permute-start(bf16[256,2048]{1,0:T(8,128)(2,1)} %pad_maximum_fusion.10), channel_id=1, source_target_pairs={{0,4},{2,6},{4,0},{6,2},{8,12},{10,14},{12,8},{14,10},{16,20},{18,... | collective-permute-start | bytes 3145736 | tf_op jit(solution)/shard_map/ppermute | solution.py:26
  461.2 25.3 %collective-permute-start.20 = (bf16[256,2048]{1,0:T(8,128)(2,1)}, bf16[256,2048]{1,0:T(8,128)(2,1)}, u32[]{:S(2)}, u32[]{:S(2)}) collective-permute-start(bf16[256,2048]{1,0:T(8,128)(2,1)} %slice.355), channel_id=1, source_target_pairs={{0,1},{1,0},{2,3},{3,2},{4,5},{5,4},{6,7},{7,6},{8,9},{9,8},{10,11... | collective-permute-start | bytes 3145736 | tf_op jit(solution)/shard_map/ppermute | solution.py:26
  485.0 16.3 %collective-permute-start.19 = (bf16[128,2048]{1,0:T(8,128)(2,1)S(1)}, bf16[128,2048]{1,0:T(8,128)(2,1)S(1)}, u32[]{:S(2)}, u32[]{:S(2)}) collective-permute-start(bf16[128,2048]{1,0:T(8,128)(2,1)S(1)} %get-tuple-element.119), channel_id=1, source_target_pairs={{0,1},{1,0},{2,3},{3,2},{4,5},{5,4},{6,7},{7,6},{8,9},{9,8},{10,11... | collective-permute-start | bytes 1572872 | tf_op jit(solution)/shard_map/ppermute | solution.py:26
  488.6 12.6 %collective-permute-start.21 = (bf16[128,2048]{1,0:T(8,128)(2,1)S(1)}, bf16[128,2048]{1,0:T(8,128)(2,1)S(1)}, u32[]{:S(2)}, u32[]{:S(2)}) collective-permute-start(bf16[128,2048]{1,0:T(8,128)(2,1)S(1)} %get-tuple-element.148), channel_id=1, source_target_pairs={{0,4},{2,6},{4,0},{6,2},{8,12},{10,14},{12,8},{14,10},{16,20},{18,... | collective-permute-start | bytes 1572872 | tf_op jit(solution)/shard_map/ppermute | solution.py:26
  505.0 33.6 %copy-start.12 = (f32[256,2048]{1,0:T(8,128)}, f32[256,2048]{1,0:T(8,128)S(1)}, u32[]{:S(2)}) copy-start(f32[256,2048]{1,0:T(8,128)S(1)} %get-tuple-element.69.refs_0_) | copy-start | bytes 6291460
  505.1 11.4 %collective-permute-start.22 = (bf16[128,2048]{1,0:T(8,128)(2,1)S(1)}, bf16[128,2048]{1,0:T(8,128)(2,1)S(1)}, u32[]{:S(2)}, u32[]{:S(2)}) collective-permute-start(bf16[128,2048]{1,0:T(8,128)(2,1)S(1)} %get-tuple-element.147.refs_1_), channel_id=1, source_target_pairs={{0,1},{1,0},{2,3},{3,2},{4,5},{5,4},{6,7},{7,6},{8,9},{9,8},{10,11... | collective-permute-start | bytes 1572872 | tf_op jit(solution)/shard_map/ppermute | solution.py:26
  505.7 12.0 %collective-permute-start.24 = (bf16[128,2048]{1,0:T(8,128)(2,1)S(1)}, bf16[128,2048]{1,0:T(8,128)(2,1)S(1)}, u32[]{:S(2)}, u32[]{:S(2)}) collective-permute-start(bf16[128,2048]{1,0:T(8,128)(2,1)S(1)} %get-tuple-element.146), channel_id=1, source_target_pairs={{0,4},{2,6},{4,0},{6,2},{8,12},{10,14},{12,8},{14,10},{16,20},{18,... | collective-permute-start | bytes 1572872 | tf_op jit(solution)/shard_map/ppermute | solution.py:26
  516.6 21.8 %collective-permute-start.23 = (bf16[256,2048]{1,0:T(8,128)(2,1)S(1)}, bf16[256,2048]{1,0:T(8,128)(2,1)S(1)}, u32[]{:S(2)}, u32[]{:S(2)}) collective-permute-start(bf16[256,2048]{1,0:T(8,128)(2,1)S(1)} %pad_maximum_fusion.11), channel_id=1, source_target_pairs={{0,4},{2,6},{4,0},{6,2},{8,12},{10,14},{12,8},{14,10},{16,20},{18,... | collective-permute-start | bytes 3145736 | tf_op jit(solution)/shard_map/ppermute | solution.py:26
  517.8 22.8 %copy-start.22 = (bf16[2,4,128,512]{3,2,1,0:T(8,128)(2,1)S(1)}, bf16[2,4,128,512]{3,2,1,0:T(8,128)(2,1)}, u32[]{:S(2)}) copy-start(bf16[2,4,128,512]{3,2,1,0:T(8,128)(2,1)} %copy-done.21) | copy-start | bytes 3145732
  517.8 20.6 %collective-permute-start.25 = (bf16[256,2048]{1,0:T(8,128)(2,1)S(1)}, bf16[256,2048]{1,0:T(8,128)(2,1)S(1)}, u32[]{:S(2)}, u32[]{:S(2)}) collective-permute-start(bf16[256,2048]{1,0:T(8,128)(2,1)S(1)} %pad_maximum_fusion.12.refs_3_), channel_id=1, source_target_pairs={{0,1},{1,0},{2,3},{3,2},{4,5},{5,4},{6,7},{7,6},{8,9},{9,8},{10,11... | collective-permute-start | bytes 3145736 | tf_op jit(solution)/shard_map/ppermute | solution.py:26
  544.3 141.6 %reduce-scatter.13.cloned.1.call-start = ((), (), s32[]{:S(2)}) async-start(), calls=%async_computation.15 | async-start | bytes 9437184 | tf_op jit(solution)/shard_map/reduce_scatter | solution.py:254
  585.1 190.2 %reduce-scatter.15.cloned.1.call-start = ((), (), s32[]{:S(2)}) async-start(), calls=%async_computation.16 | async-start | bytes 7077888 | tf_op jit(solution)/shard_map/reduce_scatter | solution.py:254
  585.8 221.8 %reduce-scatter.17.cloned.1.call-start = ((), (), s32[]{:S(2)}) async-start(), calls=%async_computation.17 | async-start | bytes 4718592 | tf_op jit(solution)/shard_map/reduce_scatter | solution.py:254
  588.4 22.4 %collective-permute-start.26 = (bf16[256,2048]{1,0:T(8,128)(2,1)}, bf16[256,2048]{1,0:T(8,128)(2,1)}, u32[]{:S(2)}, u32[]{:S(2)}) collective-permute-start(bf16[256,2048]{1,0:T(8,128)(2,1)} %pad_maximum_fusion.13), channel_id=1, source_target_pairs={{0,4},{2,6},{4,0},{6,2},{8,12},{10,14},{12,8},{14,10},{16,20},{18,... | collective-permute-start | bytes 3145736 | tf_op jit(solution)/shard_map/ppermute | solution.py:26
  592.0 24.7 %collective-permute-start.28 = (bf16[256,2048]{1,0:T(8,128)(2,1)}, bf16[256,2048]{1,0:T(8,128)(2,1)}, u32[]{:S(2)}, u32[]{:S(2)}) collective-permute-start(bf16[256,2048]{1,0:T(8,128)(2,1)} %slice.297), channel_id=1, source_target_pairs={{0,1},{1,0},{2,3},{3,2},{4,5},{5,4},{6,7},{7,6},{8,9},{9,8},{10,11... | collective-permute-start | bytes 3145736 | tf_op jit(solution)/shard_map/ppermute | solution.py:26
  612.8 14.0 %collective-permute-start.27 = (bf16[128,2048]{1,0:T(8,128)(2,1)S(1)}, bf16[128,2048]{1,0:T(8,128)(2,1)S(1)}, u32[]{:S(2)}, u32[]{:S(2)}) collective-permute-start(bf16[128,2048]{1,0:T(8,128)(2,1)S(1)} %get-tuple-element.117), channel_id=1, source_target_pairs={{0,1},{1,0},{2,3},{3,2},{4,5},{5,4},{6,7},{7,6},{8,9},{9,8},{10,11... | collective-permute-start | bytes 1572872 | tf_op jit(solution)/shard_map/ppermute | solution.py:26
  618.8 14.9 %collective-permute-start.29 = (bf16[128,2048]{1,0:T(8,128)(2,1)S(1)}, bf16[128,2048]{1,0:T(8,128)(2,1)S(1)}, u32[]{:S(2)}, u32[]{:S(2)}) collective-permute-start(bf16[128,2048]{1,0:T(8,128)(2,1)S(1)} %get-tuple-element.144), channel_id=1, source_target_pairs={{0,4},{2,6},{4,0},{6,2},{8,12},{10,14},{12,8},{14,10},{16,20},{18,... | collective-permute-start | bytes 1572872 | tf_op jit(solution)/shard_map/ppermute | solution.py:26
  618.9 20.0 %collective-permute-start.30 = (bf16[128,1536]{1,0:T(8,128)(2,1)S(1)}, bf16[128,1536]{1,0:T(8,128)(2,1)S(1)}, u32[]{:S(2)}, u32[]{:S(2)}) collective-permute-start(bf16[128,1536]{1,0:T(8,128)(2,1)S(1)} %constant_dynamic-slice_fusion.5), channel_id=1, source_target_pairs={{0,4},{2,6},{4,0},{6,2},{8,12},{10,14},{12,8},{14,10},{16,20},{18,... | collective-permute-start | bytes 1179656 | tf_op jit(solution)/shard_map/ppermute | solution.py:26
  635.1 9.5 %collective-permute-start.31 = (bf16[128,1536]{1,0:T(8,128)(2,1)S(1)}, bf16[128,1536]{1,0:T(8,128)(2,1)S(1)}, u32[]{:S(2)}, u32[]{:S(2)}) collective-permute-start(bf16[128,1536]{1,0:T(8,128)(2,1)S(1)} %constant_dynamic-slice_fusion.4), channel_id=1, source_target_pairs={{0,4},{2,6},{4,0},{6,2},{8,12},{10,14},{12,8},{14,10},{16,20},{18,... | collective-permute-start | bytes 1179656 | tf_op jit(solution)/shard_map/ppermute | solution.py:26
  644.7 5.0 collective-permute-start.32
  710.5 23.7 %collective-permute-start.33 = (bf16[256,2048]{1,0:T(8,128)(2,1)S(1)}, bf16[256,2048]{1,0:T(8,128)(2,1)S(1)}, u32[]{:S(2)}, u32[]{:S(2)}) collective-permute-start(bf16[256,2048]{1,0:T(8,128)(2,1)S(1)} %pad_maximum_fusion.14), channel_id=1, source_target_pairs={{0,4},{2,6},{4,0},{6,2},{8,12},{10,14},{12,8},{14,10},{16,20},{18,... | collective-permute-start | bytes 3145736 | tf_op jit(solution)/shard_map/ppermute | solution.py:26
  712.2 35.9 %copy-start.13 = (f32[256,2048]{1,0:T(8,128)S(1)}, f32[256,2048]{1,0:T(8,128)}, u32[]{:S(2)}) copy-start(f32[256,2048]{1,0:T(8,128)} %copy-done.12) | copy-start | bytes 6291460
  712.2 35.9 %copy-start.18 = (f32[1,4,2,2,128]{4,3,2,1,0:T(2,128)S(1)}, f32[1,4,2,2,128]{4,3,2,1,0:T(2,128)}, u32[]{:S(2)}) copy-start(f32[1,4,2,2,128]{4,3,2,1,0:T(2,128)} %copy-done.17) | copy-start | bytes 24580
  712.2 23.9 %collective-permute-start.35 = (bf16[256,2048]{1,0:T(8,128)(2,1)S(1)}, bf16[256,2048]{1,0:T(8,128)(2,1)S(1)}, u32[]{:S(2)}, u32[]{:S(2)}) collective-permute-start(bf16[256,2048]{1,0:T(8,128)(2,1)S(1)} %slice.371), channel_id=1, source_target_pairs={{0,1},{1,0},{2,3},{3,2},{4,5},{5,4},{6,7},{7,6},{8,9},{9,8},{10,11... | collective-permute-start | bytes 3145736 | tf_op jit(solution)/shard_map/ppermute | solution.py:26
  734.6 12.2 %collective-permute-start.34 = (bf16[128,2048]{1,0:T(8,128)(2,1)S(1)}, bf16[128,2048]{1,0:T(8,128)(2,1)S(1)}, u32[]{:S(2)}, u32[]{:S(2)}) collective-permute-start(bf16[128,2048]{1,0:T(8,128)(2,1)S(1)} %get-tuple-element.115), channel_id=1, source_target_pairs={{0,1},{1,0},{2,3},{3,2},{4,5},{5,4},{6,7},{7,6},{8,9},{9,8},{10,11... | collective-permute-start | bytes 1572872 | tf_op jit(solution)/shard_map/ppermute | solution.py:26
  736.6 11.4 %collective-permute-start.36 = (bf16[128,2048]{1,0:T(8,128)(2,1)S(1)}, bf16[128,2048]{1,0:T(8,128)(2,1)S(1)}, u32[]{:S(2)}, u32[]{:S(2)}) collective-permute-start(bf16[128,2048]{1,0:T(8,128)(2,1)S(1)} %get-tuple-element.142), channel_id=1, source_target_pairs={{0,4},{2,6},{4,0},{6,2},{8,12},{10,14},{12,8},{14,10},{16,20},{18,... | collective-permute-start | bytes 1572872 | tf_op jit(solution)/shard_map/ppermute | solution.py:26
  753.2 1.3 collective-permute-start.40
  754.5 3.8 collective-permute-start.41
  758.3 5.9 collective-permute-start.42
  764.3 5.5 collective-permute-start.43
  769.7 3.8 collective-permute-start.44
  775.3 47.8 %copy-start.28 = (bf16[256,1536]{1,0:T(8,128)(2,1)S(1)}, bf16[256,1536]{1,0:T(8,128)(2,1)}, u32[]{:S(2)}) copy-start(bf16[256,1536]{1,0:T(8,128)(2,1)} %reduce-scatter.15.cloned.1.call-done) | copy-start | bytes 2359300
  808.8 12.6 %collective-permute-start.37 = (bf16[128,512]{1,0:T(8,128)(2,1)S(1)}, bf16[128,512]{1,0:T(8,128)(2,1)S(1)}, u32[]{:S(2)}, u32[]{:S(2)}) collective-permute-start(bf16[128,512]{1,0:T(8,128)(2,1)S(1)} %constant_dynamic-slice_fusion.2), channel_id=1, source_target_pairs={{0,4},{2,6},{4,0},{6,2},{8,12},{10,14},{12,8},{14,10},{16,20},{18,... | collective-permute-start | bytes 393224 | tf_op jit(solution)/shard_map/ppermute | solution.py:26
  810.3 7.7 collective-permute-start.38
  811.9 11.1 %collective-permute-start.39 = (bf16[128,1536]{1,0:T(8,128)(2,1)S(1)}, bf16[128,1536]{1,0:T(8,128)(2,1)S(1)}, u32[]{:S(2)}, u32[]{:S(2)}) collective-permute-start(bf16[128,1536]{1,0:T(8,128)(2,1)S(1)} %constant_dynamic-slice_fusion), channel_id=1, source_target_pairs={{0,4},{2,6},{4,0},{6,2},{8,12},{10,14},{12,8},{14,10},{16,20},{18,... | collective-permute-start | bytes 1179656 | tf_op jit(solution)/shard_map/ppermute | solution.py:26
  (37 other events, 339.0 us)
Sparse Core Ops, SparseCore 0:
  26.9 48.3 all-gather.6
  77.4 27.9 all-gather.8
  107.6 81.4 all-gather.10
  190.6 63.2 all-gather.12
  255.3 63.4 all-gather.14
  320.3 63.3 all-gather.16
  386.0 68.3 reduce-scatter.6
  456.7 68.1 reduce-scatter.8
  544.4 40.5 reduce-scatter.10
  587.2 98.6 reduce-scatter.12
  688.2 68.1 reduce-scatter.14
  758.6 48.9 reduce-scatter.16

commit v3 on v2

--- a/solution.py
+++ b/solution.py
@@ -88,7 +88,7 @@
     return assemble([others] + lows + highs, plan)
 
 
-def return_rows(partial, ways):
+def return_rows(partial, ways, filler=None):
     count = lax.axis_size("fsdp")
     if ways == 1:
         rows = partial.shape[0] // count
@@ -104,6 +104,8 @@
     sent = jnp.concatenate([rows(4 * r + 1, 1) for r in range(count)], axis=0)
     pairs = [xor_send(rows(4 * r + 2, 2), "fsdp", r) for r in range(1, count)]
     other = xor_send(sent, "ctx", 2)
+    if filler is not None:
+        other = after(other, filler)
     first = [
         (rows(4 * r, 1).astype(F32) + other[r * block : (r + 1) * block].astype(F32)).astype(BF16)
         for r in range(count)
@@ -267,14 +269,39 @@
     return ctx_scatter(grad, ways)
 
 
-def own_rows(both, pair, ways):
+def own_kernel(plan, pair_ref, both_ref, other_ref, *outs):
+    pair = pair_ref[0]
+    rows, width = other_ref.shape
+    mine = pl.ds(pl.multiple_of(pair * rows, rows), rows)
+    for source, columns, target, place in plan:
+        half = outs[target].shape[1] // 2
+        for ref, at, which in ((both_ref, mine, pair), (other_ref, slice(None), 1 - pair)):
+            start = pl.multiple_of(which * half + place, HD)
+            outs[target][:, pl.ds(start, columns)] = ref[at, source : source + columns].astype(F32)
+
+
+def own_rows(both, pair, ways, plan, widths):
     if ways == 1:
-        return both.astype(F32)
+        return [
+            jnp.concatenate([both[:, s : s + n] for s, n, t, _ in plan if t == i], axis=1).astype(F32)
+            for i in range(len(widths))
+        ]
     rows = both.shape[0] // 2
-    kept = lax.dynamic_slice_in_dim(both, pair * rows, rows, 0)
     other = xor_send(lax.dynamic_slice_in_dim(both, (1 - pair) * rows, rows, 0), "ctx", 2)
-    low, high = jnp.where(pair == 0, kept, other), jnp.where(pair == 0, other, kept)
-    return jnp.concatenate([low, high], axis=1).astype(F32)
+    shapes = tuple(jax.ShapeDtypeStruct((rows, 2 * width), F32) for width in widths)
+    whole = [pl.BlockSpec(t.shape, lambda i, m: (0, 0)) for t in (both, other) + shapes]
+    return pl.pallas_call(
+        functools.partial(own_kernel, plan),
+        out_shape=shapes,
+        grid_spec=pltpu.PrefetchScalarGridSpec(
+            num_scalar_prefetch=1,
+            grid=(1,),
+            in_specs=whole[:2],
+            out_specs=tuple(whole[2:]),
+        ),
+        cost_estimate=pl.CostEstimate(flops=0, bytes_accessed=8 * both.size, transcendentals=0),
+        name="own_rows",
+    )(pair.reshape(1), both, other)
 
 
 def butterfly_sum(value):
@@ -352,7 +379,7 @@
     gain_sum = jnp.zeros((1, HD), F32)
     for h in range(heads):
         cols = slice(h * HD, (h + 1) * HD)
-        d = d_ref[:, cols]
+        d = d_ref[:, cols].astype(F32)
         if plain and h % 2 == 1:
             out_ref[:, cols] = d.astype(BF16)
             continue
@@ -690,52 +717,56 @@
     d_gate = (d_act * up * sg * (1.0 + gate * (1.0 - sg))).astype(BF16)
     d_up = (d_act * gate * sg).astype(BF16)
     d_h2_part = (dot_cols(d_gate, full_gate) + dot_cols(d_up, full_up)).astype(BF16)
-    lows, highs = return_rows(d_h2_part, 2)
-    h2_late, act_late = after((h2, act), d_h2_part)
+    h2_late = after(h2, d_h2_part)
     grad_gate = dot_rows(h2_late, d_gate).astype(BF16)
     grad_up = dot_rows(h2_late, d_up).astype(BF16)
-    y_part = dot_cols(act_late, full_down).astype(BF16)
-    lows[0] = after(lows[0], (grad_gate, grad_up, y_part))
+    lows, highs = return_rows(d_h2_part, 2, (grad_gate, grad_up))
+    returned = lows + highs
     d_x2, d_x2_low, gain_mlp = row_pass(
         functools.partial(back_kernel, len(lows), len(highs), None),
         (cot_own, x2, gain_mlp_row, *lows, *highs),
         (row_f32, row_bf16, gain_shape),
         "middle_back",
     )
+    y_part = dot_cols(after(act, d_x2_low), full_down).astype(BF16)
     branch = gather_rows(d_x2_low, ways)
     rows_down = scatter_weight(grad_down, 2)
-    rows_gate = scatter_weight(after(grad_gate, rows_down), 2)
-    grad_output = after(dot_rows(branch, mixed).astype(BF16), rows_gate)
-    rows_output = scatter_weight(grad_output, ways)
+    rows_gate = scatter_weight(after(grad_gate, (rows_down, returned)), 2)
     d_att = dot(branch, full_output).astype(BF16).reshape(q.shape)
-
+    rows_up = scatter_weight(after(grad_up, (rows_gate, d_att)), 2)
+    grad_output = dot_rows(branch, mixed).astype(BF16)
+
+    def one(both, split):
+        return own_rows(both, pair, split, [(0, both.shape[1], 0, 0)], [both.shape[1]])[0]
+
+    shard_down = one(rows_down, 2)
+    shard_gate = one(rows_gate, 2)
+    d_q, d_kv = attend_back(info, q, d_att, heads, lse, full_kv, count, ways)
+    d_qp, gain_q_sum = head_prep_back(
+        d_q.reshape(-1, q_width), raw, cos, sin, gain_q, 0, False
+    )
+    d_h1_query = dot_cols(d_qp, full_qkv[:, :q_width])
+    d_kv = after(
+        d_kv.reshape(-1, kv_width),
+        (rows_up, d_h1_query, grad_output, y_part, shard_down, shard_gate),
+    )
+    d_kv = ctx_scatter(d_kv, ways)
+    rows_output = scatter_weight(after(grad_output, d_kv), ways)
+    d_kvp, gain_k_sum = head_prep_back(d_kv, raw, cos, sin, gain_k, q_width // kv_width, True)
+    d_h1 = (
+        d_h1_query + dot_cols(d_kvp, full_qkv[:, q_width:])
+    ).astype(BF16)
     lows, highs = return_rows(after(y_part, branch), 2)
     out_tokens = row_pass(
         functools.partial(result_kernel, len(lows), len(highs), ctx_count),
-        (x2, *lows, *highs),
+        (after(x2, d_h1), *lows, *highs),
         row_bf16,
         "result",
     ).reshape(tokens.shape)
-
-    d_q, d_kv = attend_back(info, q, d_att, heads, lse, full_kv, count, ways)
-    d_kv = after(d_kv.reshape(-1, kv_width), rows_output)
-    d_kv = ctx_scatter(d_kv, ways).astype(F32)
-    shard_down = own_rows(rows_down, pair, 2)
-    shard_gate = own_rows(rows_gate, pair, 2)
-    shard_output = own_rows(rows_output, pair, ways)
-    d_kv = after(d_kv, (out_tokens, shard_down, shard_gate, shard_output))
-    d_qp, gain_q_sum = head_prep_back(
-        d_q.reshape(-1, q_width), raw, cos, sin, gain_q, 0, False
-    )
-    d_kvp, gain_k_sum = head_prep_back(d_kv, raw, cos, sin, gain_k, q_width // kv_width, True)
-    d_h1 = (
-        dot_cols(d_qp, full_qkv[:, :q_width]) + dot_cols(d_kvp, full_qkv[:, q_width:])
-    ).astype(BF16)
     lows, highs = return_rows(d_h1, ways)
     d_raw = jnp.concatenate([d_qp, d_kvp], axis=1)
     grad_qkv = dot_rows(after(h1, d_h1), d_raw).astype(BF16)
 
-    rows_up = scatter_weight(grad_up, 2)
     rows_qkv = scatter_weight(grad_qkv, ways)
     grad_tokens, gain_attn = row_pass(
         functools.partial(back_kernel, len(lows), len(highs), ctx_count),
@@ -743,11 +774,16 @@
         (row_f32, gain_shape),
         "entry_back",
     )
-    rows_up, rows_qkv = after((rows_up, rows_qkv), gain_attn)
-    shard_up = own_rows(rows_up, pair, 2)
-    shard_query = own_rows(rows_qkv[:, :q_width], pair, ways)
-    shard_kv = own_rows(rows_qkv[:, q_width:], pair, ways)
-    shard_kv = shard_kv.reshape(shard_kv.shape[0], -1, 2, HD)
+    rows_output, rows_up, rows_qkv = after((rows_output, rows_up, rows_qkv), gain_attn)
+    shard_output = one(rows_output, ways)
+    shard_up = one(rows_up, 2)
+    plan = [(0, q_width, 0, 0)]
+    for h in range(groups):
+        for t in (0, 1):
+            plan.append((q_width + (2 * h + t) * HD, HD, 1 + t, h * HD))
+    shard_query, shard_key, shard_value = own_rows(
+        rows_qkv, pair, ways, plan, [q_width, groups * HD, groups * HD]
+    )
     grad_tokens = grad_tokens.reshape(tokens.shape)
     gains = butterfly_sum(
         jnp.concatenate([gain_attn[0], gain_mlp[0], gain_q_sum[0], gain_k_sum[0]])
@@ -756,8 +792,8 @@
         out_tokens,
         grad_tokens,
         shard_query,
-        shard_kv[:, :, 0].reshape(key_weight_matrix.shape),
-        shard_kv[:, :, 1].reshape(value_weight_matrix.shape),
+        shard_key,
+        shard_value,
         shard_output,
         shard_gate,
         shard_up,

time: 840 us -> 870 us (1.036)
  waiting for transfers between devices: 406 us -> 445 us
  other arithmetic: 62.7 us -> 50.6 us
    reduce_scatter x6, waiting for transfers between devices: 101 us -> 130 us  [ctx_scatter(): lax.psum_scatter(rows, 'ctx', scatter_dimension=0, tiled=True, axis_index...]
    pallas_call x0 -> x5, Pallas kernels: none -> 11.4 us  [own_rows(): pl.pallas_call(functools.partial(own_kernel, plan), out_shape=shapes, gri...]
    convert_element_type x7 -> x0, other arithmetic: 8.71 us -> none  [the longest x6 5.87 us: own_rows(): return jnp.concatenate([low, high], axis=1).astype(F32)]
    ppermute x45 -> x44, waiting for transfers between devices: 236 us -> 242 us  [xor_send(): return lax.ppermute(value, axis, [(i, i ^ step) for i in range(count)])]
    unnamed x90 -> x92, local copies, waits for them, and re-layouts: 17.4 us -> 23.8 us
    ppermute x45 -> x44, starting transfers between devices: 63.4 us -> 58.7 us  [xor_send(): return lax.ppermute(value, axis, [(i, i ^ step) for i in range(count)])]
  transfers between devices with their start and end apart: 57 -> 56, of which waited for: 41 -> 38; matrix products, arithmetic and copies ran while one was open for 29% -> 26% of each run, Pallas kernels for 10% -> 10%
where the time goes in v3:
time: 870 us; the launch traced here: 863 us
  waiting for transfers between devices  445 us (51%)
  matrix products  144 us (17%)
  Pallas kernels  87.3 us (10%)
  local copies, waits for them, and re-layouts  61.2 us (7%)
  starting transfers between devices  59.9 us (7%)
  other arithmetic  50.6 us (6%)
  between operations  15.3 us (2%)
    ppermute x44, waiting for transfers between devices, xor_send(): return lax.ppermute(value, axis, [(i, i ^ step) for i in range(count)])  242 us
    reduce_scatter x6, waiting for transfers between devices, ctx_scatter(): lax.psum_scatter(rows, 'ctx', scatter_dimension=0, tiled=True, axis_index...  130 us
    all_gather x6, waiting for transfers between devices, ctx_gather(): lax.all_gather(rows, 'ctx', axis=0, tiled=True, axis_index_groups=groups)  71.3 us
    ppermute x44, starting transfers between devices, xor_send(): return lax.ppermute(value, axis, [(i, i ^ step) for i in range(count)])  58.7 us
    dot_general x5, matrix products, dot(): return jnp.dot(left, right, preferred_element_type=F32)  52.4 us
    dot_general x6, matrix products, dot_cols(): lax.dot_general(left, right, (((1,), (1,)), ((), ())), preferred_element_...  49.6 us
    dot_general x5, matrix products, dot_rows(): lax.dot_general(left, right, (((0,), (0,)), ((), ())), preferred_element_...  41.9 us
    pallas_call x1, Pallas kernels, attend_back(): pl.pallas_call(functools.partial(backward_kernel, ways, count), out_shape...  24.7 us
  transfers between devices with their start and end apart: 56, of which 38 were waited for; matrix products, arithmetic and copies ran while one was open for 26% of the time, Pallas kernels for 10%

profile of v3, /device:TPU:0, one launch (start us, length us, event | category | flops | bytes accessed | tf_op | source)
XLA Modules:
  0.0 862.8 jit_solution(12032059819848262451)
XLA Ops:
  12.8 3.1 collective-permute-start.4
  15.9 9.1 %collective-permute-done.4 = bf16[128,1536]{1,0:T(8,128)(2,1)S(1)} collective-permute-done((bf16[128,1536]{1,0:T(8,128)(2,1)S(1)}, bf16[128,1536]{1,0:T(8,128)(2,1)S(1)}, u32[]{:S(2)}, u32[]{:S(2)}) %collective-permute-start.4) | collective-permute-done | bytes 393248 | tf_op jit(solution)/shard_map/ppermute | solution.py:26
  39.1 3.3 constant_dynamic-update-slice_fusion.7
  42.5 3.3 constant_dynamic-update-slice_fusion.6
  45.8 3.3 constant_dynamic-update-slice_fusion.5
  51.7 3.3 constant_dynamic-update-slice_fusion.4
  55.1 3.4 constant_dynamic-update-slice_fusion.3
  58.4 3.4 constant_dynamic-update-slice_fusion.2
  61.8 3.4 constant_dynamic-update-slice_fusion.1
  65.1 3.4 constant_dynamic-update-slice_fusion
  76.6 10.0 %fusion.74.raw_ref = f32[1024,1024]{1,0:T(8,128)} fusion(bf16[1024,2048]{1,0:T(8,128)(2,1)} %copy-done.2, bf16[2048,1024]{1,0:T(8,128)(2,1)} %all-gather.7.cloned.1.call-done), kind=kOutput, calls=%fused_computation.202 | convolution fusion | flops 4294967296 | bytes 12582912 | tf_op jit(solution)/shard_map/dot_general | solution.py:317
  86.6 6.2 head_prep.1
  92.8 11.9 %all-gather.9.cloned.1.call-done = bf16[2048,512]{1,0:T(8,128)(2,1)} async-done(((bf16[256,512]{1,0:T(8,128)(2,1)}), bf16[2048,512]{1,0:T(8,128)(2,1)}) %all-gather.9.cloned.1.call-update) | async-done | bytes 2097168 | tf_op jit(solution)/shard_map/all_gather | solution.py:251
  108.0 26.6 %collective-permute-done.5 = bf16[128,4608]{1,0:T(8,128)(2,1)S(1)} collective-permute-done((bf16[128,4608]{1,0:T(8,128)(2,1)S(1)}, bf16[128,4608]{1,0:T(8,128)(2,1)S(1)}, u32[]{:S(2)}, u32[]{:S(2)}) %collective-permute-start.5) | collective-permute-done | bytes 1179680 | tf_op jit(solution)/shard_map/ppermute | solution.py:26
  140.9 10.4 %collective-permute-done.6.refs_2_ = bf16[128,2048]{1,0:T(8,128)(2,1)S(1)} collective-permute-done((bf16[128,2048]{1,0:T(8,128)(2,1)S(1)}, bf16[128,2048]{1,0:T(8,128)(2,1)S(1)}, u32[]{:S(2)}, u32[]{:S(2)}) %collective-permute-start.6) | collective-permute-done | bytes 524320 | tf_op jit(solution)/shard_map/ppermute | solution.py:26
  160.2 10.3 %stack.31.info_ref = s32[26]{0:T(128)S(1)} concatenate(s32[1]{0:T(128)} %bitcast.8.pair_ref, s32[1]{0:T(128)} %bitcast.9, s32[1]{0:T(128)} %bitcast.10, s32[1]{0:T(128)} %bitcast.11, s32[1]{0:T(128)} %bitcast.12, s32[1]{0:T(128)} %bitcast.13, s32[1]{0:T(128)} %bitcast.14, s32[1]{0:T(128)} %bitcast.15, s32[1]{0:T(128)} %bitcast.16, s32[1]{0:T(128)} %bitcast.17, s32[1]{0:T(128)} %bitcast.18, ...), dimensions={0} | concatenate | bytes 208 | tf_op jit(solution)/shard_map/stack | solution.py:680
  170.5 5.9 collective-permute-done.7.refs_0_
  181.3 7.1 all-gather.11.cloned.1.call-done
  189.6 17.8 %attend.1 = (bf16[2,4,128,512]{3,2,1,0:T(8,128)(2,1)S(1)}, f32[2,2,4,1,256]{4,3,2,1,0:T(1,128)S(1)}) custom-call(s32[26]{0:T(128)S(1)} %stack.31.info_ref, bf16[2,4,128,512]{3,2,1,0:T(8,128)(2,1)S(1)} %bitcast.125, bf16[8,2,4,128,512]{4,3,2,1,0:T(8,128)(2,1)} %bitcast.145), custom_call_target="tpu_custom_call" | custom-call | flops 4294967296 | bytes 8388608 | tf_op jit(solution)/shard_map/attend/pallas_call | solution.py:552
  207.4 2.4 convolution_convert_fusion.4
  215.2 21.5 %collective-permute-done.10 = bf16[256,2048]{1,0:T(8,128)(2,1)S(1)} collective-permute-done((bf16[256,2048]{1,0:T(8,128)(2,1)}, bf16[256,2048]{1,0:T(8,128)(2,1)S(1)}, u32[]{:S(2)}, u32[]{:S(2)}) %collective-permute-start.10) | collective-permute-done | bytes 1048608 | tf_op jit(solution)/shard_map/ppermute | solution.py:26
  243.1 8.6 collective-permute-done.11.refs_3_
  251.6 3.0 collective-permute-done.13.refs_5_
  259.0 9.9 %collective-permute-done.14.refs_2_ = bf16[128,2048]{1,0:T(8,128)(2,1)S(1)} collective-permute-done((bf16[128,2048]{1,0:T(8,128)(2,1)S(1)}, bf16[128,2048]{1,0:T(8,128)(2,1)S(1)}, u32[]{:S(2)}, u32[]{:S(2)}) %collective-permute-start.14) | collective-permute-done | bytes 524320 | tf_op jit(solution)/shard_map/ppermute | solution.py:26
  271.8 20.1 %collective-permute-done.15.refs_0_ = bf16[256,2048]{1,0:T(8,128)(2,1)S(1)} collective-permute-done((bf16[256,2048]{1,0:T(8,128)(2,1)S(1)}, bf16[256,2048]{1,0:T(8,128)(2,1)S(1)}, u32[]{:S(2)}, u32[]{:S(2)}) %collective-permute-start.15) | collective-permute-done | bytes 1048608 | tf_op jit(solution)/shard_map/ppermute | solution.py:26
  295.6 11.8 %fusion.75 = f32[1024,1536]{1,0:T(8,128)} fusion(bf16[1024,2048]{1,0:T(8,128)(2,1)} %copy-done.6, bf16[2048,1536]{1,0:T(8,128)(2,1)} %all-gather.13.cloned.1.call-done), kind=kOutput, calls=%fused_computation.203 | convolution fusion | flops 6442450944 | bytes 16777216 | tf_op jit(solution)/shard_map/dot_general | solution.py:317
  307.4 10.7 %all-gather.15.cloned.1.call-done = bf16[2048,1536]{1,0:T(8,128)(2,1)} async-done(((bf16[256,1536]{1,0:T(8,128)(2,1)}), bf16[2048,1536]{1,0:T(8,128)(2,1)}) %all-gather.15.cloned.1.call-update) | async-done | bytes 6291472 | tf_op jit(solution)/shard_map/all_gather | solution.py:251
  318.1 13.1 %multiply_convert_fusion.2 = (bf16[1024,1536]{1,0:T(8,128)(2,1)S(1)}, f32[1024,1536]{1,0:T(8,128)}) fusion(f32[1024,1536]{1,0:T(8,128)} %fusion.75, bf16[1024,2048]{1,0:T(8,128)(2,1)} %copy-done.6, bf16[2048,1536]{1,0:T(8,128)(2,1)} %all-gather.15.cloned.1.call-done), kind=kOutput, calls=%fused_computation.7 | convolution fusion | flops 6450315264 | bytes 26214400 | tf_op jit(solution)/shard_map/dot_general | solution.py:317
  332.9 8.8 %convolution_convert_fusion.2 = bf16[2048,1536]{1,0:T(8,128)(2,1)} fusion(bf16[1024,2048]{1,0:T(8,128)(2,1)S(1)} %copy-done.5, bf16[1024,1536]{1,0:T(8,128)(2,1)S(1)} %get-tuple-element.78), kind=kOutput, calls=%fused_computation.4 | convolution fusion | flops 6445596672 | bytes 13631488 | tf_op jit(solution)/shard_map/dot_general | solution.py:321
  341.9 41.6 %all-gather.17.cloned.1.call-done = bf16[2048,1536]{1,0:T(8,128)(2,1)} async-done(((bf16[256,1536]{1,0:T(8,128)(2,1)}), bf16[2048,1536]{1,0:T(8,128)(2,1)}) %all-gather.17.cloned.1.call-update) | async-done | bytes 6291472 | tf_op jit(solution)/shard_map/all_gather | solution.py:251
  383.5 14.2 %multiply_convert_fusion = (bf16[1024,1536]{1,0:T(8,128)(2,1)S(1)}, bf16[1024,1536]{1,0:T(8,128)(2,1)S(1)}) fusion(f32[1024,1536]{1,0:T(8,128)} %fusion.75, f32[1024,1536]{1,0:T(8,128)} %get-tuple-element.198, bf16[1024,2048]{1,0:T(8,128)(2,1)} %copy-done.4, bf16[2048,1536]{1,0:T(8,128)(2,1)} %all-gather.17.cloned.1.call-done), kind=kOutput, calls=%fused_computation.5 | convolution fusion | flops 6462898176 | bytes 29360128 | tf_op jit(solution)/shard_map/dot_general | solution.py:317
  397.7 10.0 %fusion.76 = f32[1024,2048]{1,0:T(8,128)S(1)} fusion(bf16[1024,1536]{1,0:T(8,128)(2,1)S(1)} %get-tuple-element.122, bf16[2048,1536]{1,0:T(8,128)(2,1)} %all-gather.13.cloned.1.call-done), kind=kOutput, calls=%fused_computation.204 | convolution fusion | flops 6442450944 | bytes 17825792 | tf_op jit(solution)/shard_map/dot_general | solution.py:325
  407.7 8.9 %add_convert_fusion.1 = bf16[1024,2048]{1,0:T(8,128)(2,1)S(1)} fusion(f32[1024,2048]{1,0:T(8,128)S(1)} %fusion.76, bf16[1024,1536]{1,0:T(8,128)(2,1)S(1)} %get-tuple-element.121, bf16[2048,1536]{1,0:T(8,128)(2,1)} %all-gather.15.cloned.1.call-done), kind=kOutput, calls=%fused_computation.1 | convolution fusion | flops 6446645248 | bytes 22020096 | tf_op jit(solution)/shard_map/dot_general | solution.py:325
  423.4 8.8 %convolution_convert_fusion = bf16[2048,1536]{1,0:T(8,128)(2,1)} fusion(bf16[1024,2048]{1,0:T(8,128)(2,1)S(1)} %copy-done.7, bf16[1024,1536]{1,0:T(8,128)(2,1)S(1)} %get-tuple-element.121), kind=kOutput, calls=%fused_computation.2 | convolution fusion | flops 6445596672 | bytes 13631488 | tf_op jit(solution)/shard_map/dot_general | solution.py:321
  432.2 11.7 %convolution_convert_fusion.1 = bf16[2048,1536]{1,0:T(8,128)(2,1)} fusion(bf16[1024,2048]{1,0:T(8,128)(2,1)} %copy-done.6, bf16[1024,1536]{1,0:T(8,128)(2,1)} %copy-done.44), kind=kOutput, calls=%fused_computation.3 | convolution fusion | flops 6445596672 | bytes 13631488 | tf_op jit(solution)/shard_map/dot_general | solution.py:321
  443.9 3.3 collective-permute-done.20
  450.6 2.7 add_convert_fusion.10
  454.7 8.2 collective-permute-done.21.refs_6_
  472.3 3.7 middle_back.1
  479.2 8.7 %collective-permute-done.22.refs_2_ = bf16[128,2048]{1,0:T(8,128)(2,1)S(1)} collective-permute-done((bf16[128,2048]{1,0:T(8,128)(2,1)S(1)}, bf16[128,2048]{1,0:T(8,128)(2,1)S(1)}, u32[]{:S(2)}, u32[]{:S(2)}) %collective-permute-start.22) | collective-permute-done | bytes 524320 | tf_op jit(solution)/shard_map/ppermute | solution.py:26
  491.2 20.5 %collective-permute-done.23.refs_0_ = bf16[256,2048]{1,0:T(8,128)(2,1)S(1)} collective-permute-done((bf16[256,2048]{1,0:T(8,128)(2,1)S(1)}, bf16[256,2048]{1,0:T(8,128)(2,1)S(1)}, u32[]{:S(2)}, u32[]{:S(2)}) %collective-permute-start.23) | collective-permute-done | bytes 1048608 | tf_op jit(solution)/shard_map/ppermute | solution.py:26
  513.9 3.3 convolution_convert_fusion.7
  517.2 18.2 %reduce-scatter.9.cloned.1.call-done.both_ref = bf16[256,1536]{1,0:T(8,128)(2,1)} async-done(((bf16[2048,1536]{1,0:T(8,128)(2,1)}), bf16[256,1536]{1,0:T(8,128)(2,1)}) %reduce-scatter.9.cloned.1.call-update) | async-done | bytes 786448 | tf_op jit(solution)/shard_map/reduce_scatter | solution.py:256
  535.5 11.6 %convolution_convert_fusion.3 = bf16[1024,2048]{1,0:T(8,128)(2,1)} fusion(bf16[1024,1536]{1,0:T(8,128)(2,1)} %copy-done.45, bf16[2048,1536]{1,0:T(8,128)(2,1)} %all-gather.17.cloned.1.call-done), kind=kOutput, calls=%fused_computation.10 | convolution fusion | flops 6444548096 | bytes 13631488 | tf_op jit(solution)/shard_map/dot_general | solution.py:325
  547.1 24.7 %attend_back.1 = (f32[2,4,128,512]{3,2,1,0:T(8,128)}, bf16[8,2,4,128,512]{4,3,2,1,0:T(8,128)(2,1)}) custom-call(s32[26]{0:T(128)} %copy-done.22, bf16[2,4,128,512]{3,2,1,0:T(8,128)(2,1)} %bitcast.124, bf16[2,4,128,512]{3,2,1,0:T(8,128)(2,1)} %bitcast.148, bf16[2,4,128,512]{3,2,1,0:T(8,128)(2,1)} %copy-done.24, f32[2,2,4,1,256]{4,3,2,1,0:T(1,128)} %copy-done.25, ...), custom_call_target="tpu_custom_call" | custom-call | flops 10737418240 | bytes 16777216 | tf_op jit(solution)/shard_map/attend_back/pallas_call | solution.py:575
  571.7 5.8 head_prep_back.2
  577.6 6.3 convolution_convert_fusion.6
  588.0 7.7 fusion.2
  597.0 2.5 own_rows.5
  599.5 2.8 collective-permute-done.27.other_ref
  602.3 2.5 own_rows.6
  605.7 111.1 %reduce-scatter.13.cloned.1.call-done.d_ref = bf16[1024,512]{1,0:T(8,128)(2,1)} async-done(((bf16[8192,512]{1,0:T(8,128)(2,1)}), bf16[1024,512]{1,0:T(8,128)(2,1)}) %reduce-scatter.13.cloned.1.call-update) | async-done | bytes 1048592 | tf_op jit(solution)/shard_map/reduce_scatter | solution.py:256
  716.9 4.9 head_prep_back.3
  721.8 9.1 %add_convert_fusion = bf16[1024,2048]{1,0:T(8,128)(2,1)} fusion(f32[1024,2048]{1,0:T(8,128)} %fusion.2, bf16[1024,512]{1,0:T(8,128)(2,1)} %get-tuple-element.80, bf16[2048,1024]{1,0:T(8,128)(2,1)} %all-gather.7.cloned.1.call-done), kind=kOutput, calls=%fused_computation | convolution fusion | flops 2151677952 | bytes 15728640 | tf_op jit(solution)/shard_map/dot_general | solution.py:325
  730.9 6.3 convolution_convert_fusion.5
  745.2 19.8 %collective-permute-done.28 = bf16[256,2048]{1,0:T(8,128)(2,1)S(1)} collective-permute-done((bf16[256,2048]{1,0:T(8,128)(2,1)S(1)}, bf16[256,2048]{1,0:T(8,128)(2,1)S(1)}, u32[]{:S(2)}, u32[]{:S(2)}) %collective-permute-start.28) | collective-permute-done | bytes 1048608 | tf_op jit(solution)/shard_map/ppermute | solution.py:26
  767.2 17.1 %collective-permute-done.32 = bf16[256,2048]{1,0:T(8,128)(2,1)S(1)} collective-permute-done((bf16[256,2048]{1,0:T(8,128)(2,1)S(1)}, bf16[256,2048]{1,0:T(8,128)(2,1)S(1)}, u32[]{:S(2)}, u32[]{:S(2)}) %collective-permute-start.32) | collective-permute-done | bytes 1048608 | tf_op jit(solution)/shard_map/ppermute | solution.py:26
  786.2 2.9 collective-permute-done.34
  791.8 16.2 %collective-permute-done.33.refs_4_ = bf16[128,2048]{1,0:T(8,128)(2,1)S(1)} collective-permute-done((bf16[128,2048]{1,0:T(8,128)(2,1)S(1)}, bf16[128,2048]{1,0:T(8,128)(2,1)S(1)}, u32[]{:S(2)}, u32[]{:S(2)}) %collective-permute-start.33) | collective-permute-done | bytes 524320 | tf_op jit(solution)/shard_map/ppermute | solution.py:26
  808.1 5.0 entry_back.1
  815.6 2.6 collective-permute-done.40
  821.9 2.9 collective-permute-start.42
  837.5 9.7 %collective-permute-done.37.other_ref = bf16[128,512]{1,0:T(8,128)(2,1)S(1)} collective-permute-done((bf16[128,512]{1,0:T(8,128)(2,1)S(1)}, bf16[128,512]{1,0:T(8,128)(2,1)S(1)}, u32[]{:S(2)}, u32[]{:S(2)}) %collective-permute-start.37) | collective-permute-done | bytes 131104 | tf_op jit(solution)/shard_map/ppermute | solution.py:26
  853.3 2.5 own_rows.9
  (279 shorter events, 155.0 us)
Async XLA Ops:
  7.2 19.0 %copy-start.13 = (bf16[1,1,2,128,2048]{4,3,2,1,0:T(8,128)(2,1)S(1)}, bf16[1,1,2,128,2048]{4,3,2,1,0:T(8,128)(2,1)}, u32[]{:S(2)}) copy-start(bf16[1,1,2,128,2048]{4,3,2,1,0:T(8,128)(2,1)} %param.14) | copy-start | bytes 3145732
  7.2 69.4 %all-gather.7.cloned.1.call-start = ((), (), s32[]{:S(2)}) async-start(), calls=%async_computation.6 | async-start | bytes 4718592 | tf_op jit(solution)/shard_map/all_gather | solution.py:251
  12.8 12.2 %collective-permute-start.4 = (bf16[128,1536]{1,0:T(8,128)(2,1)S(1)}, bf16[128,1536]{1,0:T(8,128)(2,1)S(1)}, u32[]{:S(2)}, u32[]{:S(2)}) collective-permute-start(bf16[128,1536]{1,0:T(8,128)(2,1)S(1)} %pad_maximum_fusion.18), channel_id=1, source_target_pairs={{0,4},{2,6},{4,0},{6,2},{8,12},{10,14},{12,8},{14,10},{16,20},{18,... | collective-permute-start | bytes 1179656 | tf_op jit(solution)/shard_map/ppermute | solution.py:26
  26.1 78.7 %all-gather.9.cloned.1.call-start = ((), (), s32[]{:S(2)}) async-start(), calls=%async_computation.7 | async-start | bytes 2359296 | tf_op jit(solution)/shard_map/all_gather | solution.py:251
  30.2 107.5 %copy-start = (bf16[256,2048]{1,0:T(8,128)(2,1)}, bf16[256,2048]{1,0:T(8,128)(2,1)S(1)}, u32[]{:S(2)}) copy-start(bf16[256,2048]{1,0:T(8,128)(2,1)S(1)} %get-tuple-element.62.refs_0_) | copy-start | bytes 3145732
  32.0 156.4 %all-gather.11.cloned.1.call-start = ((), (), s32[]{:S(2)}) async-start(), calls=%async_computation.8 | async-start | bytes 9437184 | tf_op jit(solution)/shard_map/all_gather | solution.py:251
  34.1 15.0 %collective-permute-start = (bf16[128,2048]{1,0:T(8,128)(2,1)S(1)}, bf16[128,2048]{1,0:T(8,128)(2,1)S(1)}, u32[]{:S(2)}, u32[]{:S(2)}) collective-permute-start(bf16[128,2048]{1,0:T(8,128)(2,1)S(1)} %get-tuple-element.159.refs_1_), channel_id=1, source_target_pairs={{0,1},{1,0},{2,3},{3,2},{4,5},{5,4},{6,7},{7,6},{8,9},{9,8},{10,11... | collective-permute-start | bytes 1572872 | tf_op jit(solution)/shard_map/ppermute | solution.py:26
  35.9 14.0 %collective-permute-start.2 = (bf16[128,2048]{1,0:T(8,128)(2,1)}, bf16[128,2048]{1,0:T(8,128)(2,1)}, u32[]{:S(2)}, u32[]{:S(2)}) collective-permute-start(bf16[128,2048]{1,0:T(8,128)(2,1)} %get-tuple-element.158), channel_id=1, source_target_pairs={{0,4},{2,6},{4,0},{6,2},{8,12},{10,14},{12,8},{14,10},{16,20},{18,... | collective-permute-start | bytes 1572872 | tf_op jit(solution)/shard_map/ppermute | solution.py:26
  49.2 23.5 %collective-permute-start.1 = (bf16[256,2048]{1,0:T(8,128)(2,1)S(1)}, bf16[256,2048]{1,0:T(8,128)(2,1)S(1)}, u32[]{:S(2)}, u32[]{:S(2)}) collective-permute-start(bf16[256,2048]{1,0:T(8,128)(2,1)S(1)} %pad_maximum_fusion.3), channel_id=1, source_target_pairs={{0,4},{2,6},{4,0},{6,2},{8,12},{10,14},{12,8},{14,10},{16,20},{18,... | collective-permute-start | bytes 3145736 | tf_op jit(solution)/shard_map/ppermute | solution.py:26
  51.1 23.3 %collective-permute-start.3 = (bf16[256,2048]{1,0:T(8,128)(2,1)S(1)}, bf16[256,2048]{1,0:T(8,128)(2,1)S(1)}, u32[]{:S(2)}, u32[]{:S(2)}) collective-permute-start(bf16[256,2048]{1,0:T(8,128)(2,1)S(1)} %pad_maximum_fusion.4.refs_3_), channel_id=1, source_target_pairs={{0,1},{1,0},{2,3},{3,2},{4,5},{5,4},{6,7},{7,6},{8,9},{9,8},{10,11... | collective-permute-start | bytes 3145736 | tf_op jit(solution)/shard_map/ppermute | solution.py:26
  104.8 190.8 %all-gather.13.cloned.1.call-start = ((), (), s32[]{:S(2)}) async-start(), calls=%async_computation.9 | async-start | bytes 7077888 | tf_op jit(solution)/shard_map/all_gather | solution.py:251
  106.5 28.2 %collective-permute-start.5 = (bf16[128,4608]{1,0:T(8,128)(2,1)S(1)}, bf16[128,4608]{1,0:T(8,128)(2,1)S(1)}, u32[]{:S(2)}, u32[]{:S(2)}) collective-permute-start(bf16[128,4608]{1,0:T(8,128)(2,1)S(1)} %pad_maximum_fusion.2), channel_id=1, source_target_pairs={{0,4},{2,6},{4,0},{6,2},{8,12},{10,14},{12,8},{14,10},{16,20},{18,... | collective-permute-start | bytes 3538952 | tf_op jit(solution)/shard_map/ppermute | solution.py:26
  136.7 181.4 %all-gather.15.cloned.1.call-start = ((), (), s32[]{:S(2)}) async-start(), calls=%async_computation.10 | async-start | bytes 7077888 | tf_op jit(solution)/shard_map/all_gather | solution.py:251
  137.3 246.2 %all-gather.17.cloned.1.call-start = ((), (), s32[]{:S(2)}) async-start(), calls=%async_computation.11 | async-start | bytes 7077888 | tf_op jit(solution)/shard_map/all_gather | solution.py:251
  137.9 13.4 %collective-permute-start.6 = (bf16[128,2048]{1,0:T(8,128)(2,1)S(1)}, bf16[128,2048]{1,0:T(8,128)(2,1)S(1)}, u32[]{:S(2)}, u32[]{:S(2)}) collective-permute-start(bf16[128,2048]{1,0:T(8,128)(2,1)S(1)} %get-tuple-element.157.refs_1_), channel_id=1, source_target_pairs={{0,1},{1,0},{2,3},{3,2},{4,5},{5,4},{6,7},{7,6},{8,9},{9,8},{10,11... | collective-permute-start | bytes 1572872 | tf_op jit(solution)/shard_map/ppermute | solution.py:26
  139.4 14.3 %collective-permute-start.8 = (bf16[128,2048]{1,0:T(8,128)(2,1)S(1)}, bf16[128,2048]{1,0:T(8,128)(2,1)S(1)}, u32[]{:S(2)}, u32[]{:S(2)}) collective-permute-start(bf16[128,2048]{1,0:T(8,128)(2,1)S(1)} %get-tuple-element.156), channel_id=1, source_target_pairs={{0,4},{2,6},{4,0},{6,2},{8,12},{10,14},{12,8},{14,10},{16,20},{18,... | collective-permute-start | bytes 1572872 | tf_op jit(solution)/shard_map/ppermute | solution.py:26
  152.3 24.1 %collective-permute-start.7 = (bf16[256,2048]{1,0:T(8,128)(2,1)}, bf16[256,2048]{1,0:T(8,128)(2,1)}, u32[]{:S(2)}, u32[]{:S(2)}) collective-permute-start(bf16[256,2048]{1,0:T(8,128)(2,1)} %pad_maximum_fusion.5), channel_id=1, source_target_pairs={{0,4},{2,6},{4,0},{6,2},{8,12},{10,14},{12,8},{14,10},{16,20},{18,... | collective-permute-start | bytes 3145736 | tf_op jit(solution)/shard_map/ppermute | solution.py:26
  153.8 23.7 %collective-permute-start.9 = (bf16[256,2048]{1,0:T(8,128)(2,1)S(1)}, bf16[256,2048]{1,0:T(8,128)(2,1)}, u32[]{:S(2)}, u32[]{:S(2)}) collective-permute-start(bf16[256,2048]{1,0:T(8,128)(2,1)S(1)} %pad_maximum_fusion.6.refs_3_), channel_id=1, source_target_pairs={{0,1},{1,0},{2,3},{3,2},{4,5},{5,4},{6,7},{7,6},{8,9},{9,8},{10,11... | collective-permute-start | bytes 3145736 | tf_op jit(solution)/shard_map/ppermute | solution.py:26
  211.1 25.5 %collective-permute-start.10 = (bf16[256,2048]{1,0:T(8,128)(2,1)}, bf16[256,2048]{1,0:T(8,128)(2,1)S(1)}, u32[]{:S(2)}, u32[]{:S(2)}) collective-permute-start(bf16[256,2048]{1,0:T(8,128)(2,1)} %pad_maximum_fusion.7), channel_id=1, source_target_pairs={{0,4},{2,6},{4,0},{6,2},{8,12},{10,14},{12,8},{14,10},{16,20},{18,... | collective-permute-start | bytes 3145736 | tf_op jit(solution)/shard_map/ppermute | solution.py:26
  213.7 26.1 %collective-permute-start.12 = (bf16[256,2048]{1,0:T(8,128)(2,1)}, bf16[256,2048]{1,0:T(8,128)(2,1)S(1)}, u32[]{:S(2)}, u32[]{:S(2)}) collective-permute-start(bf16[256,2048]{1,0:T(8,128)(2,1)} %slice.329), channel_id=1, source_target_pairs={{0,1},{1,0},{2,3},{3,2},{4,5},{5,4},{6,7},{7,6},{8,9},{9,8},{10,11... | collective-permute-start | bytes 3145736 | tf_op jit(solution)/shard_map/ppermute | solution.py:26
  215.1 27.9 %copy-start.37 = (f32[2048]{0:T(1024)S(1)}, f32[2048]{0:T(1024)}, u32[]{:S(2)}) copy-start(f32[2048]{0:T(1024)} %param.25) | copy-start | bytes 24580
  215.2 251.6 %reduce-scatter.7.cloned.1.call-start = ((), (), s32[]{:S(2)}) async-start(), calls=%async_computation.12 | async-start | bytes 7077888 | tf_op jit(solution)/shard_map/reduce_scatter | solution.py:256
  238.2 13.4 %collective-permute-start.11 = (bf16[128,2048]{1,0:T(8,128)(2,1)S(1)}, bf16[128,2048]{1,0:T(8,128)(2,1)S(1)}, u32[]{:S(2)}, u32[]{:S(2)}) collective-permute-start(bf16[128,2048]{1,0:T(8,128)(2,1)S(1)} %get-tuple-element.129), channel_id=1, source_target_pairs={{0,1},{1,0},{2,3},{3,2},{4,5},{5,4},{6,7},{7,6},{8,9},{9,8},{10,11... | collective-permute-start | bytes 1572872 | tf_op jit(solution)/shard_map/ppermute | solution.py:26
  241.5 13.1 %collective-permute-start.13 = (bf16[128,2048]{1,0:T(8,128)(2,1)S(1)}, bf16[128,2048]{1,0:T(8,128)(2,1)S(1)}, u32[]{:S(2)}, u32[]{:S(2)}) collective-permute-start(bf16[128,2048]{1,0:T(8,128)(2,1)S(1)} %get-tuple-element.154), channel_id=1, source_target_pairs={{0,4},{2,6},{4,0},{6,2},{8,12},{10,14},{12,8},{14,10},{16,20},{18,... | collective-permute-start | bytes 1572872 | tf_op jit(solution)/shard_map/ppermute | solution.py:26
  256.8 12.2 %collective-permute-start.14 = (bf16[128,2048]{1,0:T(8,128)(2,1)S(1)}, bf16[128,2048]{1,0:T(8,128)(2,1)S(1)}, u32[]{:S(2)}, u32[]{:S(2)}) collective-permute-start(bf16[128,2048]{1,0:T(8,128)(2,1)S(1)} %get-tuple-element.153.refs_1_), channel_id=1, source_target_pairs={{0,1},{1,0},{2,3},{3,2},{4,5},{5,4},{6,7},{7,6},{8,9},{9,8},{10,11... | collective-permute-start | bytes 1572872 | tf_op jit(solution)/shard_map/ppermute | solution.py:26
  257.4 13.3 %collective-permute-start.16 = (bf16[128,2048]{1,0:T(8,128)(2,1)S(1)}, bf16[128,2048]{1,0:T(8,128)(2,1)S(1)}, u32[]{:S(2)}, u32[]{:S(2)}) collective-permute-start(bf16[128,2048]{1,0:T(8,128)(2,1)S(1)} %get-tuple-element.152), channel_id=1, source_target_pairs={{0,4},{2,6},{4,0},{6,2},{8,12},{10,14},{12,8},{14,10},{16,20},{18,... | collective-permute-start | bytes 1572872 | tf_op jit(solution)/shard_map/ppermute | solution.py:26
  269.1 22.8 %collective-permute-start.15 = (bf16[256,2048]{1,0:T(8,128)(2,1)S(1)}, bf16[256,2048]{1,0:T(8,128)(2,1)S(1)}, u32[]{:S(2)}, u32[]{:S(2)}) collective-permute-start(bf16[256,2048]{1,0:T(8,128)(2,1)S(1)} %pad_maximum_fusion.8), channel_id=1, source_target_pairs={{0,4},{2,6},{4,0},{6,2},{8,12},{10,14},{12,8},{14,10},{16,20},{18,... | collective-permute-start | bytes 3145736 | tf_op jit(solution)/shard_map/ppermute | solution.py:26
  270.8 22.5 %collective-permute-start.17 = (bf16[256,2048]{1,0:T(8,128)(2,1)S(1)}, bf16[256,2048]{1,0:T(8,128)(2,1)S(1)}, u32[]{:S(2)}, u32[]{:S(2)}) collective-permute-start(bf16[256,2048]{1,0:T(8,128)(2,1)S(1)} %pad_maximum_fusion.9.refs_3_), channel_id=1, source_target_pairs={{0,1},{1,0},{2,3},{3,2},{4,5},{5,4},{6,7},{7,6},{8,9},{9,8},{10,11... | collective-permute-start | bytes 3145736 | tf_op jit(solution)/shard_map/ppermute | solution.py:26
  341.7 193.7 %reduce-scatter.9.cloned.1.call-start = ((), (), s32[]{:S(2)}) async-start(), calls=%async_computation.13 | async-start | bytes 7077888 | tf_op jit(solution)/shard_map/reduce_scatter | solution.py:256
  420.4 30.1 %collective-permute-start.18 = (bf16[256,2048]{1,0:T(8,128)(2,1)}, bf16[256,2048]{1,0:T(8,128)(2,1)}, u32[]{:S(2)}, u32[]{:S(2)}) collective-permute-start(bf16[256,2048]{1,0:T(8,128)(2,1)} %pad_maximum_fusion.10), channel_id=1, source_target_pairs={{0,4},{2,6},{4,0},{6,2},{8,12},{10,14},{12,8},{14,10},{16,20},{18,... | collective-permute-start | bytes 3145736 | tf_op jit(solution)/shard_map/ppermute | solution.py:26
  421.9 25.3 %collective-permute-start.20 = (bf16[256,2048]{1,0:T(8,128)(2,1)}, bf16[256,2048]{1,0:T(8,128)(2,1)}, u32[]{:S(2)}, u32[]{:S(2)}) collective-permute-start(bf16[256,2048]{1,0:T(8,128)(2,1)} %slice.337), channel_id=1, source_target_pairs={{0,1},{1,0},{2,3},{3,2},{4,5},{5,4},{6,7},{7,6},{8,9},{9,8},{10,11... | collective-permute-start | bytes 3145736 | tf_op jit(solution)/shard_map/ppermute | solution.py:26
  450.1 12.9 %collective-permute-start.21 = (bf16[128,2048]{1,0:T(8,128)(2,1)S(1)}, bf16[128,2048]{1,0:T(8,128)(2,1)S(1)}, u32[]{:S(2)}, u32[]{:S(2)}) collective-permute-start(bf16[128,2048]{1,0:T(8,128)(2,1)S(1)} %get-tuple-element.150), channel_id=1, source_target_pairs={{0,4},{2,6},{4,0},{6,2},{8,12},{10,14},{12,8},{14,10},{16,20},{18,... | collective-permute-start | bytes 1572872 | tf_op jit(solution)/shard_map/ppermute | solution.py:26
  453.2 12.7 %collective-permute-start.19 = (bf16[128,2048]{1,0:T(8,128)(2,1)S(1)}, bf16[128,2048]{1,0:T(8,128)(2,1)S(1)}, u32[]{:S(2)}, u32[]{:S(2)}) collective-permute-start(bf16[128,2048]{1,0:T(8,128)(2,1)S(1)} %get-tuple-element.127), channel_id=1, source_target_pairs={{0,1},{1,0},{2,3},{3,2},{4,5},{5,4},{6,7},{7,6},{8,9},{9,8},{10,11... | collective-permute-start | bytes 1572872 | tf_op jit(solution)/shard_map/ppermute | solution.py:26
  466.8 138.9 %reduce-scatter.11.cloned.1.call-start = ((), (), s32[]{:S(2)}) async-start(), calls=%async_computation.14 | async-start | bytes 7077888 | tf_op jit(solution)/shard_map/reduce_scatter | solution.py:256
  476.2 11.8 %collective-permute-start.22 = (bf16[128,2048]{1,0:T(8,128)(2,1)S(1)}, bf16[128,2048]{1,0:T(8,128)(2,1)S(1)}, u32[]{:S(2)}, u32[]{:S(2)}) collective-permute-start(bf16[128,2048]{1,0:T(8,128)(2,1)S(1)} %get-tuple-element.149.refs_1_), channel_id=1, source_target_pairs={{0,1},{1,0},{2,3},{3,2},{4,5},{5,4},{6,7},{7,6},{8,9},{9,8},{10,11... | collective-permute-start | bytes 1572872 | tf_op jit(solution)/shard_map/ppermute | solution.py:26
  477.8 12.7 %collective-permute-start.24 = (bf16[128,2048]{1,0:T(8,128)(2,1)S(1)}, bf16[128,2048]{1,0:T(8,128)(2,1)S(1)}, u32[]{:S(2)}, u32[]{:S(2)}) collective-permute-start(bf16[128,2048]{1,0:T(8,128)(2,1)S(1)} %get-tuple-element.148), channel_id=1, source_target_pairs={{0,4},{2,6},{4,0},{6,2},{8,12},{10,14},{12,8},{14,10},{16,20},{18,... | collective-permute-start | bytes 1572872 | tf_op jit(solution)/shard_map/ppermute | solution.py:26
  488.1 23.6 %collective-permute-start.23 = (bf16[256,2048]{1,0:T(8,128)(2,1)S(1)}, bf16[256,2048]{1,0:T(8,128)(2,1)S(1)}, u32[]{:S(2)}, u32[]{:S(2)}) collective-permute-start(bf16[256,2048]{1,0:T(8,128)(2,1)S(1)} %pad_maximum_fusion.11), channel_id=1, source_target_pairs={{0,4},{2,6},{4,0},{6,2},{8,12},{10,14},{12,8},{14,10},{16,20},{18,... | collective-permute-start | bytes 3145736 | tf_op jit(solution)/shard_map/ppermute | solution.py:26
  490.6 23.3 %copy-start.41 = (bf16[2048,512]{1,0:T(8,128)(2,1)S(1)}, bf16[2048,512]{1,0:T(8,128)(2,1)}, u32[]{:S(2)}) copy-start(bf16[2048,512]{1,0:T(8,128)(2,1)} %all-gather.9.cloned.1.call-done) | copy-start | bytes 6291460
  490.6 21.1 %collective-permute-start.25 = (bf16[256,2048]{1,0:T(8,128)(2,1)S(1)}, bf16[256,2048]{1,0:T(8,128)(2,1)S(1)}, u32[]{:S(2)}, u32[]{:S(2)}) collective-permute-start(bf16[256,2048]{1,0:T(8,128)(2,1)S(1)} %pad_maximum_fusion.12.refs_3_), channel_id=1, source_target_pairs={{0,1},{1,0},{2,3},{3,2},{4,5},{5,4},{6,7},{7,6},{8,9},{9,8},{10,11... | collective-permute-start | bytes 3145736 | tf_op jit(solution)/shard_map/ppermute | solution.py:26
  535.4 181.4 %reduce-scatter.13.cloned.1.call-start = ((), (), s32[]{:S(2)}) async-start(), calls=%async_computation.15 | async-start | bytes 9437184 | tf_op jit(solution)/shard_map/reduce_scatter | solution.py:256
  584.9 12.2 %collective-permute-start.26 = (bf16[128,1536]{1,0:T(8,128)(2,1)S(1)}, bf16[128,1536]{1,0:T(8,128)(2,1)}, u32[]{:S(2)}, u32[]{:S(2)}) collective-permute-start(bf16[128,1536]{1,0:T(8,128)(2,1)S(1)} %constant_dynamic-slice_fusion.3), channel_id=1, source_target_pairs={{0,4},{2,6},{4,0},{6,2},{8,12},{10,14},{12,8},{14,10},{16,20},{18,... | collective-permute-start | bytes 1179656 | tf_op jit(solution)/shard_map/ppermute | solution.py:26
  587.4 14.9 %collective-permute-start.27 = (bf16[128,1536]{1,0:T(8,128)(2,1)S(1)}, bf16[128,1536]{1,0:T(8,128)(2,1)}, u32[]{:S(2)}, u32[]{:S(2)}) collective-permute-start(bf16[128,1536]{1,0:T(8,128)(2,1)S(1)} %constant_dynamic-slice_fusion.2), channel_id=1, source_target_pairs={{0,4},{2,6},{4,0},{6,2},{8,12},{10,14},{12,8},{14,10},{16,20},{18,... | collective-permute-start | bytes 1179656 | tf_op jit(solution)/shard_map/ppermute | solution.py:26
  605.6 226.0 %reduce-scatter.15.cloned.1.call-start = ((), (), s32[]{:S(2)}) async-start(), calls=%async_computation.16 | async-start | bytes 2359296 | tf_op jit(solution)/shard_map/reduce_scatter | solution.py:256
  716.9 114.8 %reduce-scatter.17.cloned.1.call-start = ((), (), s32[]{:S(2)}) async-start(), calls=%async_computation.17 | async-start | bytes 4718592 | tf_op jit(solution)/shard_map/reduce_scatter | solution.py:256
  738.8 26.1 %collective-permute-start.28 = (bf16[256,2048]{1,0:T(8,128)(2,1)S(1)}, bf16[256,2048]{1,0:T(8,128)(2,1)S(1)}, u32[]{:S(2)}, u32[]{:S(2)}) collective-permute-start(bf16[256,2048]{1,0:T(8,128)(2,1)S(1)} %pad_maximum_fusion.13), channel_id=1, source_target_pairs={{0,4},{2,6},{4,0},{6,2},{8,12},{10,14},{12,8},{14,10},{16,20},{18,... | collective-permute-start | bytes 3145736 | tf_op jit(solution)/shard_map/ppermute | solution.py:26
  740.5 26.3 %collective-permute-start.30 = (bf16[256,2048]{1,0:T(8,128)(2,1)S(1)}, bf16[256,2048]{1,0:T(8,128)(2,1)S(1)}, u32[]{:S(2)}, u32[]{:S(2)}) collective-permute-start(bf16[256,2048]{1,0:T(8,128)(2,1)S(1)} %slice.287), channel_id=1, source_target_pairs={{0,1},{1,0},{2,3},{3,2},{4,5},{5,4},{6,7},{7,6},{8,9},{9,8},{10,11... | collective-permute-start | bytes 3145736 | tf_op jit(solution)/shard_map/ppermute | solution.py:26
  743.4 40.9 %collective-permute-start.32 = (bf16[256,2048]{1,0:T(8,128)(2,1)S(1)}, bf16[256,2048]{1,0:T(8,128)(2,1)S(1)}, u32[]{:S(2)}, u32[]{:S(2)}) collective-permute-start(bf16[256,2048]{1,0:T(8,128)(2,1)S(1)} %pad_maximum_fusion.14), channel_id=1, source_target_pairs={{0,4},{2,6},{4,0},{6,2},{8,12},{10,14},{12,8},{14,10},{16,20},{18,... | collective-permute-start | bytes 3145736 | tf_op jit(solution)/shard_map/ppermute | solution.py:26
  744.5 44.5 %collective-permute-start.34 = (bf16[256,2048]{1,0:T(8,128)(2,1)S(1)}, bf16[256,2048]{1,0:T(8,128)(2,1)S(1)}, u32[]{:S(2)}, u32[]{:S(2)}) collective-permute-start(bf16[256,2048]{1,0:T(8,128)(2,1)S(1)} %slice.353), channel_id=1, source_target_pairs={{0,1},{1,0},{2,3},{3,2},{4,5},{5,4},{6,7},{7,6},{8,9},{9,8},{10,11... | collective-permute-start | bytes 3145736 | tf_op jit(solution)/shard_map/ppermute | solution.py:26
  765.3 62.8 %collective-permute-start.29 = (bf16[128,2048]{1,0:T(8,128)(2,1)S(1)}, bf16[128,2048]{1,0:T(8,128)(2,1)S(1)}, u32[]{:S(2)}, u32[]{:S(2)}) collective-permute-start(bf16[128,2048]{1,0:T(8,128)(2,1)S(1)} %get-tuple-element.125), channel_id=1, source_target_pairs={{0,1},{1,0},{2,3},{3,2},{4,5},{5,4},{6,7},{7,6},{8,9},{9,8},{10,11... | collective-permute-start | bytes 1572872 | tf_op jit(solution)/shard_map/ppermute | solution.py:26
  784.7 23.3 %copy-start.10 = (f32[256,2048]{1,0:T(8,128)S(1)}, f32[256,2048]{1,0:T(8,128)}, u32[]{:S(2)}) copy-start(f32[256,2048]{1,0:T(8,128)} %copy-done.9) | copy-start | bytes 6291460
  784.7 23.3 %copy-start.21 = (f32[1,4,2,2,128]{4,3,2,1,0:T(2,128)S(1)}, f32[1,4,2,2,128]{4,3,2,1,0:T(2,128)}, u32[]{:S(2)}) copy-start(f32[1,4,2,2,128]{4,3,2,1,0:T(2,128)} %copy-done.20) | copy-start | bytes 24580
  784.7 23.3 %collective-permute-start.33 = (bf16[128,2048]{1,0:T(8,128)(2,1)S(1)}, bf16[128,2048]{1,0:T(8,128)(2,1)S(1)}, u32[]{:S(2)}, u32[]{:S(2)}) collective-permute-start(bf16[128,2048]{1,0:T(8,128)(2,1)S(1)} %get-tuple-element.123), channel_id=1, source_target_pairs={{0,1},{1,0},{2,3},{3,2},{4,5},{5,4},{6,7},{7,6},{8,9},{9,8},{10,11... | collective-permute-start | bytes 1572872 | tf_op jit(solution)/shard_map/ppermute | solution.py:26
  789.5 23.5 %copy-start.38 = (f32[1,128]{1,0:T(1,128)S(1)}, f32[1,128]{1,0:T(1,128)}, u32[]{:S(2)}) copy-start(f32[1,128]{1,0:T(1,128)} %get-tuple-element.95) | copy-start | bytes 1540
  789.5 23.5 %copy-start.39 = (f32[1,128]{1,0:T(1,128)S(1)}, f32[1,128]{1,0:T(1,128)}, u32[]{:S(2)}) copy-start(f32[1,128]{1,0:T(1,128)} %get-tuple-element.96) | copy-start | bytes 1540
  789.6 18.5 %collective-permute-start.35 = (bf16[128,2048]{1,0:T(8,128)(2,1)S(1)}, bf16[128,2048]{1,0:T(8,128)(2,1)S(1)}, u32[]{:S(2)}, u32[]{:S(2)}) collective-permute-start(bf16[128,2048]{1,0:T(8,128)(2,1)S(1)} %get-tuple-element.144), channel_id=1, source_target_pairs={{0,4},{2,6},{4,0},{6,2},{8,12},{10,14},{12,8},{14,10},{16,20},{18,... | collective-permute-start | bytes 1572872 | tf_op jit(solution)/shard_map/ppermute | solution.py:26
  790.7 37.4 %collective-permute-start.31 = (bf16[128,2048]{1,0:T(8,128)(2,1)S(1)}, bf16[128,2048]{1,0:T(8,128)(2,1)S(1)}, u32[]{:S(2)}, u32[]{:S(2)}) collective-permute-start(bf16[128,2048]{1,0:T(8,128)(2,1)S(1)} %get-tuple-element.146), channel_id=1, source_target_pairs={{0,4},{2,6},{4,0},{6,2},{8,12},{10,14},{12,8},{14,10},{16,20},{18,... | collective-permute-start | bytes 1572872 | tf_op jit(solution)/shard_map/ppermute | solution.py:26
  813.0 1.3 collective-permute-start.39
  814.3 3.8 collective-permute-start.40
  818.2 3.8 collective-permute-start.41
  821.9 4.7 collective-permute-start.42
  826.6 3.8 collective-permute-start.43
  831.7 20.9 %collective-permute-start.38 = (bf16[128,1536]{1,0:T(8,128)(2,1)S(1)}, bf16[128,1536]{1,0:T(8,128)(2,1)S(1)}, u32[]{:S(2)}, u32[]{:S(2)}) collective-permute-start(bf16[128,1536]{1,0:T(8,128)(2,1)S(1)} %constant_dynamic-slice_fusion.17), channel_id=1, source_target_pairs={{0,4},{2,6},{4,0},{6,2},{8,12},{10,14},{12,8},{14,10},{16,20},{18,... | collective-permute-start | bytes 1179656 | tf_op jit(solution)/shard_map/ppermute | solution.py:26
  833.9 15.8 %collective-permute-start.36 = (bf16[128,1024]{1,0:T(8,128)(2,1)S(1)}, bf16[128,1024]{1,0:T(8,128)(2,1)S(1)}, u32[]{:S(2)}, u32[]{:S(2)}) collective-permute-start(bf16[128,1024]{1,0:T(8,128)(2,1)S(1)} %constant_dynamic-slice_fusion.1), channel_id=1, source_target_pairs={{0,4},{2,6},{4,0},{6,2},{8,12},{10,14},{12,8},{14,10},{16,20},{18,... | collective-permute-start | bytes 786440 | tf_op jit(solution)/shard_map/ppermute | solution.py:26
  835.7 11.5 %collective-permute-start.37 = (bf16[128,512]{1,0:T(8,128)(2,1)S(1)}, bf16[128,512]{1,0:T(8,128)(2,1)S(1)}, u32[]{:S(2)}, u32[]{:S(2)}) collective-permute-start(bf16[128,512]{1,0:T(8,128)(2,1)S(1)} %constant_dynamic-slice_fusion), channel_id=1, source_target_pairs={{0,4},{2,6},{4,0},{6,2},{8,12},{10,14},{12,8},{14,10},{16,20},{18,... | collective-permute-start | bytes 393224 | tf_op jit(solution)/shard_map/ppermute | solution.py:26
  (38 other events, 209.3 us)
Sparse Core Ops, SparseCore 0:
  26.2 48.3 all-gather.6
  76.8 27.9 all-gather.8
  106.9 81.4 all-gather.10
  189.9 63.2 all-gather.12
  254.7 63.3 all-gather.14
  320.1 63.3 all-gather.16
  385.8 68.3 reduce-scatter.6
  466.9 68.4 reduce-scatter.8
  537.7 67.8 reduce-scatter.10
  607.8 109.0 reduce-scatter.12
  719.1 34.4 reduce-scatter.14
  755.8 48.6 reduce-scatter.16

commit v4 on v3

--- a/solution.py
+++ b/solution.py
@@ -721,7 +721,7 @@
     grad_gate = dot_rows(h2_late, d_gate).astype(BF16)
     grad_up = dot_rows(h2_late, d_up).astype(BF16)
     lows, highs = return_rows(d_h2_part, 2, (grad_gate, grad_up))
-    returned = lows + highs
+    returned = (lows[0], highs[0])
     d_x2, d_x2_low, gain_mlp = row_pass(
         functools.partial(back_kernel, len(lows), len(highs), None),
         (cot_own, x2, gain_mlp_row, *lows, *highs),
@@ -729,7 +729,14 @@
         "middle_back",
     )
     y_part = dot_cols(after(act, d_x2_low), full_down).astype(BF16)
-    branch = gather_rows(d_x2_low, ways)
+    branch = after(gather_rows(d_x2_low, ways), y_part)
+    y_lows, y_highs = return_rows(after(y_part, branch), 2)
+    out_tokens = row_pass(
+        functools.partial(result_kernel, len(y_lows), len(y_highs), ctx_count),
+        (x2, *y_lows, *y_highs),
+        row_bf16,
+        "result",
+    ).reshape(tokens.shape)
     rows_down = scatter_weight(grad_down, 2)
     rows_gate = scatter_weight(after(grad_gate, (rows_down, returned)), 2)
     d_att = dot(branch, full_output).astype(BF16).reshape(q.shape)
@@ -748,7 +755,7 @@
     d_h1_query = dot_cols(d_qp, full_qkv[:, :q_width])
     d_kv = after(
         d_kv.reshape(-1, kv_width),
-        (rows_up, d_h1_query, grad_output, y_part, shard_down, shard_gate),
+        (rows_up, d_h1_query, out_tokens, shard_down, shard_gate),
     )
     d_kv = ctx_scatter(d_kv, ways)
     rows_output = scatter_weight(after(grad_output, d_kv), ways)
@@ -756,13 +763,6 @@
     d_h1 = (
         d_h1_query + dot_cols(d_kvp, full_qkv[:, q_width:])
     ).astype(BF16)
-    lows, highs = return_rows(after(y_part, branch), 2)
-    out_tokens = row_pass(
-        functools.partial(result_kernel, len(lows), len(highs), ctx_count),
-        (after(x2, d_h1), *lows, *highs),
-        row_bf16,
-        "result",
-    ).reshape(tokens.shape)
     lows, highs = return_rows(d_h1, ways)
     d_raw = jnp.concatenate([d_qp, d_kvp], axis=1)
     grad_qkv = dot_rows(after(h1, d_h1), d_raw).astype(BF16)
@@ -774,7 +774,7 @@
         (row_f32, gain_shape),
         "entry_back",
     )
-    rows_output, rows_up, rows_qkv = after((rows_output, rows_up, rows_qkv), gain_attn)
+    rows_output, rows_up, rows_qkv = after((rows_output, rows_up, rows_qkv), (lows, highs))
     shard_output = one(rows_output, ways)
     shard_up = one(rows_up, 2)
     plan = [(0, q_width, 0, 0)]

time: 870 us -> 837 us (0.962)
  waiting for transfers between devices: 445 us -> 409 us
    reduce_scatter x6, waiting for transfers between devices: 130 us -> 112 us  [ctx_scatter(): lax.psum_scatter(rows, 'ctx', scatter_dimension=0, tiled=True, axis_index...]
    ppermute x44, waiting for transfers between devices: 242 us -> 228 us  [xor_send(): return lax.ppermute(value, axis, [(i, i ^ step) for i in range(count)])]
    unnamed x92 -> x94, local copies, waits for them, and re-layouts: 23.8 us -> 21.5 us
  transfers between devices with their start and end apart: 56 -> 56, of which waited for: 38 -> 42; matrix products, arithmetic and copies ran while one was open for 26% -> 27% of each run, Pallas kernels for 10% -> 10%
where the time goes in v4:
time: 837 us; the launch traced here: 829 us
  waiting for transfers between devices  409 us (49%)
  matrix products  141 us (17%)
  Pallas kernels  87.8 us (10%)
  starting transfers between devices  61.2 us (7%)
  local copies, waits for them, and re-layouts  59.2 us (7%)
  other arithmetic  55.6 us (7%)
  between operations  15.3 us (2%)
    ppermute x44, waiting for transfers between devices, xor_send(): return lax.ppermute(value, axis, [(i, i ^ step) for i in range(count)])  228 us
    reduce_scatter x6, waiting for transfers between devices, ctx_scatter(): lax.psum_scatter(rows, 'ctx', scatter_dimension=0, tiled=True, axis_index...  112 us
    all_gather x6, waiting for transfers between devices, ctx_gather(): lax.all_gather(rows, 'ctx', axis=0, tiled=True, axis_index_groups=groups)  68.2 us
    ppermute x44, starting transfers between devices, xor_send(): return lax.ppermute(value, axis, [(i, i ^ step) for i in range(count)])  60.1 us
    dot_general x5, matrix products, dot(): return jnp.dot(left, right, preferred_element_type=F32)  52.3 us
    dot_general x6, matrix products, dot_cols(): lax.dot_general(left, right, (((1,), (1,)), ((), ())), preferred_element_...  47 us
    dot_general x5, matrix products, dot_rows(): lax.dot_general(left, right, (((0,), (0,)), ((), ())), preferred_element_...  41.6 us
    pallas_call x1, Pallas kernels, attend_back(): pl.pallas_call(functools.partial(backward_kernel, ways, count), out_shape...  25.1 us
  transfers between devices with their start and end apart: 56, of which 42 were waited for; matrix products, arithmetic and copies ran while one was open for 27% of the time, Pallas kernels for 10%

profile of v4, /device:TPU:0, one launch (start us, length us, event | category | flops | bytes accessed | tf_op | source)
XLA Modules:
  0.0 828.9 jit_solution(10283574275886716271)
XLA Ops:
  12.8 3.1 collective-permute-start.4
  15.9 9.1 %collective-permute-done.4 = bf16[128,1536]{1,0:T(8,128)(2,1)S(1)} collective-permute-done((bf16[128,1536]{1,0:T(8,128)(2,1)S(1)}, bf16[128,1536]{1,0:T(8,128)(2,1)S(1)}, u32[]{:S(2)}, u32[]{:S(2)}) %collective-permute-start.4) | collective-permute-done | bytes 393248 | tf_op jit(solution)/shard_map/ppermute | solution.py:26
  39.2 3.4 constant_dynamic-update-slice_fusion.7
  42.6 3.4 constant_dynamic-update-slice_fusion.6
  46.0 3.4 constant_dynamic-update-slice_fusion.5
  51.7 3.4 constant_dynamic-update-slice_fusion.4
  55.1 3.4 constant_dynamic-update-slice_fusion.3
  58.5 3.4 constant_dynamic-update-slice_fusion.2
  61.8 3.4 constant_dynamic-update-slice_fusion.1
  65.2 3.4 constant_dynamic-update-slice_fusion
  76.9 10.0 %fusion.74.raw_ref = f32[1024,1024]{1,0:T(8,128)} fusion(bf16[1024,2048]{1,0:T(8,128)(2,1)} %copy-done.2, bf16[2048,1024]{1,0:T(8,128)(2,1)} %all-gather.7.cloned.1.call-done), kind=kOutput, calls=%fused_computation.202 | convolution fusion | flops 4294967296 | bytes 12582912 | tf_op jit(solution)/shard_map/dot_general | solution.py:317
  86.9 6.3 head_prep.1
  93.2 11.6 %all-gather.9.cloned.1.call-done = bf16[2048,512]{1,0:T(8,128)(2,1)} async-done(((bf16[256,512]{1,0:T(8,128)(2,1)}), bf16[2048,512]{1,0:T(8,128)(2,1)}) %all-gather.9.cloned.1.call-update) | async-done | bytes 2097168 | tf_op jit(solution)/shard_map/all_gather | solution.py:251
  108.0 26.6 %collective-permute-done.5 = bf16[128,4608]{1,0:T(8,128)(2,1)S(1)} collective-permute-done((bf16[128,4608]{1,0:T(8,128)(2,1)S(1)}, bf16[128,4608]{1,0:T(8,128)(2,1)S(1)}, u32[]{:S(2)}, u32[]{:S(2)}) %collective-permute-start.5) | collective-permute-done | bytes 1179680 | tf_op jit(solution)/shard_map/ppermute | solution.py:26
  140.9 10.4 %collective-permute-done.6.refs_2_ = bf16[128,2048]{1,0:T(8,128)(2,1)S(1)} collective-permute-done((bf16[128,2048]{1,0:T(8,128)(2,1)S(1)}, bf16[128,2048]{1,0:T(8,128)(2,1)S(1)}, u32[]{:S(2)}, u32[]{:S(2)}) %collective-permute-start.6) | collective-permute-done | bytes 524320 | tf_op jit(solution)/shard_map/ppermute | solution.py:26
  160.2 10.2 %stack.31.info_ref = s32[26]{0:T(128)S(1)} concatenate(s32[1]{0:T(128)} %bitcast.8.pair_ref, s32[1]{0:T(128)} %bitcast.9, s32[1]{0:T(128)} %bitcast.10, s32[1]{0:T(128)} %bitcast.11, s32[1]{0:T(128)} %bitcast.12, s32[1]{0:T(128)} %bitcast.13, s32[1]{0:T(128)} %bitcast.14, s32[1]{0:T(128)} %bitcast.15, s32[1]{0:T(128)} %bitcast.16, s32[1]{0:T(128)} %bitcast.17, s32[1]{0:T(128)} %bitcast.18, ...), dimensions={0} | concatenate | bytes 208 | tf_op jit(solution)/shard_map/stack | solution.py:680
  170.4 5.9 collective-permute-done.7.refs_0_
  181.5 6.9 all-gather.11.cloned.1.call-done
  189.6 17.8 %attend.1 = (bf16[2,4,128,512]{3,2,1,0:T(8,128)(2,1)S(1)}, f32[2,2,4,1,256]{4,3,2,1,0:T(1,128)S(1)}) custom-call(s32[26]{0:T(128)S(1)} %stack.31.info_ref, bf16[2,4,128,512]{3,2,1,0:T(8,128)(2,1)S(1)} %bitcast.125, bf16[8,2,4,128,512]{4,3,2,1,0:T(8,128)(2,1)} %bitcast.145), custom_call_target="tpu_custom_call" | custom-call | flops 4294967296 | bytes 8388608 | tf_op jit(solution)/shard_map/attend/pallas_call | solution.py:552
  215.2 19.2 %collective-permute-done.10 = bf16[256,2048]{1,0:T(8,128)(2,1)S(1)} collective-permute-done((bf16[256,2048]{1,0:T(8,128)(2,1)}, bf16[256,2048]{1,0:T(8,128)(2,1)S(1)}, u32[]{:S(2)}, u32[]{:S(2)}) %collective-permute-start.10) | collective-permute-done | bytes 1048608 | tf_op jit(solution)/shard_map/ppermute | solution.py:26
  240.8 8.4 %collective-permute-done.11.refs_3_ = bf16[128,2048]{1,0:T(8,128)(2,1)S(1)} collective-permute-done((bf16[128,2048]{1,0:T(8,128)(2,1)S(1)}, bf16[128,2048]{1,0:T(8,128)(2,1)S(1)}, u32[]{:S(2)}, u32[]{:S(2)}) %collective-permute-start.11) | collective-permute-done | bytes 524320 | tf_op jit(solution)/shard_map/ppermute | solution.py:26
  249.2 2.9 collective-permute-done.13.refs_5_
  256.2 12.0 %collective-permute-done.14.refs_2_ = bf16[128,2048]{1,0:T(8,128)(2,1)S(1)} collective-permute-done((bf16[128,2048]{1,0:T(8,128)(2,1)S(1)}, bf16[128,2048]{1,0:T(8,128)(2,1)S(1)}, u32[]{:S(2)}, u32[]{:S(2)}) %collective-permute-start.14) | collective-permute-done | bytes 524320 | tf_op jit(solution)/shard_map/ppermute | solution.py:26
  270.7 23.6 %collective-permute-done.15.refs_0_ = bf16[256,2048]{1,0:T(8,128)(2,1)S(1)} collective-permute-done((bf16[256,2048]{1,0:T(8,128)(2,1)S(1)}, bf16[256,2048]{1,0:T(8,128)(2,1)S(1)}, u32[]{:S(2)}, u32[]{:S(2)}) %collective-permute-start.15) | collective-permute-done | bytes 1048608 | tf_op jit(solution)/shard_map/ppermute | solution.py:26
  298.3 11.7 %fusion.75 = f32[1024,1536]{1,0:T(8,128)} fusion(bf16[1024,2048]{1,0:T(8,128)(2,1)} %copy-done.7, bf16[2048,1536]{1,0:T(8,128)(2,1)} %all-gather.13.cloned.1.call-done), kind=kOutput, calls=%fused_computation.203 | convolution fusion | flops 6442450944 | bytes 16777216 | tf_op jit(solution)/shard_map/dot_general | solution.py:317
  309.9 8.1 all-gather.15.cloned.1.call-done
  318.0 13.1 %multiply_convert_fusion.2 = (bf16[1024,1536]{1,0:T(8,128)(2,1)S(1)}, f32[1024,1536]{1,0:T(8,128)}) fusion(f32[1024,1536]{1,0:T(8,128)} %fusion.75, bf16[1024,2048]{1,0:T(8,128)(2,1)} %copy-done.7, bf16[2048,1536]{1,0:T(8,128)(2,1)} %all-gather.15.cloned.1.call-done), kind=kOutput, calls=%fused_computation.7 | convolution fusion | flops 6450315264 | bytes 26214400 | tf_op jit(solution)/shard_map/dot_general | solution.py:317
  332.8 8.8 %convolution_convert_fusion.2 = bf16[2048,1536]{1,0:T(8,128)(2,1)} fusion(bf16[1024,2048]{1,0:T(8,128)(2,1)S(1)} %copy-done.5, bf16[1024,1536]{1,0:T(8,128)(2,1)S(1)} %get-tuple-element.72), kind=kOutput, calls=%fused_computation.4 | convolution fusion | flops 6445596672 | bytes 13631488 | tf_op jit(solution)/shard_map/dot_general | solution.py:321
  341.8 41.6 %all-gather.17.cloned.1.call-done = bf16[2048,1536]{1,0:T(8,128)(2,1)} async-done(((bf16[256,1536]{1,0:T(8,128)(2,1)}), bf16[2048,1536]{1,0:T(8,128)(2,1)}) %all-gather.17.cloned.1.call-update) | async-done | bytes 6291472 | tf_op jit(solution)/shard_map/all_gather | solution.py:251
  383.5 14.2 %multiply_convert_fusion = (bf16[1024,1536]{1,0:T(8,128)(2,1)S(1)}, bf16[1024,1536]{1,0:T(8,128)(2,1)S(1)}) fusion(f32[1024,1536]{1,0:T(8,128)} %fusion.75, f32[1024,1536]{1,0:T(8,128)} %get-tuple-element.198, bf16[1024,2048]{1,0:T(8,128)(2,1)} %copy-done.4, bf16[2048,1536]{1,0:T(8,128)(2,1)} %all-gather.17.cloned.1.call-done), kind=kOutput, calls=%fused_computation.5 | convolution fusion | flops 6462898176 | bytes 29360128 | tf_op jit(solution)/shard_map/dot_general | solution.py:317
  397.7 10.0 %fusion.76 = f32[1024,2048]{1,0:T(8,128)S(1)} fusion(bf16[1024,1536]{1,0:T(8,128)(2,1)S(1)} %get-tuple-element.122, bf16[2048,1536]{1,0:T(8,128)(2,1)} %all-gather.13.cloned.1.call-done), kind=kOutput, calls=%fused_computation.204 | convolution fusion | flops 6442450944 | bytes 17825792 | tf_op jit(solution)/shard_map/dot_general | solution.py:325
  407.7 8.9 %add_convert_fusion.1 = bf16[1024,2048]{1,0:T(8,128)(2,1)S(1)} fusion(f32[1024,2048]{1,0:T(8,128)S(1)} %fusion.76, bf16[1024,1536]{1,0:T(8,128)(2,1)S(1)} %get-tuple-element.121, bf16[2048,1536]{1,0:T(8,128)(2,1)} %all-gather.15.cloned.1.call-done), kind=kOutput, calls=%fused_computation.1 | convolution fusion | flops 6446645248 | bytes 22020096 | tf_op jit(solution)/shard_map/dot_general | solution.py:325
  423.3 8.8 %convolution_convert_fusion = bf16[2048,1536]{1,0:T(8,128)(2,1)} fusion(bf16[1024,2048]{1,0:T(8,128)(2,1)S(1)} %copy-done.8, bf16[1024,1536]{1,0:T(8,128)(2,1)S(1)} %get-tuple-element.121), kind=kOutput, calls=%fused_computation.2 | convolution fusion | flops 6445596672 | bytes 13631488 | tf_op jit(solution)/shard_map/dot_general | solution.py:321
  432.1 11.8 %convolution_convert_fusion.1 = bf16[2048,1536]{1,0:T(8,128)(2,1)} fusion(bf16[1024,2048]{1,0:T(8,128)(2,1)} %copy-done.7, bf16[1024,1536]{1,0:T(8,128)(2,1)} %copy-done.44), kind=kOutput, calls=%fused_computation.3 | convolution fusion | flops 6445596672 | bytes 13631488 | tf_op jit(solution)/shard_map/dot_general | solution.py:321
  450.2 2.9 add_convert_fusion.10
  457.3 9.1 %collective-permute-done.21.refs_6_ = bf16[128,2048]{1,0:T(8,128)(2,1)S(1)} collective-permute-done((bf16[128,2048]{1,0:T(8,128)(2,1)}, bf16[128,2048]{1,0:T(8,128)(2,1)S(1)}, u32[]{:S(2)}, u32[]{:S(2)}) %collective-permute-start.21) | collective-permute-done | bytes 524320 | tf_op jit(solution)/shard_map/ppermute | solution.py:26
  470.9 3.7 middle_back.1
  476.8 8.9 %collective-permute-done.22.refs_2_ = bf16[128,2048]{1,0:T(8,128)(2,1)S(1)} collective-permute-done((bf16[128,2048]{1,0:T(8,128)(2,1)S(1)}, bf16[128,2048]{1,0:T(8,128)(2,1)S(1)}, u32[]{:S(2)}, u32[]{:S(2)}) %collective-permute-start.22) | collective-permute-done | bytes 524320 | tf_op jit(solution)/shard_map/ppermute | solution.py:26
  486.1 2.8 collective-permute-done.24
  489.2 11.1 %convolution_convert_fusion.3 = bf16[1024,2048]{1,0:T(8,128)(2,1)} fusion(bf16[1024,1536]{1,0:T(8,128)(2,1)S(1)} %copy-done.46, bf16[2048,1536]{1,0:T(8,128)(2,1)} %all-gather.17.cloned.1.call-done), kind=kOutput, calls=%fused_computation.10 | convolution fusion | flops 6444548096 | bytes 13631488 | tf_op jit(solution)/shard_map/dot_general | solution.py:325
  500.3 8.8 %collective-permute-done.23.refs_0_ = bf16[256,2048]{1,0:T(8,128)(2,1)S(1)} collective-permute-done((bf16[256,2048]{1,0:T(8,128)(2,1)S(1)}, bf16[256,2048]{1,0:T(8,128)(2,1)S(1)}, u32[]{:S(2)}, u32[]{:S(2)}) %collective-permute-start.23) | collective-permute-done | bytes 1048608 | tf_op jit(solution)/shard_map/ppermute | solution.py:26
  511.4 3.3 convolution_convert_fusion.7
  514.7 10.0 %reduce-scatter.9.cloned.1.call-done.both_ref = bf16[256,1536]{1,0:T(8,128)(2,1)} async-done(((bf16[2048,1536]{1,0:T(8,128)(2,1)}), bf16[256,1536]{1,0:T(8,128)(2,1)}) %reduce-scatter.9.cloned.1.call-update) | async-done | bytes 786448 | tf_op jit(solution)/shard_map/reduce_scatter | solution.py:256
  532.4 25.1 %attend_back.1 = (f32[2,4,128,512]{3,2,1,0:T(8,128)}, bf16[8,2,4,128,512]{4,3,2,1,0:T(8,128)(2,1)}) custom-call(s32[26]{0:T(128)} %copy-done.18, bf16[2,4,128,512]{3,2,1,0:T(8,128)(2,1)} %bitcast.124, bf16[2,4,128,512]{3,2,1,0:T(8,128)(2,1)} %bitcast.148, bf16[2,4,128,512]{3,2,1,0:T(8,128)(2,1)} %copy-done.20, f32[2,2,4,1,256]{4,3,2,1,0:T(1,128)} %copy-done.22, ...), custom_call_target="tpu_custom_call" | custom-call | flops 10737418240 | bytes 16777216 | tf_op jit(solution)/shard_map/attend_back/pallas_call | solution.py:575
  557.5 5.8 head_prep_back.2
  571.5 5.6 fusion.2
  578.9 3.8 collective-permute-done.29.refs_4_
  584.2 7.2 collective-permute-done.30.other_ref
  591.3 2.5 own_rows.5
  593.8 5.9 collective-permute-done.31.other_ref
  599.7 2.5 own_rows.6
  603.5 5.9 convolution_convert_fusion.6
  609.3 98.0 %reduce-scatter.13.cloned.1.call-done.d_ref = bf16[1024,512]{1,0:T(8,128)(2,1)} async-done(((bf16[8192,512]{1,0:T(8,128)(2,1)}), bf16[1024,512]{1,0:T(8,128)(2,1)}) %reduce-scatter.13.cloned.1.call-update) | async-done | bytes 1048592 | tf_op jit(solution)/shard_map/reduce_scatter | solution.py:256
  707.4 4.9 head_prep_back.3
  712.3 9.1 %add_convert_fusion = bf16[1024,2048]{1,0:T(8,128)(2,1)} fusion(f32[1024,2048]{1,0:T(8,128)} %fusion.2, bf16[1024,512]{1,0:T(8,128)(2,1)} %get-tuple-element.83, bf16[2048,1024]{1,0:T(8,128)(2,1)} %all-gather.7.cloned.1.call-done), kind=kOutput, calls=%fused_computation | convolution fusion | flops 2151677952 | bytes 15728640 | tf_op jit(solution)/shard_map/dot_general | solution.py:325
  721.5 6.3 convolution_convert_fusion.5
  732.6 19.8 %collective-permute-done.32 = bf16[256,2048]{1,0:T(8,128)(2,1)S(1)} collective-permute-done((bf16[256,2048]{1,0:T(8,128)(2,1)S(1)}, bf16[256,2048]{1,0:T(8,128)(2,1)S(1)}, u32[]{:S(2)}, u32[]{:S(2)}) %collective-permute-start.32) | collective-permute-done | bytes 1048608 | tf_op jit(solution)/shard_map/ppermute | solution.py:26
  756.5 8.4 %collective-permute-done.33.refs_4_ = bf16[128,2048]{1,0:T(8,128)(2,1)S(1)} collective-permute-done((bf16[128,2048]{1,0:T(8,128)(2,1)S(1)}, bf16[128,2048]{1,0:T(8,128)(2,1)S(1)}, u32[]{:S(2)}, u32[]{:S(2)}) %collective-permute-start.33) | collective-permute-done | bytes 524320 | tf_op jit(solution)/shard_map/ppermute | solution.py:26
  765.4 5.0 entry_back.1
  775.5 4.8 collective-permute-start.41
  780.4 2.5 collective-permute-done.41
  782.9 3.0 collective-permute-start.42
  785.9 2.5 collective-permute-done.42
  802.0 11.4 %collective-permute-done.37.other_ref = bf16[128,512]{1,0:T(8,128)(2,1)S(1)} collective-permute-done((bf16[128,512]{1,0:T(8,128)(2,1)S(1)}, bf16[128,512]{1,0:T(8,128)(2,1)S(1)}, u32[]{:S(2)}, u32[]{:S(2)}) %collective-permute-start.37) | collective-permute-done | bytes 131104 | tf_op jit(solution)/shard_map/ppermute | solution.py:26
  (281 shorter events, 165.0 us)
Async XLA Ops:
  7.2 19.0 %copy-start.34 = (f32[2048]{0:T(1024)S(1)}, f32[2048]{0:T(1024)}, u32[]{:S(2)}) copy-start(f32[2048]{0:T(1024)} %param.24) | copy-start | bytes 24580
  7.2 19.0 %copy-start.13 = (bf16[1,1,2,128,2048]{4,3,2,1,0:T(8,128)(2,1)S(1)}, bf16[1,1,2,128,2048]{4,3,2,1,0:T(8,128)(2,1)}, u32[]{:S(2)}) copy-start(bf16[1,1,2,128,2048]{4,3,2,1,0:T(8,128)(2,1)} %param.14) | copy-start | bytes 3145732
  7.2 69.7 %all-gather.7.cloned.1.call-start = ((), (), s32[]{:S(2)}) async-start(), calls=%async_computation.6 | async-start | bytes 4718592 | tf_op jit(solution)/shard_map/all_gather | solution.py:251
  12.8 12.2 %collective-permute-start.4 = (bf16[128,1536]{1,0:T(8,128)(2,1)S(1)}, bf16[128,1536]{1,0:T(8,128)(2,1)S(1)}, u32[]{:S(2)}, u32[]{:S(2)}) collective-permute-start(bf16[128,1536]{1,0:T(8,128)(2,1)S(1)} %pad_maximum_fusion.18), channel_id=1, source_target_pairs={{0,4},{2,6},{4,0},{6,2},{8,12},{10,14},{12,8},{14,10},{16,20},{18,... | collective-permute-start | bytes 1179656 | tf_op jit(solution)/shard_map/ppermute | solution.py:26
  26.1 78.7 %all-gather.9.cloned.1.call-start = ((), (), s32[]{:S(2)}) async-start(), calls=%async_computation.7 | async-start | bytes 2359296 | tf_op jit(solution)/shard_map/all_gather | solution.py:251
  30.2 107.5 %copy-start = (bf16[256,2048]{1,0:T(8,128)(2,1)}, bf16[256,2048]{1,0:T(8,128)(2,1)S(1)}, u32[]{:S(2)}) copy-start(bf16[256,2048]{1,0:T(8,128)(2,1)S(1)} %get-tuple-element.62.refs_0_) | copy-start | bytes 3145732
  32.0 156.4 %all-gather.11.cloned.1.call-start = ((), (), s32[]{:S(2)}) async-start(), calls=%async_computation.8 | async-start | bytes 9437184 | tf_op jit(solution)/shard_map/all_gather | solution.py:251
  34.1 15.2 %collective-permute-start = (bf16[128,2048]{1,0:T(8,128)(2,1)S(1)}, bf16[128,2048]{1,0:T(8,128)(2,1)S(1)}, u32[]{:S(2)}, u32[]{:S(2)}) collective-permute-start(bf16[128,2048]{1,0:T(8,128)(2,1)S(1)} %get-tuple-element.159.refs_1_), channel_id=1, source_target_pairs={{0,1},{1,0},{2,3},{3,2},{4,5},{5,4},{6,7},{7,6},{8,9},{9,8},{10,11... | collective-permute-start | bytes 1572872 | tf_op jit(solution)/shard_map/ppermute | solution.py:26
  35.9 14.2 %collective-permute-start.2 = (bf16[128,2048]{1,0:T(8,128)(2,1)}, bf16[128,2048]{1,0:T(8,128)(2,1)}, u32[]{:S(2)}, u32[]{:S(2)}) collective-permute-start(bf16[128,2048]{1,0:T(8,128)(2,1)} %get-tuple-element.158), channel_id=1, source_target_pairs={{0,4},{2,6},{4,0},{6,2},{8,12},{10,14},{12,8},{14,10},{16,20},{18,... | collective-permute-start | bytes 1572872 | tf_op jit(solution)/shard_map/ppermute | solution.py:26
  49.5 23.6 %collective-permute-start.1 = (bf16[256,2048]{1,0:T(8,128)(2,1)S(1)}, bf16[256,2048]{1,0:T(8,128)(2,1)S(1)}, u32[]{:S(2)}, u32[]{:S(2)}) collective-permute-start(bf16[256,2048]{1,0:T(8,128)(2,1)S(1)} %pad_maximum_fusion.3), channel_id=1, source_target_pairs={{0,4},{2,6},{4,0},{6,2},{8,12},{10,14},{12,8},{14,10},{16,20},{18,... | collective-permute-start | bytes 3145736 | tf_op jit(solution)/shard_map/ppermute | solution.py:26
  51.3 23.3 %collective-permute-start.3 = (bf16[256,2048]{1,0:T(8,128)(2,1)S(1)}, bf16[256,2048]{1,0:T(8,128)(2,1)S(1)}, u32[]{:S(2)}, u32[]{:S(2)}) collective-permute-start(bf16[256,2048]{1,0:T(8,128)(2,1)S(1)} %pad_maximum_fusion.4.refs_3_), channel_id=1, source_target_pairs={{0,1},{1,0},{2,3},{3,2},{4,5},{5,4},{6,7},{7,6},{8,9},{9,8},{10,11... | collective-permute-start | bytes 3145736 | tf_op jit(solution)/shard_map/ppermute | solution.py:26
  104.8 193.5 %all-gather.13.cloned.1.call-start = ((), (), s32[]{:S(2)}) async-start(), calls=%async_computation.9 | async-start | bytes 7077888 | tf_op jit(solution)/shard_map/all_gather | solution.py:251
  106.5 28.2 %collective-permute-start.5 = (bf16[128,4608]{1,0:T(8,128)(2,1)S(1)}, bf16[128,4608]{1,0:T(8,128)(2,1)S(1)}, u32[]{:S(2)}, u32[]{:S(2)}) collective-permute-start(bf16[128,4608]{1,0:T(8,128)(2,1)S(1)} %pad_maximum_fusion.2), channel_id=1, source_target_pairs={{0,4},{2,6},{4,0},{6,2},{8,12},{10,14},{12,8},{14,10},{16,20},{18,... | collective-permute-start | bytes 3538952 | tf_op jit(solution)/shard_map/ppermute | solution.py:26
  136.7 181.3 %all-gather.15.cloned.1.call-start = ((), (), s32[]{:S(2)}) async-start(), calls=%async_computation.10 | async-start | bytes 7077888 | tf_op jit(solution)/shard_map/all_gather | solution.py:251
  137.3 246.2 %all-gather.17.cloned.1.call-start = ((), (), s32[]{:S(2)}) async-start(), calls=%async_computation.11 | async-start | bytes 7077888 | tf_op jit(solution)/shard_map/all_gather | solution.py:251
  137.9 13.4 %collective-permute-start.6 = (bf16[128,2048]{1,0:T(8,128)(2,1)S(1)}, bf16[128,2048]{1,0:T(8,128)(2,1)S(1)}, u32[]{:S(2)}, u32[]{:S(2)}) collective-permute-start(bf16[128,2048]{1,0:T(8,128)(2,1)S(1)} %get-tuple-element.157.refs_1_), channel_id=1, source_target_pairs={{0,1},{1,0},{2,3},{3,2},{4,5},{5,4},{6,7},{7,6},{8,9},{9,8},{10,11... | collective-permute-start | bytes 1572872 | tf_op jit(solution)/shard_map/ppermute | solution.py:26
  139.4 14.4 %collective-permute-start.8 = (bf16[128,2048]{1,0:T(8,128)(2,1)S(1)}, bf16[128,2048]{1,0:T(8,128)(2,1)S(1)}, u32[]{:S(2)}, u32[]{:S(2)}) collective-permute-start(bf16[128,2048]{1,0:T(8,128)(2,1)S(1)} %get-tuple-element.156), channel_id=1, source_target_pairs={{0,4},{2,6},{4,0},{6,2},{8,12},{10,14},{12,8},{14,10},{16,20},{18,... | collective-permute-start | bytes 1572872 | tf_op jit(solution)/shard_map/ppermute | solution.py:26
  152.3 24.1 %collective-permute-start.7 = (bf16[256,2048]{1,0:T(8,128)(2,1)}, bf16[256,2048]{1,0:T(8,128)(2,1)}, u32[]{:S(2)}, u32[]{:S(2)}) collective-permute-start(bf16[256,2048]{1,0:T(8,128)(2,1)} %pad_maximum_fusion.5), channel_id=1, source_target_pairs={{0,4},{2,6},{4,0},{6,2},{8,12},{10,14},{12,8},{14,10},{16,20},{18,... | collective-permute-start | bytes 3145736 | tf_op jit(solution)/shard_map/ppermute | solution.py:26
  153.8 23.7 %collective-permute-start.9 = (bf16[256,2048]{1,0:T(8,128)(2,1)S(1)}, bf16[256,2048]{1,0:T(8,128)(2,1)}, u32[]{:S(2)}, u32[]{:S(2)}) collective-permute-start(bf16[256,2048]{1,0:T(8,128)(2,1)S(1)} %pad_maximum_fusion.6.refs_3_), channel_id=1, source_target_pairs={{0,1},{1,0},{2,3},{3,2},{4,5},{5,4},{6,7},{7,6},{8,9},{9,8},{10,11... | collective-permute-start | bytes 3145736 | tf_op jit(solution)/shard_map/ppermute | solution.py:26
  170.4 18.0 %copy-start.18 = (s32[26]{0:T(128)}, s32[26]{0:T(128)S(1)}, u32[]{:S(2)}) copy-start(s32[26]{0:T(128)S(1)} %stack.31.info_ref) | copy-start | bytes 316
  211.1 23.2 %collective-permute-start.10 = (bf16[256,2048]{1,0:T(8,128)(2,1)}, bf16[256,2048]{1,0:T(8,128)(2,1)S(1)}, u32[]{:S(2)}, u32[]{:S(2)}) collective-permute-start(bf16[256,2048]{1,0:T(8,128)(2,1)} %pad_maximum_fusion.7), channel_id=1, source_target_pairs={{0,4},{2,6},{4,0},{6,2},{8,12},{10,14},{12,8},{14,10},{16,20},{18,... | collective-permute-start | bytes 3145736 | tf_op jit(solution)/shard_map/ppermute | solution.py:26
  213.6 23.8 %collective-permute-start.12 = (bf16[256,2048]{1,0:T(8,128)(2,1)}, bf16[256,2048]{1,0:T(8,128)(2,1)S(1)}, u32[]{:S(2)}, u32[]{:S(2)}) collective-permute-start(bf16[256,2048]{1,0:T(8,128)(2,1)} %slice.329), channel_id=1, source_target_pairs={{0,1},{1,0},{2,3},{3,2},{4,5},{5,4},{6,7},{7,6},{8,9},{9,8},{10,11... | collective-permute-start | bytes 3145736 | tf_op jit(solution)/shard_map/ppermute | solution.py:26
  215.2 25.6 %copy-start.35 = (f32[2048]{0:T(1024)S(1)}, f32[2048]{0:T(1024)}, u32[]{:S(2)}) copy-start(f32[2048]{0:T(1024)} %param.25) | copy-start | bytes 24580
  215.2 239.0 %reduce-scatter.7.cloned.1.call-start = ((), (), s32[]{:S(2)}) async-start(), calls=%async_computation.12 | async-start | bytes 7077888 | tf_op jit(solution)/shard_map/reduce_scatter | solution.py:256
  236.0 13.2 %collective-permute-start.11 = (bf16[128,2048]{1,0:T(8,128)(2,1)S(1)}, bf16[128,2048]{1,0:T(8,128)(2,1)S(1)}, u32[]{:S(2)}, u32[]{:S(2)}) collective-permute-start(bf16[128,2048]{1,0:T(8,128)(2,1)S(1)} %get-tuple-element.129), channel_id=1, source_target_pairs={{0,1},{1,0},{2,3},{3,2},{4,5},{5,4},{6,7},{7,6},{8,9},{9,8},{10,11... | collective-permute-start | bytes 1572872 | tf_op jit(solution)/shard_map/ppermute | solution.py:26
  239.2 12.9 %collective-permute-start.13 = (bf16[128,2048]{1,0:T(8,128)(2,1)S(1)}, bf16[128,2048]{1,0:T(8,128)(2,1)S(1)}, u32[]{:S(2)}, u32[]{:S(2)}) collective-permute-start(bf16[128,2048]{1,0:T(8,128)(2,1)S(1)} %get-tuple-element.154), channel_id=1, source_target_pairs={{0,4},{2,6},{4,0},{6,2},{8,12},{10,14},{12,8},{14,10},{16,20},{18,... | collective-permute-start | bytes 1572872 | tf_op jit(solution)/shard_map/ppermute | solution.py:26
  254.2 14.0 %collective-permute-start.14 = (bf16[128,2048]{1,0:T(8,128)(2,1)S(1)}, bf16[128,2048]{1,0:T(8,128)(2,1)S(1)}, u32[]{:S(2)}, u32[]{:S(2)}) collective-permute-start(bf16[128,2048]{1,0:T(8,128)(2,1)S(1)} %get-tuple-element.153.refs_1_), channel_id=1, source_target_pairs={{0,1},{1,0},{2,3},{3,2},{4,5},{5,4},{6,7},{7,6},{8,9},{9,8},{10,11... | collective-permute-start | bytes 1572872 | tf_op jit(solution)/shard_map/ppermute | solution.py:26
  255.1 14.8 %collective-permute-start.16 = (bf16[128,2048]{1,0:T(8,128)(2,1)S(1)}, bf16[128,2048]{1,0:T(8,128)(2,1)S(1)}, u32[]{:S(2)}, u32[]{:S(2)}) collective-permute-start(bf16[128,2048]{1,0:T(8,128)(2,1)S(1)} %get-tuple-element.152), channel_id=1, source_target_pairs={{0,4},{2,6},{4,0},{6,2},{8,12},{10,14},{12,8},{14,10},{16,20},{18,... | collective-permute-start | bytes 1572872 | tf_op jit(solution)/shard_map/ppermute | solution.py:26
  268.3 26.0 %collective-permute-start.15 = (bf16[256,2048]{1,0:T(8,128)(2,1)S(1)}, bf16[256,2048]{1,0:T(8,128)(2,1)S(1)}, u32[]{:S(2)}, u32[]{:S(2)}) collective-permute-start(bf16[256,2048]{1,0:T(8,128)(2,1)S(1)} %pad_maximum_fusion.8), channel_id=1, source_target_pairs={{0,4},{2,6},{4,0},{6,2},{8,12},{10,14},{12,8},{14,10},{16,20},{18,... | collective-permute-start | bytes 3145736 | tf_op jit(solution)/shard_map/ppermute | solution.py:26
  270.0 25.9 %collective-permute-start.17 = (bf16[256,2048]{1,0:T(8,128)(2,1)S(1)}, bf16[256,2048]{1,0:T(8,128)(2,1)S(1)}, u32[]{:S(2)}, u32[]{:S(2)}) collective-permute-start(bf16[256,2048]{1,0:T(8,128)(2,1)S(1)} %pad_maximum_fusion.9.refs_3_), channel_id=1, source_target_pairs={{0,1},{1,0},{2,3},{3,2},{4,5},{5,4},{6,7},{7,6},{8,9},{9,8},{10,11... | collective-permute-start | bytes 3145736 | tf_op jit(solution)/shard_map/ppermute | solution.py:26
  341.6 183.1 %reduce-scatter.9.cloned.1.call-start = ((), (), s32[]{:S(2)}) async-start(), calls=%async_computation.13 | async-start | bytes 7077888 | tf_op jit(solution)/shard_map/reduce_scatter | solution.py:256
  420.4 25.6 %collective-permute-start.18 = (bf16[256,2048]{1,0:T(8,128)(2,1)}, bf16[256,2048]{1,0:T(8,128)(2,1)}, u32[]{:S(2)}, u32[]{:S(2)}) collective-permute-start(bf16[256,2048]{1,0:T(8,128)(2,1)} %pad_maximum_fusion.10), channel_id=1, source_target_pairs={{0,4},{2,6},{4,0},{6,2},{8,12},{10,14},{12,8},{14,10},{16,20},{18,... | collective-permute-start | bytes 3145736 | tf_op jit(solution)/shard_map/ppermute | solution.py:26
  421.8 25.3 %collective-permute-start.20 = (bf16[256,2048]{1,0:T(8,128)(2,1)}, bf16[256,2048]{1,0:T(8,128)(2,1)}, u32[]{:S(2)}, u32[]{:S(2)}) collective-permute-start(bf16[256,2048]{1,0:T(8,128)(2,1)} %slice.337), channel_id=1, source_target_pairs={{0,1},{1,0},{2,3},{3,2},{4,5},{5,4},{6,7},{7,6},{8,9},{9,8},{10,11... | collective-permute-start | bytes 3145736 | tf_op jit(solution)/shard_map/ppermute | solution.py:26
  454.2 148.0 %reduce-scatter.11.cloned.1.call-start = ((), (), s32[]{:S(2)}) async-start(), calls=%async_computation.14 | async-start | bytes 7077888 | tf_op jit(solution)/shard_map/reduce_scatter | solution.py:256
  454.3 12.1 %collective-permute-start.21 = (bf16[128,2048]{1,0:T(8,128)(2,1)}, bf16[128,2048]{1,0:T(8,128)(2,1)S(1)}, u32[]{:S(2)}, u32[]{:S(2)}) collective-permute-start(bf16[128,2048]{1,0:T(8,128)(2,1)} %get-tuple-element.150), channel_id=1, source_target_pairs={{0,4},{2,6},{4,0},{6,2},{8,12},{10,14},{12,8},{14,10},{16,20},{18,... | collective-permute-start | bytes 1572872 | tf_op jit(solution)/shard_map/ppermute | solution.py:26
  455.8 11.7 %collective-permute-start.19 = (bf16[128,2048]{1,0:T(8,128)(2,1)}, bf16[128,2048]{1,0:T(8,128)(2,1)S(1)}, u32[]{:S(2)}, u32[]{:S(2)}) collective-permute-start(bf16[128,2048]{1,0:T(8,128)(2,1)} %get-tuple-element.127), channel_id=1, source_target_pairs={{0,1},{1,0},{2,3},{3,2},{4,5},{5,4},{6,7},{7,6},{8,9},{9,8},{10,11... | collective-permute-start | bytes 1572872 | tf_op jit(solution)/shard_map/ppermute | solution.py:26
  474.7 11.0 %collective-permute-start.22 = (bf16[128,2048]{1,0:T(8,128)(2,1)S(1)}, bf16[128,2048]{1,0:T(8,128)(2,1)S(1)}, u32[]{:S(2)}, u32[]{:S(2)}) collective-permute-start(bf16[128,2048]{1,0:T(8,128)(2,1)S(1)} %get-tuple-element.149.refs_1_), channel_id=1, source_target_pairs={{0,1},{1,0},{2,3},{3,2},{4,5},{5,4},{6,7},{7,6},{8,9},{9,8},{10,11... | collective-permute-start | bytes 1572872 | tf_op jit(solution)/shard_map/ppermute | solution.py:26
  476.2 12.7 %collective-permute-start.24 = (bf16[128,2048]{1,0:T(8,128)(2,1)S(1)}, bf16[128,2048]{1,0:T(8,128)(2,1)S(1)}, u32[]{:S(2)}, u32[]{:S(2)}) collective-permute-start(bf16[128,2048]{1,0:T(8,128)(2,1)S(1)} %get-tuple-element.148), channel_id=1, source_target_pairs={{0,4},{2,6},{4,0},{6,2},{8,12},{10,14},{12,8},{14,10},{16,20},{18,... | collective-permute-start | bytes 1572872 | tf_op jit(solution)/shard_map/ppermute | solution.py:26
  485.8 23.3 %collective-permute-start.23 = (bf16[256,2048]{1,0:T(8,128)(2,1)S(1)}, bf16[256,2048]{1,0:T(8,128)(2,1)S(1)}, u32[]{:S(2)}, u32[]{:S(2)}) collective-permute-start(bf16[256,2048]{1,0:T(8,128)(2,1)S(1)} %pad_maximum_fusion.11), channel_id=1, source_target_pairs={{0,4},{2,6},{4,0},{6,2},{8,12},{10,14},{12,8},{14,10},{16,20},{18,... | collective-permute-start | bytes 3145736 | tf_op jit(solution)/shard_map/ppermute | solution.py:26
  489.1 20.0 %collective-permute-start.25 = (bf16[256,2048]{1,0:T(8,128)(2,1)S(1)}, bf16[256,2048]{1,0:T(8,128)(2,1)S(1)}, u32[]{:S(2)}, u32[]{:S(2)}) collective-permute-start(bf16[256,2048]{1,0:T(8,128)(2,1)S(1)} %pad_maximum_fusion.12.refs_3_), channel_id=1, source_target_pairs={{0,1},{1,0},{2,3},{3,2},{4,5},{5,4},{6,7},{7,6},{8,9},{9,8},{10,11... | collective-permute-start | bytes 3145736 | tf_op jit(solution)/shard_map/ppermute | solution.py:26
  524.7 182.6 %reduce-scatter.13.cloned.1.call-start = ((), (), s32[]{:S(2)}) async-start(), calls=%async_computation.15 | async-start | bytes 9437184 | tf_op jit(solution)/shard_map/reduce_scatter | solution.py:256
  527.2 36.1 %collective-permute-start.26 = (bf16[256,2048]{1,0:T(8,128)(2,1)}, bf16[256,2048]{1,0:T(8,128)(2,1)}, u32[]{:S(2)}, u32[]{:S(2)}) collective-permute-start(bf16[256,2048]{1,0:T(8,128)(2,1)} %pad_maximum_fusion.13), channel_id=1, source_target_pairs={{0,4},{2,6},{4,0},{6,2},{8,12},{10,14},{12,8},{14,10},{16,20},{18,... | collective-permute-start | bytes 3145736 | tf_op jit(solution)/shard_map/ppermute | solution.py:26
  531.0 35.1 %collective-permute-start.28 = (bf16[256,2048]{1,0:T(8,128)(2,1)}, bf16[256,2048]{1,0:T(8,128)(2,1)}, u32[]{:S(2)}, u32[]{:S(2)}) collective-permute-start(bf16[256,2048]{1,0:T(8,128)(2,1)} %slice.285), channel_id=1, source_target_pairs={{0,1},{1,0},{2,3},{3,2},{4,5},{5,4},{6,7},{7,6},{8,9},{9,8},{10,11... | collective-permute-start | bytes 3145736 | tf_op jit(solution)/shard_map/ppermute | solution.py:26
  565.4 13.5 %collective-permute-start.27 = (bf16[128,2048]{1,0:T(8,128)(2,1)S(1)}, bf16[128,2048]{1,0:T(8,128)(2,1)S(1)}, u32[]{:S(2)}, u32[]{:S(2)}) collective-permute-start(bf16[128,2048]{1,0:T(8,128)(2,1)S(1)} %get-tuple-element.125), channel_id=1, source_target_pairs={{0,1},{1,0},{2,3},{3,2},{4,5},{5,4},{6,7},{7,6},{8,9},{9,8},{10,11... | collective-permute-start | bytes 1572872 | tf_op jit(solution)/shard_map/ppermute | solution.py:26
  568.5 14.3 %collective-permute-start.29 = (bf16[128,2048]{1,0:T(8,128)(2,1)S(1)}, bf16[128,2048]{1,0:T(8,128)(2,1)S(1)}, u32[]{:S(2)}, u32[]{:S(2)}) collective-permute-start(bf16[128,2048]{1,0:T(8,128)(2,1)S(1)} %get-tuple-element.146), channel_id=1, source_target_pairs={{0,4},{2,6},{4,0},{6,2},{8,12},{10,14},{12,8},{14,10},{16,20},{18,... | collective-permute-start | bytes 1572872 | tf_op jit(solution)/shard_map/ppermute | solution.py:26
  569.3 22.0 %collective-permute-start.30 = (bf16[128,1536]{1,0:T(8,128)(2,1)S(1)}, bf16[128,1536]{1,0:T(8,128)(2,1)}, u32[]{:S(2)}, u32[]{:S(2)}) collective-permute-start(bf16[128,1536]{1,0:T(8,128)(2,1)S(1)} %constant_dynamic-slice_fusion.3), channel_id=1, source_target_pairs={{0,4},{2,6},{4,0},{6,2},{8,12},{10,14},{12,8},{14,10},{16,20},{18,... | collective-permute-start | bytes 1179656 | tf_op jit(solution)/shard_map/ppermute | solution.py:26
  570.7 29.1 %collective-permute-start.31 = (bf16[128,1536]{1,0:T(8,128)(2,1)S(1)}, bf16[128,1536]{1,0:T(8,128)(2,1)}, u32[]{:S(2)}, u32[]{:S(2)}) collective-permute-start(bf16[128,1536]{1,0:T(8,128)(2,1)S(1)} %constant_dynamic-slice_fusion.2), channel_id=1, source_target_pairs={{0,4},{2,6},{4,0},{6,2},{8,12},{10,14},{12,8},{14,10},{16,20},{18,... | collective-permute-start | bytes 1179656 | tf_op jit(solution)/shard_map/ppermute | solution.py:26
  602.3 191.2 %reduce-scatter.15.cloned.1.call-start = ((), (), s32[]{:S(2)}) async-start(), calls=%async_computation.16 | async-start | bytes 2359296 | tf_op jit(solution)/shard_map/reduce_scatter | solution.py:256
  707.3 88.5 %reduce-scatter.17.cloned.1.call-start = ((), (), s32[]{:S(2)}) async-start(), calls=%async_computation.17 | async-start | bytes 4718592 | tf_op jit(solution)/shard_map/reduce_scatter | solution.py:256
  729.3 23.1 %collective-permute-start.32 = (bf16[256,2048]{1,0:T(8,128)(2,1)S(1)}, bf16[256,2048]{1,0:T(8,128)(2,1)S(1)}, u32[]{:S(2)}, u32[]{:S(2)}) collective-permute-start(bf16[256,2048]{1,0:T(8,128)(2,1)S(1)} %pad_maximum_fusion.14), channel_id=1, source_target_pairs={{0,4},{2,6},{4,0},{6,2},{8,12},{10,14},{12,8},{14,10},{16,20},{18,... | collective-permute-start | bytes 3145736 | tf_op jit(solution)/shard_map/ppermute | solution.py:26
  731.0 34.4 %copy-start.10 = (f32[256,2048]{1,0:T(8,128)S(1)}, f32[256,2048]{1,0:T(8,128)}, u32[]{:S(2)}) copy-start(f32[256,2048]{1,0:T(8,128)} %copy-done.9) | copy-start | bytes 6291460
  731.0 34.4 %copy-start.17 = (f32[1,4,2,2,128]{4,3,2,1,0:T(2,128)S(1)}, f32[1,4,2,2,128]{4,3,2,1,0:T(2,128)}, u32[]{:S(2)}) copy-start(f32[1,4,2,2,128]{4,3,2,1,0:T(2,128)} %copy-done.16) | copy-start | bytes 24580
  731.0 23.9 %collective-permute-start.34 = (bf16[256,2048]{1,0:T(8,128)(2,1)S(1)}, bf16[256,2048]{1,0:T(8,128)(2,1)S(1)}, u32[]{:S(2)}, u32[]{:S(2)}) collective-permute-start(bf16[256,2048]{1,0:T(8,128)(2,1)S(1)} %slice.353), channel_id=1, source_target_pairs={{0,1},{1,0},{2,3},{3,2},{4,5},{5,4},{6,7},{7,6},{8,9},{9,8},{10,11... | collective-permute-start | bytes 3145736 | tf_op jit(solution)/shard_map/ppermute | solution.py:26
  752.8 12.1 %collective-permute-start.33 = (bf16[128,2048]{1,0:T(8,128)(2,1)S(1)}, bf16[128,2048]{1,0:T(8,128)(2,1)S(1)}, u32[]{:S(2)}, u32[]{:S(2)}) collective-permute-start(bf16[128,2048]{1,0:T(8,128)(2,1)S(1)} %get-tuple-element.123), channel_id=1, source_target_pairs={{0,1},{1,0},{2,3},{3,2},{4,5},{5,4},{6,7},{7,6},{8,9},{9,8},{10,11... | collective-permute-start | bytes 1572872 | tf_op jit(solution)/shard_map/ppermute | solution.py:26
  755.3 40.5 %copy-start.27 = (bf16[256,1536]{1,0:T(8,128)(2,1)S(1)}, bf16[256,1536]{1,0:T(8,128)(2,1)}, u32[]{:S(2)}) copy-start(bf16[256,1536]{1,0:T(8,128)(2,1)} %reduce-scatter.11.cloned.1.call-done.both_ref) | copy-start | bytes 2359300
  755.4 10.0 %collective-permute-start.35 = (bf16[128,2048]{1,0:T(8,128)(2,1)S(1)}, bf16[128,2048]{1,0:T(8,128)(2,1)S(1)}, u32[]{:S(2)}, u32[]{:S(2)}) collective-permute-start(bf16[128,2048]{1,0:T(8,128)(2,1)S(1)} %get-tuple-element.144), channel_id=1, source_target_pairs={{0,4},{2,6},{4,0},{6,2},{8,12},{10,14},{12,8},{14,10},{16,20},{18,... | collective-permute-start | bytes 1572872 | tf_op jit(solution)/shard_map/ppermute | solution.py:26
  770.4 1.3 collective-permute-start.39
  771.7 3.8 collective-permute-start.40
  775.5 7.4 collective-permute-start.41
  782.9 5.5 collective-permute-start.42
  788.4 3.8 collective-permute-start.43
  795.9 22.8 %collective-permute-start.38 = (bf16[128,1536]{1,0:T(8,128)(2,1)S(1)}, bf16[128,1536]{1,0:T(8,128)(2,1)S(1)}, u32[]{:S(2)}, u32[]{:S(2)}) collective-permute-start(bf16[128,1536]{1,0:T(8,128)(2,1)S(1)} %constant_dynamic-slice_fusion.17), channel_id=1, source_target_pairs={{0,4},{2,6},{4,0},{6,2},{8,12},{10,14},{12,8},{14,10},{16,20},{18,... | collective-permute-start | bytes 1179656 | tf_op jit(solution)/shard_map/ppermute | solution.py:26
  798.4 17.4 %collective-permute-start.36 = (bf16[128,1024]{1,0:T(8,128)(2,1)S(1)}, bf16[128,1024]{1,0:T(8,128)(2,1)S(1)}, u32[]{:S(2)}, u32[]{:S(2)}) collective-permute-start(bf16[128,1024]{1,0:T(8,128)(2,1)S(1)} %constant_dynamic-slice_fusion.1), channel_id=1, source_target_pairs={{0,4},{2,6},{4,0},{6,2},{8,12},{10,14},{12,8},{14,10},{16,20},{18,... | collective-permute-start | bytes 786440 | tf_op jit(solution)/shard_map/ppermute | solution.py:26
  799.9 13.4 %collective-permute-start.37 = (bf16[128,512]{1,0:T(8,128)(2,1)S(1)}, bf16[128,512]{1,0:T(8,128)(2,1)S(1)}, u32[]{:S(2)}, u32[]{:S(2)}) collective-permute-start(bf16[128,512]{1,0:T(8,128)(2,1)S(1)} %constant_dynamic-slice_fusion), channel_id=1, source_target_pairs={{0,4},{2,6},{4,0},{6,2},{8,12},{10,14},{12,8},{14,10},{16,20},{18,... | collective-permute-start | bytes 393224 | tf_op jit(solution)/shard_map/ppermute | solution.py:26
  (39 other events, 224.9 us)
Sparse Core Ops, SparseCore 0:
  26.2 48.3 all-gather.6
  76.8 27.9 all-gather.8
  106.9 81.4 all-gather.10
  189.9 63.2 all-gather.12
  254.7 63.2 all-gather.14
  320.1 63.3 all-gather.16
  385.8 68.3 reduce-scatter.6
  456.5 68.1 reduce-scatter.8
  527.0 68.1 reduce-scatter.10
  602.4 104.8 reduce-scatter.12
  709.6 34.5 reduce-scatter.14
  746.3 49.4 reduce-scatter.16

commit v5 on v4

--- a/solution.py
+++ b/solution.py
@@ -105,7 +105,7 @@
     pairs = [xor_send(rows(4 * r + 2, 2), "fsdp", r) for r in range(1, count)]
     other = xor_send(sent, "ctx", 2)
     if filler is not None:
-        other = after(other, filler)
+        other, pairs = after((other, pairs), filler)
     first = [
         (rows(4 * r, 1).astype(F32) + other[r * block : (r + 1) * block].astype(F32)).astype(BF16)
         for r in range(count)
@@ -640,10 +640,9 @@
     gain_attn_row = swap_blocks(norm_attn[None], ctx_count, 1)
     gain_mlp_row = swap_blocks(norm_mlp[None], ctx_count, 1)
 
-    qkv_width = q_width + kv_width
     if ways == 2:
-        early = swap_shards(*pair_columns([w_query, w_kv, w_output], pair, 2), pair)
-        qkv_shard, output_shard = early[:, :qkv_width], early[:, qkv_width:]
+        qkv_shard = swap_shards(*pair_columns([w_query, w_kv], pair, 2), pair)
+        output_shard = swap_shards(*pair_columns([w_output], pair, 2), pair)
     else:
         qkv_shard, output_shard = jnp.concatenate([w_query, w_kv], axis=1), w_output
     full_qkv = gather_weight(qkv_shard, ways)
@@ -730,35 +729,35 @@
     )
     y_part = dot_cols(after(act, d_x2_low), full_down).astype(BF16)
     branch = after(gather_rows(d_x2_low, ways), y_part)
-    y_lows, y_highs = return_rows(after(y_part, branch), 2)
+    rows_down = scatter_weight(grad_down, 2)
+    rows_gate = scatter_weight(after(grad_gate, (rows_down, returned)), 2)
+    def one(both, split):
+        return own_rows(both, pair, split, [(0, both.shape[1], 0, 0)], [both.shape[1]])[0]
+
+    d_att = dot(branch, full_output).astype(BF16).reshape(q.shape)
+    rows_up = scatter_weight(after(grad_up, (rows_gate, d_att)), 2)
+    grad_output = dot_rows(branch, mixed).astype(BF16)
+    rows_output = scatter_weight(after(grad_output, rows_gate), ways)
+    shard_down = one(rows_down, 2)
+    shard_gate = one(rows_gate, 2)
+    shard_up = one(rows_up, 2)
+    d_q, d_kv = attend_back(info, q, d_att, heads, lse, full_kv, count, ways)
+    y_lows, y_highs = return_rows(after(y_part, branch), 2, d_q)
     out_tokens = row_pass(
         functools.partial(result_kernel, len(y_lows), len(y_highs), ctx_count),
         (x2, *y_lows, *y_highs),
         row_bf16,
         "result",
     ).reshape(tokens.shape)
-    rows_down = scatter_weight(grad_down, 2)
-    rows_gate = scatter_weight(after(grad_gate, (rows_down, returned)), 2)
-    d_att = dot(branch, full_output).astype(BF16).reshape(q.shape)
-    rows_up = scatter_weight(after(grad_up, (rows_gate, d_att)), 2)
-    grad_output = dot_rows(branch, mixed).astype(BF16)
-
-    def one(both, split):
-        return own_rows(both, pair, split, [(0, both.shape[1], 0, 0)], [both.shape[1]])[0]
-
-    shard_down = one(rows_down, 2)
-    shard_gate = one(rows_gate, 2)
-    d_q, d_kv = attend_back(info, q, d_att, heads, lse, full_kv, count, ways)
     d_qp, gain_q_sum = head_prep_back(
         d_q.reshape(-1, q_width), raw, cos, sin, gain_q, 0, False
     )
     d_h1_query = dot_cols(d_qp, full_qkv[:, :q_width])
     d_kv = after(
         d_kv.reshape(-1, kv_width),
-        (rows_up, d_h1_query, out_tokens, shard_down, shard_gate),
+        (rows_output, d_h1_query, out_tokens, shard_down, shard_gate, shard_up),
     )
     d_kv = ctx_scatter(d_kv, ways)
-    rows_output = scatter_weight(after(grad_output, d_kv), ways)
     d_kvp, gain_k_sum = head_prep_back(d_kv, raw, cos, sin, gain_k, q_width // kv_width, True)
     d_h1 = (
         d_h1_query + dot_cols(d_kvp, full_qkv[:, q_width:])
@@ -774,9 +773,8 @@
         (row_f32, gain_shape),
         "entry_back",
     )
-    rows_output, rows_up, rows_qkv = after((rows_output, rows_up, rows_qkv), (lows, highs))
+    rows_output, rows_qkv = after((rows_output, rows_qkv), (lows, highs))
     shard_output = one(rows_output, ways)
-    shard_up = one(rows_up, 2)
     plan = [(0, q_width, 0, 0)]
     for h in range(groups):
         for t in (0, 1):

time: 837 us -> 832 us (level)
  waiting for transfers between devices: 409 us -> 391 us
  Pallas kernels: 87.8 us -> 105 us
    ppermute x44 -> x45, waiting for transfers between devices: 228 us -> 206 us  [xor_send(): return lax.ppermute(value, axis, [(i, i ^ step) for i in range(count)])]
    pallas_call x1, Pallas kernels: 25.1 us -> 33.4 us  [attend_back(): pl.pallas_call(functools.partial(backward_kernel, ways, count), out_shape...]
    unnamed x94 -> x92, local copies, waits for them, and re-layouts: 21.5 us -> 19.5 us
    ppermute x44 -> x45, starting transfers between devices: 60.1 us -> 60.4 us  [xor_send(): return lax.ppermute(value, axis, [(i, i ^ step) for i in range(count)])]
  transfers between devices with their start and end apart: 56 -> 57, of which waited for: 42 -> 43; matrix products, arithmetic and copies ran while one was open for 27% -> 25% of each run, Pallas kernels for 10% -> 12%
where the time goes in v5:
time: 832 us; the launch traced here: 823 us
  waiting for transfers between devices  391 us (47%)
  matrix products  143 us (17%)
  Pallas kernels  105 us (13%)
  starting transfers between devices  62.1 us (7%)
  local copies, waits for them, and re-layouts  58.6 us (7%)
  other arithmetic  48.5 us (6%)
  between operations  15.3 us (2%)
    ppermute x45, waiting for transfers between devices, xor_send(): return lax.ppermute(value, axis, [(i, i ^ step) for i in range(count)])  206 us
    reduce_scatter x6, waiting for transfers between devices, ctx_scatter(): lax.psum_scatter(rows, 'ctx', scatter_dimension=0, tiled=True, axis_index...  119 us
    all_gather x6, waiting for transfers between devices, ctx_gather(): lax.all_gather(rows, 'ctx', axis=0, tiled=True, axis_index_groups=groups)  64.9 us
    ppermute x45, starting transfers between devices, xor_send(): return lax.ppermute(value, axis, [(i, i ^ step) for i in range(count)])  60.4 us
    dot_general x5, matrix products, dot(): return jnp.dot(left, right, preferred_element_type=F32)  52.3 us
    dot_general x6, matrix products, dot_cols(): lax.dot_general(left, right, (((1,), (1,)), ((), ())), preferred_element_...  48.8 us
    dot_general x5, matrix products, dot_rows(): lax.dot_general(left, right, (((0,), (0,)), ((), ())), preferred_element_...  41.9 us
    pallas_call x1, Pallas kernels, attend_back(): pl.pallas_call(functools.partial(backward_kernel, ways, count), out_shape...  33.4 us
  transfers between devices with their start and end apart: 57, of which 43 were waited for; matrix products, arithmetic and copies ran while one was open for 25% of the time, Pallas kernels for 12%

profile of v5, /device:TPU:0, one launch (start us, length us, event | category | flops | bytes accessed | tf_op | source)
XLA Modules:
  0.0 823.2 jit_solution(2947444993187163774)
XLA Ops:
  11.1 3.1 collective-permute-start.4
  14.2 6.3 collective-permute-done.4
  33.6 2.7 constant_dynamic-update-slice_fusion.7
  36.3 2.7 constant_dynamic-update-slice_fusion.6
  39.1 2.7 constant_dynamic-update-slice_fusion.5
  46.7 2.7 constant_dynamic-update-slice_fusion.4
  49.4 2.7 constant_dynamic-update-slice_fusion.3
  52.1 2.7 constant_dynamic-update-slice_fusion.2
  54.7 2.7 constant_dynamic-update-slice_fusion.1
  57.4 2.7 constant_dynamic-update-slice_fusion
  63.3 3.5 collective-permute-done.1.refs_0_
  70.8 10.0 %fusion.73.raw_ref = f32[1024,1024]{1,0:T(8,128)} fusion(bf16[1024,2048]{1,0:T(8,128)(2,1)} %copy-done.2, bf16[2048,1024]{1,0:T(8,128)(2,1)} %all-gather.7.cloned.1.call-done), kind=kOutput, calls=%fused_computation.201 | convolution fusion | flops 4294967296 | bytes 12582912 | tf_op jit(solution)/shard_map/dot_general | solution.py:317
  80.8 6.2 head_prep.1
  87.1 13.0 %all-gather.9.cloned.1.call-done = bf16[2048,512]{1,0:T(8,128)(2,1)} async-done(((bf16[256,512]{1,0:T(8,128)(2,1)}), bf16[2048,512]{1,0:T(8,128)(2,1)}) %all-gather.9.cloned.1.call-update) | async-done | bytes 2097168 | tf_op jit(solution)/shard_map/all_gather | solution.py:251
  103.3 26.6 %collective-permute-done.5 = bf16[128,4608]{1,0:T(8,128)(2,1)S(1)} collective-permute-done((bf16[128,4608]{1,0:T(8,128)(2,1)S(1)}, bf16[128,4608]{1,0:T(8,128)(2,1)S(1)}, u32[]{:S(2)}, u32[]{:S(2)}) %collective-permute-start.5) | collective-permute-done | bytes 1179680 | tf_op jit(solution)/shard_map/ppermute | solution.py:26
  136.2 10.4 %collective-permute-done.6.refs_2_ = bf16[128,2048]{1,0:T(8,128)(2,1)S(1)} collective-permute-done((bf16[128,2048]{1,0:T(8,128)(2,1)S(1)}, bf16[128,2048]{1,0:T(8,128)(2,1)S(1)}, u32[]{:S(2)}, u32[]{:S(2)}) %collective-permute-start.6) | collective-permute-done | bytes 524320 | tf_op jit(solution)/shard_map/ppermute | solution.py:26
  155.6 10.2 %stack.31.info_ref = s32[26]{0:T(128)S(1)} concatenate(s32[1]{0:T(128)} %bitcast.8.pair_ref, s32[1]{0:T(128)} %bitcast.9, s32[1]{0:T(128)} %bitcast.10, s32[1]{0:T(128)} %bitcast.11, s32[1]{0:T(128)} %bitcast.12, s32[1]{0:T(128)} %bitcast.13, s32[1]{0:T(128)} %bitcast.14, s32[1]{0:T(128)} %bitcast.15, s32[1]{0:T(128)} %bitcast.16, s32[1]{0:T(128)} %bitcast.17, s32[1]{0:T(128)} %bitcast.18, ...), dimensions={0} | concatenate | bytes 208 | tf_op jit(solution)/shard_map/stack | solution.py:679
  165.8 5.9 collective-permute-done.7.refs_0_
  176.8 6.9 all-gather.11.cloned.1.call-done
  185.0 25.3 %attend.1 = (bf16[2,4,128,512]{3,2,1,0:T(8,128)(2,1)S(1)}, f32[2,2,4,1,256]{4,3,2,1,0:T(1,128)S(1)}) custom-call(s32[26]{0:T(128)S(1)} %stack.31.info_ref, bf16[2,4,128,512]{3,2,1,0:T(8,128)(2,1)S(1)} %bitcast.125, bf16[8,2,4,128,512]{4,3,2,1,0:T(8,128)(2,1)} %bitcast.145), custom_call_target="tpu_custom_call" | custom-call | flops 4294967296 | bytes 8388608 | tf_op jit(solution)/shard_map/attend/pallas_call | solution.py:552
  218.0 21.5 %collective-permute-done.11 = bf16[256,2048]{1,0:T(8,128)(2,1)S(1)} collective-permute-done((bf16[256,2048]{1,0:T(8,128)(2,1)}, bf16[256,2048]{1,0:T(8,128)(2,1)S(1)}, u32[]{:S(2)}, u32[]{:S(2)}) %collective-permute-start.11) | collective-permute-done | bytes 1048608 | tf_op jit(solution)/shard_map/ppermute | solution.py:26
  245.9 8.6 %collective-permute-done.12.refs_3_ = bf16[128,2048]{1,0:T(8,128)(2,1)S(1)} collective-permute-done((bf16[128,2048]{1,0:T(8,128)(2,1)S(1)}, bf16[128,2048]{1,0:T(8,128)(2,1)S(1)}, u32[]{:S(2)}, u32[]{:S(2)}) %collective-permute-start.12) | collective-permute-done | bytes 524320 | tf_op jit(solution)/shard_map/ppermute | solution.py:26
  254.5 2.9 collective-permute-done.14.refs_5_
  261.8 10.0 %collective-permute-done.15.refs_2_ = bf16[128,2048]{1,0:T(8,128)(2,1)S(1)} collective-permute-done((bf16[128,2048]{1,0:T(8,128)(2,1)S(1)}, bf16[128,2048]{1,0:T(8,128)(2,1)S(1)}, u32[]{:S(2)}, u32[]{:S(2)}) %collective-permute-start.15) | collective-permute-done | bytes 524320 | tf_op jit(solution)/shard_map/ppermute | solution.py:26
  274.5 20.1 %collective-permute-done.16.refs_0_ = bf16[256,2048]{1,0:T(8,128)(2,1)S(1)} collective-permute-done((bf16[256,2048]{1,0:T(8,128)(2,1)S(1)}, bf16[256,2048]{1,0:T(8,128)(2,1)S(1)}, u32[]{:S(2)}, u32[]{:S(2)}) %collective-permute-start.16) | collective-permute-done | bytes 1048608 | tf_op jit(solution)/shard_map/ppermute | solution.py:26
  298.3 11.7 %fusion.74 = f32[1024,1536]{1,0:T(8,128)} fusion(bf16[1024,2048]{1,0:T(8,128)(2,1)} %copy-done.6, bf16[2048,1536]{1,0:T(8,128)(2,1)} %all-gather.13.cloned.1.call-done), kind=kOutput, calls=%fused_computation.202 | convolution fusion | flops 6442450944 | bytes 16777216 | tf_op jit(solution)/shard_map/dot_general | solution.py:317
  310.0 3.3 all-gather.15.cloned.1.call-done
  313.4 13.1 %multiply_convert_fusion.2 = (bf16[1024,1536]{1,0:T(8,128)(2,1)S(1)}, f32[1024,1536]{1,0:T(8,128)}) fusion(f32[1024,1536]{1,0:T(8,128)} %fusion.74, bf16[1024,2048]{1,0:T(8,128)(2,1)} %copy-done.6, bf16[2048,1536]{1,0:T(8,128)(2,1)} %all-gather.15.cloned.1.call-done), kind=kOutput, calls=%fused_computation.7 | convolution fusion | flops 6450315264 | bytes 26214400 | tf_op jit(solution)/shard_map/dot_general | solution.py:317
  328.1 8.8 %convolution_convert_fusion.2 = bf16[2048,1536]{1,0:T(8,128)(2,1)} fusion(bf16[1024,2048]{1,0:T(8,128)(2,1)S(1)} %copy-done.5, bf16[1024,1536]{1,0:T(8,128)(2,1)S(1)} %get-tuple-element.75), kind=kOutput, calls=%fused_computation.4 | convolution fusion | flops 6445596672 | bytes 13631488 | tf_op jit(solution)/shard_map/dot_general | solution.py:321
  337.2 41.6 %all-gather.17.cloned.1.call-done = bf16[2048,1536]{1,0:T(8,128)(2,1)} async-done(((bf16[256,1536]{1,0:T(8,128)(2,1)}), bf16[2048,1536]{1,0:T(8,128)(2,1)}) %all-gather.17.cloned.1.call-update) | async-done | bytes 6291472 | tf_op jit(solution)/shard_map/all_gather | solution.py:251
  378.8 14.2 %multiply_convert_fusion = (bf16[1024,1536]{1,0:T(8,128)(2,1)S(1)}, bf16[1024,1536]{1,0:T(8,128)(2,1)S(1)}) fusion(f32[1024,1536]{1,0:T(8,128)} %fusion.74, f32[1024,1536]{1,0:T(8,128)} %get-tuple-element.202, bf16[1024,2048]{1,0:T(8,128)(2,1)} %copy-done.4, bf16[2048,1536]{1,0:T(8,128)(2,1)} %all-gather.17.cloned.1.call-done), kind=kOutput, calls=%fused_computation.5 | convolution fusion | flops 6462898176 | bytes 29360128 | tf_op jit(solution)/shard_map/dot_general | solution.py:317
  393.0 10.0 %fusion.75 = f32[1024,2048]{1,0:T(8,128)S(1)} fusion(bf16[1024,1536]{1,0:T(8,128)(2,1)S(1)} %get-tuple-element.126, bf16[2048,1536]{1,0:T(8,128)(2,1)} %all-gather.13.cloned.1.call-done), kind=kOutput, calls=%fused_computation.203 | convolution fusion | flops 6442450944 | bytes 17825792 | tf_op jit(solution)/shard_map/dot_general | solution.py:325
  403.0 8.9 %add_convert_fusion.1 = bf16[1024,2048]{1,0:T(8,128)(2,1)S(1)} fusion(f32[1024,2048]{1,0:T(8,128)S(1)} %fusion.75, bf16[1024,1536]{1,0:T(8,128)(2,1)S(1)} %get-tuple-element.125, bf16[2048,1536]{1,0:T(8,128)(2,1)} %all-gather.15.cloned.1.call-done), kind=kOutput, calls=%fused_computation.1 | convolution fusion | flops 6446645248 | bytes 22020096 | tf_op jit(solution)/shard_map/dot_general | solution.py:325
  418.6 8.8 %convolution_convert_fusion = bf16[2048,1536]{1,0:T(8,128)(2,1)} fusion(bf16[1024,2048]{1,0:T(8,128)(2,1)S(1)} %copy-done.7, bf16[1024,1536]{1,0:T(8,128)(2,1)S(1)} %get-tuple-element.125), kind=kOutput, calls=%fused_computation.2 | convolution fusion | flops 6445596672 | bytes 13631488 | tf_op jit(solution)/shard_map/dot_general | solution.py:321
  427.4 11.8 %convolution_convert_fusion.1 = bf16[2048,1536]{1,0:T(8,128)(2,1)} fusion(bf16[1024,2048]{1,0:T(8,128)(2,1)} %copy-done.6, bf16[1024,1536]{1,0:T(8,128)(2,1)} %copy-done.43), kind=kOutput, calls=%fused_computation.3 | convolution fusion | flops 6445596672 | bytes 13631488 | tf_op jit(solution)/shard_map/dot_general | solution.py:321
  445.5 2.9 add_convert_fusion.10
  452.6 9.1 %collective-permute-done.22.refs_6_ = bf16[128,2048]{1,0:T(8,128)(2,1)S(1)} collective-permute-done((bf16[128,2048]{1,0:T(8,128)(2,1)}, bf16[128,2048]{1,0:T(8,128)(2,1)S(1)}, u32[]{:S(2)}, u32[]{:S(2)}) %collective-permute-start.22) | collective-permute-done | bytes 524320 | tf_op jit(solution)/shard_map/ppermute | solution.py:26
  466.2 3.7 middle_back.1
  472.1 8.9 %collective-permute-done.23.refs_2_ = bf16[128,2048]{1,0:T(8,128)(2,1)S(1)} collective-permute-done((bf16[128,2048]{1,0:T(8,128)(2,1)S(1)}, bf16[128,2048]{1,0:T(8,128)(2,1)S(1)}, u32[]{:S(2)}, u32[]{:S(2)}) %collective-permute-start.23) | collective-permute-done | bytes 524320 | tf_op jit(solution)/shard_map/ppermute | solution.py:26
  481.5 2.8 collective-permute-done.25
  484.5 11.1 %convolution_convert_fusion.3 = bf16[1024,2048]{1,0:T(8,128)(2,1)} fusion(bf16[1024,1536]{1,0:T(8,128)(2,1)S(1)} %copy-done.45, bf16[2048,1536]{1,0:T(8,128)(2,1)} %all-gather.17.cloned.1.call-done), kind=kOutput, calls=%fused_computation.10 | convolution fusion | flops 6444548096 | bytes 13631488 | tf_op jit(solution)/shard_map/dot_general | solution.py:325
  495.6 8.8 %collective-permute-done.24.refs_0_ = bf16[256,2048]{1,0:T(8,128)(2,1)S(1)} collective-permute-done((bf16[256,2048]{1,0:T(8,128)(2,1)S(1)}, bf16[256,2048]{1,0:T(8,128)(2,1)S(1)}, u32[]{:S(2)}, u32[]{:S(2)}) %collective-permute-start.24) | collective-permute-done | bytes 1048608 | tf_op jit(solution)/shard_map/ppermute | solution.py:26
  506.6 3.3 convolution_convert_fusion.7
  509.9 10.1 %reduce-scatter.9.cloned.1.call-done.both_ref = bf16[256,1536]{1,0:T(8,128)(2,1)} async-done(((bf16[2048,1536]{1,0:T(8,128)(2,1)}), bf16[256,1536]{1,0:T(8,128)(2,1)}) %reduce-scatter.9.cloned.1.call-update) | async-done | bytes 786448 | tf_op jit(solution)/shard_map/reduce_scatter | solution.py:256
  520.1 6.2 convolution_convert_fusion.6
  534.6 33.4 %attend_back.1 = (f32[2,4,128,512]{3,2,1,0:T(8,128)}, bf16[8,2,4,128,512]{4,3,2,1,0:T(8,128)(2,1)}) custom-call(s32[26]{0:T(128)} %copy-done.20, bf16[2,4,128,512]{3,2,1,0:T(8,128)(2,1)} %bitcast.124, bf16[2,4,128,512]{3,2,1,0:T(8,128)(2,1)} %bitcast.148, bf16[2,4,128,512]{3,2,1,0:T(8,128)(2,1)} %copy-done.22, f32[2,2,4,1,256]{4,3,2,1,0:T(1,128)} %copy-done.23, ...), custom_call_target="tpu_custom_call" | custom-call | flops 10737418240 | bytes 16777216 | tf_op jit(solution)/shard_map/attend_back/pallas_call | solution.py:575
  568.0 5.9 head_prep_back.2
  577.6 2.9 add_convert_fusion.8
  583.8 6.8 reduce-scatter.13.cloned.1.call-done.both_ref
  593.8 7.6 fusion.2
  601.5 2.6 result.1
  604.0 2.5 own_rows.5
  613.7 2.5 own_rows.7
  616.2 11.0 %reduce-scatter.11.cloned.1.call-done.both_ref = bf16[256,512]{1,0:T(8,128)(2,1)} async-done(((bf16[2048,512]{1,0:T(8,128)(2,1)}), bf16[256,512]{1,0:T(8,128)(2,1)}) %reduce-scatter.11.cloned.1.call-update) | async-done | bytes 262160 | tf_op jit(solution)/shard_map/reduce_scatter | solution.py:256
  627.4 90.4 %reduce-scatter.15.cloned.1.call-done.d_ref = bf16[1024,512]{1,0:T(8,128)(2,1)} async-done(((bf16[8192,512]{1,0:T(8,128)(2,1)}), bf16[1024,512]{1,0:T(8,128)(2,1)}) %reduce-scatter.15.cloned.1.call-update) | async-done | bytes 1048592 | tf_op jit(solution)/shard_map/reduce_scatter | solution.py:256
  717.8 4.8 head_prep_back.3
  722.6 8.9 %add_convert_fusion = bf16[1024,2048]{1,0:T(8,128)(2,1)} fusion(f32[1024,2048]{1,0:T(8,128)} %fusion.2, bf16[1024,512]{1,0:T(8,128)(2,1)} %get-tuple-element.89, bf16[2048,1024]{1,0:T(8,128)(2,1)} %all-gather.7.cloned.1.call-done), kind=kOutput, calls=%fused_computation | convolution fusion | flops 2151677952 | bytes 15728640 | tf_op jit(solution)/shard_map/dot_general | solution.py:325
  731.6 6.3 convolution_convert_fusion.5
  742.6 19.9 %collective-permute-done.34 = bf16[256,2048]{1,0:T(8,128)(2,1)S(1)} collective-permute-done((bf16[256,2048]{1,0:T(8,128)(2,1)S(1)}, bf16[256,2048]{1,0:T(8,128)(2,1)S(1)}, u32[]{:S(2)}, u32[]{:S(2)}) %collective-permute-start.34) | collective-permute-done | bytes 1048608 | tf_op jit(solution)/shard_map/ppermute | solution.py:26
  766.5 8.6 %collective-permute-done.35.refs_4_ = bf16[128,2048]{1,0:T(8,128)(2,1)S(1)} collective-permute-done((bf16[128,2048]{1,0:T(8,128)(2,1)S(1)}, bf16[128,2048]{1,0:T(8,128)(2,1)S(1)}, u32[]{:S(2)}, u32[]{:S(2)}) %collective-permute-start.35) | collective-permute-done | bytes 524320 | tf_op jit(solution)/shard_map/ppermute | solution.py:26
  775.8 5.0 entry_back.1
  785.9 4.7 collective-permute-start.42
  792.4 2.9 collective-permute-start.43
  805.7 5.2 collective-permute-done.39.other_ref
  (283 shorter events, 164.8 us)
Async XLA Ops:
  7.2 63.6 %all-gather.7.cloned.1.call-start = ((), (), s32[]{:S(2)}) async-start(), calls=%async_computation.6 | async-start | bytes 4718592 | tf_op jit(solution)/shard_map/all_gather | solution.py:251
  11.1 9.4 %collective-permute-start.4 = (bf16[128,1024]{1,0:T(8,128)(2,1)S(1)}, bf16[128,1024]{1,0:T(8,128)(2,1)S(1)}, u32[]{:S(2)}, u32[]{:S(2)}) collective-permute-start(bf16[128,1024]{1,0:T(8,128)(2,1)S(1)} %pad_maximum_fusion.20), channel_id=1, source_target_pairs={{0,4},{2,6},{4,0},{6,2},{8,12},{10,14},{12,8},{14,10},{16,20},{18,... | collective-permute-start | bytes 786440 | tf_op jit(solution)/shard_map/ppermute | solution.py:26
  21.4 78.7 %all-gather.9.cloned.1.call-start = ((), (), s32[]{:S(2)}) async-start(), calls=%async_computation.7 | async-start | bytes 2359296 | tf_op jit(solution)/shard_map/all_gather | solution.py:251
  21.5 5.9 collective-permute-start.10
  27.4 105.7 %copy-start = (bf16[256,2048]{1,0:T(8,128)(2,1)}, bf16[256,2048]{1,0:T(8,128)(2,1)S(1)}, u32[]{:S(2)}) copy-start(bf16[256,2048]{1,0:T(8,128)(2,1)S(1)} %get-tuple-element.64.refs_0_) | copy-start | bytes 3145732
  28.3 155.4 %all-gather.11.cloned.1.call-start = ((), (), s32[]{:S(2)}) async-start(), calls=%async_computation.8 | async-start | bytes 9437184 | tf_op jit(solution)/shard_map/all_gather | solution.py:251
  30.5 12.5 %collective-permute-start = (bf16[128,2048]{1,0:T(8,128)(2,1)S(1)}, bf16[128,2048]{1,0:T(8,128)(2,1)S(1)}, u32[]{:S(2)}, u32[]{:S(2)}) collective-permute-start(bf16[128,2048]{1,0:T(8,128)(2,1)S(1)} %get-tuple-element.163.refs_1_), channel_id=1, source_target_pairs={{0,1},{1,0},{2,3},{3,2},{4,5},{5,4},{6,7},{7,6},{8,9},{9,8},{10,11... | collective-permute-start | bytes 1572872 | tf_op jit(solution)/shard_map/ppermute | solution.py:26
  31.9 13.3 %collective-permute-start.2 = (bf16[128,2048]{1,0:T(8,128)(2,1)}, bf16[128,2048]{1,0:T(8,128)(2,1)}, u32[]{:S(2)}, u32[]{:S(2)}) collective-permute-start(bf16[128,2048]{1,0:T(8,128)(2,1)} %get-tuple-element.162), channel_id=1, source_target_pairs={{0,4},{2,6},{4,0},{6,2},{8,12},{10,14},{12,8},{14,10},{16,20},{18,... | collective-permute-start | bytes 1572872 | tf_op jit(solution)/shard_map/ppermute | solution.py:26
  43.1 23.8 %collective-permute-start.1 = (bf16[256,2048]{1,0:T(8,128)(2,1)S(1)}, bf16[256,2048]{1,0:T(8,128)(2,1)S(1)}, u32[]{:S(2)}, u32[]{:S(2)}) collective-permute-start(bf16[256,2048]{1,0:T(8,128)(2,1)S(1)} %pad_maximum_fusion.3), channel_id=1, source_target_pairs={{0,4},{2,6},{4,0},{6,2},{8,12},{10,14},{12,8},{14,10},{16,20},{18,... | collective-permute-start | bytes 3145736 | tf_op jit(solution)/shard_map/ppermute | solution.py:26
  46.6 21.9 %collective-permute-start.3 = (bf16[256,2048]{1,0:T(8,128)(2,1)S(1)}, bf16[256,2048]{1,0:T(8,128)(2,1)S(1)}, u32[]{:S(2)}, u32[]{:S(2)}) collective-permute-start(bf16[256,2048]{1,0:T(8,128)(2,1)S(1)} %pad_maximum_fusion.4.refs_3_), channel_id=1, source_target_pairs={{0,1},{1,0},{2,3},{3,2},{4,5},{5,4},{6,7},{7,6},{8,9},{9,8},{10,11... | collective-permute-start | bytes 3145736 | tf_op jit(solution)/shard_map/ppermute | solution.py:26
  80.8 19.4 %copy-start.29 = (bf16[128,3072]{1,0:T(8,128)(2,1)S(1)}, bf16[128,3072]{1,0:T(8,128)(2,1)}, u32[]{:S(2)}) copy-start(bf16[128,3072]{1,0:T(8,128)(2,1)} %param.21) | copy-start | bytes 2359300
  100.1 198.2 %all-gather.13.cloned.1.call-start = ((), (), s32[]{:S(2)}) async-start(), calls=%async_computation.9 | async-start | bytes 7077888 | tf_op jit(solution)/shard_map/all_gather | solution.py:251
  101.8 28.2 %collective-permute-start.5 = (bf16[128,4608]{1,0:T(8,128)(2,1)S(1)}, bf16[128,4608]{1,0:T(8,128)(2,1)S(1)}, u32[]{:S(2)}, u32[]{:S(2)}) collective-permute-start(bf16[128,4608]{1,0:T(8,128)(2,1)S(1)} %pad_maximum_fusion.2), channel_id=1, source_target_pairs={{0,4},{2,6},{4,0},{6,2},{8,12},{10,14},{12,8},{14,10},{16,20},{18,... | collective-permute-start | bytes 3538952 | tf_op jit(solution)/shard_map/ppermute | solution.py:26
  132.0 181.3 %all-gather.15.cloned.1.call-start = ((), (), s32[]{:S(2)}) async-start(), calls=%async_computation.10 | async-start | bytes 7077888 | tf_op jit(solution)/shard_map/all_gather | solution.py:251
  132.6 246.2 %all-gather.17.cloned.1.call-start = ((), (), s32[]{:S(2)}) async-start(), calls=%async_computation.11 | async-start | bytes 7077888 | tf_op jit(solution)/shard_map/all_gather | solution.py:251
  133.2 13.4 %collective-permute-start.6 = (bf16[128,2048]{1,0:T(8,128)(2,1)S(1)}, bf16[128,2048]{1,0:T(8,128)(2,1)S(1)}, u32[]{:S(2)}, u32[]{:S(2)}) collective-permute-start(bf16[128,2048]{1,0:T(8,128)(2,1)S(1)} %get-tuple-element.161.refs_1_), channel_id=1, source_target_pairs={{0,1},{1,0},{2,3},{3,2},{4,5},{5,4},{6,7},{7,6},{8,9},{9,8},{10,11... | collective-permute-start | bytes 1572872 | tf_op jit(solution)/shard_map/ppermute | solution.py:26
  134.7 14.3 %collective-permute-start.8 = (bf16[128,2048]{1,0:T(8,128)(2,1)S(1)}, bf16[128,2048]{1,0:T(8,128)(2,1)S(1)}, u32[]{:S(2)}, u32[]{:S(2)}) collective-permute-start(bf16[128,2048]{1,0:T(8,128)(2,1)S(1)} %get-tuple-element.160), channel_id=1, source_target_pairs={{0,4},{2,6},{4,0},{6,2},{8,12},{10,14},{12,8},{14,10},{16,20},{18,... | collective-permute-start | bytes 1572872 | tf_op jit(solution)/shard_map/ppermute | solution.py:26
  147.6 24.1 %collective-permute-start.7 = (bf16[256,2048]{1,0:T(8,128)(2,1)}, bf16[256,2048]{1,0:T(8,128)(2,1)}, u32[]{:S(2)}, u32[]{:S(2)}) collective-permute-start(bf16[256,2048]{1,0:T(8,128)(2,1)} %pad_maximum_fusion.5), channel_id=1, source_target_pairs={{0,4},{2,6},{4,0},{6,2},{8,12},{10,14},{12,8},{14,10},{16,20},{18,... | collective-permute-start | bytes 3145736 | tf_op jit(solution)/shard_map/ppermute | solution.py:26
  149.2 23.7 %collective-permute-start.9 = (bf16[256,2048]{1,0:T(8,128)(2,1)S(1)}, bf16[256,2048]{1,0:T(8,128)(2,1)}, u32[]{:S(2)}, u32[]{:S(2)}) collective-permute-start(bf16[256,2048]{1,0:T(8,128)(2,1)S(1)} %pad_maximum_fusion.6.refs_3_), channel_id=1, source_target_pairs={{0,1},{1,0},{2,3},{3,2},{4,5},{5,4},{6,7},{7,6},{8,9},{9,8},{10,11... | collective-permute-start | bytes 3145736 | tf_op jit(solution)/shard_map/ppermute | solution.py:26
  185.0 25.3 %copy-start.39 = (bf16[2048,512]{1,0:T(8,128)(2,1)S(1)}, bf16[2048,512]{1,0:T(8,128)(2,1)}, u32[]{:S(2)}) copy-start(bf16[2048,512]{1,0:T(8,128)(2,1)} %all-gather.9.cloned.1.call-done) | copy-start | bytes 6291460
  214.0 25.5 %collective-permute-start.11 = (bf16[256,2048]{1,0:T(8,128)(2,1)}, bf16[256,2048]{1,0:T(8,128)(2,1)S(1)}, u32[]{:S(2)}, u32[]{:S(2)}) collective-permute-start(bf16[256,2048]{1,0:T(8,128)(2,1)} %pad_maximum_fusion.7), channel_id=1, source_target_pairs={{0,4},{2,6},{4,0},{6,2},{8,12},{10,14},{12,8},{14,10},{16,20},{18,... | collective-permute-start | bytes 3145736 | tf_op jit(solution)/shard_map/ppermute | solution.py:26
  216.5 26.1 %collective-permute-start.13 = (bf16[256,2048]{1,0:T(8,128)(2,1)}, bf16[256,2048]{1,0:T(8,128)(2,1)S(1)}, u32[]{:S(2)}, u32[]{:S(2)}) collective-permute-start(bf16[256,2048]{1,0:T(8,128)(2,1)} %slice.319), channel_id=1, source_target_pairs={{0,1},{1,0},{2,3},{3,2},{4,5},{5,4},{6,7},{7,6},{8,9},{9,8},{10,11... | collective-permute-start | bytes 3145736 | tf_op jit(solution)/shard_map/ppermute | solution.py:26
  218.0 27.9 %copy-start.36 = (f32[2048]{0:T(1024)S(1)}, f32[2048]{0:T(1024)}, u32[]{:S(2)}) copy-start(f32[2048]{0:T(1024)} %param.25) | copy-start | bytes 24580
  218.0 231.5 %reduce-scatter.7.cloned.1.call-start = ((), (), s32[]{:S(2)}) async-start(), calls=%async_computation.12 | async-start | bytes 7077888 | tf_op jit(solution)/shard_map/reduce_scatter | solution.py:256
  241.1 13.4 %collective-permute-start.12 = (bf16[128,2048]{1,0:T(8,128)(2,1)S(1)}, bf16[128,2048]{1,0:T(8,128)(2,1)S(1)}, u32[]{:S(2)}, u32[]{:S(2)}) collective-permute-start(bf16[128,2048]{1,0:T(8,128)(2,1)S(1)} %get-tuple-element.133), channel_id=1, source_target_pairs={{0,1},{1,0},{2,3},{3,2},{4,5},{5,4},{6,7},{7,6},{8,9},{9,8},{10,11... | collective-permute-start | bytes 1572872 | tf_op jit(solution)/shard_map/ppermute | solution.py:26
  244.3 13.1 %collective-permute-start.14 = (bf16[128,2048]{1,0:T(8,128)(2,1)S(1)}, bf16[128,2048]{1,0:T(8,128)(2,1)S(1)}, u32[]{:S(2)}, u32[]{:S(2)}) collective-permute-start(bf16[128,2048]{1,0:T(8,128)(2,1)S(1)} %get-tuple-element.158), channel_id=1, source_target_pairs={{0,4},{2,6},{4,0},{6,2},{8,12},{10,14},{12,8},{14,10},{16,20},{18,... | collective-permute-start | bytes 1572872 | tf_op jit(solution)/shard_map/ppermute | solution.py:26
  259.6 12.2 %collective-permute-start.15 = (bf16[128,2048]{1,0:T(8,128)(2,1)S(1)}, bf16[128,2048]{1,0:T(8,128)(2,1)S(1)}, u32[]{:S(2)}, u32[]{:S(2)}) collective-permute-start(bf16[128,2048]{1,0:T(8,128)(2,1)S(1)} %get-tuple-element.157.refs_1_), channel_id=1, source_target_pairs={{0,1},{1,0},{2,3},{3,2},{4,5},{5,4},{6,7},{7,6},{8,9},{9,8},{10,11... | collective-permute-start | bytes 1572872 | tf_op jit(solution)/shard_map/ppermute | solution.py:26
  260.2 13.2 %collective-permute-start.17 = (bf16[128,2048]{1,0:T(8,128)(2,1)S(1)}, bf16[128,2048]{1,0:T(8,128)(2,1)S(1)}, u32[]{:S(2)}, u32[]{:S(2)}) collective-permute-start(bf16[128,2048]{1,0:T(8,128)(2,1)S(1)} %get-tuple-element.156), channel_id=1, source_target_pairs={{0,4},{2,6},{4,0},{6,2},{8,12},{10,14},{12,8},{14,10},{16,20},{18,... | collective-permute-start | bytes 1572872 | tf_op jit(solution)/shard_map/ppermute | solution.py:26
  271.9 22.7 %collective-permute-start.16 = (bf16[256,2048]{1,0:T(8,128)(2,1)S(1)}, bf16[256,2048]{1,0:T(8,128)(2,1)S(1)}, u32[]{:S(2)}, u32[]{:S(2)}) collective-permute-start(bf16[256,2048]{1,0:T(8,128)(2,1)S(1)} %pad_maximum_fusion.8), channel_id=1, source_target_pairs={{0,4},{2,6},{4,0},{6,2},{8,12},{10,14},{12,8},{14,10},{16,20},{18,... | collective-permute-start | bytes 3145736 | tf_op jit(solution)/shard_map/ppermute | solution.py:26
  273.6 22.4 %collective-permute-start.18 = (bf16[256,2048]{1,0:T(8,128)(2,1)S(1)}, bf16[256,2048]{1,0:T(8,128)(2,1)S(1)}, u32[]{:S(2)}, u32[]{:S(2)}) collective-permute-start(bf16[256,2048]{1,0:T(8,128)(2,1)S(1)} %pad_maximum_fusion.9.refs_3_), channel_id=1, source_target_pairs={{0,1},{1,0},{2,3},{3,2},{4,5},{5,4},{6,7},{7,6},{8,9},{9,8},{10,11... | collective-permute-start | bytes 3145736 | tf_op jit(solution)/shard_map/ppermute | solution.py:26
  336.9 183.1 %reduce-scatter.9.cloned.1.call-start = ((), (), s32[]{:S(2)}) async-start(), calls=%async_computation.13 | async-start | bytes 7077888 | tf_op jit(solution)/shard_map/reduce_scatter | solution.py:256
  415.7 25.6 %collective-permute-start.19 = (bf16[256,2048]{1,0:T(8,128)(2,1)}, bf16[256,2048]{1,0:T(8,128)(2,1)}, u32[]{:S(2)}, u32[]{:S(2)}) collective-permute-start(bf16[256,2048]{1,0:T(8,128)(2,1)} %pad_maximum_fusion.10), channel_id=1, source_target_pairs={{0,4},{2,6},{4,0},{6,2},{8,12},{10,14},{12,8},{14,10},{16,20},{18,... | collective-permute-start | bytes 3145736 | tf_op jit(solution)/shard_map/ppermute | solution.py:26
  417.2 25.3 %collective-permute-start.20 = (bf16[256,2048]{1,0:T(8,128)(2,1)}, bf16[256,2048]{1,0:T(8,128)(2,1)}, u32[]{:S(2)}, u32[]{:S(2)}) collective-permute-start(bf16[256,2048]{1,0:T(8,128)(2,1)} %slice.325), channel_id=1, source_target_pairs={{0,1},{1,0},{2,3},{3,2},{4,5},{5,4},{6,7},{7,6},{8,9},{9,8},{10,11... | collective-permute-start | bytes 3145736 | tf_op jit(solution)/shard_map/ppermute | solution.py:26
  449.5 141.0 %reduce-scatter.13.cloned.1.call-start = ((), (), s32[]{:S(2)}) async-start(), calls=%async_computation.15 | async-start | bytes 7077888 | tf_op jit(solution)/shard_map/reduce_scatter | solution.py:256
  449.6 12.1 %collective-permute-start.22 = (bf16[128,2048]{1,0:T(8,128)(2,1)}, bf16[128,2048]{1,0:T(8,128)(2,1)S(1)}, u32[]{:S(2)}, u32[]{:S(2)}) collective-permute-start(bf16[128,2048]{1,0:T(8,128)(2,1)} %get-tuple-element.154), channel_id=1, source_target_pairs={{0,4},{2,6},{4,0},{6,2},{8,12},{10,14},{12,8},{14,10},{16,20},{18,... | collective-permute-start | bytes 1572872 | tf_op jit(solution)/shard_map/ppermute | solution.py:26
  451.1 11.7 %collective-permute-start.21 = (bf16[128,2048]{1,0:T(8,128)(2,1)}, bf16[128,2048]{1,0:T(8,128)(2,1)S(1)}, u32[]{:S(2)}, u32[]{:S(2)}) collective-permute-start(bf16[128,2048]{1,0:T(8,128)(2,1)} %get-tuple-element.131), channel_id=1, source_target_pairs={{0,1},{1,0},{2,3},{3,2},{4,5},{5,4},{6,7},{7,6},{8,9},{9,8},{10,11... | collective-permute-start | bytes 1572872 | tf_op jit(solution)/shard_map/ppermute | solution.py:26
  470.0 11.0 %collective-permute-start.23 = (bf16[128,2048]{1,0:T(8,128)(2,1)S(1)}, bf16[128,2048]{1,0:T(8,128)(2,1)S(1)}, u32[]{:S(2)}, u32[]{:S(2)}) collective-permute-start(bf16[128,2048]{1,0:T(8,128)(2,1)S(1)} %get-tuple-element.153.refs_1_), channel_id=1, source_target_pairs={{0,1},{1,0},{2,3},{3,2},{4,5},{5,4},{6,7},{7,6},{8,9},{9,8},{10,11... | collective-permute-start | bytes 1572872 | tf_op jit(solution)/shard_map/ppermute | solution.py:26
  471.6 12.7 %collective-permute-start.25 = (bf16[128,2048]{1,0:T(8,128)(2,1)S(1)}, bf16[128,2048]{1,0:T(8,128)(2,1)S(1)}, u32[]{:S(2)}, u32[]{:S(2)}) collective-permute-start(bf16[128,2048]{1,0:T(8,128)(2,1)S(1)} %get-tuple-element.152), channel_id=1, source_target_pairs={{0,4},{2,6},{4,0},{6,2},{8,12},{10,14},{12,8},{14,10},{16,20},{18,... | collective-permute-start | bytes 1572872 | tf_op jit(solution)/shard_map/ppermute | solution.py:26
  481.1 23.3 %collective-permute-start.24 = (bf16[256,2048]{1,0:T(8,128)(2,1)S(1)}, bf16[256,2048]{1,0:T(8,128)(2,1)S(1)}, u32[]{:S(2)}, u32[]{:S(2)}) collective-permute-start(bf16[256,2048]{1,0:T(8,128)(2,1)S(1)} %pad_maximum_fusion.11), channel_id=1, source_target_pairs={{0,4},{2,6},{4,0},{6,2},{8,12},{10,14},{12,8},{14,10},{16,20},{18,... | collective-permute-start | bytes 3145736 | tf_op jit(solution)/shard_map/ppermute | solution.py:26
  484.4 20.0 %collective-permute-start.26 = (bf16[256,2048]{1,0:T(8,128)(2,1)S(1)}, bf16[256,2048]{1,0:T(8,128)(2,1)S(1)}, u32[]{:S(2)}, u32[]{:S(2)}) collective-permute-start(bf16[256,2048]{1,0:T(8,128)(2,1)S(1)} %pad_maximum_fusion.12.refs_3_), channel_id=1, source_target_pairs={{0,1},{1,0},{2,3},{3,2},{4,5},{5,4},{6,7},{7,6},{8,9},{9,8},{10,11... | collective-permute-start | bytes 3145736 | tf_op jit(solution)/shard_map/ppermute | solution.py:26
  520.1 107.1 %reduce-scatter.11.cloned.1.call-start = ((), (), s32[]{:S(2)}) async-start(), calls=%async_computation.14 | async-start | bytes 2359296 | tf_op jit(solution)/shard_map/reduce_scatter | solution.py:256
  526.3 191.5 %reduce-scatter.15.cloned.1.call-start = ((), (), s32[]{:S(2)}) async-start(), calls=%async_computation.16 | async-start | bytes 9437184 | tf_op jit(solution)/shard_map/reduce_scatter | solution.py:256
  531.5 42.3 %collective-permute-start.27 = (bf16[256,2048]{1,0:T(8,128)(2,1)}, bf16[256,2048]{1,0:T(8,128)(2,1)}, u32[]{:S(2)}, u32[]{:S(2)}) collective-permute-start(bf16[256,2048]{1,0:T(8,128)(2,1)} %pad_maximum_fusion.13), channel_id=1, source_target_pairs={{0,4},{2,6},{4,0},{6,2},{8,12},{10,14},{12,8},{14,10},{16,20},{18,... | collective-permute-start | bytes 3145736 | tf_op jit(solution)/shard_map/ppermute | solution.py:26
  533.1 40.8 %collective-permute-start.28 = (bf16[256,2048]{1,0:T(8,128)(2,1)}, bf16[256,2048]{1,0:T(8,128)(2,1)}, u32[]{:S(2)}, u32[]{:S(2)}) collective-permute-start(bf16[256,2048]{1,0:T(8,128)(2,1)} %slice.273), channel_id=1, source_target_pairs={{0,1},{1,0},{2,3},{3,2},{4,5},{5,4},{6,7},{7,6},{8,9},{9,8},{10,11... | collective-permute-start | bytes 3145736 | tf_op jit(solution)/shard_map/ppermute | solution.py:26
  577.0 24.5 %collective-permute-start.30 = (bf16[128,2048]{1,0:T(8,128)(2,1)}, bf16[128,2048]{1,0:T(8,128)(2,1)}, u32[]{:S(2)}, u32[]{:S(2)}) collective-permute-start(bf16[128,2048]{1,0:T(8,128)(2,1)} %get-tuple-element.150), channel_id=1, source_target_pairs={{0,4},{2,6},{4,0},{6,2},{8,12},{10,14},{12,8},{14,10},{16,20},{18,... | collective-permute-start | bytes 1572872 | tf_op jit(solution)/shard_map/ppermute | solution.py:26
  580.5 21.0 %collective-permute-start.29 = (bf16[128,2048]{1,0:T(8,128)(2,1)}, bf16[128,2048]{1,0:T(8,128)(2,1)}, u32[]{:S(2)}, u32[]{:S(2)}) collective-permute-start(bf16[128,2048]{1,0:T(8,128)(2,1)} %get-tuple-element.129), channel_id=1, source_target_pairs={{0,1},{1,0},{2,3},{3,2},{4,5},{5,4},{6,7},{7,6},{8,9},{9,8},{10,11... | collective-permute-start | bytes 1572872 | tf_op jit(solution)/shard_map/ppermute | solution.py:26
  581.6 22.4 %collective-permute-start.31 = (bf16[128,1536]{1,0:T(8,128)(2,1)}, bf16[128,1536]{1,0:T(8,128)(2,1)}, u32[]{:S(2)}, u32[]{:S(2)}) collective-permute-start(bf16[128,1536]{1,0:T(8,128)(2,1)} %constant_dynamic-slice_fusion.4), channel_id=1, source_target_pairs={{0,4},{2,6},{4,0},{6,2},{8,12},{10,14},{12,8},{14,10},{16,20},{18,... | collective-permute-start | bytes 1179656 | tf_op jit(solution)/shard_map/ppermute | solution.py:26
  583.3 25.6 %collective-permute-start.32 = (bf16[128,1536]{1,0:T(8,128)(2,1)S(1)}, bf16[128,1536]{1,0:T(8,128)(2,1)}, u32[]{:S(2)}, u32[]{:S(2)}) collective-permute-start(bf16[128,1536]{1,0:T(8,128)(2,1)S(1)} %constant_dynamic-slice_fusion.3), channel_id=1, source_target_pairs={{0,4},{2,6},{4,0},{6,2},{8,12},{10,14},{12,8},{14,10},{16,20},{18,... | collective-permute-start | bytes 1179656 | tf_op jit(solution)/shard_map/ppermute | solution.py:26
  592.3 21.4 %collective-permute-start.33 = (bf16[128,1536]{1,0:T(8,128)(2,1)}, bf16[128,1536]{1,0:T(8,128)(2,1)}, u32[]{:S(2)}, u32[]{:S(2)}) collective-permute-start(bf16[128,1536]{1,0:T(8,128)(2,1)} %constant_dynamic-slice_fusion.2), channel_id=1, source_target_pairs={{0,4},{2,6},{4,0},{6,2},{8,12},{10,14},{12,8},{14,10},{16,20},{18,... | collective-permute-start | bytes 1179656 | tf_op jit(solution)/shard_map/ppermute | solution.py:26
  627.2 174.9 %reduce-scatter.17.cloned.1.call-start = ((), (), s32[]{:S(2)}) async-start(), calls=%async_computation.17 | async-start | bytes 4718592 | tf_op jit(solution)/shard_map/reduce_scatter | solution.py:256
  739.4 23.1 %collective-permute-start.34 = (bf16[256,2048]{1,0:T(8,128)(2,1)S(1)}, bf16[256,2048]{1,0:T(8,128)(2,1)S(1)}, u32[]{:S(2)}, u32[]{:S(2)}) collective-permute-start(bf16[256,2048]{1,0:T(8,128)(2,1)S(1)} %pad_maximum_fusion.14), channel_id=1, source_target_pairs={{0,4},{2,6},{4,0},{6,2},{8,12},{10,14},{12,8},{14,10},{16,20},{18,... | collective-permute-start | bytes 3145736 | tf_op jit(solution)/shard_map/ppermute | solution.py:26
  741.1 34.7 %copy-start.10 = (f32[256,2048]{1,0:T(8,128)S(1)}, f32[256,2048]{1,0:T(8,128)}, u32[]{:S(2)}) copy-start(f32[256,2048]{1,0:T(8,128)} %copy-done.9) | copy-start | bytes 6291460
  741.1 34.7 %copy-start.19 = (f32[1,4,2,2,128]{4,3,2,1,0:T(2,128)S(1)}, f32[1,4,2,2,128]{4,3,2,1,0:T(2,128)}, u32[]{:S(2)}) copy-start(f32[1,4,2,2,128]{4,3,2,1,0:T(2,128)} %copy-done.18) | copy-start | bytes 24580
  741.1 23.9 %collective-permute-start.36 = (bf16[256,2048]{1,0:T(8,128)(2,1)S(1)}, bf16[256,2048]{1,0:T(8,128)(2,1)S(1)}, u32[]{:S(2)}, u32[]{:S(2)}) collective-permute-start(bf16[256,2048]{1,0:T(8,128)(2,1)S(1)} %slice.341), channel_id=1, source_target_pairs={{0,1},{1,0},{2,3},{3,2},{4,5},{5,4},{6,7},{7,6},{8,9},{9,8},{10,11... | collective-permute-start | bytes 3145736 | tf_op jit(solution)/shard_map/ppermute | solution.py:26
  762.9 12.2 %collective-permute-start.35 = (bf16[128,2048]{1,0:T(8,128)(2,1)S(1)}, bf16[128,2048]{1,0:T(8,128)(2,1)S(1)}, u32[]{:S(2)}, u32[]{:S(2)}) collective-permute-start(bf16[128,2048]{1,0:T(8,128)(2,1)S(1)} %get-tuple-element.127), channel_id=1, source_target_pairs={{0,1},{1,0},{2,3},{3,2},{4,5},{5,4},{6,7},{7,6},{8,9},{9,8},{10,11... | collective-permute-start | bytes 1572872 | tf_op jit(solution)/shard_map/ppermute | solution.py:26
  765.4 39.1 %copy-start.30 = (bf16[256,512]{1,0:T(8,128)(2,1)S(1)}, bf16[256,512]{1,0:T(8,128)(2,1)}, u32[]{:S(2)}) copy-start(bf16[256,512]{1,0:T(8,128)(2,1)} %reduce-scatter.11.cloned.1.call-done.both_ref) | copy-start | bytes 786436
  765.5 10.3 %collective-permute-start.37 = (bf16[128,2048]{1,0:T(8,128)(2,1)S(1)}, bf16[128,2048]{1,0:T(8,128)(2,1)S(1)}, u32[]{:S(2)}, u32[]{:S(2)}) collective-permute-start(bf16[128,2048]{1,0:T(8,128)(2,1)S(1)} %get-tuple-element.148), channel_id=1, source_target_pairs={{0,4},{2,6},{4,0},{6,2},{8,12},{10,14},{12,8},{14,10},{16,20},{18,... | collective-permute-start | bytes 1572872 | tf_op jit(solution)/shard_map/ppermute | solution.py:26
  780.8 1.3 collective-permute-start.40
  782.0 3.8 collective-permute-start.41
  785.9 6.5 collective-permute-start.42
  792.4 4.7 collective-permute-start.43
  797.1 3.8 collective-permute-start.44
  803.0 10.3 %collective-permute-start.38 = (bf16[128,1024]{1,0:T(8,128)(2,1)S(1)}, bf16[128,1024]{1,0:T(8,128)(2,1)S(1)}, u32[]{:S(2)}, u32[]{:S(2)}) collective-permute-start(bf16[128,1024]{1,0:T(8,128)(2,1)S(1)} %constant_dynamic-slice_fusion.1), channel_id=1, source_target_pairs={{0,4},{2,6},{4,0},{6,2},{8,12},{10,14},{12,8},{14,10},{16,20},{18,... | collective-permute-start | bytes 786440 | tf_op jit(solution)/shard_map/ppermute | solution.py:26
  804.6 6.3 collective-permute-start.39
  (39 other events, 269.0 us)
Sparse Core Ops, SparseCore 0:
  21.6 48.3 all-gather.6
  72.1 27.9 all-gather.8
  102.3 81.4 all-gather.10
  185.2 63.2 all-gather.12
  250.0 63.3 all-gather.14
  315.4 63.3 all-gather.16
  381.1 68.3 reduce-scatter.6
  451.8 68.1 reduce-scatter.8
  522.3 68.1 reduce-scatter.12
  592.7 34.4 reduce-scatter.10
  629.5 88.2 reduce-scatter.14
  738.0 48.4 reduce-scatter.16

commit v6 on v5

--- a/solution.py
+++ b/solution.py
@@ -192,7 +192,7 @@
     wide_ref, gain_out = refs[3 + lows + highs], refs[-1]
     low_ref = refs[4 + lows + highs] if count is None else None
     block = x_ref.shape[0] // 2
-    total = jnp.zeros((ROWS, x_ref.shape[1]), F32)
+    total = jnp.zeros((ROWS, x_ref.shape[1]), F32) if count is None else 0
     for half, terms in ((0, refs[3 : 3 + lows]), (1, refs[3 + lows : 3 + lows + highs])):
 
         def body(at, carry):
@@ -210,10 +210,11 @@
                 low_ref[rows, :] = out.astype(BF16)
             else:
                 wide_ref[rows, :] = natural_columns(out, count)
-            return carry + grad * unit
+            return carry + grad * unit if count is None else carry
 
         total = over_rows(block, body, total)
-    gain_out[...] = jnp.sum(total, axis=0, keepdims=True)
+    if count is None:
+        gain_out[...] = jnp.sum(total, axis=0, keepdims=True)
 
 
 def row_pass(kernel, args, outs, name):
@@ -758,34 +759,35 @@
         (rows_output, d_h1_query, out_tokens, shard_down, shard_gate, shard_up),
     )
     d_kv = ctx_scatter(d_kv, ways)
+    grad_query = dot_rows(h1, d_qp).astype(BF16)
+    rows_query = scatter_weight(after(grad_query, d_kv), ways)
     d_kvp, gain_k_sum = head_prep_back(d_kv, raw, cos, sin, gain_k, q_width // kv_width, True)
+    grad_kv = dot_rows(h1, d_kvp).astype(BF16)
+    rows_kv = scatter_weight(grad_kv, ways)
     d_h1 = (
-        d_h1_query + dot_cols(d_kvp, full_qkv[:, q_width:])
+        d_h1_query + dot_cols(after(d_kvp, grad_kv), full_qkv[:, q_width:])
     ).astype(BF16)
+    gain_attn = jnp.sum(d_h1.astype(F32) * h1.astype(F32), axis=0) / gain_attn_row[0]
+    gains = butterfly_sum(
+        jnp.concatenate([gain_attn, gain_mlp[0], gain_q_sum[0], gain_k_sum[0]])
+    )
     lows, highs = return_rows(d_h1, ways)
-    d_raw = jnp.concatenate([d_qp, d_kvp], axis=1)
-    grad_qkv = dot_rows(after(h1, d_h1), d_raw).astype(BF16)
-
-    rows_qkv = scatter_weight(grad_qkv, ways)
-    grad_tokens, gain_attn = row_pass(
+    lows[0] = after(lows[0], gains)
+    grad_tokens = row_pass(
         functools.partial(back_kernel, len(lows), len(highs), ctx_count),
         (d_x2, inputs, gain_attn_row, *lows, *highs),
-        (row_f32, gain_shape),
+        row_f32,
         "entry_back",
     )
-    rows_output, rows_qkv = after((rows_output, rows_qkv), (lows, highs))
+    rows_output, rows_query, rows_kv = after((rows_output, rows_query, rows_kv), (lows, highs))
     shard_output = one(rows_output, ways)
-    plan = [(0, q_width, 0, 0)]
+    shard_query = one(rows_query, ways)
+    plan = []
     for h in range(groups):
         for t in (0, 1):
-            plan.append((q_width + (2 * h + t) * HD, HD, 1 + t, h * HD))
-    shard_query, shard_key, shard_value = own_rows(
-        rows_qkv, pair, ways, plan, [q_width, groups * HD, groups * HD]
-    )
+            plan.append(((2 * h + t) * HD, HD, t, h * HD))
+    shard_key, shard_value = own_rows(rows_kv, pair, ways, plan, [groups * HD, groups * HD])
     grad_tokens = grad_tokens.reshape(tokens.shape)
-    gains = butterfly_sum(
-        jnp.concatenate([gain_attn[0], gain_mlp[0], gain_q_sum[0], gain_k_sum[0]])
-    )
     return (
         out_tokens,
         grad_tokens,

time: 832 us -> 829 us (level)
    ppermute x45 -> x46, waiting for transfers between devices: 206 us -> 198 us  [xor_send(): return lax.ppermute(value, axis, [(i, i ^ step) for i in range(count)])]
    dot_general x5 -> x6, matrix products: 41.9 us -> 47.6 us  [dot_rows(): lax.dot_general(left, right, (((0,), (0,)), ((), ())), preferred_element_...]
    reduce_scatter x6 -> x7, waiting for transfers between devices: 119 us -> 114 us  [ctx_scatter(): lax.psum_scatter(rows, 'ctx', scatter_dimension=0, tiled=True, axis_index...]
    unnamed x92 -> x96, local copies, waits for them, and re-layouts: 19.5 us -> 21.6 us
    ppermute x45 -> x46, starting transfers between devices: 60.4 us -> 60.9 us  [xor_send(): return lax.ppermute(value, axis, [(i, i ^ step) for i in range(count)])]
  transfers between devices with their start and end apart: 57 -> 59, of which waited for: 43 -> 40; matrix products, arithmetic and copies ran while one was open for 25% -> 27% of each run, Pallas kernels for 12% -> 13%
where the time goes in v6:
time: 829 us; the launch traced here: 820 us
  waiting for transfers between devices  384 us (46%)
  matrix products  148 us (18%)
  Pallas kernels  105 us (13%)
  starting transfers between devices  62.7 us (8%)
  local copies, waits for them, and re-layouts  59.4 us (7%)
  other arithmetic  46.7 us (6%)
  between operations  15 us (2%)
    ppermute x46, waiting for transfers between devices, xor_send(): return lax.ppermute(value, axis, [(i, i ^ step) for i in range(count)])  198 us
    reduce_scatter x7, waiting for transfers between devices, ctx_scatter(): lax.psum_scatter(rows, 'ctx', scatter_dimension=0, tiled=True, axis_index...  114 us
    all_gather x6, waiting for transfers between devices, ctx_gather(): lax.all_gather(rows, 'ctx', axis=0, tiled=True, axis_index_groups=groups)  71.6 us
    ppermute x46, starting transfers between devices, xor_send(): return lax.ppermute(value, axis, [(i, i ^ step) for i in range(count)])  60.9 us
    dot_general x5, matrix products, dot(): return jnp.dot(left, right, preferred_element_type=F32)  52.4 us
    dot_general x6, matrix products, dot_cols(): lax.dot_general(left, right, (((1,), (1,)), ((), ())), preferred_element_...  47.7 us
    dot_general x6, matrix products, dot_rows(): lax.dot_general(left, right, (((0,), (0,)), ((), ())), preferred_element_...  47.6 us
    pallas_call x1, Pallas kernels, attend_back(): pl.pallas_call(functools.partial(backward_kernel, ways, count), out_shape...  32.6 us
  transfers between devices with their start and end apart: 59, of which 40 were waited for; matrix products, arithmetic and copies ran while one was open for 27% of the time, Pallas kernels for 13%

profile of v6, /device:TPU:0, one launch (start us, length us, event | category | flops | bytes accessed | tf_op | source)
XLA Modules:
  0.0 819.7 jit_solution(12256456342443092542)
XLA Ops:
  11.2 3.1 collective-permute-start.4
  14.2 6.3 collective-permute-done.4
  32.9 2.7 constant_dynamic-update-slice_fusion.7
  35.5 2.7 constant_dynamic-update-slice_fusion.6
  38.2 2.7 constant_dynamic-update-slice_fusion.5
  44.2 2.7 constant_dynamic-update-slice_fusion.4
  46.9 2.7 constant_dynamic-update-slice_fusion.3
  49.6 2.7 constant_dynamic-update-slice_fusion.2
  52.3 2.7 constant_dynamic-update-slice_fusion.1
  54.9 2.7 constant_dynamic-update-slice_fusion
  60.9 4.8 collective-permute-done.1.refs_0_
  70.0 9.9 %fusion.69.raw_ref = f32[1024,1024]{1,0:T(8,128)} fusion(bf16[1024,2048]{1,0:T(8,128)(2,1)} %copy-done, bf16[2048,1024]{1,0:T(8,128)(2,1)} %all-gather.7.cloned.1.call-done), kind=kOutput, calls=%fused_computation.200 | convolution fusion | flops 4294967296 | bytes 12582912 | tf_op jit(solution)/shard_map/dot_general | solution.py:318
  79.9 6.3 head_prep.1
  86.2 14.0 %all-gather.9.cloned.1.call-done = bf16[2048,512]{1,0:T(8,128)(2,1)} async-done(((bf16[256,512]{1,0:T(8,128)(2,1)}), bf16[2048,512]{1,0:T(8,128)(2,1)}) %all-gather.9.cloned.1.call-update) | async-done | bytes 2097168 | tf_op jit(solution)/shard_map/all_gather | solution.py:252
  102.1 26.6 %collective-permute-done.5 = bf16[128,4608]{1,0:T(8,128)(2,1)S(1)} collective-permute-done((bf16[128,4608]{1,0:T(8,128)(2,1)S(1)}, bf16[128,4608]{1,0:T(8,128)(2,1)S(1)}, u32[]{:S(2)}, u32[]{:S(2)}) %collective-permute-start.5) | collective-permute-done | bytes 1179680 | tf_op jit(solution)/shard_map/ppermute | solution.py:26
  135.0 10.4 %collective-permute-done.6.refs_2_ = bf16[128,2048]{1,0:T(8,128)(2,1)S(1)} collective-permute-done((bf16[128,2048]{1,0:T(8,128)(2,1)S(1)}, bf16[128,2048]{1,0:T(8,128)(2,1)S(1)}, u32[]{:S(2)}, u32[]{:S(2)}) %collective-permute-start.6) | collective-permute-done | bytes 524320 | tf_op jit(solution)/shard_map/ppermute | solution.py:26
  154.3 10.2 %stack.31.info_ref = s32[26]{0:T(128)S(1)} concatenate(s32[1]{0:T(128)} %bitcast.8.pair_ref, s32[1]{0:T(128)} %bitcast.9, s32[1]{0:T(128)} %bitcast.10, s32[1]{0:T(128)} %bitcast.11, s32[1]{0:T(128)} %bitcast.12, s32[1]{0:T(128)} %bitcast.13, s32[1]{0:T(128)} %bitcast.14, s32[1]{0:T(128)} %bitcast.15, s32[1]{0:T(128)} %bitcast.16, s32[1]{0:T(128)} %bitcast.17, s32[1]{0:T(128)} %bitcast.18, ...), dimensions={0} | concatenate | bytes 208 | tf_op jit(solution)/shard_map/stack | solution.py:680
  164.5 6.0 collective-permute-done.7.refs_0_
  175.5 8.3 %all-gather.11.cloned.1.call-done = bf16[8192,512]{1,0:T(8,128)(2,1)} async-done(((bf16[1024,512]{1,0:T(8,128)(2,1)}), bf16[8192,512]{1,0:T(8,128)(2,1)}) %all-gather.11.cloned.1.call-update) | async-done | bytes 8388624 | tf_op jit(solution)/shard_map/all_gather | solution.py:252
  185.0 24.5 %attend.1 = (bf16[2,4,128,512]{3,2,1,0:T(8,128)(2,1)S(1)}, f32[2,2,4,1,256]{4,3,2,1,0:T(1,128)S(1)}) custom-call(s32[26]{0:T(128)S(1)} %stack.31.info_ref, bf16[2,4,128,512]{3,2,1,0:T(8,128)(2,1)S(1)} %bitcast.127, bf16[8,2,4,128,512]{4,3,2,1,0:T(8,128)(2,1)} %bitcast.148), custom_call_target="tpu_custom_call" | custom-call | flops 4294967296 | bytes 8388608 | tf_op jit(solution)/shard_map/attend/pallas_call | solution.py:553
  217.5 17.6 %collective-permute-done.11 = bf16[256,2048]{1,0:T(8,128)(2,1)S(1)} collective-permute-done((bf16[256,2048]{1,0:T(8,128)(2,1)}, bf16[256,2048]{1,0:T(8,128)(2,1)S(1)}, u32[]{:S(2)}, u32[]{:S(2)}) %collective-permute-start.11) | collective-permute-done | bytes 1048608 | tf_op jit(solution)/shard_map/ppermute | solution.py:26
  241.5 9.9 %collective-permute-done.12.refs_3_ = bf16[128,2048]{1,0:T(8,128)(2,1)S(1)} collective-permute-done((bf16[128,2048]{1,0:T(8,128)(2,1)S(1)}, bf16[128,2048]{1,0:T(8,128)(2,1)S(1)}, u32[]{:S(2)}, u32[]{:S(2)}) %collective-permute-start.12) | collective-permute-done | bytes 524320 | tf_op jit(solution)/shard_map/ppermute | solution.py:26
  255.5 10.8 %collective-permute-done.15.refs_2_ = bf16[128,2048]{1,0:T(8,128)(2,1)S(1)} collective-permute-done((bf16[128,2048]{1,0:T(8,128)(2,1)S(1)}, bf16[128,2048]{1,0:T(8,128)(2,1)S(1)}, u32[]{:S(2)}, u32[]{:S(2)}) %collective-permute-start.15) | collective-permute-done | bytes 524320 | tf_op jit(solution)/shard_map/ppermute | solution.py:26
  268.7 22.3 %collective-permute-done.16.refs_0_ = bf16[256,2048]{1,0:T(8,128)(2,1)S(1)} collective-permute-done((bf16[256,2048]{1,0:T(8,128)(2,1)S(1)}, bf16[256,2048]{1,0:T(8,128)(2,1)S(1)}, u32[]{:S(2)}, u32[]{:S(2)}) %collective-permute-start.16) | collective-permute-done | bytes 1048608 | tf_op jit(solution)/shard_map/ppermute | solution.py:26
  291.0 2.8 collective-permute-done.18.refs_4_
  296.0 11.8 %fusion.70 = f32[1024,1536]{1,0:T(8,128)} fusion(bf16[1024,2048]{1,0:T(8,128)(2,1)} %copy-done.3, bf16[2048,1536]{1,0:T(8,128)(2,1)} %all-gather.13.cloned.1.call-done), kind=kOutput, calls=%fused_computation.201 | convolution fusion | flops 6442450944 | bytes 16777216 | tf_op jit(solution)/shard_map/dot_general | solution.py:318
  307.8 6.2 all-gather.15.cloned.1.call-done
  314.0 13.2 %multiply_convert_fusion.2 = (bf16[1024,1536]{1,0:T(8,128)(2,1)S(1)}, f32[1024,1536]{1,0:T(8,128)}) fusion(f32[1024,1536]{1,0:T(8,128)} %fusion.70, bf16[1024,2048]{1,0:T(8,128)(2,1)} %copy-done.3, bf16[2048,1536]{1,0:T(8,128)(2,1)} %all-gather.15.cloned.1.call-done), kind=kOutput, calls=%fused_computation.8 | convolution fusion | flops 6450315264 | bytes 26214400 | tf_op jit(solution)/shard_map/dot_general | solution.py:318
  328.8 8.8 %convolution_convert_fusion.2 = bf16[2048,1536]{1,0:T(8,128)(2,1)} fusion(bf16[1024,2048]{1,0:T(8,128)(2,1)S(1)} %copy-done.2, bf16[1024,1536]{1,0:T(8,128)(2,1)S(1)} %get-tuple-element.75), kind=kOutput, calls=%fused_computation.5 | convolution fusion | flops 6445596672 | bytes 13631488 | tf_op jit(solution)/shard_map/dot_general | solution.py:322
  337.9 41.6 %all-gather.17.cloned.1.call-done = bf16[2048,1536]{1,0:T(8,128)(2,1)} async-done(((bf16[256,1536]{1,0:T(8,128)(2,1)}), bf16[2048,1536]{1,0:T(8,128)(2,1)}) %all-gather.17.cloned.1.call-update) | async-done | bytes 6291472 | tf_op jit(solution)/shard_map/all_gather | solution.py:252
  379.5 14.2 %multiply_convert_fusion = (bf16[1024,1536]{1,0:T(8,128)(2,1)S(1)}, bf16[1024,1536]{1,0:T(8,128)(2,1)S(1)}) fusion(f32[1024,1536]{1,0:T(8,128)} %fusion.70, f32[1024,1536]{1,0:T(8,128)} %get-tuple-element.202, bf16[1024,2048]{1,0:T(8,128)(2,1)} %copy-done.1, bf16[2048,1536]{1,0:T(8,128)(2,1)} %all-gather.17.cloned.1.call-done), kind=kOutput, calls=%fused_computation.6 | convolution fusion | flops 6462898176 | bytes 29360128 | tf_op jit(solution)/shard_map/dot_general | solution.py:318
  393.6 10.0 %fusion.71 = f32[1024,2048]{1,0:T(8,128)S(1)} fusion(bf16[1024,1536]{1,0:T(8,128)(2,1)S(1)} %get-tuple-element.126, bf16[2048,1536]{1,0:T(8,128)(2,1)} %all-gather.13.cloned.1.call-done), kind=kOutput, calls=%fused_computation.202 | convolution fusion | flops 6442450944 | bytes 17825792 | tf_op jit(solution)/shard_map/dot_general | solution.py:326
  403.6 8.9 %add_convert_fusion.1 = bf16[1024,2048]{1,0:T(8,128)(2,1)S(1)} fusion(f32[1024,2048]{1,0:T(8,128)S(1)} %fusion.71, bf16[1024,1536]{1,0:T(8,128)(2,1)S(1)} %get-tuple-element.125, bf16[2048,1536]{1,0:T(8,128)(2,1)} %all-gather.15.cloned.1.call-done), kind=kOutput, calls=%fused_computation.2 | convolution fusion | flops 6446645248 | bytes 22020096 | tf_op jit(solution)/shard_map/dot_general | solution.py:326
  419.3 8.8 %convolution_convert_fusion = bf16[2048,1536]{1,0:T(8,128)(2,1)} fusion(bf16[1024,2048]{1,0:T(8,128)(2,1)S(1)} %copy-done.4, bf16[1024,1536]{1,0:T(8,128)(2,1)S(1)} %get-tuple-element.125), kind=kOutput, calls=%fused_computation.3 | convolution fusion | flops 6445596672 | bytes 13631488 | tf_op jit(solution)/shard_map/dot_general | solution.py:322
  428.1 11.7 %convolution_convert_fusion.1 = bf16[2048,1536]{1,0:T(8,128)(2,1)} fusion(bf16[1024,2048]{1,0:T(8,128)(2,1)} %copy-done.3, bf16[1024,1536]{1,0:T(8,128)(2,1)} %copy-done.45), kind=kOutput, calls=%fused_computation.4 | convolution fusion | flops 6445596672 | bytes 13631488 | tf_op jit(solution)/shard_map/dot_general | solution.py:322
  446.2 2.9 add_convert_fusion.10
  453.2 9.1 %collective-permute-done.22.refs_6_ = bf16[128,2048]{1,0:T(8,128)(2,1)S(1)} collective-permute-done((bf16[128,2048]{1,0:T(8,128)(2,1)}, bf16[128,2048]{1,0:T(8,128)(2,1)S(1)}, u32[]{:S(2)}, u32[]{:S(2)}) %collective-permute-start.22) | collective-permute-done | bytes 524320 | tf_op jit(solution)/shard_map/ppermute | solution.py:26
  465.6 3.7 middle_back.1
  471.5 8.9 %collective-permute-done.23.refs_2_ = bf16[128,2048]{1,0:T(8,128)(2,1)S(1)} collective-permute-done((bf16[128,2048]{1,0:T(8,128)(2,1)S(1)}, bf16[128,2048]{1,0:T(8,128)(2,1)S(1)}, u32[]{:S(2)}, u32[]{:S(2)}) %collective-permute-start.23) | collective-permute-done | bytes 524320 | tf_op jit(solution)/shard_map/ppermute | solution.py:26
  480.9 2.8 collective-permute-done.25
  483.9 11.1 %convolution_convert_fusion.3 = bf16[1024,2048]{1,0:T(8,128)(2,1)} fusion(bf16[1024,1536]{1,0:T(8,128)(2,1)S(1)} %copy-done.47, bf16[2048,1536]{1,0:T(8,128)(2,1)} %all-gather.17.cloned.1.call-done), kind=kOutput, calls=%fused_computation.11 | convolution fusion | flops 6444548096 | bytes 13631488 | tf_op jit(solution)/shard_map/dot_general | solution.py:326
  495.0 8.9 %collective-permute-done.24.refs_0_ = bf16[256,2048]{1,0:T(8,128)(2,1)S(1)} collective-permute-done((bf16[256,2048]{1,0:T(8,128)(2,1)S(1)}, bf16[256,2048]{1,0:T(8,128)(2,1)S(1)}, u32[]{:S(2)}, u32[]{:S(2)}) %collective-permute-start.24) | collective-permute-done | bytes 1048608 | tf_op jit(solution)/shard_map/ppermute | solution.py:26
  506.1 3.3 convolution_convert_fusion.8
  509.4 11.3 %reduce-scatter.10.cloned.1.call-done.both_ref = bf16[256,1536]{1,0:T(8,128)(2,1)} async-done(((bf16[2048,1536]{1,0:T(8,128)(2,1)}), bf16[256,1536]{1,0:T(8,128)(2,1)}) %reduce-scatter.10.cloned.1.call-update) | async-done | bytes 786448 | tf_op jit(solution)/shard_map/reduce_scatter | solution.py:257
  520.8 5.9 convolution_convert_fusion.7
  535.0 32.6 %attend_back.1 = (f32[2,4,128,512]{3,2,1,0:T(8,128)}, bf16[8,2,4,128,512]{4,3,2,1,0:T(8,128)(2,1)}) custom-call(s32[26]{0:T(128)} %copy-done.18, bf16[2,4,128,512]{3,2,1,0:T(8,128)(2,1)} %bitcast.126, bf16[2,4,128,512]{3,2,1,0:T(8,128)(2,1)} %bitcast.150, bf16[2,4,128,512]{3,2,1,0:T(8,128)(2,1)} %copy-done.20, f32[2,2,4,1,256]{4,3,2,1,0:T(1,128)} %copy-done.22, ...), custom_call_target="tpu_custom_call" | custom-call | flops 10737418240 | bytes 16777216 | tf_op jit(solution)/shard_map/attend_back/pallas_call | solution.py:576
  567.6 5.9 head_prep_back.2
  577.8 2.8 add_convert_fusion.8
  583.8 7.4 reduce-scatter.14.cloned.1.call-done.both_ref
  594.5 7.5 fusion.2
  602.0 2.6 result.1
  609.5 5.8 collective-permute-done.33.other_ref
  617.8 10.1 %reduce-scatter.12.cloned.1.call-done.both_ref = bf16[256,512]{1,0:T(8,128)(2,1)} async-done(((bf16[2048,512]{1,0:T(8,128)(2,1)}), bf16[256,512]{1,0:T(8,128)(2,1)}) %reduce-scatter.12.cloned.1.call-update) | async-done | bytes 262160 | tf_op jit(solution)/shard_map/reduce_scatter | solution.py:257
  629.2 5.9 convolution_convert_fusion.5
  635.1 83.3 %reduce-scatter.16.cloned.1.call-done.d_ref = bf16[1024,512]{1,0:T(8,128)(2,1)} async-done(((bf16[8192,512]{1,0:T(8,128)(2,1)}), bf16[1024,512]{1,0:T(8,128)(2,1)}) %reduce-scatter.16.cloned.1.call-update) | async-done | bytes 1048592 | tf_op jit(solution)/shard_map/reduce_scatter | solution.py:257
  718.7 4.7 head_prep_back.3
  723.4 6.6 convolution_convert_fusion.6
  730.0 7.9 multiply_reduce_fusion
  741.5 19.6 %collective-permute-done.34 = bf16[256,2048]{1,0:T(8,128)(2,1)S(1)} collective-permute-done((bf16[256,2048]{1,0:T(8,128)(2,1)S(1)}, bf16[256,2048]{1,0:T(8,128)(2,1)S(1)}, u32[]{:S(2)}, u32[]{:S(2)}) %collective-permute-start.34) | collective-permute-done | bytes 1048608 | tf_op jit(solution)/shard_map/ppermute | solution.py:26
  766.5 7.9 collective-permute-done.36
  774.4 5.0 collective-permute-start.37
  781.4 2.9 collective-permute-start.38
  784.3 2.6 collective-permute-done.38
  801.4 4.8 entry_back.1
  (296 shorter events, 161.0 us)
Async XLA Ops:
  7.2 62.8 %all-gather.7.cloned.1.call-start = ((), (), s32[]{:S(2)}) async-start(), calls=%async_computation.7 | async-start | bytes 4718592 | tf_op jit(solution)/shard_map/all_gather | solution.py:252
  11.2 9.4 %collective-permute-start.4 = (bf16[128,1024]{1,0:T(8,128)(2,1)S(1)}, bf16[128,1024]{1,0:T(8,128)(2,1)S(1)}, u32[]{:S(2)}, u32[]{:S(2)}) collective-permute-start(bf16[128,1024]{1,0:T(8,128)(2,1)S(1)} %pad_maximum_fusion.20), channel_id=1, source_target_pairs={{0,4},{2,6},{4,0},{6,2},{8,12},{10,14},{12,8},{14,10},{16,20},{18,... | collective-permute-start | bytes 786440 | tf_op jit(solution)/shard_map/ppermute | solution.py:26
  21.5 78.7 %all-gather.9.cloned.1.call-start = ((), (), s32[]{:S(2)}) async-start(), calls=%async_computation.8 | async-start | bytes 2359296 | tf_op jit(solution)/shard_map/all_gather | solution.py:252
  21.6 5.6 collective-permute-start.10
  28.0 155.8 %all-gather.11.cloned.1.call-start = ((), (), s32[]{:S(2)}) async-start(), calls=%async_computation.9 | async-start | bytes 9437184 | tf_op jit(solution)/shard_map/all_gather | solution.py:252
  29.4 12.6 %collective-permute-start = (bf16[128,2048]{1,0:T(8,128)(2,1)S(1)}, bf16[128,2048]{1,0:T(8,128)(2,1)S(1)}, u32[]{:S(2)}, u32[]{:S(2)}) collective-permute-start(bf16[128,2048]{1,0:T(8,128)(2,1)S(1)} %get-tuple-element.163.refs_1_), channel_id=1, source_target_pairs={{0,1},{1,0},{2,3},{3,2},{4,5},{5,4},{6,7},{7,6},{8,9},{9,8},{10,11... | collective-permute-start | bytes 1572872 | tf_op jit(solution)/shard_map/ppermute | solution.py:26
  30.9 12.8 %collective-permute-start.2 = (bf16[128,2048]{1,0:T(8,128)(2,1)S(1)}, bf16[128,2048]{1,0:T(8,128)(2,1)S(1)}, u32[]{:S(2)}, u32[]{:S(2)}) collective-permute-start(bf16[128,2048]{1,0:T(8,128)(2,1)S(1)} %get-tuple-element.162), channel_id=1, source_target_pairs={{0,4},{2,6},{4,0},{6,2},{8,12},{10,14},{12,8},{14,10},{16,20},{18,... | collective-permute-start | bytes 1572872 | tf_op jit(solution)/shard_map/ppermute | solution.py:26
  42.0 23.6 %collective-permute-start.1 = (bf16[256,2048]{1,0:T(8,128)(2,1)S(1)}, bf16[256,2048]{1,0:T(8,128)(2,1)S(1)}, u32[]{:S(2)}, u32[]{:S(2)}) collective-permute-start(bf16[256,2048]{1,0:T(8,128)(2,1)S(1)} %pad_maximum_fusion.3), channel_id=1, source_target_pairs={{0,4},{2,6},{4,0},{6,2},{8,12},{10,14},{12,8},{14,10},{16,20},{18,... | collective-permute-start | bytes 3145736 | tf_op jit(solution)/shard_map/ppermute | solution.py:26
  43.8 22.3 %collective-permute-start.3 = (bf16[256,2048]{1,0:T(8,128)(2,1)S(1)}, bf16[256,2048]{1,0:T(8,128)(2,1)S(1)}, u32[]{:S(2)}, u32[]{:S(2)}) collective-permute-start(bf16[256,2048]{1,0:T(8,128)(2,1)S(1)} %pad_maximum_fusion.4.refs_3_), channel_id=1, source_target_pairs={{0,1},{1,0},{2,3},{3,2},{4,5},{5,4},{6,7},{7,6},{8,9},{9,8},{10,11... | collective-permute-start | bytes 3145736 | tf_op jit(solution)/shard_map/ppermute | solution.py:26
  100.2 195.8 %all-gather.13.cloned.1.call-start = ((), (), s32[]{:S(2)}) async-start(), calls=%async_computation.10 | async-start | bytes 7077888 | tf_op jit(solution)/shard_map/all_gather | solution.py:252
  100.6 28.2 %collective-permute-start.5 = (bf16[128,4608]{1,0:T(8,128)(2,1)S(1)}, bf16[128,4608]{1,0:T(8,128)(2,1)S(1)}, u32[]{:S(2)}, u32[]{:S(2)}) collective-permute-start(bf16[128,4608]{1,0:T(8,128)(2,1)S(1)} %pad_maximum_fusion.2), channel_id=1, source_target_pairs={{0,4},{2,6},{4,0},{6,2},{8,12},{10,14},{12,8},{14,10},{16,20},{18,... | collective-permute-start | bytes 3538952 | tf_op jit(solution)/shard_map/ppermute | solution.py:26
  130.8 183.2 %all-gather.15.cloned.1.call-start = ((), (), s32[]{:S(2)}) async-start(), calls=%async_computation.11 | async-start | bytes 7077888 | tf_op jit(solution)/shard_map/all_gather | solution.py:252
  131.4 248.1 %all-gather.17.cloned.1.call-start = ((), (), s32[]{:S(2)}) async-start(), calls=%async_computation.12 | async-start | bytes 7077888 | tf_op jit(solution)/shard_map/all_gather | solution.py:252
  132.0 13.4 %collective-permute-start.6 = (bf16[128,2048]{1,0:T(8,128)(2,1)S(1)}, bf16[128,2048]{1,0:T(8,128)(2,1)S(1)}, u32[]{:S(2)}, u32[]{:S(2)}) collective-permute-start(bf16[128,2048]{1,0:T(8,128)(2,1)S(1)} %get-tuple-element.161.refs_1_), channel_id=1, source_target_pairs={{0,1},{1,0},{2,3},{3,2},{4,5},{5,4},{6,7},{7,6},{8,9},{9,8},{10,11... | collective-permute-start | bytes 1572872 | tf_op jit(solution)/shard_map/ppermute | solution.py:26
  133.5 14.4 %collective-permute-start.8 = (bf16[128,2048]{1,0:T(8,128)(2,1)S(1)}, bf16[128,2048]{1,0:T(8,128)(2,1)S(1)}, u32[]{:S(2)}, u32[]{:S(2)}) collective-permute-start(bf16[128,2048]{1,0:T(8,128)(2,1)S(1)} %get-tuple-element.160), channel_id=1, source_target_pairs={{0,4},{2,6},{4,0},{6,2},{8,12},{10,14},{12,8},{14,10},{16,20},{18,... | collective-permute-start | bytes 1572872 | tf_op jit(solution)/shard_map/ppermute | solution.py:26
  146.4 24.1 %collective-permute-start.7 = (bf16[256,2048]{1,0:T(8,128)(2,1)}, bf16[256,2048]{1,0:T(8,128)(2,1)}, u32[]{:S(2)}, u32[]{:S(2)}) collective-permute-start(bf16[256,2048]{1,0:T(8,128)(2,1)} %pad_maximum_fusion.5), channel_id=1, source_target_pairs={{0,4},{2,6},{4,0},{6,2},{8,12},{10,14},{12,8},{14,10},{16,20},{18,... | collective-permute-start | bytes 3145736 | tf_op jit(solution)/shard_map/ppermute | solution.py:26
  147.9 23.7 %collective-permute-start.9 = (bf16[256,2048]{1,0:T(8,128)(2,1)S(1)}, bf16[256,2048]{1,0:T(8,128)(2,1)}, u32[]{:S(2)}, u32[]{:S(2)}) collective-permute-start(bf16[256,2048]{1,0:T(8,128)(2,1)S(1)} %pad_maximum_fusion.6.refs_3_), channel_id=1, source_target_pairs={{0,1},{1,0},{2,3},{3,2},{4,5},{5,4},{6,7},{7,6},{8,9},{9,8},{10,11... | collective-permute-start | bytes 3145736 | tf_op jit(solution)/shard_map/ppermute | solution.py:26
  185.0 24.6 %copy-start.42 = (bf16[2048,512]{1,0:T(8,128)(2,1)S(1)}, bf16[2048,512]{1,0:T(8,128)(2,1)}, u32[]{:S(2)}) copy-start(bf16[2048,512]{1,0:T(8,128)(2,1)} %all-gather.9.cloned.1.call-done) | copy-start | bytes 6291460
  213.4 21.7 %collective-permute-start.11 = (bf16[256,2048]{1,0:T(8,128)(2,1)}, bf16[256,2048]{1,0:T(8,128)(2,1)S(1)}, u32[]{:S(2)}, u32[]{:S(2)}) collective-permute-start(bf16[256,2048]{1,0:T(8,128)(2,1)} %pad_maximum_fusion.7), channel_id=1, source_target_pairs={{0,4},{2,6},{4,0},{6,2},{8,12},{10,14},{12,8},{14,10},{16,20},{18,... | collective-permute-start | bytes 3145736 | tf_op jit(solution)/shard_map/ppermute | solution.py:26
  215.9 22.3 %collective-permute-start.13 = (bf16[256,2048]{1,0:T(8,128)(2,1)}, bf16[256,2048]{1,0:T(8,128)(2,1)S(1)}, u32[]{:S(2)}, u32[]{:S(2)}) collective-permute-start(bf16[256,2048]{1,0:T(8,128)(2,1)} %slice.319), channel_id=1, source_target_pairs={{0,1},{1,0},{2,3},{3,2},{4,5},{5,4},{6,7},{7,6},{8,9},{9,8},{10,11... | collective-permute-start | bytes 3145736 | tf_op jit(solution)/shard_map/ppermute | solution.py:26
  217.4 24.1 %copy-start.39 = (f32[2048]{0:T(1024)S(1)}, f32[2048]{0:T(1024)}, u32[]{:S(2)}) copy-start(f32[2048]{0:T(1024)} %param.25) | copy-start | bytes 24580
  217.4 232.7 %reduce-scatter.8.cloned.1.call-start = ((), (), s32[]{:S(2)}) async-start(), calls=%async_computation.13 | async-start | bytes 7077888 | tf_op jit(solution)/shard_map/reduce_scatter | solution.py:257
  217.5 34.0 %copy-start.7 = (bf16[256,2048]{1,0:T(8,128)(2,1)S(1)}, bf16[256,2048]{1,0:T(8,128)(2,1)}, u32[]{:S(2)}) copy-start(bf16[256,2048]{1,0:T(8,128)(2,1)} %copy-done.6) | copy-start | bytes 3145732
  236.8 14.7 %collective-permute-start.12 = (bf16[128,2048]{1,0:T(8,128)(2,1)S(1)}, bf16[128,2048]{1,0:T(8,128)(2,1)S(1)}, u32[]{:S(2)}, u32[]{:S(2)}) collective-permute-start(bf16[128,2048]{1,0:T(8,128)(2,1)S(1)} %get-tuple-element.133), channel_id=1, source_target_pairs={{0,1},{1,0},{2,3},{3,2},{4,5},{5,4},{6,7},{7,6},{8,9},{9,8},{10,11... | collective-permute-start | bytes 1572872 | tf_op jit(solution)/shard_map/ppermute | solution.py:26
  240.0 11.5 %collective-permute-start.14 = (bf16[128,2048]{1,0:T(8,128)(2,1)S(1)}, bf16[128,2048]{1,0:T(8,128)(2,1)S(1)}, u32[]{:S(2)}, u32[]{:S(2)}) collective-permute-start(bf16[128,2048]{1,0:T(8,128)(2,1)S(1)} %get-tuple-element.158), channel_id=1, source_target_pairs={{0,4},{2,6},{4,0},{6,2},{8,12},{10,14},{12,8},{14,10},{16,20},{18,... | collective-permute-start | bytes 1572872 | tf_op jit(solution)/shard_map/ppermute | solution.py:26
  253.6 12.6 %collective-permute-start.15 = (bf16[128,2048]{1,0:T(8,128)(2,1)S(1)}, bf16[128,2048]{1,0:T(8,128)(2,1)S(1)}, u32[]{:S(2)}, u32[]{:S(2)}) collective-permute-start(bf16[128,2048]{1,0:T(8,128)(2,1)S(1)} %get-tuple-element.157.refs_1_), channel_id=1, source_target_pairs={{0,1},{1,0},{2,3},{3,2},{4,5},{5,4},{6,7},{7,6},{8,9},{9,8},{10,11... | collective-permute-start | bytes 1572872 | tf_op jit(solution)/shard_map/ppermute | solution.py:26
  255.2 13.2 %collective-permute-start.17 = (bf16[128,2048]{1,0:T(8,128)(2,1)S(1)}, bf16[128,2048]{1,0:T(8,128)(2,1)S(1)}, u32[]{:S(2)}, u32[]{:S(2)}) collective-permute-start(bf16[128,2048]{1,0:T(8,128)(2,1)S(1)} %get-tuple-element.156), channel_id=1, source_target_pairs={{0,4},{2,6},{4,0},{6,2},{8,12},{10,14},{12,8},{14,10},{16,20},{18,... | collective-permute-start | bytes 1572872 | tf_op jit(solution)/shard_map/ppermute | solution.py:26
  266.4 24.6 %collective-permute-start.16 = (bf16[256,2048]{1,0:T(8,128)(2,1)S(1)}, bf16[256,2048]{1,0:T(8,128)(2,1)S(1)}, u32[]{:S(2)}, u32[]{:S(2)}) collective-permute-start(bf16[256,2048]{1,0:T(8,128)(2,1)S(1)} %pad_maximum_fusion.8), channel_id=1, source_target_pairs={{0,4},{2,6},{4,0},{6,2},{8,12},{10,14},{12,8},{14,10},{16,20},{18,... | collective-permute-start | bytes 3145736 | tf_op jit(solution)/shard_map/ppermute | solution.py:26
  268.5 25.2 %collective-permute-start.18 = (bf16[256,2048]{1,0:T(8,128)(2,1)S(1)}, bf16[256,2048]{1,0:T(8,128)(2,1)S(1)}, u32[]{:S(2)}, u32[]{:S(2)}) collective-permute-start(bf16[256,2048]{1,0:T(8,128)(2,1)S(1)} %pad_maximum_fusion.9.refs_3_), channel_id=1, source_target_pairs={{0,1},{1,0},{2,3},{3,2},{4,5},{5,4},{6,7},{7,6},{8,9},{9,8},{10,11... | collective-permute-start | bytes 3145736 | tf_op jit(solution)/shard_map/ppermute | solution.py:26
  337.6 183.1 %reduce-scatter.10.cloned.1.call-start = ((), (), s32[]{:S(2)}) async-start(), calls=%async_computation.14 | async-start | bytes 7077888 | tf_op jit(solution)/shard_map/reduce_scatter | solution.py:257
  416.4 25.6 %collective-permute-start.19 = (bf16[256,2048]{1,0:T(8,128)(2,1)}, bf16[256,2048]{1,0:T(8,128)(2,1)}, u32[]{:S(2)}, u32[]{:S(2)}) collective-permute-start(bf16[256,2048]{1,0:T(8,128)(2,1)} %pad_maximum_fusion.10), channel_id=1, source_target_pairs={{0,4},{2,6},{4,0},{6,2},{8,12},{10,14},{12,8},{14,10},{16,20},{18,... | collective-permute-start | bytes 3145736 | tf_op jit(solution)/shard_map/ppermute | solution.py:26
  417.8 25.3 %collective-permute-start.20 = (bf16[256,2048]{1,0:T(8,128)(2,1)}, bf16[256,2048]{1,0:T(8,128)(2,1)}, u32[]{:S(2)}, u32[]{:S(2)}) collective-permute-start(bf16[256,2048]{1,0:T(8,128)(2,1)} %slice.325), channel_id=1, source_target_pairs={{0,1},{1,0},{2,3},{3,2},{4,5},{5,4},{6,7},{7,6},{8,9},{9,8},{10,11... | collective-permute-start | bytes 3145736 | tf_op jit(solution)/shard_map/ppermute | solution.py:26
  450.2 141.0 %reduce-scatter.14.cloned.1.call-start = ((), (), s32[]{:S(2)}) async-start(), calls=%async_computation.16 | async-start | bytes 7077888 | tf_op jit(solution)/shard_map/reduce_scatter | solution.py:257
  450.2 12.1 %collective-permute-start.22 = (bf16[128,2048]{1,0:T(8,128)(2,1)}, bf16[128,2048]{1,0:T(8,128)(2,1)S(1)}, u32[]{:S(2)}, u32[]{:S(2)}) collective-permute-start(bf16[128,2048]{1,0:T(8,128)(2,1)} %get-tuple-element.154), channel_id=1, source_target_pairs={{0,4},{2,6},{4,0},{6,2},{8,12},{10,14},{12,8},{14,10},{16,20},{18,... | collective-permute-start | bytes 1572872 | tf_op jit(solution)/shard_map/ppermute | solution.py:26
  451.8 11.7 %collective-permute-start.21 = (bf16[128,2048]{1,0:T(8,128)(2,1)}, bf16[128,2048]{1,0:T(8,128)(2,1)S(1)}, u32[]{:S(2)}, u32[]{:S(2)}) collective-permute-start(bf16[128,2048]{1,0:T(8,128)(2,1)} %get-tuple-element.131), channel_id=1, source_target_pairs={{0,1},{1,0},{2,3},{3,2},{4,5},{5,4},{6,7},{7,6},{8,9},{9,8},{10,11... | collective-permute-start | bytes 1572872 | tf_op jit(solution)/shard_map/ppermute | solution.py:26
  469.4 11.0 %collective-permute-start.23 = (bf16[128,2048]{1,0:T(8,128)(2,1)S(1)}, bf16[128,2048]{1,0:T(8,128)(2,1)S(1)}, u32[]{:S(2)}, u32[]{:S(2)}) collective-permute-start(bf16[128,2048]{1,0:T(8,128)(2,1)S(1)} %get-tuple-element.153.refs_1_), channel_id=1, source_target_pairs={{0,1},{1,0},{2,3},{3,2},{4,5},{5,4},{6,7},{7,6},{8,9},{9,8},{10,11... | collective-permute-start | bytes 1572872 | tf_op jit(solution)/shard_map/ppermute | solution.py:26
  471.0 12.7 %collective-permute-start.25 = (bf16[128,2048]{1,0:T(8,128)(2,1)S(1)}, bf16[128,2048]{1,0:T(8,128)(2,1)S(1)}, u32[]{:S(2)}, u32[]{:S(2)}) collective-permute-start(bf16[128,2048]{1,0:T(8,128)(2,1)S(1)} %get-tuple-element.152), channel_id=1, source_target_pairs={{0,4},{2,6},{4,0},{6,2},{8,12},{10,14},{12,8},{14,10},{16,20},{18,... | collective-permute-start | bytes 1572872 | tf_op jit(solution)/shard_map/ppermute | solution.py:26
  480.5 23.3 %collective-permute-start.24 = (bf16[256,2048]{1,0:T(8,128)(2,1)S(1)}, bf16[256,2048]{1,0:T(8,128)(2,1)S(1)}, u32[]{:S(2)}, u32[]{:S(2)}) collective-permute-start(bf16[256,2048]{1,0:T(8,128)(2,1)S(1)} %pad_maximum_fusion.11), channel_id=1, source_target_pairs={{0,4},{2,6},{4,0},{6,2},{8,12},{10,14},{12,8},{14,10},{16,20},{18,... | collective-permute-start | bytes 3145736 | tf_op jit(solution)/shard_map/ppermute | solution.py:26
  483.8 20.0 %collective-permute-start.26 = (bf16[256,2048]{1,0:T(8,128)(2,1)S(1)}, bf16[256,2048]{1,0:T(8,128)(2,1)S(1)}, u32[]{:S(2)}, u32[]{:S(2)}) collective-permute-start(bf16[256,2048]{1,0:T(8,128)(2,1)S(1)} %pad_maximum_fusion.12.refs_3_), channel_id=1, source_target_pairs={{0,1},{1,0},{2,3},{3,2},{4,5},{5,4},{6,7},{7,6},{8,9},{9,8},{10,11... | collective-permute-start | bytes 3145736 | tf_op jit(solution)/shard_map/ppermute | solution.py:26
  520.7 107.2 %reduce-scatter.12.cloned.1.call-start = ((), (), s32[]{:S(2)}) async-start(), calls=%async_computation.15 | async-start | bytes 2359296 | tf_op jit(solution)/shard_map/reduce_scatter | solution.py:257
  526.7 191.8 %reduce-scatter.16.cloned.1.call-start = ((), (), s32[]{:S(2)}) async-start(), calls=%async_computation.17 | async-start | bytes 9437184 | tf_op jit(solution)/shard_map/reduce_scatter | solution.py:257
  532.0 41.5 %collective-permute-start.27 = (bf16[256,2048]{1,0:T(8,128)(2,1)}, bf16[256,2048]{1,0:T(8,128)(2,1)S(1)}, u32[]{:S(2)}, u32[]{:S(2)}) collective-permute-start(bf16[256,2048]{1,0:T(8,128)(2,1)} %pad_maximum_fusion.13), channel_id=1, source_target_pairs={{0,4},{2,6},{4,0},{6,2},{8,12},{10,14},{12,8},{14,10},{16,20},{18,... | collective-permute-start | bytes 3145736 | tf_op jit(solution)/shard_map/ppermute | solution.py:26
  533.5 40.0 %collective-permute-start.28 = (bf16[256,2048]{1,0:T(8,128)(2,1)}, bf16[256,2048]{1,0:T(8,128)(2,1)}, u32[]{:S(2)}, u32[]{:S(2)}) collective-permute-start(bf16[256,2048]{1,0:T(8,128)(2,1)} %slice.273), channel_id=1, source_target_pairs={{0,1},{1,0},{2,3},{3,2},{4,5},{5,4},{6,7},{7,6},{8,9},{9,8},{10,11... | collective-permute-start | bytes 3145736 | tf_op jit(solution)/shard_map/ppermute | solution.py:26
  577.3 24.7 %collective-permute-start.30 = (bf16[128,2048]{1,0:T(8,128)(2,1)}, bf16[128,2048]{1,0:T(8,128)(2,1)}, u32[]{:S(2)}, u32[]{:S(2)}) collective-permute-start(bf16[128,2048]{1,0:T(8,128)(2,1)} %get-tuple-element.150), channel_id=1, source_target_pairs={{0,4},{2,6},{4,0},{6,2},{8,12},{10,14},{12,8},{14,10},{16,20},{18,... | collective-permute-start | bytes 1572872 | tf_op jit(solution)/shard_map/ppermute | solution.py:26
  580.5 21.5 %collective-permute-start.29 = (bf16[128,2048]{1,0:T(8,128)(2,1)}, bf16[128,2048]{1,0:T(8,128)(2,1)}, u32[]{:S(2)}, u32[]{:S(2)}) collective-permute-start(bf16[128,2048]{1,0:T(8,128)(2,1)} %get-tuple-element.129), channel_id=1, source_target_pairs={{0,1},{1,0},{2,3},{3,2},{4,5},{5,4},{6,7},{7,6},{8,9},{9,8},{10,11... | collective-permute-start | bytes 1572872 | tf_op jit(solution)/shard_map/ppermute | solution.py:26
  581.7 22.8 %collective-permute-start.31 = (bf16[128,1536]{1,0:T(8,128)(2,1)}, bf16[128,1536]{1,0:T(8,128)(2,1)}, u32[]{:S(2)}, u32[]{:S(2)}) collective-permute-start(bf16[128,1536]{1,0:T(8,128)(2,1)} %constant_dynamic-slice_fusion.5), channel_id=1, source_target_pairs={{0,4},{2,6},{4,0},{6,2},{8,12},{10,14},{12,8},{14,10},{16,20},{18,... | collective-permute-start | bytes 1179656 | tf_op jit(solution)/shard_map/ppermute | solution.py:26
  583.4 23.7 %collective-permute-start.32 = (bf16[128,1536]{1,0:T(8,128)(2,1)S(1)}, bf16[128,1536]{1,0:T(8,128)(2,1)}, u32[]{:S(2)}, u32[]{:S(2)}) collective-permute-start(bf16[128,1536]{1,0:T(8,128)(2,1)S(1)} %constant_dynamic-slice_fusion.4), channel_id=1, source_target_pairs={{0,4},{2,6},{4,0},{6,2},{8,12},{10,14},{12,8},{14,10},{16,20},{18,... | collective-permute-start | bytes 1179656 | tf_op jit(solution)/shard_map/ppermute | solution.py:26
  593.0 22.4 %collective-permute-start.33 = (bf16[128,1536]{1,0:T(8,128)(2,1)}, bf16[128,1536]{1,0:T(8,128)(2,1)}, u32[]{:S(2)}, u32[]{:S(2)}) collective-permute-start(bf16[128,1536]{1,0:T(8,128)(2,1)} %constant_dynamic-slice_fusion.3), channel_id=1, source_target_pairs={{0,4},{2,6},{4,0},{6,2},{8,12},{10,14},{12,8},{14,10},{16,20},{18,... | collective-permute-start | bytes 1179656 | tf_op jit(solution)/shard_map/ppermute | solution.py:26
  628.0 163.9 %reduce-scatter.18.cloned.1.call-start = ((), (), s32[]{:S(2)}) async-start(), calls=%async_computation.18 | async-start | bytes 2359296 | tf_op jit(solution)/shard_map/reduce_scatter | solution.py:257
  718.5 73.9 %reduce-scatter.20.cloned.1.call-start = ((), (), s32[]{:S(2)}) async-start(), calls=%async_computation.19 | async-start | bytes 2359296 | tf_op jit(solution)/shard_map/reduce_scatter | solution.py:257
  738.2 22.9 %collective-permute-start.34 = (bf16[256,2048]{1,0:T(8,128)(2,1)S(1)}, bf16[256,2048]{1,0:T(8,128)(2,1)S(1)}, u32[]{:S(2)}, u32[]{:S(2)}) collective-permute-start(bf16[256,2048]{1,0:T(8,128)(2,1)S(1)} %pad_maximum_fusion.14), channel_id=1, source_target_pairs={{0,4},{2,6},{4,0},{6,2},{8,12},{10,14},{12,8},{14,10},{16,20},{18,... | collective-permute-start | bytes 3145736 | tf_op jit(solution)/shard_map/ppermute | solution.py:26
  739.8 24.1 %collective-permute-start.41 = (bf16[256,2048]{1,0:T(8,128)(2,1)S(1)}, bf16[256,2048]{1,0:T(8,128)(2,1)S(1)}, u32[]{:S(2)}, u32[]{:S(2)}) collective-permute-start(bf16[256,2048]{1,0:T(8,128)(2,1)S(1)} %slice.341), channel_id=1, source_target_pairs={{0,1},{1,0},{2,3},{3,2},{4,5},{5,4},{6,7},{7,6},{8,9},{9,8},{10,11... | collective-permute-start | bytes 3145736 | tf_op jit(solution)/shard_map/ppermute | solution.py:26
  741.4 53.5 %copy-start.32 = (bf16[256,512]{1,0:T(8,128)(2,1)S(1)}, bf16[256,512]{1,0:T(8,128)(2,1)}, u32[]{:S(2)}) copy-start(bf16[256,512]{1,0:T(8,128)(2,1)} %reduce-scatter.12.cloned.1.call-done.both_ref) | copy-start | bytes 786436
  741.4 58.5 %copy-start.8 = (bf16[256,2048]{1,0:T(8,128)(2,1)S(1)}, bf16[256,2048]{1,0:T(8,128)(2,1)}, u32[]{:S(2)}) copy-start(bf16[256,2048]{1,0:T(8,128)(2,1)} %copy-done.6) | copy-start | bytes 3145732
  741.4 23.6 %collective-permute-start.35 = (f32[4352]{0:T(1024)S(1)}, f32[4352]{0:T(1024)S(1)}, u32[]{:S(2)}, u32[]{:S(2)}) collective-permute-start(f32[4352]{0:T(1024)S(1)} %pad_maximum_fusion.22), channel_id=1, source_target_pairs={{0,2},{2,0},{4,6},{6,4},{8,10},{10,8},{12,14},{14,12},{16,18},{18,... | collective-permute-start | bytes 52232 | tf_op jit(solution)/shard_map/ppermute | solution.py:26
  761.4 30.5 %collective-permute-start.40 = (bf16[128,2048]{1,0:T(8,128)(2,1)S(1)}, bf16[128,2048]{1,0:T(8,128)(2,1)S(1)}, u32[]{:S(2)}, u32[]{:S(2)}) collective-permute-start(bf16[128,2048]{1,0:T(8,128)(2,1)S(1)} %get-tuple-element.127), channel_id=1, source_target_pairs={{0,1},{1,0},{2,3},{3,2},{4,5},{5,4},{6,7},{7,6},{8,9},{9,8},{10,11... | collective-permute-start | bytes 1572872 | tf_op jit(solution)/shard_map/ppermute | solution.py:26
  764.4 27.6 %collective-permute-start.42 = (bf16[128,2048]{1,0:T(8,128)(2,1)S(1)}, bf16[128,2048]{1,0:T(8,128)(2,1)S(1)}, u32[]{:S(2)}, u32[]{:S(2)}) collective-permute-start(bf16[128,2048]{1,0:T(8,128)(2,1)S(1)} %get-tuple-element.148), channel_id=1, source_target_pairs={{0,4},{2,6},{4,0},{6,2},{8,12},{10,14},{12,8},{14,10},{16,20},{18,... | collective-permute-start | bytes 1572872 | tf_op jit(solution)/shard_map/ppermute | solution.py:26
  765.0 9.4 %collective-permute-start.36 = (f32[4352]{0:T(1024)S(1)}, f32[4352]{0:T(1024)S(1)}, u32[]{:S(2)}, u32[]{:S(2)}) collective-permute-start(f32[4352]{0:T(1024)S(1)} %fusion.37), channel_id=1, source_target_pairs={{0,4},{2,6},{4,0},{6,2},{8,12},{10,14},{12,8},{14,10},{16,20},{18,... | collective-permute-start | bytes 52232 | tf_op jit(solution)/shard_map/ppermute | solution.py:26
  774.4 7.0 collective-permute-start.37
  781.4 5.5 collective-permute-start.38
  786.9 3.8 collective-permute-start.39
  794.9 11.3 %collective-permute-start.45 = (bf16[128,512]{1,0:T(8,128)(2,1)S(1)}, bf16[128,512]{1,0:T(8,128)(2,1)S(1)}, u32[]{:S(2)}, u32[]{:S(2)}) collective-permute-start(bf16[128,512]{1,0:T(8,128)(2,1)S(1)} %constant_dynamic-slice_fusion), channel_id=1, source_target_pairs={{0,4},{2,6},{4,0},{6,2},{8,12},{10,14},{12,8},{14,10},{16,20},{18,... | collective-permute-start | bytes 393224 | tf_op jit(solution)/shard_map/ppermute | solution.py:26
  796.5 12.2 %collective-permute-start.44 = (bf16[128,512]{1,0:T(8,128)(2,1)}, bf16[128,512]{1,0:T(8,128)(2,1)}, u32[]{:S(2)}, u32[]{:S(2)}) collective-permute-start(bf16[128,512]{1,0:T(8,128)(2,1)} %constant_dynamic-slice_fusion.1), channel_id=1, source_target_pairs={{0,4},{2,6},{4,0},{6,2},{8,12},{10,14},{12,8},{14,10},{16,20},{18,... | collective-permute-start | bytes 393224 | tf_op jit(solution)/shard_map/ppermute | solution.py:26
  797.0 13.5 %collective-permute-start.43 = (bf16[128,512]{1,0:T(8,128)(2,1)S(1)}, bf16[128,512]{1,0:T(8,128)(2,1)S(1)}, u32[]{:S(2)}, u32[]{:S(2)}) collective-permute-start(bf16[128,512]{1,0:T(8,128)(2,1)S(1)} %constant_dynamic-slice_fusion.2), channel_id=1, source_target_pairs={{0,4},{2,6},{4,0},{6,2},{8,12},{10,14},{12,8},{14,10},{16,20},{18,... | collective-permute-start | bytes 393224 | tf_op jit(solution)/shard_map/ppermute | solution.py:26
  (43 other events, 303.0 us)
Sparse Core Ops, SparseCore 0:
  21.6 48.3 all-gather.6
  72.2 27.9 all-gather.8
  102.4 81.4 all-gather.10
  185.3 63.2 all-gather.12
  250.7 63.3 all-gather.14
  316.1 63.3 all-gather.16
  381.8 68.3 reduce-scatter.7
  452.5 68.1 reduce-scatter.9
  523.0 68.1 reduce-scatter.13
  593.4 34.5 reduce-scatter.11
  630.3 88.1 reduce-scatter.15
  720.6 34.5 reduce-scatter.17
  757.5 34.8 reduce-scatter.19

commit v7 on v6

--- a/solution.py
+++ b/solution.py
@@ -738,10 +738,8 @@
     d_att = dot(branch, full_output).astype(BF16).reshape(q.shape)
     rows_up = scatter_weight(after(grad_up, (rows_gate, d_att)), 2)
     grad_output = dot_rows(branch, mixed).astype(BF16)
-    rows_output = scatter_weight(after(grad_output, rows_gate), ways)
     shard_down = one(rows_down, 2)
     shard_gate = one(rows_gate, 2)
-    shard_up = one(rows_up, 2)
     d_q, d_kv = attend_back(info, q, d_att, heads, lse, full_kv, count, ways)
     y_lows, y_highs = return_rows(after(y_part, branch), 2, d_q)
     out_tokens = row_pass(
@@ -756,14 +754,16 @@
     d_h1_query = dot_cols(d_qp, full_qkv[:, :q_width])
     d_kv = after(
         d_kv.reshape(-1, kv_width),
-        (rows_output, d_h1_query, out_tokens, shard_down, shard_gate, shard_up),
+        (rows_up, out_tokens),
     )
     d_kv = ctx_scatter(d_kv, ways)
-    grad_query = dot_rows(h1, d_qp).astype(BF16)
-    rows_query = scatter_weight(after(grad_query, d_kv), ways)
+    h1_late = after(h1, (d_h1_query, shard_down, shard_gate))
+    grad_query = dot_rows(h1_late, d_qp).astype(BF16)
+    grad_both = jnp.concatenate([grad_output, grad_query], axis=1)
+    rows_both = scatter_weight(after(grad_both, d_kv), ways)
+    d_kv = after(d_kv, grad_both)
     d_kvp, gain_k_sum = head_prep_back(d_kv, raw, cos, sin, gain_k, q_width // kv_width, True)
     grad_kv = dot_rows(h1, d_kvp).astype(BF16)
-    rows_kv = scatter_weight(grad_kv, ways)
     d_h1 = (
         d_h1_query + dot_cols(after(d_kvp, grad_kv), full_qkv[:, q_width:])
     ).astype(BF16)
@@ -772,6 +772,7 @@
         jnp.concatenate([gain_attn, gain_mlp[0], gain_q_sum[0], gain_k_sum[0]])
     )
     lows, highs = return_rows(d_h1, ways)
+    rows_kv = scatter_weight(after(grad_kv, (rows_both, lows[0], highs[0])), ways)
     lows[0] = after(lows[0], gains)
     grad_tokens = row_pass(
         functools.partial(back_kernel, len(lows), len(highs), ctx_count),
@@ -779,9 +780,10 @@
         row_f32,
         "entry_back",
     )
-    rows_output, rows_query, rows_kv = after((rows_output, rows_query, rows_kv), (lows, highs))
-    shard_output = one(rows_output, ways)
-    shard_query = one(rows_query, ways)
+    rows_up, rows_both, rows_kv = after((rows_up, rows_both, rows_kv), (lows, highs))
+    shard_up = one(rows_up, 2)
+    plan = [(0, q_width, 0, 0), (q_width, q_width, 1, 0)]
+    shard_output, shard_query = own_rows(rows_both, pair, ways, plan, [q_width, q_width])
     plan = []
     for h in range(groups):
         for t in (0, 1):

time: 829 us -> 809 us (0.976)
  Pallas kernels: 105 us -> 89.5 us
  waiting for transfers between devices: 384 us -> 394 us
  starting transfers between devices: 62.7 us -> 53.2 us
    ppermute x46 -> x45, waiting for transfers between devices: 198 us -> 228 us  [xor_send(): return lax.ppermute(value, axis, [(i, i ^ step) for i in range(count)])]
    reduce_scatter x7 -> x6, waiting for transfers between devices: 114 us -> 92.4 us  [ctx_scatter(): lax.psum_scatter(rows, 'ctx', scatter_dimension=0, tiled=True, axis_index...]
    ppermute x46 -> x45, starting transfers between devices: 60.9 us -> 52.1 us  [xor_send(): return lax.ppermute(value, axis, [(i, i ^ step) for i in range(count)])]
    unnamed x96 -> x98, local copies, waits for them, and re-layouts: 21.6 us -> 19.9 us
  transfers between devices with their start and end apart: 59 -> 57, of which waited for: 40 -> 44; matrix products, arithmetic and copies ran while one was open for 27% -> 28% of each run, Pallas kernels for 13% -> 11%
where the time goes in v7:
time: 809 us; the launch traced here: 800 us
  waiting for transfers between devices  394 us (49%)
  matrix products  144 us (18%)
  Pallas kernels  89.5 us (11%)
  local copies, waits for them, and re-layouts  56.3 us (7%)
  starting transfers between devices  53.2 us (7%)
  other arithmetic  47.6 us (6%)
  between operations  15.4 us (2%)
    ppermute x45, waiting for transfers between devices, xor_send(): return lax.ppermute(value, axis, [(i, i ^ step) for i in range(count)])  228 us
    reduce_scatter x6, waiting for transfers between devices, ctx_scatter(): lax.psum_scatter(rows, 'ctx', scatter_dimension=0, tiled=True, axis_index...  92.4 us
    all_gather x6, waiting for transfers between devices, ctx_gather(): lax.all_gather(rows, 'ctx', axis=0, tiled=True, axis_index_groups=groups)  72.9 us
    dot_general x5, matrix products, dot(): return jnp.dot(left, right, preferred_element_type=F32)  52.4 us
    ppermute x45, starting transfers between devices, xor_send(): return lax.ppermute(value, axis, [(i, i ^ step) for i in range(count)])  52.1 us
    dot_general x6, matrix products, dot_cols(): lax.dot_general(left, right, (((1,), (1,)), ((), ())), preferred_element_...  45.9 us
    dot_general x6, matrix products, dot_rows(): lax.dot_general(left, right, (((0,), (0,)), ((), ())), preferred_element_...  45.9 us
    pallas_call x1, Pallas kernels, attend_back(): pl.pallas_call(functools.partial(backward_kernel, ways, count), out_shape...  26.1 us
  transfers between devices with their start and end apart: 57, of which 44 were waited for; matrix products, arithmetic and copies ran while one was open for 28% of the time, Pallas kernels for 11%

profile of v7, /device:TPU:0, one launch (start us, length us, event | category | flops | bytes accessed | tf_op | source)
XLA Modules:
  0.0 799.7 jit_solution(2215229369731308717)
XLA Ops:
  11.2 3.1 collective-permute-start.4
  14.2 6.3 collective-permute-done.4
  35.5 2.7 constant_dynamic-update-slice_fusion.6
  38.2 2.7 constant_dynamic-update-slice_fusion.5
  44.2 2.7 constant_dynamic-update-slice_fusion.4
  46.9 2.7 constant_dynamic-update-slice_fusion.3
  49.6 2.7 constant_dynamic-update-slice_fusion.2
  52.3 2.7 constant_dynamic-update-slice_fusion.1
  60.8 4.8 collective-permute-done.1.refs_0_
  70.0 10.0 %fusion.69.raw_ref = f32[1024,1024]{1,0:T(8,128)} fusion(bf16[1024,2048]{1,0:T(8,128)(2,1)} %copy-done, bf16[2048,1024]{1,0:T(8,128)(2,1)} %all-gather.7.cloned.1.call-done), kind=kOutput, calls=%fused_computation.200 | convolution fusion | flops 4294967296 | bytes 12582912 | tf_op jit(solution)/shard_map/dot_general | solution.py:318
  80.0 6.3 head_prep.1
  86.2 13.9 %all-gather.9.cloned.1.call-done = bf16[2048,512]{1,0:T(8,128)(2,1)} async-done(((bf16[256,512]{1,0:T(8,128)(2,1)}), bf16[2048,512]{1,0:T(8,128)(2,1)}) %all-gather.9.cloned.1.call-update) | async-done | bytes 2097168 | tf_op jit(solution)/shard_map/all_gather | solution.py:252
  102.1 26.6 %collective-permute-done.5 = bf16[128,4608]{1,0:T(8,128)(2,1)S(1)} collective-permute-done((bf16[128,4608]{1,0:T(8,128)(2,1)S(1)}, bf16[128,4608]{1,0:T(8,128)(2,1)S(1)}, u32[]{:S(2)}, u32[]{:S(2)}) %collective-permute-start.5) | collective-permute-done | bytes 1179680 | tf_op jit(solution)/shard_map/ppermute | solution.py:26
  135.0 10.4 %collective-permute-done.6.refs_2_ = bf16[128,2048]{1,0:T(8,128)(2,1)S(1)} collective-permute-done((bf16[128,2048]{1,0:T(8,128)(2,1)S(1)}, bf16[128,2048]{1,0:T(8,128)(2,1)S(1)}, u32[]{:S(2)}, u32[]{:S(2)}) %collective-permute-start.6) | collective-permute-done | bytes 524320 | tf_op jit(solution)/shard_map/ppermute | solution.py:26
  154.3 10.2 %stack.31.info_ref = s32[26]{0:T(128)S(1)} concatenate(s32[1]{0:T(128)} %bitcast.8.pair_ref, s32[1]{0:T(128)} %bitcast.9, s32[1]{0:T(128)} %bitcast.10, s32[1]{0:T(128)} %bitcast.11, s32[1]{0:T(128)} %bitcast.12, s32[1]{0:T(128)} %bitcast.13, s32[1]{0:T(128)} %bitcast.14, s32[1]{0:T(128)} %bitcast.15, s32[1]{0:T(128)} %bitcast.16, s32[1]{0:T(128)} %bitcast.17, s32[1]{0:T(128)} %bitcast.18, ...), dimensions={0} | concatenate | bytes 208 | tf_op jit(solution)/shard_map/stack | solution.py:680
  164.5 5.9 collective-permute-done.7.refs_0_
  175.4 8.4 %all-gather.11.cloned.1.call-done = bf16[8192,512]{1,0:T(8,128)(2,1)} async-done(((bf16[1024,512]{1,0:T(8,128)(2,1)}), bf16[8192,512]{1,0:T(8,128)(2,1)}) %all-gather.11.cloned.1.call-update) | async-done | bytes 8388624 | tf_op jit(solution)/shard_map/all_gather | solution.py:252
  185.0 18.5 %attend.1 = (bf16[2,4,128,512]{3,2,1,0:T(8,128)(2,1)S(1)}, f32[2,2,4,1,256]{4,3,2,1,0:T(1,128)S(1)}) custom-call(s32[26]{0:T(128)S(1)} %stack.31.info_ref, bf16[2,4,128,512]{3,2,1,0:T(8,128)(2,1)S(1)} %bitcast.127, bf16[8,2,4,128,512]{4,3,2,1,0:T(8,128)(2,1)} %bitcast.148), custom_call_target="tpu_custom_call" | custom-call | flops 4294967296 | bytes 8388608 | tf_op jit(solution)/shard_map/attend/pallas_call | solution.py:553
  211.5 19.1 %collective-permute-done.11 = bf16[256,2048]{1,0:T(8,128)(2,1)S(1)} collective-permute-done((bf16[256,2048]{1,0:T(8,128)(2,1)}, bf16[256,2048]{1,0:T(8,128)(2,1)S(1)}, u32[]{:S(2)}, u32[]{:S(2)}) %collective-permute-start.11) | collective-permute-done | bytes 1048608 | tf_op jit(solution)/shard_map/ppermute | solution.py:26
  237.0 8.5 %collective-permute-done.12.refs_3_ = bf16[128,2048]{1,0:T(8,128)(2,1)S(1)} collective-permute-done((bf16[128,2048]{1,0:T(8,128)(2,1)S(1)}, bf16[128,2048]{1,0:T(8,128)(2,1)S(1)}, u32[]{:S(2)}, u32[]{:S(2)}) %collective-permute-start.12) | collective-permute-done | bytes 524320 | tf_op jit(solution)/shard_map/ppermute | solution.py:26
  245.5 2.8 collective-permute-done.14.refs_5_
  252.3 12.1 %collective-permute-done.15.refs_2_ = bf16[128,2048]{1,0:T(8,128)(2,1)S(1)} collective-permute-done((bf16[128,2048]{1,0:T(8,128)(2,1)S(1)}, bf16[128,2048]{1,0:T(8,128)(2,1)S(1)}, u32[]{:S(2)}, u32[]{:S(2)}) %collective-permute-start.15) | collective-permute-done | bytes 524320 | tf_op jit(solution)/shard_map/ppermute | solution.py:26
  266.9 23.6 %collective-permute-done.16.refs_0_ = bf16[256,2048]{1,0:T(8,128)(2,1)S(1)} collective-permute-done((bf16[256,2048]{1,0:T(8,128)(2,1)S(1)}, bf16[256,2048]{1,0:T(8,128)(2,1)S(1)}, u32[]{:S(2)}, u32[]{:S(2)}) %collective-permute-start.16) | collective-permute-done | bytes 1048608 | tf_op jit(solution)/shard_map/ppermute | solution.py:26
  294.6 11.8 %fusion.70 = f32[1024,1536]{1,0:T(8,128)} fusion(bf16[1024,2048]{1,0:T(8,128)(2,1)} %copy-done.4, bf16[2048,1536]{1,0:T(8,128)(2,1)} %all-gather.13.cloned.1.call-done), kind=kOutput, calls=%fused_computation.201 | convolution fusion | flops 6442450944 | bytes 16777216 | tf_op jit(solution)/shard_map/dot_general | solution.py:318
  306.3 7.2 all-gather.15.cloned.1.call-done
  313.6 13.1 %multiply_convert_fusion.2 = (bf16[1024,1536]{1,0:T(8,128)(2,1)S(1)}, f32[1024,1536]{1,0:T(8,128)}) fusion(f32[1024,1536]{1,0:T(8,128)} %fusion.70, bf16[1024,2048]{1,0:T(8,128)(2,1)} %copy-done.4, bf16[2048,1536]{1,0:T(8,128)(2,1)} %all-gather.15.cloned.1.call-done), kind=kOutput, calls=%fused_computation.8 | convolution fusion | flops 6450315264 | bytes 26214400 | tf_op jit(solution)/shard_map/dot_general | solution.py:318
  328.4 8.8 %convolution_convert_fusion.2 = bf16[2048,1536]{1,0:T(8,128)(2,1)} fusion(bf16[1024,2048]{1,0:T(8,128)(2,1)S(1)} %copy-done.2, bf16[1024,1536]{1,0:T(8,128)(2,1)S(1)} %get-tuple-element.79), kind=kOutput, calls=%fused_computation.5 | convolution fusion | flops 6445596672 | bytes 13631488 | tf_op jit(solution)/shard_map/dot_general | solution.py:322
  337.4 41.6 %all-gather.17.cloned.1.call-done = bf16[2048,1536]{1,0:T(8,128)(2,1)} async-done(((bf16[256,1536]{1,0:T(8,128)(2,1)}), bf16[2048,1536]{1,0:T(8,128)(2,1)}) %all-gather.17.cloned.1.call-update) | async-done | bytes 6291472 | tf_op jit(solution)/shard_map/all_gather | solution.py:252
  379.0 14.2 %multiply_convert_fusion = (bf16[1024,1536]{1,0:T(8,128)(2,1)S(1)}, bf16[1024,1536]{1,0:T(8,128)(2,1)S(1)}) fusion(f32[1024,1536]{1,0:T(8,128)} %fusion.70, f32[1024,1536]{1,0:T(8,128)} %get-tuple-element.210, bf16[1024,2048]{1,0:T(8,128)(2,1)} %copy-done.1, bf16[2048,1536]{1,0:T(8,128)(2,1)} %all-gather.17.cloned.1.call-done), kind=kOutput, calls=%fused_computation.6 | convolution fusion | flops 6462898176 | bytes 29360128 | tf_op jit(solution)/shard_map/dot_general | solution.py:318
  393.2 10.0 %fusion.71 = f32[1024,2048]{1,0:T(8,128)S(1)} fusion(bf16[1024,1536]{1,0:T(8,128)(2,1)S(1)} %get-tuple-element.134, bf16[2048,1536]{1,0:T(8,128)(2,1)} %all-gather.13.cloned.1.call-done), kind=kOutput, calls=%fused_computation.202 | convolution fusion | flops 6442450944 | bytes 17825792 | tf_op jit(solution)/shard_map/dot_general | solution.py:326
  403.2 8.9 %add_convert_fusion.1 = bf16[1024,2048]{1,0:T(8,128)(2,1)S(1)} fusion(f32[1024,2048]{1,0:T(8,128)S(1)} %fusion.71, bf16[1024,1536]{1,0:T(8,128)(2,1)S(1)} %get-tuple-element.133, bf16[2048,1536]{1,0:T(8,128)(2,1)} %all-gather.15.cloned.1.call-done), kind=kOutput, calls=%fused_computation.2 | convolution fusion | flops 6446645248 | bytes 22020096 | tf_op jit(solution)/shard_map/dot_general | solution.py:326
  418.8 8.8 %convolution_convert_fusion = bf16[2048,1536]{1,0:T(8,128)(2,1)} fusion(bf16[1024,2048]{1,0:T(8,128)(2,1)S(1)} %copy-done.5, bf16[1024,1536]{1,0:T(8,128)(2,1)S(1)} %get-tuple-element.133), kind=kOutput, calls=%fused_computation.3 | convolution fusion | flops 6445596672 | bytes 13631488 | tf_op jit(solution)/shard_map/dot_general | solution.py:322
  427.6 11.7 %convolution_convert_fusion.1 = bf16[2048,1536]{1,0:T(8,128)(2,1)} fusion(bf16[1024,2048]{1,0:T(8,128)(2,1)} %copy-done.4, bf16[1024,1536]{1,0:T(8,128)(2,1)} %copy-done.46), kind=kOutput, calls=%fused_computation.4 | convolution fusion | flops 6445596672 | bytes 13631488 | tf_op jit(solution)/shard_map/dot_general | solution.py:322
  445.7 2.9 add_convert_fusion.10
  452.8 9.1 %collective-permute-done.22.refs_6_ = bf16[128,2048]{1,0:T(8,128)(2,1)S(1)} collective-permute-done((bf16[128,2048]{1,0:T(8,128)(2,1)}, bf16[128,2048]{1,0:T(8,128)(2,1)S(1)}, u32[]{:S(2)}, u32[]{:S(2)}) %collective-permute-start.22) | collective-permute-done | bytes 524320 | tf_op jit(solution)/shard_map/ppermute | solution.py:26
  465.1 3.7 middle_back.1
  471.1 8.9 %collective-permute-done.23.refs_2_ = bf16[128,2048]{1,0:T(8,128)(2,1)S(1)} collective-permute-done((bf16[128,2048]{1,0:T(8,128)(2,1)S(1)}, bf16[128,2048]{1,0:T(8,128)(2,1)S(1)}, u32[]{:S(2)}, u32[]{:S(2)}) %collective-permute-start.23) | collective-permute-done | bytes 524320 | tf_op jit(solution)/shard_map/ppermute | solution.py:26
  480.4 2.8 collective-permute-done.25
  483.4 11.1 %convolution_convert_fusion.3 = bf16[1024,2048]{1,0:T(8,128)(2,1)} fusion(bf16[1024,1536]{1,0:T(8,128)(2,1)S(1)} %copy-done.48, bf16[2048,1536]{1,0:T(8,128)(2,1)} %all-gather.17.cloned.1.call-done), kind=kOutput, calls=%fused_computation.12 | convolution fusion | flops 6444548096 | bytes 13631488 | tf_op jit(solution)/shard_map/dot_general | solution.py:326
  494.5 8.9 %collective-permute-done.24.refs_0_ = bf16[256,2048]{1,0:T(8,128)(2,1)S(1)} collective-permute-done((bf16[256,2048]{1,0:T(8,128)(2,1)S(1)}, bf16[256,2048]{1,0:T(8,128)(2,1)S(1)}, u32[]{:S(2)}, u32[]{:S(2)}) %collective-permute-start.24) | collective-permute-done | bytes 1048608 | tf_op jit(solution)/shard_map/ppermute | solution.py:26
  505.7 3.4 convolution_convert_fusion.8
  509.1 11.2 %reduce-scatter.9.cloned.1.call-done.both_ref = bf16[256,1536]{1,0:T(8,128)(2,1)} async-done(((bf16[2048,1536]{1,0:T(8,128)(2,1)}), bf16[256,1536]{1,0:T(8,128)(2,1)}) %reduce-scatter.9.cloned.1.call-update) | async-done | bytes 786448 | tf_op jit(solution)/shard_map/reduce_scatter | solution.py:257
  528.0 26.1 %attend_back.1 = (f32[2,4,128,512]{3,2,1,0:T(8,128)}, bf16[8,2,4,128,512]{4,3,2,1,0:T(8,128)(2,1)}) custom-call(s32[26]{0:T(128)} %copy-done.18, bf16[2,4,128,512]{3,2,1,0:T(8,128)(2,1)} %bitcast.126, bf16[2,4,128,512]{3,2,1,0:T(8,128)(2,1)} %bitcast.150, bf16[2,4,128,512]{3,2,1,0:T(8,128)(2,1)} %copy-done.20, f32[2,2,4,1,256]{4,3,2,1,0:T(1,128)} %copy-done.22, ...), custom_call_target="tpu_custom_call" | custom-call | flops 10737418240 | bytes 16777216 | tf_op jit(solution)/shard_map/attend_back/pallas_call | solution.py:576
  559.0 11.3 %collective-permute-done.30.refs_4_ = bf16[128,2048]{1,0:T(8,128)(2,1)S(1)} collective-permute-done((bf16[128,2048]{1,0:T(8,128)(2,1)S(1)}, bf16[128,2048]{1,0:T(8,128)(2,1)S(1)}, u32[]{:S(2)}, u32[]{:S(2)}) %collective-permute-start.30) | collective-permute-done | bytes 524320 | tf_op jit(solution)/shard_map/ppermute | solution.py:26
  573.7 17.1 %reduce-scatter.11.cloned.1.call-done.both_ref = bf16[256,1536]{1,0:T(8,128)(2,1)} async-done(((bf16[2048,1536]{1,0:T(8,128)(2,1)}), bf16[256,1536]{1,0:T(8,128)(2,1)}) %reduce-scatter.11.cloned.1.call-update) | async-done | bytes 786448 | tf_op jit(solution)/shard_map/reduce_scatter | solution.py:257
  590.9 5.9 head_prep_back.2
  596.8 5.1 convolution_convert_fusion.7
  604.2 5.7 fusion.2
  609.9 4.2 collective-permute-done.31.other_ref
  622.3 4.9 convolution_convert_fusion.6
  627.1 2.7 pad_maximum_fusion
  629.8 51.1 %reduce-scatter.13.cloned.1.call-done.d_ref = bf16[1024,512]{1,0:T(8,128)(2,1)} async-done(((bf16[8192,512]{1,0:T(8,128)(2,1)}), bf16[1024,512]{1,0:T(8,128)(2,1)}) %reduce-scatter.13.cloned.1.call-update) | async-done | bytes 1048592 | tf_op jit(solution)/shard_map/reduce_scatter | solution.py:257
  681.0 4.9 head_prep_back.3
  685.9 6.7 convolution_convert_fusion.5
  692.5 7.9 multiply_reduce_fusion
  703.8 19.5 %collective-permute-done.40 = bf16[256,2048]{1,0:T(8,128)(2,1)S(1)} collective-permute-done((bf16[256,2048]{1,0:T(8,128)(2,1)S(1)}, bf16[256,2048]{1,0:T(8,128)(2,1)S(1)}, u32[]{:S(2)}, u32[]{:S(2)}) %collective-permute-start.40) | collective-permute-done | bytes 1048608 | tf_op jit(solution)/shard_map/ppermute | solution.py:26
  725.9 5.7 reduce-scatter.15.cloned.1.call-done.both_ref
  735.4 12.5 %collective-permute-done.35 = f32[4352]{0:T(1024)S(1)} collective-permute-done((f32[4352]{0:T(1024)S(1)}, f32[4352]{0:T(1024)S(1)}, u32[]{:S(2)}, u32[]{:S(2)}) %collective-permute-start.35) | collective-permute-done | bytes 17440 | tf_op jit(solution)/shard_map/ppermute | solution.py:26
  748.0 4.4 collective-permute-done.36
  752.4 5.1 collective-permute-done.37
  757.7 3.6 collective-permute-done.38
  762.5 6.2 reduce-scatter.17.cloned.1.call-done.both_ref
  778.8 4.8 entry_back.1
  783.6 2.7 collective-permute-done.43.other_ref
  (292 shorter events, 161.8 us)
Async XLA Ops:
  7.2 62.8 %all-gather.7.cloned.1.call-start = ((), (), s32[]{:S(2)}) async-start(), calls=%async_computation.6 | async-start | bytes 4718592 | tf_op jit(solution)/shard_map/all_gather | solution.py:252
  11.2 9.4 %collective-permute-start.4 = (bf16[128,1024]{1,0:T(8,128)(2,1)S(1)}, bf16[128,1024]{1,0:T(8,128)(2,1)S(1)}, u32[]{:S(2)}, u32[]{:S(2)}) collective-permute-start(bf16[128,1024]{1,0:T(8,128)(2,1)S(1)} %pad_maximum_fusion.21), channel_id=1, source_target_pairs={{0,4},{2,6},{4,0},{6,2},{8,12},{10,14},{12,8},{14,10},{16,20},{18,... | collective-permute-start | bytes 786440 | tf_op jit(solution)/shard_map/ppermute | solution.py:26
  21.5 78.7 %all-gather.9.cloned.1.call-start = ((), (), s32[]{:S(2)}) async-start(), calls=%async_computation.7 | async-start | bytes 2359296 | tf_op jit(solution)/shard_map/all_gather | solution.py:252
  21.6 5.6 collective-permute-start.10
  28.0 155.8 %all-gather.11.cloned.1.call-start = ((), (), s32[]{:S(2)}) async-start(), calls=%async_computation.8 | async-start | bytes 9437184 | tf_op jit(solution)/shard_map/all_gather | solution.py:252
  29.4 12.6 %collective-permute-start = (bf16[128,2048]{1,0:T(8,128)(2,1)S(1)}, bf16[128,2048]{1,0:T(8,128)(2,1)S(1)}, u32[]{:S(2)}, u32[]{:S(2)}) collective-permute-start(bf16[128,2048]{1,0:T(8,128)(2,1)S(1)} %get-tuple-element.171.refs_1_), channel_id=1, source_target_pairs={{0,1},{1,0},{2,3},{3,2},{4,5},{5,4},{6,7},{7,6},{8,9},{9,8},{10,11... | collective-permute-start | bytes 1572872 | tf_op jit(solution)/shard_map/ppermute | solution.py:26
  30.9 12.8 %collective-permute-start.2 = (bf16[128,2048]{1,0:T(8,128)(2,1)S(1)}, bf16[128,2048]{1,0:T(8,128)(2,1)S(1)}, u32[]{:S(2)}, u32[]{:S(2)}) collective-permute-start(bf16[128,2048]{1,0:T(8,128)(2,1)S(1)} %get-tuple-element.170), channel_id=1, source_target_pairs={{0,4},{2,6},{4,0},{6,2},{8,12},{10,14},{12,8},{14,10},{16,20},{18,... | collective-permute-start | bytes 1572872 | tf_op jit(solution)/shard_map/ppermute | solution.py:26
  42.0 23.6 %collective-permute-start.1 = (bf16[256,2048]{1,0:T(8,128)(2,1)S(1)}, bf16[256,2048]{1,0:T(8,128)(2,1)S(1)}, u32[]{:S(2)}, u32[]{:S(2)}) collective-permute-start(bf16[256,2048]{1,0:T(8,128)(2,1)S(1)} %pad_maximum_fusion.4), channel_id=1, source_target_pairs={{0,4},{2,6},{4,0},{6,2},{8,12},{10,14},{12,8},{14,10},{16,20},{18,... | collective-permute-start | bytes 3145736 | tf_op jit(solution)/shard_map/ppermute | solution.py:26
  43.8 22.3 %collective-permute-start.3 = (bf16[256,2048]{1,0:T(8,128)(2,1)S(1)}, bf16[256,2048]{1,0:T(8,128)(2,1)S(1)}, u32[]{:S(2)}, u32[]{:S(2)}) collective-permute-start(bf16[256,2048]{1,0:T(8,128)(2,1)S(1)} %pad_maximum_fusion.5.refs_3_), channel_id=1, source_target_pairs={{0,1},{1,0},{2,3},{3,2},{4,5},{5,4},{6,7},{7,6},{8,9},{9,8},{10,11... | collective-permute-start | bytes 3145736 | tf_op jit(solution)/shard_map/ppermute | solution.py:26
  80.0 20.3 %copy-start.32 = (bf16[128,3072]{1,0:T(8,128)(2,1)S(1)}, bf16[128,3072]{1,0:T(8,128)(2,1)}, u32[]{:S(2)}) copy-start(bf16[128,3072]{1,0:T(8,128)(2,1)} %param.21) | copy-start | bytes 2359300
  80.0 20.4 %copy-start.33 = (bf16[128,3072]{1,0:T(8,128)(2,1)S(1)}, bf16[128,3072]{1,0:T(8,128)(2,1)}, u32[]{:S(2)}) copy-start(bf16[128,3072]{1,0:T(8,128)(2,1)} %param.23) | copy-start | bytes 2359300
  80.0 20.4 %copy-start.34 = (bf16[128,3072]{1,0:T(8,128)(2,1)S(1)}, bf16[128,3072]{1,0:T(8,128)(2,1)}, u32[]{:S(2)}) copy-start(bf16[128,3072]{1,0:T(8,128)(2,1)} %param.22) | copy-start | bytes 2359300
  100.2 194.4 %all-gather.13.cloned.1.call-start = ((), (), s32[]{:S(2)}) async-start(), calls=%async_computation.9 | async-start | bytes 7077888 | tf_op jit(solution)/shard_map/all_gather | solution.py:252
  100.6 28.2 %collective-permute-start.5 = (bf16[128,4608]{1,0:T(8,128)(2,1)S(1)}, bf16[128,4608]{1,0:T(8,128)(2,1)S(1)}, u32[]{:S(2)}, u32[]{:S(2)}) collective-permute-start(bf16[128,4608]{1,0:T(8,128)(2,1)S(1)} %pad_maximum_fusion.3), channel_id=1, source_target_pairs={{0,4},{2,6},{4,0},{6,2},{8,12},{10,14},{12,8},{14,10},{16,20},{18,... | collective-permute-start | bytes 3538952 | tf_op jit(solution)/shard_map/ppermute | solution.py:26
  130.8 182.8 %all-gather.15.cloned.1.call-start = ((), (), s32[]{:S(2)}) async-start(), calls=%async_computation.10 | async-start | bytes 7077888 | tf_op jit(solution)/shard_map/all_gather | solution.py:252
  131.4 247.6 %all-gather.17.cloned.1.call-start = ((), (), s32[]{:S(2)}) async-start(), calls=%async_computation.11 | async-start | bytes 7077888 | tf_op jit(solution)/shard_map/all_gather | solution.py:252
  132.0 13.4 %collective-permute-start.6 = (bf16[128,2048]{1,0:T(8,128)(2,1)S(1)}, bf16[128,2048]{1,0:T(8,128)(2,1)S(1)}, u32[]{:S(2)}, u32[]{:S(2)}) collective-permute-start(bf16[128,2048]{1,0:T(8,128)(2,1)S(1)} %get-tuple-element.169.refs_1_), channel_id=1, source_target_pairs={{0,1},{1,0},{2,3},{3,2},{4,5},{5,4},{6,7},{7,6},{8,9},{9,8},{10,11... | collective-permute-start | bytes 1572872 | tf_op jit(solution)/shard_map/ppermute | solution.py:26
  133.5 14.4 %collective-permute-start.8 = (bf16[128,2048]{1,0:T(8,128)(2,1)S(1)}, bf16[128,2048]{1,0:T(8,128)(2,1)S(1)}, u32[]{:S(2)}, u32[]{:S(2)}) collective-permute-start(bf16[128,2048]{1,0:T(8,128)(2,1)S(1)} %get-tuple-element.168), channel_id=1, source_target_pairs={{0,4},{2,6},{4,0},{6,2},{8,12},{10,14},{12,8},{14,10},{16,20},{18,... | collective-permute-start | bytes 1572872 | tf_op jit(solution)/shard_map/ppermute | solution.py:26
  146.4 24.1 %collective-permute-start.7 = (bf16[256,2048]{1,0:T(8,128)(2,1)}, bf16[256,2048]{1,0:T(8,128)(2,1)}, u32[]{:S(2)}, u32[]{:S(2)}) collective-permute-start(bf16[256,2048]{1,0:T(8,128)(2,1)} %pad_maximum_fusion.6), channel_id=1, source_target_pairs={{0,4},{2,6},{4,0},{6,2},{8,12},{10,14},{12,8},{14,10},{16,20},{18,... | collective-permute-start | bytes 3145736 | tf_op jit(solution)/shard_map/ppermute | solution.py:26
  147.9 23.7 %collective-permute-start.9 = (bf16[256,2048]{1,0:T(8,128)(2,1)S(1)}, bf16[256,2048]{1,0:T(8,128)(2,1)}, u32[]{:S(2)}, u32[]{:S(2)}) collective-permute-start(bf16[256,2048]{1,0:T(8,128)(2,1)S(1)} %pad_maximum_fusion.7.refs_3_), channel_id=1, source_target_pairs={{0,1},{1,0},{2,3},{3,2},{4,5},{5,4},{6,7},{7,6},{8,9},{9,8},{10,11... | collective-permute-start | bytes 3145736 | tf_op jit(solution)/shard_map/ppermute | solution.py:26
  207.4 23.2 %collective-permute-start.11 = (bf16[256,2048]{1,0:T(8,128)(2,1)}, bf16[256,2048]{1,0:T(8,128)(2,1)S(1)}, u32[]{:S(2)}, u32[]{:S(2)}) collective-permute-start(bf16[256,2048]{1,0:T(8,128)(2,1)} %pad_maximum_fusion.8), channel_id=1, source_target_pairs={{0,4},{2,6},{4,0},{6,2},{8,12},{10,14},{12,8},{14,10},{16,20},{18,... | collective-permute-start | bytes 3145736 | tf_op jit(solution)/shard_map/ppermute | solution.py:26
  209.9 23.8 %collective-permute-start.13 = (bf16[256,2048]{1,0:T(8,128)(2,1)}, bf16[256,2048]{1,0:T(8,128)(2,1)S(1)}, u32[]{:S(2)}, u32[]{:S(2)}) collective-permute-start(bf16[256,2048]{1,0:T(8,128)(2,1)} %slice.319), channel_id=1, source_target_pairs={{0,1},{1,0},{2,3},{3,2},{4,5},{5,4},{6,7},{7,6},{8,9},{9,8},{10,11... | collective-permute-start | bytes 3145736 | tf_op jit(solution)/shard_map/ppermute | solution.py:26
  211.4 25.6 %copy-start.40 = (f32[2048]{0:T(1024)S(1)}, f32[2048]{0:T(1024)}, u32[]{:S(2)}) copy-start(f32[2048]{0:T(1024)} %param.25) | copy-start | bytes 24580
  211.4 238.3 %reduce-scatter.7.cloned.1.call-start = ((), (), s32[]{:S(2)}) async-start(), calls=%async_computation.12 | async-start | bytes 7077888 | tf_op jit(solution)/shard_map/reduce_scatter | solution.py:257
  211.5 36.8 %copy-start.7 = (bf16[256,2048]{1,0:T(8,128)(2,1)S(1)}, bf16[256,2048]{1,0:T(8,128)(2,1)}, u32[]{:S(2)}) copy-start(bf16[256,2048]{1,0:T(8,128)(2,1)} %copy-done.6) | copy-start | bytes 3145732
  232.2 13.3 %collective-permute-start.12 = (bf16[128,2048]{1,0:T(8,128)(2,1)S(1)}, bf16[128,2048]{1,0:T(8,128)(2,1)S(1)}, u32[]{:S(2)}, u32[]{:S(2)}) collective-permute-start(bf16[128,2048]{1,0:T(8,128)(2,1)S(1)} %get-tuple-element.141), channel_id=1, source_target_pairs={{0,1},{1,0},{2,3},{3,2},{4,5},{5,4},{6,7},{7,6},{8,9},{9,8},{10,11... | collective-permute-start | bytes 1572872 | tf_op jit(solution)/shard_map/ppermute | solution.py:26
  235.4 12.8 %collective-permute-start.14 = (bf16[128,2048]{1,0:T(8,128)(2,1)S(1)}, bf16[128,2048]{1,0:T(8,128)(2,1)S(1)}, u32[]{:S(2)}, u32[]{:S(2)}) collective-permute-start(bf16[128,2048]{1,0:T(8,128)(2,1)S(1)} %get-tuple-element.166), channel_id=1, source_target_pairs={{0,4},{2,6},{4,0},{6,2},{8,12},{10,14},{12,8},{14,10},{16,20},{18,... | collective-permute-start | bytes 1572872 | tf_op jit(solution)/shard_map/ppermute | solution.py:26
  250.4 14.0 %collective-permute-start.15 = (bf16[128,2048]{1,0:T(8,128)(2,1)S(1)}, bf16[128,2048]{1,0:T(8,128)(2,1)S(1)}, u32[]{:S(2)}, u32[]{:S(2)}) collective-permute-start(bf16[128,2048]{1,0:T(8,128)(2,1)S(1)} %get-tuple-element.165.refs_1_), channel_id=1, source_target_pairs={{0,1},{1,0},{2,3},{3,2},{4,5},{5,4},{6,7},{7,6},{8,9},{9,8},{10,11... | collective-permute-start | bytes 1572872 | tf_op jit(solution)/shard_map/ppermute | solution.py:26
  251.3 14.9 %collective-permute-start.17 = (bf16[128,2048]{1,0:T(8,128)(2,1)S(1)}, bf16[128,2048]{1,0:T(8,128)(2,1)S(1)}, u32[]{:S(2)}, u32[]{:S(2)}) collective-permute-start(bf16[128,2048]{1,0:T(8,128)(2,1)S(1)} %get-tuple-element.164), channel_id=1, source_target_pairs={{0,4},{2,6},{4,0},{6,2},{8,12},{10,14},{12,8},{14,10},{16,20},{18,... | collective-permute-start | bytes 1572872 | tf_op jit(solution)/shard_map/ppermute | solution.py:26
  264.5 26.0 %collective-permute-start.16 = (bf16[256,2048]{1,0:T(8,128)(2,1)S(1)}, bf16[256,2048]{1,0:T(8,128)(2,1)S(1)}, u32[]{:S(2)}, u32[]{:S(2)}) collective-permute-start(bf16[256,2048]{1,0:T(8,128)(2,1)S(1)} %pad_maximum_fusion.9), channel_id=1, source_target_pairs={{0,4},{2,6},{4,0},{6,2},{8,12},{10,14},{12,8},{14,10},{16,20},{18,... | collective-permute-start | bytes 3145736 | tf_op jit(solution)/shard_map/ppermute | solution.py:26
  266.3 25.9 %collective-permute-start.18 = (bf16[256,2048]{1,0:T(8,128)(2,1)S(1)}, bf16[256,2048]{1,0:T(8,128)(2,1)S(1)}, u32[]{:S(2)}, u32[]{:S(2)}) collective-permute-start(bf16[256,2048]{1,0:T(8,128)(2,1)S(1)} %pad_maximum_fusion.10.refs_3_), channel_id=1, source_target_pairs={{0,1},{1,0},{2,3},{3,2},{4,5},{5,4},{6,7},{7,6},{8,9},{9,8},{10,11... | collective-permute-start | bytes 3145736 | tf_op jit(solution)/shard_map/ppermute | solution.py:26
  337.2 183.1 %reduce-scatter.9.cloned.1.call-start = ((), (), s32[]{:S(2)}) async-start(), calls=%async_computation.13 | async-start | bytes 7077888 | tf_op jit(solution)/shard_map/reduce_scatter | solution.py:257
  415.9 25.6 %collective-permute-start.19 = (bf16[256,2048]{1,0:T(8,128)(2,1)}, bf16[256,2048]{1,0:T(8,128)(2,1)}, u32[]{:S(2)}, u32[]{:S(2)}) collective-permute-start(bf16[256,2048]{1,0:T(8,128)(2,1)} %pad_maximum_fusion.11), channel_id=1, source_target_pairs={{0,4},{2,6},{4,0},{6,2},{8,12},{10,14},{12,8},{14,10},{16,20},{18,... | collective-permute-start | bytes 3145736 | tf_op jit(solution)/shard_map/ppermute | solution.py:26
  417.4 25.3 %collective-permute-start.20 = (bf16[256,2048]{1,0:T(8,128)(2,1)}, bf16[256,2048]{1,0:T(8,128)(2,1)}, u32[]{:S(2)}, u32[]{:S(2)}) collective-permute-start(bf16[256,2048]{1,0:T(8,128)(2,1)} %slice.325), channel_id=1, source_target_pairs={{0,1},{1,0},{2,3},{3,2},{4,5},{5,4},{6,7},{7,6},{8,9},{9,8},{10,11... | collective-permute-start | bytes 3145736 | tf_op jit(solution)/shard_map/ppermute | solution.py:26
  449.7 141.0 %reduce-scatter.11.cloned.1.call-start = ((), (), s32[]{:S(2)}) async-start(), calls=%async_computation.14 | async-start | bytes 7077888 | tf_op jit(solution)/shard_map/reduce_scatter | solution.py:257
  449.8 12.1 %collective-permute-start.22 = (bf16[128,2048]{1,0:T(8,128)(2,1)}, bf16[128,2048]{1,0:T(8,128)(2,1)S(1)}, u32[]{:S(2)}, u32[]{:S(2)}) collective-permute-start(bf16[128,2048]{1,0:T(8,128)(2,1)} %get-tuple-element.162), channel_id=1, source_target_pairs={{0,4},{2,6},{4,0},{6,2},{8,12},{10,14},{12,8},{14,10},{16,20},{18,... | collective-permute-start | bytes 1572872 | tf_op jit(solution)/shard_map/ppermute | solution.py:26
  451.3 11.7 %collective-permute-start.21 = (bf16[128,2048]{1,0:T(8,128)(2,1)}, bf16[128,2048]{1,0:T(8,128)(2,1)S(1)}, u32[]{:S(2)}, u32[]{:S(2)}) collective-permute-start(bf16[128,2048]{1,0:T(8,128)(2,1)} %get-tuple-element.139), channel_id=1, source_target_pairs={{0,1},{1,0},{2,3},{3,2},{4,5},{5,4},{6,7},{7,6},{8,9},{9,8},{10,11... | collective-permute-start | bytes 1572872 | tf_op jit(solution)/shard_map/ppermute | solution.py:26
  469.0 11.0 %collective-permute-start.23 = (bf16[128,2048]{1,0:T(8,128)(2,1)S(1)}, bf16[128,2048]{1,0:T(8,128)(2,1)S(1)}, u32[]{:S(2)}, u32[]{:S(2)}) collective-permute-start(bf16[128,2048]{1,0:T(8,128)(2,1)S(1)} %get-tuple-element.161.refs_1_), channel_id=1, source_target_pairs={{0,1},{1,0},{2,3},{3,2},{4,5},{5,4},{6,7},{7,6},{8,9},{9,8},{10,11... | collective-permute-start | bytes 1572872 | tf_op jit(solution)/shard_map/ppermute | solution.py:26
  470.5 12.7 %collective-permute-start.25 = (bf16[128,2048]{1,0:T(8,128)(2,1)S(1)}, bf16[128,2048]{1,0:T(8,128)(2,1)S(1)}, u32[]{:S(2)}, u32[]{:S(2)}) collective-permute-start(bf16[128,2048]{1,0:T(8,128)(2,1)S(1)} %get-tuple-element.160), channel_id=1, source_target_pairs={{0,4},{2,6},{4,0},{6,2},{8,12},{10,14},{12,8},{14,10},{16,20},{18,... | collective-permute-start | bytes 1572872 | tf_op jit(solution)/shard_map/ppermute | solution.py:26
  480.1 23.3 %collective-permute-start.24 = (bf16[256,2048]{1,0:T(8,128)(2,1)S(1)}, bf16[256,2048]{1,0:T(8,128)(2,1)S(1)}, u32[]{:S(2)}, u32[]{:S(2)}) collective-permute-start(bf16[256,2048]{1,0:T(8,128)(2,1)S(1)} %pad_maximum_fusion.12), channel_id=1, source_target_pairs={{0,4},{2,6},{4,0},{6,2},{8,12},{10,14},{12,8},{14,10},{16,20},{18,... | collective-permute-start | bytes 3145736 | tf_op jit(solution)/shard_map/ppermute | solution.py:26
  483.3 20.0 %collective-permute-start.26 = (bf16[256,2048]{1,0:T(8,128)(2,1)S(1)}, bf16[256,2048]{1,0:T(8,128)(2,1)S(1)}, u32[]{:S(2)}, u32[]{:S(2)}) collective-permute-start(bf16[256,2048]{1,0:T(8,128)(2,1)S(1)} %pad_maximum_fusion.13.refs_3_), channel_id=1, source_target_pairs={{0,1},{1,0},{2,3},{3,2},{4,5},{5,4},{6,7},{7,6},{8,9},{9,8},{10,11... | collective-permute-start | bytes 3145736 | tf_op jit(solution)/shard_map/ppermute | solution.py:26
  520.3 160.6 %reduce-scatter.13.cloned.1.call-start = ((), (), s32[]{:S(2)}) async-start(), calls=%async_computation.15 | async-start | bytes 9437184 | tf_op jit(solution)/shard_map/reduce_scatter | solution.py:257
  525.0 29.0 %collective-permute-start.27 = (bf16[256,2048]{1,0:T(8,128)(2,1)}, bf16[256,2048]{1,0:T(8,128)(2,1)S(1)}, u32[]{:S(2)}, u32[]{:S(2)}) collective-permute-start(bf16[256,2048]{1,0:T(8,128)(2,1)} %pad_maximum_fusion.14), channel_id=1, source_target_pairs={{0,4},{2,6},{4,0},{6,2},{8,12},{10,14},{12,8},{14,10},{16,20},{18,... | collective-permute-start | bytes 3145736 | tf_op jit(solution)/shard_map/ppermute | solution.py:26
  526.5 27.6 %collective-permute-start.28 = (bf16[256,2048]{1,0:T(8,128)(2,1)}, bf16[256,2048]{1,0:T(8,128)(2,1)}, u32[]{:S(2)}, u32[]{:S(2)}) collective-permute-start(bf16[256,2048]{1,0:T(8,128)(2,1)} %slice.273), channel_id=1, source_target_pairs={{0,1},{1,0},{2,3},{3,2},{4,5},{5,4},{6,7},{7,6},{8,9},{9,8},{10,11... | collective-permute-start | bytes 3145736 | tf_op jit(solution)/shard_map/ppermute | solution.py:26
  528.0 27.1 %copy-start.23 = (bf16[1024,2048]{1,0:T(8,128)(2,1)S(1)}, bf16[1024,2048]{1,0:T(8,128)(2,1)}, u32[]{:S(2)}) copy-start(bf16[1024,2048]{1,0:T(8,128)(2,1)} %convolution_convert_fusion.3) | copy-start | bytes 12582916
  556.9 13.5 %collective-permute-start.30 = (bf16[128,2048]{1,0:T(8,128)(2,1)S(1)}, bf16[128,2048]{1,0:T(8,128)(2,1)S(1)}, u32[]{:S(2)}, u32[]{:S(2)}) collective-permute-start(bf16[128,2048]{1,0:T(8,128)(2,1)S(1)} %get-tuple-element.158), channel_id=1, source_target_pairs={{0,4},{2,6},{4,0},{6,2},{8,12},{10,14},{12,8},{14,10},{16,20},{18,... | collective-permute-start | bytes 1572872 | tf_op jit(solution)/shard_map/ppermute | solution.py:26
  558.1 14.2 %collective-permute-start.29 = (bf16[128,2048]{1,0:T(8,128)(2,1)S(1)}, bf16[128,2048]{1,0:T(8,128)(2,1)S(1)}, u32[]{:S(2)}, u32[]{:S(2)}) collective-permute-start(bf16[128,2048]{1,0:T(8,128)(2,1)S(1)} %get-tuple-element.137), channel_id=1, source_target_pairs={{0,1},{1,0},{2,3},{3,2},{4,5},{5,4},{6,7},{7,6},{8,9},{9,8},{10,11... | collective-permute-start | bytes 1572872 | tf_op jit(solution)/shard_map/ppermute | solution.py:26
  590.8 140.8 %reduce-scatter.15.cloned.1.call-start = ((), (), s32[]{:S(2)}) async-start(), calls=%async_computation.16 | async-start | bytes 4718592 | tf_op jit(solution)/shard_map/reduce_scatter | solution.py:257
  602.0 12.2 %collective-permute-start.31 = (bf16[128,1536]{1,0:T(8,128)(2,1)S(1)}, bf16[128,1536]{1,0:T(8,128)(2,1)}, u32[]{:S(2)}, u32[]{:S(2)}) collective-permute-start(bf16[128,1536]{1,0:T(8,128)(2,1)S(1)} %constant_dynamic-slice_fusion.4), channel_id=1, source_target_pairs={{0,4},{2,6},{4,0},{6,2},{8,12},{10,14},{12,8},{14,10},{16,20},{18,... | collective-permute-start | bytes 1179656 | tf_op jit(solution)/shard_map/ppermute | solution.py:26
  603.8 15.2 %collective-permute-start.32 = (bf16[128,1536]{1,0:T(8,128)(2,1)S(1)}, bf16[128,1536]{1,0:T(8,128)(2,1)S(1)}, u32[]{:S(2)}, u32[]{:S(2)}) collective-permute-start(bf16[128,1536]{1,0:T(8,128)(2,1)S(1)} %constant_dynamic-slice_fusion.3), channel_id=1, source_target_pairs={{0,4},{2,6},{4,0},{6,2},{8,12},{10,14},{12,8},{14,10},{16,20},{18,... | collective-permute-start | bytes 1179656 | tf_op jit(solution)/shard_map/ppermute | solution.py:26
  680.9 87.8 %reduce-scatter.17.cloned.1.call-start = ((), (), s32[]{:S(2)}) async-start(), calls=%async_computation.17 | async-start | bytes 2359296 | tf_op jit(solution)/shard_map/reduce_scatter | solution.py:257
  700.5 22.7 %collective-permute-start.40 = (bf16[256,2048]{1,0:T(8,128)(2,1)S(1)}, bf16[256,2048]{1,0:T(8,128)(2,1)S(1)}, u32[]{:S(2)}, u32[]{:S(2)}) collective-permute-start(bf16[256,2048]{1,0:T(8,128)(2,1)S(1)} %slice.341), channel_id=1, source_target_pairs={{0,1},{1,0},{2,3},{3,2},{4,5},{5,4},{6,7},{7,6},{8,9},{9,8},{10,11... | collective-permute-start | bytes 3145736 | tf_op jit(solution)/shard_map/ppermute | solution.py:26
  702.2 22.5 %collective-permute-start.33 = (bf16[256,2048]{1,0:T(8,128)(2,1)S(1)}, bf16[256,2048]{1,0:T(8,128)(2,1)S(1)}, u32[]{:S(2)}, u32[]{:S(2)}) collective-permute-start(bf16[256,2048]{1,0:T(8,128)(2,1)S(1)} %pad_maximum_fusion.15), channel_id=1, source_target_pairs={{0,4},{2,6},{4,0},{6,2},{8,12},{10,14},{12,8},{14,10},{16,20},{18,... | collective-permute-start | bytes 3145736 | tf_op jit(solution)/shard_map/ppermute | solution.py:26
  723.7 53.5 %copy-start.8 = (bf16[256,2048]{1,0:T(8,128)(2,1)S(1)}, bf16[256,2048]{1,0:T(8,128)(2,1)}, u32[]{:S(2)}) copy-start(bf16[256,2048]{1,0:T(8,128)(2,1)} %copy-done.6) | copy-start | bytes 3145732
  731.7 3.1 collective-permute-start.34
  731.8 30.7 %collective-permute-start.39 = (bf16[128,2048]{1,0:T(8,128)(2,1)}, bf16[128,2048]{1,0:T(8,128)(2,1)S(1)}, u32[]{:S(2)}, u32[]{:S(2)}) collective-permute-start(bf16[128,2048]{1,0:T(8,128)(2,1)} %get-tuple-element.135), channel_id=1, source_target_pairs={{0,1},{1,0},{2,3},{3,2},{4,5},{5,4},{6,7},{7,6},{8,9},{9,8},{10,11... | collective-permute-start | bytes 1572872 | tf_op jit(solution)/shard_map/ppermute | solution.py:26
  733.3 29.2 %collective-permute-start.41 = (bf16[128,2048]{1,0:T(8,128)(2,1)}, bf16[128,2048]{1,0:T(8,128)(2,1)S(1)}, u32[]{:S(2)}, u32[]{:S(2)}) collective-permute-start(bf16[128,2048]{1,0:T(8,128)(2,1)} %get-tuple-element.156), channel_id=1, source_target_pairs={{0,4},{2,6},{4,0},{6,2},{8,12},{10,14},{12,8},{14,10},{16,20},{18,... | collective-permute-start | bytes 1572872 | tf_op jit(solution)/shard_map/ppermute | solution.py:26
  734.8 13.1 %collective-permute-start.35 = (f32[4352]{0:T(1024)S(1)}, f32[4352]{0:T(1024)S(1)}, u32[]{:S(2)}, u32[]{:S(2)}) collective-permute-start(f32[4352]{0:T(1024)S(1)} %fusion.37), channel_id=1, source_target_pairs={{0,4},{2,6},{4,0},{6,2},{8,12},{10,14},{12,8},{14,10},{16,20},{18,... | collective-permute-start | bytes 52232 | tf_op jit(solution)/shard_map/ppermute | solution.py:26
  748.0 4.4 collective-permute-start.36
  752.4 5.1 collective-permute-start.37
  757.5 3.8 collective-permute-start.38
  769.8 20.4 %collective-permute-start.44 = (bf16[128,1536]{1,0:T(8,128)(2,1)S(1)}, bf16[128,1536]{1,0:T(8,128)(2,1)}, u32[]{:S(2)}, u32[]{:S(2)}) collective-permute-start(bf16[128,1536]{1,0:T(8,128)(2,1)S(1)} %constant_dynamic-slice_fusion), channel_id=1, source_target_pairs={{0,4},{2,6},{4,0},{6,2},{8,12},{10,14},{12,8},{14,10},{16,20},{18,... | collective-permute-start | bytes 1179656 | tf_op jit(solution)/shard_map/ppermute | solution.py:26
  772.9 15.2 %collective-permute-start.42 = (bf16[128,1024]{1,0:T(8,128)(2,1)}, bf16[128,1024]{1,0:T(8,128)(2,1)}, u32[]{:S(2)}, u32[]{:S(2)}) collective-permute-start(bf16[128,1024]{1,0:T(8,128)(2,1)} %constant_dynamic-slice_fusion.2), channel_id=1, source_target_pairs={{0,4},{2,6},{4,0},{6,2},{8,12},{10,14},{12,8},{14,10},{16,20},{18,... | collective-permute-start | bytes 786440 | tf_op jit(solution)/shard_map/ppermute | solution.py:26
  774.5 11.8 %collective-permute-start.43 = (bf16[128,512]{1,0:T(8,128)(2,1)S(1)}, bf16[128,512]{1,0:T(8,128)(2,1)}, u32[]{:S(2)}, u32[]{:S(2)}) collective-permute-start(bf16[128,512]{1,0:T(8,128)(2,1)S(1)} %constant_dynamic-slice_fusion.1), channel_id=1, source_target_pairs={{0,4},{2,6},{4,0},{6,2},{8,12},{10,14},{12,8},{14,10},{16,20},{18,... | collective-permute-start | bytes 393224 | tf_op jit(solution)/shard_map/ppermute | solution.py:26
  (42 other events, 279.1 us)
Sparse Core Ops, SparseCore 0:
  21.6 48.3 all-gather.6
  72.2 27.9 all-gather.8
  102.4 81.4 all-gather.10
  185.3 63.2 all-gather.12
  250.1 63.3 all-gather.14
  315.6 63.3 all-gather.16
  381.3 68.3 reduce-scatter.6
  452.0 68.1 reduce-scatter.8
  522.6 68.1 reduce-scatter.10
  592.9 87.9 reduce-scatter.12
  683.2 48.3 reduce-scatter.14
  733.8 34.9 reduce-scatter.16

commit v8 on v7

--- a/solution.py
+++ b/solution.py
@@ -757,7 +757,8 @@
         (rows_up, out_tokens),
     )
     d_kv = ctx_scatter(d_kv, ways)
-    h1_late = after(h1, (d_h1_query, shard_down, shard_gate))
+    shard_up = one(rows_up, 2)
+    h1_late = after(h1, (d_h1_query, shard_down, shard_gate, shard_up))
     grad_query = dot_rows(h1_late, d_qp).astype(BF16)
     grad_both = jnp.concatenate([grad_output, grad_query], axis=1)
     rows_both = scatter_weight(after(grad_both, d_kv), ways)
@@ -773,17 +774,18 @@
     )
     lows, highs = return_rows(d_h1, ways)
     rows_kv = scatter_weight(after(grad_kv, (rows_both, lows[0], highs[0])), ways)
-    lows[0] = after(lows[0], gains)
+    plan = [(0, q_width, 0, 0), (q_width, q_width, 1, 0)]
+    shard_output, shard_query = own_rows(
+        after(rows_both, lows[0]), pair, ways, plan, [q_width, q_width]
+    )
+    lows[0] = after(lows[0], (gains, shard_output, shard_query))
     grad_tokens = row_pass(
         functools.partial(back_kernel, len(lows), len(highs), ctx_count),
         (d_x2, inputs, gain_attn_row, *lows, *highs),
         row_f32,
         "entry_back",
     )
-    rows_up, rows_both, rows_kv = after((rows_up, rows_both, rows_kv), (lows, highs))
-    shard_up = one(rows_up, 2)
-    plan = [(0, q_width, 0, 0), (q_width, q_width, 1, 0)]
-    shard_output, shard_query = own_rows(rows_both, pair, ways, plan, [q_width, q_width])
+    rows_kv = after(rows_kv, (lows, highs))
     plan = []
     for h in range(groups):
         for t in (0, 1):

time: 809 us -> 797 us (0.985)
  waiting for transfers between devices: 394 us -> 365 us
  Pallas kernels: 89.5 us -> 104 us
    reduce_scatter x6, waiting for transfers between devices: 92.4 us -> 77.1 us  [ctx_scatter(): lax.psum_scatter(rows, 'ctx', scatter_dimension=0, tiled=True, axis_index...]
    ppermute x45, waiting for transfers between devices: 228 us -> 213 us  [xor_send(): return lax.ppermute(value, axis, [(i, i ^ step) for i in range(count)])]
    unnamed x98 -> x102, local copies, waits for them, and re-layouts: 19.9 us -> 21.4 us
  transfers between devices with their start and end apart: 57 -> 57, of which waited for: 44 -> 43; matrix products, arithmetic and copies ran while one was open for 28% -> 28% of each run, Pallas kernels for 11% -> 13%
where the time goes in v8:
time: 797 us; the launch traced here: 789 us
  waiting for transfers between devices  365 us (46%)
  matrix products  145 us (18%)
  Pallas kernels  104 us (13%)
  starting transfers between devices  56.6 us (7%)
  local copies, waits for them, and re-layouts  55.4 us (7%)
  other arithmetic  47.7 us (6%)
  between operations  15.4 us (2%)
    ppermute x45, waiting for transfers between devices, xor_send(): return lax.ppermute(value, axis, [(i, i ^ step) for i in range(count)])  213 us
    reduce_scatter x6, waiting for transfers between devices, ctx_scatter(): lax.psum_scatter(rows, 'ctx', scatter_dimension=0, tiled=True, axis_index...  77.1 us
    all_gather x6, waiting for transfers between devices, ctx_gather(): lax.all_gather(rows, 'ctx', axis=0, tiled=True, axis_index_groups=groups)  73.6 us
    ppermute x45, starting transfers between devices, xor_send(): return lax.ppermute(value, axis, [(i, i ^ step) for i in range(count)])  55.5 us
    dot_general x5, matrix products, dot(): return jnp.dot(left, right, preferred_element_type=F32)  52.4 us
    dot_general x6, matrix products, dot_rows(): lax.dot_general(left, right, (((0,), (0,)), ((), ())), preferred_element_...  46.4 us
    dot_general x6, matrix products, dot_cols(): lax.dot_general(left, right, (((1,), (1,)), ((), ())), preferred_element_...  45.9 us
    pallas_call x1, Pallas kernels, attend_back(): pl.pallas_call(functools.partial(backward_kernel, ways, count), out_shape...  34 us
  transfers between devices with their start and end apart: 57, of which 43 were waited for; matrix products, arithmetic and copies ran while one was open for 28% of the time, Pallas kernels for 13%

profile of v8, /device:TPU:0, one launch (start us, length us, event | category | flops | bytes accessed | tf_op | source)
XLA Modules:
  0.0 788.6 jit_solution(15333921390765244481)
XLA Ops:
  11.2 3.1 collective-permute-start.4
  14.2 6.3 collective-permute-done.4
  32.9 2.7 constant_dynamic-update-slice_fusion.7
  35.5 2.7 constant_dynamic-update-slice_fusion.6
  38.2 2.7 constant_dynamic-update-slice_fusion.5
  44.3 2.7 constant_dynamic-update-slice_fusion.4
  47.0 2.7 constant_dynamic-update-slice_fusion.3
  49.6 2.7 constant_dynamic-update-slice_fusion.2
  52.3 2.7 constant_dynamic-update-slice_fusion.1
  55.0 2.7 constant_dynamic-update-slice_fusion
  60.9 4.8 collective-permute-done.1.refs_0_
  70.0 10.0 %fusion.69.raw_ref = f32[1024,1024]{1,0:T(8,128)} fusion(bf16[1024,2048]{1,0:T(8,128)(2,1)} %copy-done, bf16[2048,1024]{1,0:T(8,128)(2,1)} %all-gather.7.cloned.1.call-done), kind=kOutput, calls=%fused_computation.200 | convolution fusion | flops 4294967296 | bytes 12582912 | tf_op jit(solution)/shard_map/dot_general | solution.py:318
  80.0 6.3 head_prep.1
  86.2 13.9 %all-gather.9.cloned.1.call-done = bf16[2048,512]{1,0:T(8,128)(2,1)} async-done(((bf16[256,512]{1,0:T(8,128)(2,1)}), bf16[2048,512]{1,0:T(8,128)(2,1)}) %all-gather.9.cloned.1.call-update) | async-done | bytes 2097168 | tf_op jit(solution)/shard_map/all_gather | solution.py:252
  102.1 26.6 %collective-permute-done.5 = bf16[128,4608]{1,0:T(8,128)(2,1)S(1)} collective-permute-done((bf16[128,4608]{1,0:T(8,128)(2,1)S(1)}, bf16[128,4608]{1,0:T(8,128)(2,1)S(1)}, u32[]{:S(2)}, u32[]{:S(2)}) %collective-permute-start.5) | collective-permute-done | bytes 1179680 | tf_op jit(solution)/shard_map/ppermute | solution.py:26
  135.0 10.4 %collective-permute-done.6.refs_2_ = bf16[128,2048]{1,0:T(8,128)(2,1)S(1)} collective-permute-done((bf16[128,2048]{1,0:T(8,128)(2,1)S(1)}, bf16[128,2048]{1,0:T(8,128)(2,1)S(1)}, u32[]{:S(2)}, u32[]{:S(2)}) %collective-permute-start.6) | collective-permute-done | bytes 524320 | tf_op jit(solution)/shard_map/ppermute | solution.py:26
  154.3 10.3 %stack.31.info_ref = s32[26]{0:T(128)S(1)} concatenate(s32[1]{0:T(128)} %bitcast.8.pair_ref, s32[1]{0:T(128)} %bitcast.9, s32[1]{0:T(128)} %bitcast.10, s32[1]{0:T(128)} %bitcast.11, s32[1]{0:T(128)} %bitcast.12, s32[1]{0:T(128)} %bitcast.13, s32[1]{0:T(128)} %bitcast.14, s32[1]{0:T(128)} %bitcast.15, s32[1]{0:T(128)} %bitcast.16, s32[1]{0:T(128)} %bitcast.17, s32[1]{0:T(128)} %bitcast.18, ...), dimensions={0} | concatenate | bytes 208 | tf_op jit(solution)/shard_map/stack | solution.py:680
  164.6 5.9 collective-permute-done.7.refs_0_
  175.4 8.4 %all-gather.11.cloned.1.call-done = bf16[8192,512]{1,0:T(8,128)(2,1)} async-done(((bf16[1024,512]{1,0:T(8,128)(2,1)}), bf16[8192,512]{1,0:T(8,128)(2,1)}) %all-gather.11.cloned.1.call-update) | async-done | bytes 8388624 | tf_op jit(solution)/shard_map/all_gather | solution.py:252
  185.0 25.3 %attend.1 = (bf16[2,4,128,512]{3,2,1,0:T(8,128)(2,1)S(1)}, f32[2,2,4,1,256]{4,3,2,1,0:T(1,128)S(1)}) custom-call(s32[26]{0:T(128)S(1)} %stack.31.info_ref, bf16[2,4,128,512]{3,2,1,0:T(8,128)(2,1)S(1)} %bitcast.127, bf16[8,2,4,128,512]{4,3,2,1,0:T(8,128)(2,1)} %bitcast.148), custom_call_target="tpu_custom_call" | custom-call | flops 4294967296 | bytes 8388608 | tf_op jit(solution)/shard_map/attend/pallas_call | solution.py:553
  218.2 16.9 %collective-permute-done.11 = bf16[256,2048]{1,0:T(8,128)(2,1)S(1)} collective-permute-done((bf16[256,2048]{1,0:T(8,128)(2,1)}, bf16[256,2048]{1,0:T(8,128)(2,1)S(1)}, u32[]{:S(2)}, u32[]{:S(2)}) %collective-permute-start.11) | collective-permute-done | bytes 1048608 | tf_op jit(solution)/shard_map/ppermute | solution.py:26
  241.5 10.1 %collective-permute-done.12.refs_3_ = bf16[128,2048]{1,0:T(8,128)(2,1)S(1)} collective-permute-done((bf16[128,2048]{1,0:T(8,128)(2,1)S(1)}, bf16[128,2048]{1,0:T(8,128)(2,1)S(1)}, u32[]{:S(2)}, u32[]{:S(2)}) %collective-permute-start.12) | collective-permute-done | bytes 524320 | tf_op jit(solution)/shard_map/ppermute | solution.py:26
  256.5 9.1 %collective-permute-done.15.refs_2_ = bf16[128,2048]{1,0:T(8,128)(2,1)S(1)} collective-permute-done((bf16[128,2048]{1,0:T(8,128)(2,1)S(1)}, bf16[128,2048]{1,0:T(8,128)(2,1)S(1)}, u32[]{:S(2)}, u32[]{:S(2)}) %collective-permute-start.15) | collective-permute-done | bytes 524320 | tf_op jit(solution)/shard_map/ppermute | solution.py:26
  269.4 21.7 %collective-permute-done.16.refs_0_ = bf16[256,2048]{1,0:T(8,128)(2,1)S(1)} collective-permute-done((bf16[256,2048]{1,0:T(8,128)(2,1)S(1)}, bf16[256,2048]{1,0:T(8,128)(2,1)S(1)}, u32[]{:S(2)}, u32[]{:S(2)}) %collective-permute-start.16) | collective-permute-done | bytes 1048608 | tf_op jit(solution)/shard_map/ppermute | solution.py:26
  294.0 11.7 %fusion.70 = f32[1024,1536]{1,0:T(8,128)} fusion(bf16[1024,2048]{1,0:T(8,128)(2,1)} %copy-done.4, bf16[2048,1536]{1,0:T(8,128)(2,1)} %all-gather.13.cloned.1.call-done), kind=kOutput, calls=%fused_computation.201 | convolution fusion | flops 6442450944 | bytes 16777216 | tf_op jit(solution)/shard_map/dot_general | solution.py:318
  305.7 8.3 %all-gather.15.cloned.1.call-done = bf16[2048,1536]{1,0:T(8,128)(2,1)} async-done(((bf16[256,1536]{1,0:T(8,128)(2,1)}), bf16[2048,1536]{1,0:T(8,128)(2,1)}) %all-gather.15.cloned.1.call-update) | async-done | bytes 6291472 | tf_op jit(solution)/shard_map/all_gather | solution.py:252
  314.0 13.3 %multiply_convert_fusion.2 = (bf16[1024,1536]{1,0:T(8,128)(2,1)S(1)}, f32[1024,1536]{1,0:T(8,128)}) fusion(f32[1024,1536]{1,0:T(8,128)} %fusion.70, bf16[1024,2048]{1,0:T(8,128)(2,1)} %copy-done.4, bf16[2048,1536]{1,0:T(8,128)(2,1)} %all-gather.15.cloned.1.call-done), kind=kOutput, calls=%fused_computation.8 | convolution fusion | flops 6450315264 | bytes 26214400 | tf_op jit(solution)/shard_map/dot_general | solution.py:318
  329.0 8.8 %convolution_convert_fusion.2 = bf16[2048,1536]{1,0:T(8,128)(2,1)} fusion(bf16[1024,2048]{1,0:T(8,128)(2,1)S(1)} %copy-done.2, bf16[1024,1536]{1,0:T(8,128)(2,1)S(1)} %get-tuple-element.78), kind=kOutput, calls=%fused_computation.5 | convolution fusion | flops 6445596672 | bytes 13631488 | tf_op jit(solution)/shard_map/dot_general | solution.py:322
  338.0 41.4 %all-gather.17.cloned.1.call-done = bf16[2048,1536]{1,0:T(8,128)(2,1)} async-done(((bf16[256,1536]{1,0:T(8,128)(2,1)}), bf16[2048,1536]{1,0:T(8,128)(2,1)}) %all-gather.17.cloned.1.call-update) | async-done | bytes 6291472 | tf_op jit(solution)/shard_map/all_gather | solution.py:252
  379.4 14.2 %multiply_convert_fusion = (bf16[1024,1536]{1,0:T(8,128)(2,1)S(1)}, bf16[1024,1536]{1,0:T(8,128)(2,1)S(1)}) fusion(f32[1024,1536]{1,0:T(8,128)} %fusion.70, f32[1024,1536]{1,0:T(8,128)} %get-tuple-element.208, bf16[1024,2048]{1,0:T(8,128)(2,1)} %copy-done.1, bf16[2048,1536]{1,0:T(8,128)(2,1)} %all-gather.17.cloned.1.call-done), kind=kOutput, calls=%fused_computation.6 | convolution fusion | flops 6462898176 | bytes 29360128 | tf_op jit(solution)/shard_map/dot_general | solution.py:318
  393.6 10.0 %fusion.71 = f32[1024,2048]{1,0:T(8,128)S(1)} fusion(bf16[1024,1536]{1,0:T(8,128)(2,1)S(1)} %get-tuple-element.132, bf16[2048,1536]{1,0:T(8,128)(2,1)} %all-gather.13.cloned.1.call-done), kind=kOutput, calls=%fused_computation.202 | convolution fusion | flops 6442450944 | bytes 17825792 | tf_op jit(solution)/shard_map/dot_general | solution.py:326
  403.6 8.9 %add_convert_fusion.1 = bf16[1024,2048]{1,0:T(8,128)(2,1)S(1)} fusion(f32[1024,2048]{1,0:T(8,128)S(1)} %fusion.71, bf16[1024,1536]{1,0:T(8,128)(2,1)S(1)} %get-tuple-element.131, bf16[2048,1536]{1,0:T(8,128)(2,1)} %all-gather.15.cloned.1.call-done), kind=kOutput, calls=%fused_computation.2 | convolution fusion | flops 6446645248 | bytes 22020096 | tf_op jit(solution)/shard_map/dot_general | solution.py:326
  419.3 8.8 %convolution_convert_fusion = bf16[2048,1536]{1,0:T(8,128)(2,1)} fusion(bf16[1024,2048]{1,0:T(8,128)(2,1)S(1)} %copy-done.5, bf16[1024,1536]{1,0:T(8,128)(2,1)S(1)} %get-tuple-element.131), kind=kOutput, calls=%fused_computation.3 | convolution fusion | flops 6445596672 | bytes 13631488 | tf_op jit(solution)/shard_map/dot_general | solution.py:322
  428.0 11.8 %convolution_convert_fusion.1 = bf16[2048,1536]{1,0:T(8,128)(2,1)} fusion(bf16[1024,2048]{1,0:T(8,128)(2,1)} %copy-done.4, bf16[1024,1536]{1,0:T(8,128)(2,1)} %copy-done.48), kind=kOutput, calls=%fused_computation.4 | convolution fusion | flops 6445596672 | bytes 13631488 | tf_op jit(solution)/shard_map/dot_general | solution.py:322
  446.2 2.9 add_convert_fusion.10
  453.2 9.1 %collective-permute-done.22.refs_6_ = bf16[128,2048]{1,0:T(8,128)(2,1)S(1)} collective-permute-done((bf16[128,2048]{1,0:T(8,128)(2,1)}, bf16[128,2048]{1,0:T(8,128)(2,1)S(1)}, u32[]{:S(2)}, u32[]{:S(2)}) %collective-permute-start.22) | collective-permute-done | bytes 524320 | tf_op jit(solution)/shard_map/ppermute | solution.py:26
  465.6 3.7 middle_back.1
  471.5 8.8 %collective-permute-done.23.refs_2_ = bf16[128,2048]{1,0:T(8,128)(2,1)S(1)} collective-permute-done((bf16[128,2048]{1,0:T(8,128)(2,1)S(1)}, bf16[128,2048]{1,0:T(8,128)(2,1)S(1)}, u32[]{:S(2)}, u32[]{:S(2)}) %collective-permute-start.23) | collective-permute-done | bytes 524320 | tf_op jit(solution)/shard_map/ppermute | solution.py:26
  480.9 2.9 collective-permute-done.25
  484.0 11.1 %convolution_convert_fusion.3 = bf16[1024,2048]{1,0:T(8,128)(2,1)} fusion(bf16[1024,1536]{1,0:T(8,128)(2,1)S(1)} %copy-done.50, bf16[2048,1536]{1,0:T(8,128)(2,1)} %all-gather.17.cloned.1.call-done), kind=kOutput, calls=%fused_computation.12 | convolution fusion | flops 6444548096 | bytes 13631488 | tf_op jit(solution)/shard_map/dot_general | solution.py:326
  495.0 8.8 %collective-permute-done.24.refs_0_ = bf16[256,2048]{1,0:T(8,128)(2,1)S(1)} collective-permute-done((bf16[256,2048]{1,0:T(8,128)(2,1)S(1)}, bf16[256,2048]{1,0:T(8,128)(2,1)S(1)}, u32[]{:S(2)}, u32[]{:S(2)}) %collective-permute-start.24) | collective-permute-done | bytes 1048608 | tf_op jit(solution)/shard_map/ppermute | solution.py:26
  506.1 3.3 convolution_convert_fusion.8
  509.4 11.3 %reduce-scatter.9.cloned.1.call-done.both_ref = bf16[256,1536]{1,0:T(8,128)(2,1)} async-done(((bf16[2048,1536]{1,0:T(8,128)(2,1)}), bf16[256,1536]{1,0:T(8,128)(2,1)}) %reduce-scatter.9.cloned.1.call-update) | async-done | bytes 786448 | tf_op jit(solution)/shard_map/reduce_scatter | solution.py:257
  528.4 34.0 %attend_back.1 = (f32[2,4,128,512]{3,2,1,0:T(8,128)}, bf16[8,2,4,128,512]{4,3,2,1,0:T(8,128)(2,1)}) custom-call(s32[26]{0:T(128)} %copy-done.18, bf16[2,4,128,512]{3,2,1,0:T(8,128)(2,1)} %bitcast.126, bf16[2,4,128,512]{3,2,1,0:T(8,128)(2,1)} %bitcast.150, bf16[2,4,128,512]{3,2,1,0:T(8,128)(2,1)} %copy-done.20, f32[2,2,4,1,256]{4,3,2,1,0:T(1,128)} %copy-done.22, ...), custom_call_target="tpu_custom_call" | custom-call | flops 10737418240 | bytes 16777216 | tf_op jit(solution)/shard_map/attend_back/pallas_call | solution.py:576
  567.4 8.7 %collective-permute-done.30.refs_4_ = bf16[128,2048]{1,0:T(8,128)(2,1)S(1)} collective-permute-done((bf16[128,2048]{1,0:T(8,128)(2,1)S(1)}, bf16[128,2048]{1,0:T(8,128)(2,1)S(1)}, u32[]{:S(2)}, u32[]{:S(2)}) %collective-permute-start.30) | collective-permute-done | bytes 524320 | tf_op jit(solution)/shard_map/ppermute | solution.py:26
  579.2 12.0 %reduce-scatter.11.cloned.1.call-done.both_ref = bf16[256,1536]{1,0:T(8,128)(2,1)} async-done(((bf16[2048,1536]{1,0:T(8,128)(2,1)}), bf16[256,1536]{1,0:T(8,128)(2,1)}) %reduce-scatter.11.cloned.1.call-update) | async-done | bytes 786448 | tf_op jit(solution)/shard_map/reduce_scatter | solution.py:257
  591.3 5.9 head_prep_back.2
  597.2 5.5 convolution_convert_fusion.7
  606.5 5.7 fusion.2
  612.2 2.7 collective-permute-done.31.other_ref
  617.4 5.9 collective-permute-done.32.other_ref
  631.2 4.9 convolution_convert_fusion.6
  636.1 2.7 pad_maximum_fusion
  638.8 43.3 %reduce-scatter.13.cloned.1.call-done.d_ref = bf16[1024,512]{1,0:T(8,128)(2,1)} async-done(((bf16[8192,512]{1,0:T(8,128)(2,1)}), bf16[1024,512]{1,0:T(8,128)(2,1)}) %reduce-scatter.13.cloned.1.call-update) | async-done | bytes 1048592 | tf_op jit(solution)/shard_map/reduce_scatter | solution.py:257
  682.2 4.9 head_prep_back.3
  687.1 6.7 convolution_convert_fusion.5
  693.7 7.9 %multiply_reduce_fusion = (f32[2048]{0:T(1024)S(1)}, bf16[1024,2048]{1,0:T(8,128)(2,1)S(1)}) fusion(bf16[1024,2048]{1,0:T(8,128)(2,1)} %copy-done, f32[1024,2048]{1,0:T(8,128)} %fusion.2, bf16[1024,512]{1,0:T(8,128)(2,1)S(1)} %copy-done.32, bf16[2048,1024]{1,0:T(8,128)(2,1)} %all-gather.7.cloned.1.call-done), kind=kOutput, calls=%fused_computation | convolution fusion | flops 2160064512 | bytes 19931136 | tf_op jit(solution)/shard_map/dot_general | solution.py:326
  705.0 19.5 %collective-permute-done.42 = bf16[256,2048]{1,0:T(8,128)(2,1)S(1)} collective-permute-done((bf16[256,2048]{1,0:T(8,128)(2,1)S(1)}, bf16[256,2048]{1,0:T(8,128)(2,1)S(1)}, u32[]{:S(2)}, u32[]{:S(2)}) %collective-permute-start.42) | collective-permute-done | bytes 1048608 | tf_op jit(solution)/shard_map/ppermute | solution.py:26
  727.2 5.6 reduce-scatter.15.cloned.1.call-done.both_ref
  736.6 12.5 %collective-permute-done.36 = f32[4352]{0:T(1024)S(1)} collective-permute-done((f32[4352]{0:T(1024)S(1)}, f32[4352]{0:T(1024)S(1)}, u32[]{:S(2)}, u32[]{:S(2)}) %collective-permute-start.36) | collective-permute-done | bytes 17440 | tf_op jit(solution)/shard_map/ppermute | solution.py:26
  753.7 4.7 collective-permute-done.38
  759.0 3.2 collective-permute-done.39
  766.2 3.8 reduce-scatter.17.cloned.1.call-done.both_ref
  774.3 4.8 entry_back.1
  (296 shorter events, 159.3 us)
Async XLA Ops:
  7.2 62.8 %all-gather.7.cloned.1.call-start = ((), (), s32[]{:S(2)}) async-start(), calls=%async_computation.6 | async-start | bytes 4718592 | tf_op jit(solution)/shard_map/all_gather | solution.py:252
  11.2 9.4 %collective-permute-start.4 = (bf16[128,1024]{1,0:T(8,128)(2,1)S(1)}, bf16[128,1024]{1,0:T(8,128)(2,1)S(1)}, u32[]{:S(2)}, u32[]{:S(2)}) collective-permute-start(bf16[128,1024]{1,0:T(8,128)(2,1)S(1)} %pad_maximum_fusion.21), channel_id=1, source_target_pairs={{0,4},{2,6},{4,0},{6,2},{8,12},{10,14},{12,8},{14,10},{16,20},{18,... | collective-permute-start | bytes 786440 | tf_op jit(solution)/shard_map/ppermute | solution.py:26
  21.5 78.7 %all-gather.9.cloned.1.call-start = ((), (), s32[]{:S(2)}) async-start(), calls=%async_computation.7 | async-start | bytes 2359296 | tf_op jit(solution)/shard_map/all_gather | solution.py:252
  21.6 5.7 collective-permute-start.10
  28.1 155.7 %all-gather.11.cloned.1.call-start = ((), (), s32[]{:S(2)}) async-start(), calls=%async_computation.8 | async-start | bytes 9437184 | tf_op jit(solution)/shard_map/all_gather | solution.py:252
  29.4 12.6 %collective-permute-start = (bf16[128,2048]{1,0:T(8,128)(2,1)S(1)}, bf16[128,2048]{1,0:T(8,128)(2,1)S(1)}, u32[]{:S(2)}, u32[]{:S(2)}) collective-permute-start(bf16[128,2048]{1,0:T(8,128)(2,1)S(1)} %get-tuple-element.169.refs_1_), channel_id=1, source_target_pairs={{0,1},{1,0},{2,3},{3,2},{4,5},{5,4},{6,7},{7,6},{8,9},{9,8},{10,11... | collective-permute-start | bytes 1572872 | tf_op jit(solution)/shard_map/ppermute | solution.py:26
  31.0 12.8 %collective-permute-start.2 = (bf16[128,2048]{1,0:T(8,128)(2,1)S(1)}, bf16[128,2048]{1,0:T(8,128)(2,1)S(1)}, u32[]{:S(2)}, u32[]{:S(2)}) collective-permute-start(bf16[128,2048]{1,0:T(8,128)(2,1)S(1)} %get-tuple-element.168), channel_id=1, source_target_pairs={{0,4},{2,6},{4,0},{6,2},{8,12},{10,14},{12,8},{14,10},{16,20},{18,... | collective-permute-start | bytes 1572872 | tf_op jit(solution)/shard_map/ppermute | solution.py:26
  42.1 23.6 %collective-permute-start.1 = (bf16[256,2048]{1,0:T(8,128)(2,1)S(1)}, bf16[256,2048]{1,0:T(8,128)(2,1)S(1)}, u32[]{:S(2)}, u32[]{:S(2)}) collective-permute-start(bf16[256,2048]{1,0:T(8,128)(2,1)S(1)} %pad_maximum_fusion.4), channel_id=1, source_target_pairs={{0,4},{2,6},{4,0},{6,2},{8,12},{10,14},{12,8},{14,10},{16,20},{18,... | collective-permute-start | bytes 3145736 | tf_op jit(solution)/shard_map/ppermute | solution.py:26
  43.8 22.3 %collective-permute-start.3 = (bf16[256,2048]{1,0:T(8,128)(2,1)S(1)}, bf16[256,2048]{1,0:T(8,128)(2,1)S(1)}, u32[]{:S(2)}, u32[]{:S(2)}) collective-permute-start(bf16[256,2048]{1,0:T(8,128)(2,1)S(1)} %pad_maximum_fusion.5.refs_3_), channel_id=1, source_target_pairs={{0,1},{1,0},{2,3},{3,2},{4,5},{5,4},{6,7},{7,6},{8,9},{9,8},{10,11... | collective-permute-start | bytes 3145736 | tf_op jit(solution)/shard_map/ppermute | solution.py:26
  79.9 20.4 %copy-start.34 = (bf16[128,3072]{1,0:T(8,128)(2,1)S(1)}, bf16[128,3072]{1,0:T(8,128)(2,1)}, u32[]{:S(2)}) copy-start(bf16[128,3072]{1,0:T(8,128)(2,1)} %param.23) | copy-start | bytes 2359300
  79.9 20.4 %copy-start.35 = (bf16[128,3072]{1,0:T(8,128)(2,1)S(1)}, bf16[128,3072]{1,0:T(8,128)(2,1)}, u32[]{:S(2)}) copy-start(bf16[128,3072]{1,0:T(8,128)(2,1)} %param.22) | copy-start | bytes 2359300
  100.2 193.8 %all-gather.13.cloned.1.call-start = ((), (), s32[]{:S(2)}) async-start(), calls=%async_computation.9 | async-start | bytes 7077888 | tf_op jit(solution)/shard_map/all_gather | solution.py:252
  100.5 28.2 %collective-permute-start.5 = (bf16[128,4608]{1,0:T(8,128)(2,1)S(1)}, bf16[128,4608]{1,0:T(8,128)(2,1)S(1)}, u32[]{:S(2)}, u32[]{:S(2)}) collective-permute-start(bf16[128,4608]{1,0:T(8,128)(2,1)S(1)} %pad_maximum_fusion.3), channel_id=1, source_target_pairs={{0,4},{2,6},{4,0},{6,2},{8,12},{10,14},{12,8},{14,10},{16,20},{18,... | collective-permute-start | bytes 3538952 | tf_op jit(solution)/shard_map/ppermute | solution.py:26
  130.8 183.2 %all-gather.15.cloned.1.call-start = ((), (), s32[]{:S(2)}) async-start(), calls=%async_computation.10 | async-start | bytes 7077888 | tf_op jit(solution)/shard_map/all_gather | solution.py:252
  131.4 248.1 %all-gather.17.cloned.1.call-start = ((), (), s32[]{:S(2)}) async-start(), calls=%async_computation.11 | async-start | bytes 7077888 | tf_op jit(solution)/shard_map/all_gather | solution.py:252
  132.0 13.4 %collective-permute-start.6 = (bf16[128,2048]{1,0:T(8,128)(2,1)S(1)}, bf16[128,2048]{1,0:T(8,128)(2,1)S(1)}, u32[]{:S(2)}, u32[]{:S(2)}) collective-permute-start(bf16[128,2048]{1,0:T(8,128)(2,1)S(1)} %get-tuple-element.167.refs_1_), channel_id=1, source_target_pairs={{0,1},{1,0},{2,3},{3,2},{4,5},{5,4},{6,7},{7,6},{8,9},{9,8},{10,11... | collective-permute-start | bytes 1572872 | tf_op jit(solution)/shard_map/ppermute | solution.py:26
  133.5 14.3 %collective-permute-start.8 = (bf16[128,2048]{1,0:T(8,128)(2,1)S(1)}, bf16[128,2048]{1,0:T(8,128)(2,1)S(1)}, u32[]{:S(2)}, u32[]{:S(2)}) collective-permute-start(bf16[128,2048]{1,0:T(8,128)(2,1)S(1)} %get-tuple-element.166), channel_id=1, source_target_pairs={{0,4},{2,6},{4,0},{6,2},{8,12},{10,14},{12,8},{14,10},{16,20},{18,... | collective-permute-start | bytes 1572872 | tf_op jit(solution)/shard_map/ppermute | solution.py:26
  146.4 24.1 %collective-permute-start.7 = (bf16[256,2048]{1,0:T(8,128)(2,1)}, bf16[256,2048]{1,0:T(8,128)(2,1)}, u32[]{:S(2)}, u32[]{:S(2)}) collective-permute-start(bf16[256,2048]{1,0:T(8,128)(2,1)} %pad_maximum_fusion.6), channel_id=1, source_target_pairs={{0,4},{2,6},{4,0},{6,2},{8,12},{10,14},{12,8},{14,10},{16,20},{18,... | collective-permute-start | bytes 3145736 | tf_op jit(solution)/shard_map/ppermute | solution.py:26
  147.9 23.7 %collective-permute-start.9 = (bf16[256,2048]{1,0:T(8,128)(2,1)S(1)}, bf16[256,2048]{1,0:T(8,128)(2,1)}, u32[]{:S(2)}, u32[]{:S(2)}) collective-permute-start(bf16[256,2048]{1,0:T(8,128)(2,1)S(1)} %pad_maximum_fusion.7.refs_3_), channel_id=1, source_target_pairs={{0,1},{1,0},{2,3},{3,2},{4,5},{5,4},{6,7},{7,6},{8,9},{9,8},{10,11... | collective-permute-start | bytes 3145736 | tf_op jit(solution)/shard_map/ppermute | solution.py:26
  185.0 25.3 %copy-start.45 = (bf16[2048,512]{1,0:T(8,128)(2,1)S(1)}, bf16[2048,512]{1,0:T(8,128)(2,1)}, u32[]{:S(2)}) copy-start(bf16[2048,512]{1,0:T(8,128)(2,1)} %all-gather.9.cloned.1.call-done) | copy-start | bytes 6291460
  214.1 21.0 %collective-permute-start.11 = (bf16[256,2048]{1,0:T(8,128)(2,1)}, bf16[256,2048]{1,0:T(8,128)(2,1)S(1)}, u32[]{:S(2)}, u32[]{:S(2)}) collective-permute-start(bf16[256,2048]{1,0:T(8,128)(2,1)} %pad_maximum_fusion.8), channel_id=1, source_target_pairs={{0,4},{2,6},{4,0},{6,2},{8,12},{10,14},{12,8},{14,10},{16,20},{18,... | collective-permute-start | bytes 3145736 | tf_op jit(solution)/shard_map/ppermute | solution.py:26
  216.7 21.6 %collective-permute-start.13 = (bf16[256,2048]{1,0:T(8,128)(2,1)}, bf16[256,2048]{1,0:T(8,128)(2,1)S(1)}, u32[]{:S(2)}, u32[]{:S(2)}) collective-permute-start(bf16[256,2048]{1,0:T(8,128)(2,1)} %slice.319), channel_id=1, source_target_pairs={{0,1},{1,0},{2,3},{3,2},{4,5},{5,4},{6,7},{7,6},{8,9},{9,8},{10,11... | collective-permute-start | bytes 3145736 | tf_op jit(solution)/shard_map/ppermute | solution.py:26
  218.2 23.3 %copy-start.42 = (f32[2048]{0:T(1024)S(1)}, f32[2048]{0:T(1024)}, u32[]{:S(2)}) copy-start(f32[2048]{0:T(1024)} %param.25) | copy-start | bytes 24580
  218.2 232.0 %reduce-scatter.7.cloned.1.call-start = ((), (), s32[]{:S(2)}) async-start(), calls=%async_computation.12 | async-start | bytes 7077888 | tf_op jit(solution)/shard_map/reduce_scatter | solution.py:257
  218.2 33.4 %copy-start.7 = (bf16[256,2048]{1,0:T(8,128)(2,1)S(1)}, bf16[256,2048]{1,0:T(8,128)(2,1)}, u32[]{:S(2)}) copy-start(bf16[256,2048]{1,0:T(8,128)(2,1)} %copy-done.6) | copy-start | bytes 3145732
  236.7 14.9 %collective-permute-start.12 = (bf16[128,2048]{1,0:T(8,128)(2,1)S(1)}, bf16[128,2048]{1,0:T(8,128)(2,1)S(1)}, u32[]{:S(2)}, u32[]{:S(2)}) collective-permute-start(bf16[128,2048]{1,0:T(8,128)(2,1)S(1)} %get-tuple-element.139), channel_id=1, source_target_pairs={{0,1},{1,0},{2,3},{3,2},{4,5},{5,4},{6,7},{7,6},{8,9},{9,8},{10,11... | collective-permute-start | bytes 1572872 | tf_op jit(solution)/shard_map/ppermute | solution.py:26
  240.0 11.6 %collective-permute-start.14 = (bf16[128,2048]{1,0:T(8,128)(2,1)S(1)}, bf16[128,2048]{1,0:T(8,128)(2,1)S(1)}, u32[]{:S(2)}, u32[]{:S(2)}) collective-permute-start(bf16[128,2048]{1,0:T(8,128)(2,1)S(1)} %get-tuple-element.164), channel_id=1, source_target_pairs={{0,4},{2,6},{4,0},{6,2},{8,12},{10,14},{12,8},{14,10},{16,20},{18,... | collective-permute-start | bytes 1572872 | tf_op jit(solution)/shard_map/ppermute | solution.py:26
  253.7 11.9 %collective-permute-start.15 = (bf16[128,2048]{1,0:T(8,128)(2,1)S(1)}, bf16[128,2048]{1,0:T(8,128)(2,1)S(1)}, u32[]{:S(2)}, u32[]{:S(2)}) collective-permute-start(bf16[128,2048]{1,0:T(8,128)(2,1)S(1)} %get-tuple-element.163.refs_1_), channel_id=1, source_target_pairs={{0,1},{1,0},{2,3},{3,2},{4,5},{5,4},{6,7},{7,6},{8,9},{9,8},{10,11... | collective-permute-start | bytes 1572872 | tf_op jit(solution)/shard_map/ppermute | solution.py:26
  255.3 12.4 %collective-permute-start.17 = (bf16[128,2048]{1,0:T(8,128)(2,1)S(1)}, bf16[128,2048]{1,0:T(8,128)(2,1)S(1)}, u32[]{:S(2)}, u32[]{:S(2)}) collective-permute-start(bf16[128,2048]{1,0:T(8,128)(2,1)S(1)} %get-tuple-element.162), channel_id=1, source_target_pairs={{0,4},{2,6},{4,0},{6,2},{8,12},{10,14},{12,8},{14,10},{16,20},{18,... | collective-permute-start | bytes 1572872 | tf_op jit(solution)/shard_map/ppermute | solution.py:26
  265.7 25.3 %collective-permute-start.16 = (bf16[256,2048]{1,0:T(8,128)(2,1)S(1)}, bf16[256,2048]{1,0:T(8,128)(2,1)S(1)}, u32[]{:S(2)}, u32[]{:S(2)}) collective-permute-start(bf16[256,2048]{1,0:T(8,128)(2,1)S(1)} %pad_maximum_fusion.9), channel_id=1, source_target_pairs={{0,4},{2,6},{4,0},{6,2},{8,12},{10,14},{12,8},{14,10},{16,20},{18,... | collective-permute-start | bytes 3145736 | tf_op jit(solution)/shard_map/ppermute | solution.py:26
  267.8 23.8 %collective-permute-start.18 = (bf16[256,2048]{1,0:T(8,128)(2,1)S(1)}, bf16[256,2048]{1,0:T(8,128)(2,1)S(1)}, u32[]{:S(2)}, u32[]{:S(2)}) collective-permute-start(bf16[256,2048]{1,0:T(8,128)(2,1)S(1)} %pad_maximum_fusion.10.refs_3_), channel_id=1, source_target_pairs={{0,1},{1,0},{2,3},{3,2},{4,5},{5,4},{6,7},{7,6},{8,9},{9,8},{10,11... | collective-permute-start | bytes 3145736 | tf_op jit(solution)/shard_map/ppermute | solution.py:26
  337.8 182.9 %reduce-scatter.9.cloned.1.call-start = ((), (), s32[]{:S(2)}) async-start(), calls=%async_computation.13 | async-start | bytes 7077888 | tf_op jit(solution)/shard_map/reduce_scatter | solution.py:257
  416.3 25.6 %collective-permute-start.19 = (bf16[256,2048]{1,0:T(8,128)(2,1)}, bf16[256,2048]{1,0:T(8,128)(2,1)}, u32[]{:S(2)}, u32[]{:S(2)}) collective-permute-start(bf16[256,2048]{1,0:T(8,128)(2,1)} %pad_maximum_fusion.11), channel_id=1, source_target_pairs={{0,4},{2,6},{4,0},{6,2},{8,12},{10,14},{12,8},{14,10},{16,20},{18,... | collective-permute-start | bytes 3145736 | tf_op jit(solution)/shard_map/ppermute | solution.py:26
  417.8 25.3 %collective-permute-start.20 = (bf16[256,2048]{1,0:T(8,128)(2,1)}, bf16[256,2048]{1,0:T(8,128)(2,1)}, u32[]{:S(2)}, u32[]{:S(2)}) collective-permute-start(bf16[256,2048]{1,0:T(8,128)(2,1)} %slice.325), channel_id=1, source_target_pairs={{0,1},{1,0},{2,3},{3,2},{4,5},{5,4},{6,7},{7,6},{8,9},{9,8},{10,11... | collective-permute-start | bytes 3145736 | tf_op jit(solution)/shard_map/ppermute | solution.py:26
  450.2 141.0 %reduce-scatter.11.cloned.1.call-start = ((), (), s32[]{:S(2)}) async-start(), calls=%async_computation.14 | async-start | bytes 7077888 | tf_op jit(solution)/shard_map/reduce_scatter | solution.py:257
  450.2 12.1 %collective-permute-start.22 = (bf16[128,2048]{1,0:T(8,128)(2,1)}, bf16[128,2048]{1,0:T(8,128)(2,1)S(1)}, u32[]{:S(2)}, u32[]{:S(2)}) collective-permute-start(bf16[128,2048]{1,0:T(8,128)(2,1)} %get-tuple-element.160), channel_id=1, source_target_pairs={{0,4},{2,6},{4,0},{6,2},{8,12},{10,14},{12,8},{14,10},{16,20},{18,... | collective-permute-start | bytes 1572872 | tf_op jit(solution)/shard_map/ppermute | solution.py:26
  451.8 11.7 %collective-permute-start.21 = (bf16[128,2048]{1,0:T(8,128)(2,1)}, bf16[128,2048]{1,0:T(8,128)(2,1)S(1)}, u32[]{:S(2)}, u32[]{:S(2)}) collective-permute-start(bf16[128,2048]{1,0:T(8,128)(2,1)} %get-tuple-element.137), channel_id=1, source_target_pairs={{0,1},{1,0},{2,3},{3,2},{4,5},{5,4},{6,7},{7,6},{8,9},{9,8},{10,11... | collective-permute-start | bytes 1572872 | tf_op jit(solution)/shard_map/ppermute | solution.py:26
  469.4 10.9 %collective-permute-start.23 = (bf16[128,2048]{1,0:T(8,128)(2,1)S(1)}, bf16[128,2048]{1,0:T(8,128)(2,1)S(1)}, u32[]{:S(2)}, u32[]{:S(2)}) collective-permute-start(bf16[128,2048]{1,0:T(8,128)(2,1)S(1)} %get-tuple-element.159.refs_1_), channel_id=1, source_target_pairs={{0,1},{1,0},{2,3},{3,2},{4,5},{5,4},{6,7},{7,6},{8,9},{9,8},{10,11... | collective-permute-start | bytes 1572872 | tf_op jit(solution)/shard_map/ppermute | solution.py:26
  471.0 12.8 %collective-permute-start.25 = (bf16[128,2048]{1,0:T(8,128)(2,1)S(1)}, bf16[128,2048]{1,0:T(8,128)(2,1)S(1)}, u32[]{:S(2)}, u32[]{:S(2)}) collective-permute-start(bf16[128,2048]{1,0:T(8,128)(2,1)S(1)} %get-tuple-element.158), channel_id=1, source_target_pairs={{0,4},{2,6},{4,0},{6,2},{8,12},{10,14},{12,8},{14,10},{16,20},{18,... | collective-permute-start | bytes 1572872 | tf_op jit(solution)/shard_map/ppermute | solution.py:26
  480.4 23.4 %collective-permute-start.24 = (bf16[256,2048]{1,0:T(8,128)(2,1)S(1)}, bf16[256,2048]{1,0:T(8,128)(2,1)S(1)}, u32[]{:S(2)}, u32[]{:S(2)}) collective-permute-start(bf16[256,2048]{1,0:T(8,128)(2,1)S(1)} %pad_maximum_fusion.12), channel_id=1, source_target_pairs={{0,4},{2,6},{4,0},{6,2},{8,12},{10,14},{12,8},{14,10},{16,20},{18,... | collective-permute-start | bytes 3145736 | tf_op jit(solution)/shard_map/ppermute | solution.py:26
  483.9 19.9 %collective-permute-start.26 = (bf16[256,2048]{1,0:T(8,128)(2,1)S(1)}, bf16[256,2048]{1,0:T(8,128)(2,1)S(1)}, u32[]{:S(2)}, u32[]{:S(2)}) collective-permute-start(bf16[256,2048]{1,0:T(8,128)(2,1)S(1)} %pad_maximum_fusion.13.refs_3_), channel_id=1, source_target_pairs={{0,1},{1,0},{2,3},{3,2},{4,5},{5,4},{6,7},{7,6},{8,9},{9,8},{10,11... | collective-permute-start | bytes 3145736 | tf_op jit(solution)/shard_map/ppermute | solution.py:26
  520.7 161.4 %reduce-scatter.13.cloned.1.call-start = ((), (), s32[]{:S(2)}) async-start(), calls=%async_computation.15 | async-start | bytes 9437184 | tf_op jit(solution)/shard_map/reduce_scatter | solution.py:257
  525.5 36.9 %collective-permute-start.27 = (bf16[256,2048]{1,0:T(8,128)(2,1)}, bf16[256,2048]{1,0:T(8,128)(2,1)S(1)}, u32[]{:S(2)}, u32[]{:S(2)}) collective-permute-start(bf16[256,2048]{1,0:T(8,128)(2,1)} %pad_maximum_fusion.14), channel_id=1, source_target_pairs={{0,4},{2,6},{4,0},{6,2},{8,12},{10,14},{12,8},{14,10},{16,20},{18,... | collective-permute-start | bytes 3145736 | tf_op jit(solution)/shard_map/ppermute | solution.py:26
  526.9 35.5 %collective-permute-start.28 = (bf16[256,2048]{1,0:T(8,128)(2,1)}, bf16[256,2048]{1,0:T(8,128)(2,1)}, u32[]{:S(2)}, u32[]{:S(2)}) collective-permute-start(bf16[256,2048]{1,0:T(8,128)(2,1)} %slice.273), channel_id=1, source_target_pairs={{0,1},{1,0},{2,3},{3,2},{4,5},{5,4},{6,7},{7,6},{8,9},{9,8},{10,11... | collective-permute-start | bytes 3145736 | tf_op jit(solution)/shard_map/ppermute | solution.py:26
  528.4 35.0 %copy-start.23 = (bf16[1024,2048]{1,0:T(8,128)(2,1)S(1)}, bf16[1024,2048]{1,0:T(8,128)(2,1)}, u32[]{:S(2)}) copy-start(bf16[1024,2048]{1,0:T(8,128)(2,1)} %convolution_convert_fusion.3) | copy-start | bytes 12582916
  565.2 10.9 %collective-permute-start.30 = (bf16[128,2048]{1,0:T(8,128)(2,1)S(1)}, bf16[128,2048]{1,0:T(8,128)(2,1)S(1)}, u32[]{:S(2)}, u32[]{:S(2)}) collective-permute-start(bf16[128,2048]{1,0:T(8,128)(2,1)S(1)} %get-tuple-element.156), channel_id=1, source_target_pairs={{0,4},{2,6},{4,0},{6,2},{8,12},{10,14},{12,8},{14,10},{16,20},{18,... | collective-permute-start | bytes 1572872 | tf_op jit(solution)/shard_map/ppermute | solution.py:26
  566.4 11.5 %collective-permute-start.29 = (bf16[128,2048]{1,0:T(8,128)(2,1)S(1)}, bf16[128,2048]{1,0:T(8,128)(2,1)S(1)}, u32[]{:S(2)}, u32[]{:S(2)}) collective-permute-start(bf16[128,2048]{1,0:T(8,128)(2,1)S(1)} %get-tuple-element.135), channel_id=1, source_target_pairs={{0,1},{1,0},{2,3},{3,2},{4,5},{5,4},{6,7},{7,6},{8,9},{9,8},{10,11... | collective-permute-start | bytes 1572872 | tf_op jit(solution)/shard_map/ppermute | solution.py:26
  591.3 141.6 %reduce-scatter.15.cloned.1.call-start = ((), (), s32[]{:S(2)}) async-start(), calls=%async_computation.16 | async-start | bytes 4718592 | tf_op jit(solution)/shard_map/reduce_scatter | solution.py:257
  602.8 12.2 %collective-permute-start.31 = (bf16[128,1536]{1,0:T(8,128)(2,1)S(1)}, bf16[128,1536]{1,0:T(8,128)(2,1)}, u32[]{:S(2)}, u32[]{:S(2)}) collective-permute-start(bf16[128,1536]{1,0:T(8,128)(2,1)S(1)} %constant_dynamic-slice_fusion.4), channel_id=1, source_target_pairs={{0,4},{2,6},{4,0},{6,2},{8,12},{10,14},{12,8},{14,10},{16,20},{18,... | collective-permute-start | bytes 1179656 | tf_op jit(solution)/shard_map/ppermute | solution.py:26
  604.3 19.1 %collective-permute-start.32 = (bf16[128,1536]{1,0:T(8,128)(2,1)S(1)}, bf16[128,1536]{1,0:T(8,128)(2,1)}, u32[]{:S(2)}, u32[]{:S(2)}) collective-permute-start(bf16[128,1536]{1,0:T(8,128)(2,1)S(1)} %constant_dynamic-slice_fusion.3), channel_id=1, source_target_pairs={{0,4},{2,6},{4,0},{6,2},{8,12},{10,14},{12,8},{14,10},{16,20},{18,... | collective-permute-start | bytes 1179656 | tf_op jit(solution)/shard_map/ppermute | solution.py:26
  605.0 22.9 %collective-permute-start.33 = (bf16[128,1536]{1,0:T(8,128)(2,1)S(1)}, bf16[128,1536]{1,0:T(8,128)(2,1)S(1)}, u32[]{:S(2)}, u32[]{:S(2)}) collective-permute-start(bf16[128,1536]{1,0:T(8,128)(2,1)S(1)} %constant_dynamic-slice_fusion.2), channel_id=1, source_target_pairs={{0,4},{2,6},{4,0},{6,2},{8,12},{10,14},{12,8},{14,10},{16,20},{18,... | collective-permute-start | bytes 1179656 | tf_op jit(solution)/shard_map/ppermute | solution.py:26
  682.1 87.9 %reduce-scatter.17.cloned.1.call-start = ((), (), s32[]{:S(2)}) async-start(), calls=%async_computation.17 | async-start | bytes 2359296 | tf_op jit(solution)/shard_map/reduce_scatter | solution.py:257
  701.7 22.7 %collective-permute-start.42 = (bf16[256,2048]{1,0:T(8,128)(2,1)S(1)}, bf16[256,2048]{1,0:T(8,128)(2,1)S(1)}, u32[]{:S(2)}, u32[]{:S(2)}) collective-permute-start(bf16[256,2048]{1,0:T(8,128)(2,1)S(1)} %slice.341), channel_id=1, source_target_pairs={{0,1},{1,0},{2,3},{3,2},{4,5},{5,4},{6,7},{7,6},{8,9},{9,8},{10,11... | collective-permute-start | bytes 3145736 | tf_op jit(solution)/shard_map/ppermute | solution.py:26
  703.4 22.5 %collective-permute-start.34 = (bf16[256,2048]{1,0:T(8,128)(2,1)S(1)}, bf16[256,2048]{1,0:T(8,128)(2,1)S(1)}, u32[]{:S(2)}, u32[]{:S(2)}) collective-permute-start(bf16[256,2048]{1,0:T(8,128)(2,1)S(1)} %pad_maximum_fusion.15), channel_id=1, source_target_pairs={{0,4},{2,6},{4,0},{6,2},{8,12},{10,14},{12,8},{14,10},{16,20},{18,... | collective-permute-start | bytes 3145736 | tf_op jit(solution)/shard_map/ppermute | solution.py:26
  724.9 47.8 %copy-start.8 = (bf16[256,2048]{1,0:T(8,128)(2,1)S(1)}, bf16[256,2048]{1,0:T(8,128)(2,1)}, u32[]{:S(2)}) copy-start(bf16[256,2048]{1,0:T(8,128)(2,1)} %copy-done.6) | copy-start | bytes 3145732
  732.9 3.1 collective-permute-start.35
  733.0 33.2 %collective-permute-start.41 = (bf16[128,2048]{1,0:T(8,128)(2,1)}, bf16[128,2048]{1,0:T(8,128)(2,1)S(1)}, u32[]{:S(2)}, u32[]{:S(2)}) collective-permute-start(bf16[128,2048]{1,0:T(8,128)(2,1)} %get-tuple-element.133), channel_id=1, source_target_pairs={{0,1},{1,0},{2,3},{3,2},{4,5},{5,4},{6,7},{7,6},{8,9},{9,8},{10,11... | collective-permute-start | bytes 1572872 | tf_op jit(solution)/shard_map/ppermute | solution.py:26
  734.5 31.7 %collective-permute-start.43 = (bf16[128,2048]{1,0:T(8,128)(2,1)}, bf16[128,2048]{1,0:T(8,128)(2,1)S(1)}, u32[]{:S(2)}, u32[]{:S(2)}) collective-permute-start(bf16[128,2048]{1,0:T(8,128)(2,1)} %get-tuple-element.154), channel_id=1, source_target_pairs={{0,4},{2,6},{4,0},{6,2},{8,12},{10,14},{12,8},{14,10},{16,20},{18,... | collective-permute-start | bytes 1572872 | tf_op jit(solution)/shard_map/ppermute | solution.py:26
  736.0 13.1 %collective-permute-start.36 = (f32[4352]{0:T(1024)S(1)}, f32[4352]{0:T(1024)S(1)}, u32[]{:S(2)}, u32[]{:S(2)}) collective-permute-start(f32[4352]{0:T(1024)S(1)} %fusion.37), channel_id=1, source_target_pairs={{0,4},{2,6},{4,0},{6,2},{8,12},{10,14},{12,8},{14,10},{16,20},{18,... | collective-permute-start | bytes 52232 | tf_op jit(solution)/shard_map/ppermute | solution.py:26
  749.1 4.5 collective-permute-start.37
  750.1 13.2 %collective-permute-start.40 = (bf16[128,1024]{1,0:T(8,128)(2,1)S(1)}, bf16[128,1024]{1,0:T(8,128)(2,1)S(1)}, u32[]{:S(2)}, u32[]{:S(2)}) collective-permute-start(bf16[128,1024]{1,0:T(8,128)(2,1)S(1)} %constant_dynamic-slice_fusion.1), channel_id=1, source_target_pairs={{0,4},{2,6},{4,0},{6,2},{8,12},{10,14},{12,8},{14,10},{16,20},{18,... | collective-permute-start | bytes 786440 | tf_op jit(solution)/shard_map/ppermute | solution.py:26
  753.7 4.7 collective-permute-start.38
  758.4 3.8 collective-permute-start.39
  770.9 8.2 %collective-permute-start.44 = (bf16[128,512]{1,0:T(8,128)(2,1)S(1)}, bf16[128,512]{1,0:T(8,128)(2,1)S(1)}, u32[]{:S(2)}, u32[]{:S(2)}) collective-permute-start(bf16[128,512]{1,0:T(8,128)(2,1)S(1)} %constant_dynamic-slice_fusion), channel_id=1, source_target_pairs={{0,4},{2,6},{4,0},{6,2},{8,12},{10,14},{12,8},{14,10},{16,20},{18,... | collective-permute-start | bytes 393224 | tf_op jit(solution)/shard_map/ppermute | solution.py:26
  (44 other events, 293.2 us)
Sparse Core Ops, SparseCore 0:
  21.6 48.3 all-gather.6
  72.2 27.9 all-gather.8
  102.3 81.4 all-gather.10
  185.3 63.2 all-gather.12
  250.6 63.3 all-gather.14
  316.1 63.3 all-gather.16
  381.7 68.3 reduce-scatter.6
  452.4 68.1 reduce-scatter.8
  523.0 68.1 reduce-scatter.10
  593.4 88.6 reduce-scatter.12
  684.4 48.3 reduce-scatter.14
  735.0 34.9 reduce-scatter.16
